TPU v7x, 32 devices: a whole 2x2x4 slice. The times are simulated.
32 devices in a mesh: dp: 8 (over y, x, core), tensor: 4 (over z).
Axes of the slice: x: 2, y: 2, z: 4, core: 2. Of those that a mesh axis runs over, the one named last changes fastest.
Arguments:
- x_in: bfloat16 [16384, 768], P(('dp', 'tensor')), may hold values from -6 to 6
- bucket: int32 [32], P(('dp', 'tensor')), may hold values from 0 to 1
- lengths: int32 [32, 4], P(('dp', 'tensor')), may hold values from 32 to 128, as said below
- qkv_weight: bfloat16 [2, 768, 2304], replicated, may hold values from -0.21875 to 0.21875
- out_weight: bfloat16 [2, 768, 768], replicated, may hold values from -0.875 to 0.875
- norm_gain1: float32 [2, 768], replicated, may hold values from 0.5 to 1.5
- norm_bias1: float32 [2, 768], replicated, may hold values from -1.8 to 1.8
- up_weight: bfloat16 [2, 768, 2, 3072], P(None, None, None, 'tensor'), may hold values from -0.21875 to 0.21875
- down_weight: bfloat16 [2, 3072, 768], P(None, 'tensor'), may hold values from -0.109375 to 0.109375
- norm_gain2: float32 [2, 768], replicated, may hold values from 0.5 to 1.5
- norm_bias2: float32 [2, 768], replicated, may hold values from -1.8 to 1.8
- cotangent: bfloat16 [16384, 768], P(('dp', 'tensor')), may hold values from -6 to 6
Outputs:
- activations: bfloat16 [2, 16384, 768], P(None, ('dp', 'tensor'))
- input_grad: float32 [16384, 768], P(('dp', 'tensor'))
- qkv_grad: float32 [2, 768, 2304], replicated
- out_grad: float32 [2, 768, 768], replicated
- gain1_grad: float32 [2, 768], replicated
- bias1_grad: float32 [2, 768], replicated
- up_grad: float32 [2, 768, 2, 3072], P(None, 'dp', None, 'tensor')
- down_grad: float32 [2, 3072, 768], P(None, 'tensor', 'dp')
- gain2_grad: float32 [2, 768], replicated
- bias2_grad: float32 [2, 768], replicated
Inputs may be any that keep to these rules, and one draw needn't show every extreme that they name: Every entry is a length of a short sequence; each row of lengths has an entry equal to 128. A block of bucket 1 holds one sequence whose length is the sum of its row of lengths.
All inputs are finite; a program needn't handle non-finite values.
Results may differ from a plain program's by a relative error of at most 0.033.
Values may be sent and summed in bfloat16 or wider, within the bound.
No kernel may reach another device: no remote copies, remote signals or barrier semaphores. Data moves between devices by JAX's collectives and lax.ppermute only.
A program may use at most 256 MiB of HBM per device.

v0:
```python
import jax
import jax.numpy as jnp
from jax import lax
from jax.sharding import PartitionSpec as P

HEADS = 12
HEAD_DIM = 64
SHORT = 128
LAYERS = 2


eps_norm = 1e-05
gelu_coef = 0.7978845608028654
masked_score = -1e30


def segments(bucket_one, lens, rows_dev, short_len):
    rows = jnp.arange(rows_dev, dtype=jnp.int32)
    slot = rows // short_len
    offset = rows - slot * short_len
    slots_all = jnp.arange(lens.shape[0], dtype=jnp.int32)
    slot_len = jnp.sum(jnp.where(slot[:, None] == slots_all[None, :], lens[None, :], 0), axis=1)
    total = jnp.sum(lens)
    is_long = bucket_one == 1
    real = jnp.where(is_long, rows < total, offset < slot_len)
    group = jnp.where(is_long, 0, slot)
    return jnp.where(real, group, lens.shape[0] + rows)


def alibi(rows_dev, heads):
    slopes = jnp.exp2(-8.0 * (jnp.arange(heads, dtype=jnp.float32) + 1.0) / heads)
    place = jnp.arange(rows_dev, dtype=jnp.float32)
    dist = jnp.abs(place[:, None] - place[None, :])
    return slopes[:, None, None] * dist[None, :, :]


def layer_norm(value, gain, bias):
    mean = jnp.mean(value, axis=-1, keepdims=True)
    centered = value - mean
    var = jnp.mean(centered * centered, axis=-1, keepdims=True)
    return centered * lax.rsqrt(var + eps_norm) * gain + bias


def geglu(joined):
    half = joined.shape[1] // 2
    gate = joined[:, :half]
    value = joined[:, half:]
    return 0.5 * gate * (1.0 + jnp.tanh(gelu_coef * (gate + 0.044715 * gate * gate * gate))) * value


def split_heads(qkv_low, width):
    rows = qkv_low.shape[0]
    query = qkv_low[:, :width].reshape(rows, HEADS, HEAD_DIM)
    keys = qkv_low[:, width : 2 * width].reshape(rows, HEADS, HEAD_DIM)
    values = qkv_low[:, 2 * width :].reshape(rows, HEADS, HEAD_DIM)
    return (query, keys, values)


def scores_of(query, keys, same, decay):
    raw = (
        jnp.einsum("qhe,khe->hqk", query, keys, preferred_element_type=jnp.float32)
        * HEAD_DIM ** (-0.5)
        - decay
    )
    return jnp.where(same[None, :, :], raw, masked_score)


def forward_layer(x_low, wqkv, wo, g1, b1, wup, wdown, g2, b2, same, decay):
    rows = x_low.shape[0]
    width = x_low.shape[1]
    qkv_low = jnp.dot(x_low, wqkv, preferred_element_type=jnp.float32).astype(jnp.bfloat16)
    query, keys, values = split_heads(qkv_low, width)
    scores = scores_of(query, keys, same, decay)
    top = jnp.max(scores, axis=-1, keepdims=True)
    log_total = top + jnp.log(jnp.sum(jnp.exp(scores - top), axis=-1, keepdims=True))
    probs_low = jnp.exp(scores - log_total).astype(jnp.bfloat16)
    ctx_low = (
        jnp.einsum("hqk,khe->qhe", probs_low, values, preferred_element_type=jnp.float32)
        .reshape(rows, width)
        .astype(jnp.bfloat16)
    )
    attn = jnp.dot(ctx_low, wo, preferred_element_type=jnp.float32)
    pre_first = x_low.astype(jnp.float32) + attn
    normed = layer_norm(pre_first, g1, b1)
    normed_low = normed.astype(jnp.bfloat16)
    gathered = lax.all_gather(normed_low, "tensor", axis=0, tiled=True)
    joined = jnp.dot(gathered, wup.reshape(width, -1), preferred_element_type=jnp.float32)
    act_low = geglu(joined).astype(jnp.bfloat16)
    mixed = lax.psum_scatter(
        jnp.dot(act_low, wdown, preferred_element_type=jnp.float32).astype(jnp.bfloat16),
        "tensor",
        scatter_dimension=0,
        tiled=True,
    ).astype(jnp.float32)
    pre_second = normed + mixed
    out_low = layer_norm(pre_second, g2, b2).astype(jnp.bfloat16)
    keep = (
        x_low,
        qkv_low,
        log_total,
        ctx_low,
        pre_first,
        normed_low,
        pre_second,
        gathered,
        joined,
        act_low,
    )
    return (out_low, keep)


def backward_layer(grad_out, keep, wqkv, wo, g1, b1, wup, wdown, g2, b2, same, decay):
    (
        x_low,
        qkv_low,
        log_total,
        ctx_low,
        pre_first,
        normed_low,
        pre_second,
        gathered,
        joined,
        act_low,
    ) = keep
    rows = x_low.shape[0]
    width = x_low.shape[1]
    up_flat = wup.reshape(width, -1)
    second_pull = jax.vjp(layer_norm, pre_second, g2, b2)[1]
    d_pre2, d_gain2, d_bias2 = second_pull(grad_out)
    grad_rows = lax.all_gather(d_pre2.astype(jnp.bfloat16), "tensor", axis=0, tiled=True)
    d_act = jnp.dot(grad_rows, wdown.T, preferred_element_type=jnp.float32)
    d_down = jnp.dot(act_low.T, grad_rows, preferred_element_type=jnp.float32)
    geglu_pull = jax.vjp(geglu, joined)[1]
    d_joined = geglu_pull(d_act)[0].astype(jnp.bfloat16)
    d_up = jnp.dot(gathered.T, d_joined, preferred_element_type=jnp.float32).reshape(wup.shape)
    d_normed = d_pre2 + lax.psum_scatter(
        jnp.dot(d_joined, up_flat.T, preferred_element_type=jnp.float32).astype(jnp.bfloat16),
        "tensor",
        scatter_dimension=0,
        tiled=True,
    ).astype(jnp.float32)
    first_pull = jax.vjp(layer_norm, pre_first, g1, b1)[1]
    d_pre1, d_gain1, d_bias1 = first_pull(d_normed)
    d_attn_low = d_pre1.astype(jnp.bfloat16)
    d_wo = jnp.dot(ctx_low.T, d_attn_low, preferred_element_type=jnp.float32)
    d_ctx = (
        jnp.dot(d_attn_low, wo.T, preferred_element_type=jnp.float32)
        .astype(jnp.bfloat16)
        .reshape(rows, HEADS, HEAD_DIM)
    )
    query, keys, values = split_heads(qkv_low, width)
    probs = jnp.exp(scores_of(query, keys, same, decay) - log_total)
    probs_low = probs.astype(jnp.bfloat16)
    d_values = jnp.einsum("hqk,qhe->khe", probs_low, d_ctx, preferred_element_type=jnp.float32)
    d_probs = jnp.einsum("qhe,khe->hqk", d_ctx, values, preferred_element_type=jnp.float32)
    d_scores = (probs * (d_probs - jnp.sum(probs * d_probs, axis=-1, keepdims=True))).astype(
        jnp.bfloat16
    )
    d_query = jnp.einsum(
        "hqk,khe->qhe", d_scores, keys, preferred_element_type=jnp.float32
    ) * HEAD_DIM ** (-0.5)
    d_keys = jnp.einsum(
        "hqk,qhe->khe", d_scores, query, preferred_element_type=jnp.float32
    ) * HEAD_DIM ** (-0.5)
    d_qkv = jnp.concatenate(
        [d_query.reshape(rows, width), d_keys.reshape(rows, width), d_values.reshape(rows, width)],
        axis=1,
    ).astype(jnp.bfloat16)
    d_wqkv = jnp.dot(x_low.T, d_qkv, preferred_element_type=jnp.float32)
    d_input = d_pre1 + jnp.dot(d_qkv, wqkv.T, preferred_element_type=jnp.float32)
    return (d_input, d_wqkv, d_wo, d_gain1, d_bias1, d_up, d_down, d_gain2, d_bias2)


def shards(
    x_in,
    bucket,
    lengths,
    qkv_weight,
    out_weight,
    norm_gain1,
    norm_bias1,
    up_weight,
    down_weight,
    norm_gain2,
    norm_bias2,
    cotangent,
):
    rows = x_in.shape[0]
    seg = segments(bucket[0], lengths[0], rows, SHORT)
    same = seg[:, None] == seg[None, :]
    decay = alibi(rows, HEADS)
    layer_in = x_in
    outputs = []
    kept = []
    for layer in range(LAYERS):
        layer_in, keep = forward_layer(
            layer_in,
            qkv_weight[layer],
            out_weight[layer],
            norm_gain1[layer],
            norm_bias1[layer],
            up_weight[layer],
            down_weight[layer],
            norm_gain2[layer],
            norm_bias2[layer],
            same,
            decay,
        )
        outputs.append(layer_in)
        kept.append(keep)
    grad = cotangent.astype(jnp.float32)
    found = [None] * LAYERS
    for layer in reversed(range(LAYERS)):
        grad, d_wqkv, d_wo, d_gain1, d_bias1, d_up, d_down, d_gain2, d_bias2 = backward_layer(
            grad,
            kept[layer],
            qkv_weight[layer],
            out_weight[layer],
            norm_gain1[layer],
            norm_bias1[layer],
            up_weight[layer],
            down_weight[layer],
            norm_gain2[layer],
            norm_bias2[layer],
            same,
            decay,
        )
        d_wqkv, d_wo, d_gain1, d_bias1, d_gain2, d_bias2 = lax.psum(
            (d_wqkv, d_wo, d_gain1, d_bias1, d_gain2, d_bias2), ("dp", "tensor")
        )
        d_up, d_down = (
            lax.psum_scatter(
                d_up.astype(jnp.bfloat16), "dp", scatter_dimension=0, tiled=True
            ).astype(jnp.float32),
            lax.psum_scatter(
                d_down.astype(jnp.bfloat16), "dp", scatter_dimension=1, tiled=True
            ).astype(jnp.float32),
        )
        found[layer] = (d_wqkv, d_wo, d_gain1, d_bias1, d_up, d_down, d_gain2, d_bias2)
    stacked = [jnp.stack([found[layer][index] for layer in range(LAYERS)]) for index in range(8)]
    qkv_grad, out_grad, gain1_grad, bias1_grad, up_grad, down_grad, gain2_grad, bias2_grad = stacked
    activations = jnp.stack(outputs)
    return (
        activations,
        grad,
        qkv_grad,
        out_grad,
        gain1_grad,
        bias1_grad,
        up_grad,
        down_grad,
        gain2_grad,
        bias2_grad,
    )


def solution(mesh):
    in_specs = (
        P(("dp", "tensor"), None),
        P(("dp", "tensor")),
        P(("dp", "tensor"), None),
        P(),
        P(),
        P(),
        P(),
        P(None, None, None, "tensor"),
        P(None, "tensor", None),
        P(),
        P(),
        P(("dp", "tensor"), None),
    )
    out_specs = (
        P(None, ("dp", "tensor"), None),
        P(("dp", "tensor"), None),
        P(),
        P(),
        P(),
        P(),
        P(None, "dp", None, "tensor"),
        P(None, "tensor", "dp"),
        P(),
        P(),
    )
    return jax.shard_map(shards, mesh=mesh, in_specs=in_specs, out_specs=out_specs, check_vma=False)
```

profile of v0, /device:TPU:0, one launch (start us, length us, event | category | flops | bytes accessed | tf_op | source)
XLA Modules:
  0.0 1206.9 jit_solution(10613801410674038543)
XLA Ops:
  12.0 4.2 convolution_convert_fusion.1
  17.3 5.0 fusion.103
  24.3 2.6 copy-done
  26.9 2.1 fusion.42
  32.5 7.0 fusion.100
  39.5 1.9 copy.111
  41.4 57.2 %all-gather.5.cloned.1.call-done = bf16[2048,768]{1,0:T(8,128)(2,1)} async-done(((bf16[512,768]{1,0:T(8,128)(2,1)}), bf16[2048,768]{1,0:T(8,128)(2,1)}) %all-gather.5.cloned.1.call-update) | async-done | bytes 3145744 | tf_op jit(solution)/shard_map/all_gather | solution.py:86
  98.6 7.7 fusion.107
  106.4 2.2 multiply_convert_fusion.3
  108.6 2.8 copy-done.8
  113.1 3.9 convolution_convert_fusion.5
  117.8 58.3 %reduce-scatter.7.cloned.1.call-done = bf16[512,768]{1,0:T(8,128)(2,1)} async-done(((bf16[2048,768]{1,0:T(8,128)(2,1)}), bf16[512,768]{1,0:T(8,128)(2,1)}) %reduce-scatter.7.cloned.1.call-update) | async-done | bytes 786448 | tf_op jit(solution)/shard_map/reduce_scatter | solution.py:89
  178.1 4.1 convolution_convert_fusion
  187.6 4.9 fusion.105
  194.4 2.6 copy-done.1
  197.0 2.1 fusion.48
  201.9 3.5 copy.112
  205.4 60.0 %all-gather.7.cloned.1.call-done = bf16[2048,768]{1,0:T(8,128)(2,1)} async-done(((bf16[512,768]{1,0:T(8,128)(2,1)}), bf16[2048,768]{1,0:T(8,128)(2,1)}) %all-gather.7.cloned.1.call-update) | async-done | bytes 3145744 | tf_op jit(solution)/shard_map/all_gather | solution.py:86
  265.3 7.7 fusion.108
  273.1 2.2 multiply_convert_fusion.2
  275.3 2.8 copy-done.9
  279.7 3.9 convolution_convert_fusion.4
  283.7 59.0 %reduce-scatter.9.cloned.1.call-done = bf16[512,768]{1,0:T(8,128)(2,1)} async-done(((bf16[2048,768]{1,0:T(8,128)(2,1)}), bf16[512,768]{1,0:T(8,128)(2,1)}) %reduce-scatter.9.cloned.1.call-update) | async-done | bytes 786448 | tf_op jit(solution)/shard_map/reduce_scatter | solution.py:89
  350.1 63.4 %all-gather.9.cloned.1.call-done = bf16[2048,768]{1,0:T(8,128)(2,1)} async-done(((bf16[512,768]{1,0:T(8,128)(2,1)}), bf16[2048,768]{1,0:T(8,128)(2,1)}) %all-gather.9.cloned.1.call-update) | async-done | bytes 3145744 | tf_op jit(solution)/shard_map/all_gather | solution.py:130
  413.6 12.0 fusion.25
  425.6 2.6 copy-done.79
  428.2 2.0 copy-done.80
  430.2 6.4 convolution_convert_fusion.7
  436.7 59.0 %reduce-scatter.11.cloned.1.call-done = bf16[512,768]{1,0:T(8,128)(2,1)} async-done(((bf16[2048,768]{1,0:T(8,128)(2,1)}), bf16[512,768]{1,0:T(8,128)(2,1)}) %reduce-scatter.11.cloned.1.call-update) | async-done | bytes 786448 | tf_op jit(solution)/shard_map/reduce_scatter | solution.py:136
  495.7 3.2 multiply_reduce_fusion.3
  502.1 7.7 fusion.51
  509.8 9.2 multiply_reduce_fusion.1
  519.0 6.9 multiply_convert_fusion.1
  526.0 2.0 multiply_convert_fusion.6
  531.2 2.6 multiply_reduce_fusion.2
  536.6 63.6 %all-gather.11.cloned.1.call-done = bf16[2048,768]{1,0:T(8,128)(2,1)} async-done(((bf16[512,768]{1,0:T(8,128)(2,1)}), bf16[2048,768]{1,0:T(8,128)(2,1)}) %all-gather.11.cloned.1.call-update) | async-done | bytes 3145744 | tf_op jit(solution)/shard_map/all_gather | solution.py:130
  600.3 12.6 %fusion.24 = (f32[2048,768]{1,0:T(8,128)S(1)}, f32[2048,768]{1,0:T(8,128)S(1)}) fusion(f32[2048,1536]{1,0:T(8,128)} %copy-done.8, bf16[2048,768]{1,0:T(8,128)(2,1)} %all-gather.11.cloned.1.call-done, bf16[2,768,768]{2,1,0:T(8,128)(2,1)} %param.20), kind=kOutput, calls=%fused_computation.69 | convolution fusion | flops 2456813568 | bytes 29491200 | tf_op jit(solution)/shard_map/dot_general | solution.py:131
  612.8 2.7 copy-done.81
  615.5 2.1 copy-done.82
  617.6 6.4 convolution_convert_fusion.6
  624.1 6.5 convolution_convert_fusion.8
  630.9 12.0 convolution_convert_fusion.2
  642.9 6.0 convert_element_type.181
  648.9 6.6 convolution_convert_fusion.9
  655.8 3.6 convolution_bitcast_fusion.2
  659.4 5.0 convolution_bitcast_fusion
  664.5 9.3 convolution_convert_fusion.3
  673.7 6.0 convert_element_type.179
  679.8 3.3 reduce-scatter.13.cloned.1.call-done
  683.1 2.6 multiply_reduce_fusion.4
  691.0 10.9 multiply_reduce_fusion
  704.0 7.0 multiply_convert_fusion
  711.1 2.3 convolution_bitcast_fusion.3
  713.4 2.0 multiply_convert_fusion.4
  716.6 2.0 fusion.45
  719.5 5.0 convolution_bitcast_fusion.1
  728.1 35.8 %reduce-scatter.15.cloned.1.call-done = bf16[768,96]{0,1:T(8,128)(2,1)} async-done(((bf16[768,768]{0,1:T(8,128)(2,1)}), bf16[768,96]{0,1:T(8,128)(2,1)}) %reduce-scatter.15.cloned.1.call-update) | async-done | bytes 147472 | tf_op jit(solution)/shard_map/reduce_scatter | solution.py:235
  765.8 88.5 %all-reduce.14.cloned.1.call-done = (bf16[768,2,768]{2,1,0:T(2,128)(2,1)}, bf16[768,2,768]{2,1,0:T(2,128)(2,1)}) async-done(((bf16[768,2,768]{2,1,0:T(2,128)(2,1)}, bf16[768,2,768]{2,1,0:T(2,128)(2,1)}), (bf16[768,2,768]{2,1,0:T(2,128)(2,1)}, bf16[768,2,768]{2,1,0:T(2,128)(2,1)})) %all-reduce.14.cloned.1.call-update) | async-done | bytes 4718608
  858.5 41.8 %all-reduce.6 = (f32[1,768]{1,0:T(1,128)S(1)}, f32[1,768]{1,0:T(1,128)S(1)}, f32[1,768]{1,0:T(1,128)S(1)}, f32[1,768]{1,0:T(1,128)S(1)}, f32[1,768]{1,0:T(1,128)...) all-reduce(f32[1,768]{1,0:T(1,128)S(1)} %stack.101, ...), channel_id=1, replica_groups=mesh['dp'=8,'tensor'=4] {'dp','tensor'}, use_global_device_ids=true, to_apply=%region_35.36 | all-reduce | flops 6144 | bytes 49152 | tf_op jit(solution)/shard_map/psum | solution.py:228
  902.7 5.5 add_add_fusion.4
  908.2 260.8 %all-reduce.12.cloned.1.call-done = (f32[1,768,2304]{1,2,0:T(8,128)}, f32[1,768,2304]{1,2,0:T(8,128)}, f32[1,768,768]{2,1,0:T(8,128)}, f32[1,768,768]{2,1,0:T(8,128)}) async-done(((f32[1,768,2304]{1,2,0:T(8,128)}, f32[1,768,2304]{1,2,0:T(8,128)}, f32[1,768,768]{2,1,0:T(8,128)}, f32[1,768,768]{2,1,0:T(8,128)}), (f32[1,768,2304]{1,2,0:T(8,128)}, f32[1,768,2304]{1,2,0:T(8,128)}, f32[1,768,768]{2,1,0:T(8,128)}, ...) | async-done | bytes 18874384 | tf_op jit(solution)/shard_map/psum | solution.py:228
  1169.0 11.0 pad_maximum_fusion
  1179.9 15.4 %copy.101 = f32[2,768,2304]{2,1,0:T(8,128)} copy(f32[2,768,2304]{1,2,0:T(8,128)} %pad_maximum_fusion) | data formatting | bytes 28311552
  1195.4 4.2 pad_maximum_fusion.1
  (286 shorter events, 64.2 us)
Async XLA Ops:
  7.2 91.5 %all-gather.5.cloned.1.call-start = ((), (), s32[]{:S(2)}) async-start(), calls=%async_computation.6 | async-start | bytes 3932160 | tf_op jit(solution)/shard_map/all_gather | solution.py:86
  16.7 5.7 copy-start.14
  17.0 5.4 copy-start.32
  17.3 7.0 copy-start.10
  22.3 4.5 copy-start
  24.3 4.7 copy-start.42
  29.9 146.2 %copy-start.2 = (f32[512,768]{1,0:T(8,128)}, f32[512,768]{1,0:T(8,128)S(1)}, u32[]{:S(2)}) copy-start(f32[512,768]{1,0:T(8,128)S(1)} %get-tuple-element.112) | copy-start | bytes 4718596
  30.0 146.2 %copy-start.53 = (f32[512]{0:T(512)}, f32[512]{0:T(512)S(1)}, u32[]{:S(2)}) copy-start(f32[512]{0:T(512)S(1)} %broadcast_multiply_fusion.3) | copy-start | bytes 6148
  31.0 145.1 %copy-start.55 = (f32[512]{0:T(512)}, f32[512]{0:T(512)S(1)}, u32[]{:S(2)}) copy-start(f32[512]{0:T(512)S(1)} %fusion.80) | copy-start | bytes 6148
  31.1 145.1 %copy-start.51 = (f32[768]{0:T(1024)}, f32[768]{0:T(1024)S(1)}, u32[]{:S(2)}) copy-start(f32[768]{0:T(1024)S(1)} %get-tuple-element.122) | copy-start | bytes 9220
  32.3 143.8 %reduce-scatter.7.cloned.1.call-start = ((), (), s32[]{:S(2)}) async-start(), calls=%async_computation.7 | async-start | bytes 3932160 | tf_op jit(solution)/shard_map/reduce_scatter | solution.py:89
  106.4 5.0 copy-start.8
  106.4 6.7 copy-start.70
  117.0 148.3 %all-gather.7.cloned.1.call-start = ((), (), s32[]{:S(2)}) async-start(), calls=%async_computation.8 | async-start | bytes 3932160 | tf_op jit(solution)/shard_map/all_gather | solution.py:86
  117.8 81.4 %copy-start.59 = (f32[768]{0:T(1024)}, f32[768]{0:T(1024)S(1)}, u32[]{:S(2)}) copy-start(f32[768]{0:T(1024)S(1)} %get-tuple-element.65) | copy-start | bytes 9220
  185.0 7.6 copy-start.16
  187.6 6.9 copy-start.12
  192.5 4.5 copy-start.1
  201.7 141.1 %reduce-scatter.9.cloned.1.call-start = ((), (), s32[]{:S(2)}) async-start(), calls=%async_computation.9 | async-start | bytes 3932160 | tf_op jit(solution)/shard_map/reduce_scatter | solution.py:89
  273.1 5.0 copy-start.9
  273.1 6.6 copy-start.71
  283.7 129.9 %all-gather.9.cloned.1.call-start = ((), (), s32[]{:S(2)}) async-start(), calls=%async_computation.10 | async-start | bytes 3932160 | tf_op jit(solution)/shard_map/all_gather | solution.py:130
  349.9 145.8 %reduce-scatter.11.cloned.1.call-start = ((), (), s32[]{:S(2)}) async-start(), calls=%async_computation.11 | async-start | bytes 3932160 | tf_op jit(solution)/shard_map/reduce_scatter | solution.py:136
  413.6 16.6 %copy-start.40 = (bf16[96,8,2,768]{3,1,2,0:T(8,128)(2,1)S(1)}, bf16[96,8,2,768]{3,1,2,0:T(8,128)(2,1)}, u32[]{:S(2)}) copy-start(bf16[96,8,2,768]{3,1,2,0:T(8,128)(2,1)} %copy.112) | copy-start | bytes 7077892
  425.6 4.6 copy-start.80
  436.6 163.6 %all-gather.11.cloned.1.call-start = ((), (), s32[]{:S(2)}) async-start(), calls=%async_computation.12 | async-start | bytes 3932160 | tf_op jit(solution)/shard_map/all_gather | solution.py:130
  495.7 3.2 copy-start.7
  495.7 3.2 copy-start.29
  502.1 7.7 copy-start.13
  502.1 16.9 %slice-start.3 = ((s8[12582912]{0:T(1024)(128)(4,1)}), s8[4194304]{0:T(1024)(128)(4,1)S(1)}, s32[]{:S(2)}) async-start(s8[12582912]{0:T(1024)(128)(4,1)} %bitcast.151), calls=%async_computation.21 | async-start | bytes 8388608
  502.1 16.9 %slice-start.4 = ((s8[12582912]{0:T(1024)(128)(4,1)}), s8[4194304]{0:T(1024)(128)(4,1)S(1)}, s32[]{:S(2)}) async-start(s8[12582912]{0:T(1024)(128)(4,1)} %bitcast.151), calls=%async_computation.22 | async-start | bytes 8388608
  509.8 9.2 slice-start.5
  519.0 6.9 copy-start.34
  526.0 3.2 slice-start.6
  529.2 4.6 copy-start.37
  536.6 146.5 %reduce-scatter.13.cloned.1.call-start = ((), (), s32[]{:S(2)}) async-start(), calls=%async_computation.13 | async-start | bytes 3932160 | tf_op jit(solution)/shard_map/reduce_scatter | solution.py:136
  600.3 17.3 %copy-start.39 = (bf16[96,8,2,768]{3,1,2,0:T(8,128)(2,1)S(1)}, bf16[96,8,2,768]{3,1,2,0:T(8,128)(2,1)}, u32[]{:S(2)}) copy-start(bf16[96,8,2,768]{3,1,2,0:T(8,128)(2,1)} %copy.111) | copy-start | bytes 7077892
  612.8 4.8 copy-start.82
  624.0 104.1 %reduce-scatter.17.cloned.1.call-start = ((), (), s32[]{:S(2)}) async-start(), calls=%async_computation.15 | async-start | bytes 1327104 | tf_op jit(solution)/shard_map/reduce_scatter | solution.py:235
  630.6 133.3 %reduce-scatter.15.cloned.1.call-start = ((), (), s32[]{:S(2)}) async-start(), calls=%async_computation.14 | async-start | bytes 1327104 | tf_op jit(solution)/shard_map/reduce_scatter | solution.py:235
  655.5 3.9 copy-start.60
  655.5 198.8 %all-reduce.14.cloned.1.call-start = ((), (), s32[]{:S(2)}) async-start(), calls=%async_computation.17 | async-start | bytes 9437184
  655.8 3.6 copy-start.38
  655.8 3.6 copy-start.47
  655.8 3.6 copy-start.50
  655.8 8.6 slice-start.8
  659.4 5.0 copy-start.69
  659.4 5.0 slice-start.9
  679.7 3.4 copy-start.3
  679.7 3.4 copy-start.52
  679.7 3.4 copy-start.54
  679.7 3.4 copy-start.56
  679.8 6.0 copy-start.58
  679.8 489.2 %all-reduce.12.cloned.1.call-start = ((), (), s32[]{:S(2)}) async-start(), calls=%async_computation.16 | async-start | bytes 37748736 | tf_op jit(solution)/shard_map/psum | solution.py:228
  690.9 11.0 slice-start
  691.0 11.6 slice-start.1
  691.0 13.0 %slice-start.2 = ((s8[12582912]{0:T(1024)(128)(4,1)}), s8[4194304]{0:T(1024)(128)(4,1)S(1)}, s32[]{:S(2)}) async-start(s8[12582912]{0:T(1024)(128)(4,1)} %bitcast.149), calls=%async_computation.20 | async-start | bytes 8388608
  704.0 7.0 copy-start.19
  704.0 7.0 copy-start.26
  715.4 3.2 copy-start.48
  728.0 174.6 %copy-start.20 = (f32[512,768]{1,0:T(8,128)S(1)}, f32[512,768]{1,0:T(8,128)}, u32[]{:S(2)}) copy-start(f32[512,768]{1,0:T(8,128)} %copy-done.18) | copy-start | bytes 4718596
  728.0 174.6 %copy-start.36 = (bf16[12,64,512]{2,1,0:T(8,128)(2,1)S(1)}, bf16[12,64,512]{2,1,0:T(8,128)(2,1)}, u32[]{:S(2)}) copy-start(bf16[12,64,512]{2,1,0:T(8,128)(2,1)} %copy-done.35) | copy-start | bytes 2359300
  728.0 174.6 %copy-start.45 = (bf16[12,64,512]{2,1,0:T(8,128)(2,1)S(1)}, bf16[12,64,512]{2,1,0:T(8,128)(2,1)}, u32[]{:S(2)}) copy-start(bf16[12,64,512]{2,1,0:T(8,128)(2,1)} %copy-done.44) | copy-start | bytes 2359300
  1179.9 15.4 %copy-start.41 = (f32[1,768,768]{2,1,0:T(8,128)S(1)}, f32[1,768,768]{2,1,0:T(8,128)}, u32[]{:S(2)}) copy-start(f32[1,768,768]{2,1,0:T(8,128)} %get-tuple-element.80) | copy-start | bytes 7077892
  (41 other events, 76.3 us)
Sparse Core Ops, SparseCore 0:
  32.4 66.1 all-gather.4
  117.2 58.8 reduce-scatter.6
  201.8 63.5 all-gather.6
  283.8 58.8 reduce-scatter.8
  350.0 63.5 all-gather.8
  436.7 58.8 reduce-scatter.10
  536.7 63.5 all-gather.10
  624.2 58.8 reduce-scatter.12
  686.9 36.8 reduce-scatter.16
  727.2 36.7 reduce-scatter.14
  767.3 86.9 all-reduce.13
  862.3 306.5 all-reduce.11
where the time goes:
time: 1220 us; the launch traced here: 1210 us
  waiting for transfers between devices  809 us (66%)
  matrix products  182 us (15%)
  local copies, waits for them, and re-layouts  85.4 us (7%)
  other arithmetic  69 us (6%)
  blocking collectives  41.8 us (3%)
  between operations  17.3 us (1%)
    psum x1, waiting for transfers between devices, shards(): lax.psum((d_wqkv, d_wo, d_gain1, d_bias1, d_gain2, d_bias2), ('dp', 'tens...  261 us
    all_gather x2, waiting for transfers between devices, backward_layer(): lax.all_gather(d_pre2.astype(jnp.bfloat16), 'tensor', axis=0, tiled=True)  127 us
    reduce_scatter x2, waiting for transfers between devices, forward_layer(): lax.psum_scatter(jnp.dot(act_low, wdown, preferred_element_type=jnp.float...  117 us
    all_gather x2, waiting for transfers between devices, forward_layer(): gathered = lax.all_gather(normed_low, 'tensor', axis=0, tiled=True)  117 us
    unnamed x13, waiting for transfers between devices  88.7 us
    reduce_scatter x2, waiting for transfers between devices, backward_layer(): lax.psum_scatter(jnp.dot(d_joined, up_flat.T, preferred_element_type=jnp....  62.3 us
    unnamed x190, local copies, waits for them, and re-layouts  56 us
    psum x1, blocking collectives, shards(): lax.psum((d_wqkv, d_wo, d_gain1, d_bias1, d_gain2, d_bias2), ('dp', 'tens...  41.8 us
  transfers between devices with their start and end apart: 12, of which 11 were waited for; matrix products, arithmetic and copies ran while one was open for 10% of the time, Pallas kernels for 0%

commit v1 on v0

v1 whole, which is shorter than its diff:
```python
import functools

import jax
import jax.numpy as jnp
from jax import lax
from jax.experimental import pallas as pl
from jax.experimental.pallas import tpu as pltpu
from jax.sharding import PartitionSpec as P

HEADS = 12
HEAD_DIM = 64
SHORT = 128
LAYERS = 2

eps_norm = 1e-05
gelu_coef = 0.7978845608028654
masked_score = -1e30
bf16 = jnp.bfloat16
f32 = jnp.float32
BOTH = ("dp", "tensor")


def segments(bucket_one, lens, rows_dev, short_len):
    rows = jnp.arange(rows_dev, dtype=jnp.int32)
    slot = rows // short_len
    offset = rows - slot * short_len
    slots_all = jnp.arange(lens.shape[0], dtype=jnp.int32)
    slot_len = jnp.sum(jnp.where(slot[:, None] == slots_all[None, :], lens[None, :], 0), axis=1)
    total = jnp.sum(lens)
    is_long = bucket_one == 1
    real = jnp.where(is_long, rows < total, offset < slot_len)
    group = jnp.where(is_long, 0, slot)
    return jnp.where(real, group, lens.shape[0] + rows)


def alibi(rows_dev, heads):
    slopes = jnp.exp2(-8.0 * (jnp.arange(heads, dtype=f32) + 1.0) / heads)
    place = jnp.arange(rows_dev, dtype=f32)
    dist = jnp.abs(place[:, None] - place[None, :])
    return slopes[:, None, None] * dist[None, :, :]


def layer_norm(value, gain, bias):
    mean = jnp.mean(value, axis=-1, keepdims=True)
    centered = value - mean
    var = jnp.mean(centered * centered, axis=-1, keepdims=True)
    return centered * lax.rsqrt(var + eps_norm) * gain + bias


def geglu(joined):
    half = joined.shape[1] // 2
    gate = joined[:, :half]
    value = joined[:, half:]
    return 0.5 * gate * (1.0 + jnp.tanh(gelu_coef * (gate + 0.044715 * gate * gate * gate))) * value


def split_heads(qkv_low, width):
    rows = qkv_low.shape[0]
    query = qkv_low[:, :width].reshape(rows, HEADS, HEAD_DIM)
    keys = qkv_low[:, width : 2 * width].reshape(rows, HEADS, HEAD_DIM)
    values = qkv_low[:, 2 * width :].reshape(rows, HEADS, HEAD_DIM)
    return (query, keys, values)


def scores_of(query, keys, same, decay):
    raw = (
        jnp.einsum("qhe,khe->hqk", query, keys, preferred_element_type=f32) * HEAD_DIM ** (-0.5)
        - decay
    )
    return jnp.where(same[None, :, :], raw, masked_score)


def dot(a, b):
    return jnp.dot(a, b, preferred_element_type=f32)


class Net:
    def __init__(self, mesh):
        self.n_dp = mesh.shape["dp"]
        self.n_t = mesh.shape["tensor"]

    def flip(self, value, bit):
        return lax.ppermute(value, "dp", [(i, i ^ bit) for i in range(self.n_dp)])

    def shift(self, value, step):
        n = self.n_t
        return lax.ppermute(value, "tensor", [(i, (i + step) % n) for i in range(n)])


COLOURS = ((2, 4), (4, 2))


def order_of(colour):
    one, two = COLOURS[colour]
    return [0, one, two, one ^ two]


def fold_order(colour):
    one, two = COLOURS[colour]
    return [0, two, one, one ^ two]


class Line:
    def __init__(self):
        self.last = None

    def after(self, value):
        if self.last is None:
            return value
        return lax.optimization_barrier((value, self.last))[0]

    def run(self, call, first, *rest):
        out = call(self.after(first), *rest)
        self.last = out[0] if isinstance(out, (tuple, list)) else out
        return out


class Gather:
    def __init__(self, net, line, slices):
        self.net, self.line = net, line
        half = slices[0].shape[0] // 2
        self.held = [
            jnp.stack([line.after(one)[c * half : (c + 1) * half] for one in slices])[None]
            for c in range(2)
        ]
        self.got = [net.flip(self.held[c], COLOURS[c][0]) for c in range(2)]

    def join(self):
        return [
            jnp.concatenate([self.held[c], self.line.after(self.got[c])], axis=0) for c in range(2)
        ]

    def second(self):
        self.held = self.join()
        self.got = [self.net.flip(self.held[c], COLOURS[c][1]) for c in range(2)]

    def core(self):
        self.held = self.join()
        self.got = [self.net.flip(self.held[c], 1) for c in range(2)]

    def pieces(self):
        return [one for c in range(2) for one in (self.held[c], self.got[c])]


VMEM_SPEC = pl.BlockSpec(memory_space=pltpu.VMEM)
ANY_SPEC = pl.BlockSpec(memory_space=pl.ANY)
SMEM_SPEC = pl.BlockSpec(memory_space=pltpu.SMEM)
NN = (((1,), (0,)), ((), ()))
NT = (((1,), (1,)), ((), ()))
TN = (((0,), (0,)), ((), ()))


def mm(a, b, dims=NN):
    return lax.dot_general(a, b, dims, preferred_element_type=f32)


def params(mib):
    return pltpu.CompilerParams(vmem_limit_bytes=mib << 20)


def cost(flops, nbytes):
    return pl.CostEstimate(flops=int(flops), transcendentals=0, bytes_accessed=int(nbytes))


def shape(dims, kind):
    return jax.ShapeDtypeStruct(dims, kind)


def normed_of(value):
    mean = jnp.mean(value, axis=-1, keepdims=True)
    centered = value - mean
    var = jnp.mean(centered * centered, axis=-1, keepdims=True)
    rstd = lax.rsqrt(var + eps_norm)
    return centered * rstd, rstd


def norm_back(grad, xhat, rstd, gain):
    scaled = grad * gain
    first = jnp.mean(scaled, axis=-1, keepdims=True)
    second = jnp.mean(scaled * xhat, axis=-1, keepdims=True)
    return rstd * (scaled - first - xhat * second)


def attn_fwd_kernel(slopes, x_ref, wqkv_ref, wo_ref, g_ref, b_ref, dist_ref, *outs):
    qkv_ref, lse_ref, ctx_ref, ctx_t_ref, pre_ref, hb_ref, hb_t_ref = outs
    rows, width = x_ref.shape
    x = x_ref[...]
    for c in range(3):
        cols = pl.ds(c * width, width)
        qkv_ref[:, cols] = mm(x, wqkv_ref[0, :, cols]).astype(bf16)
    lse_ref[...] = jnp.zeros_like(lse_ref)
    tile = 128

    def pair(p, _):
        def at(c):
            return pl.ds(pl.multiple_of(c * width + p * 128, 128), 128)

        key, val = qkv_ref[:, at(1)], qkv_ref[:, at(2)]
        lane = lax.broadcasted_iota(jnp.int32, (tile, 128), 1)
        for r in range(rows // tile):
            here = pl.ds(r * tile, tile)
            query = qkv_ref[here, at(0)] * bf16(HEAD_DIM ** (-0.5))
            dist = dist_ref[here, :]
            found = []
            for side in range(2):
                mine = (lane < HEAD_DIM) == (side == 0)
                s = mm(jnp.where(mine, query, bf16(0)), key, NT) - slopes[2 * p + side] * dist
                top = jnp.max(s, axis=-1, keepdims=True)
                e = jnp.exp(s - top)
                total = jnp.sum(e, axis=-1, keepdims=True)
                lse = top + jnp.log(total)
                lse_ref[here, :] += jnp.where(lane == 2 * p + side, lse, 0.0)
                found.append(mm((e * (1.0 / total)).astype(bf16), val))
            ctx_ref[here, at(0)] = jnp.where(lane < HEAD_DIM, found[0], found[1]).astype(bf16)
        return 0

    lax.fori_loop(0, width // 128, pair, 0)
    ctx = ctx_ref[...]
    ctx_t_ref[...] = ctx.T
    pre = x.astype(f32) + mm(ctx, wo_ref[0])
    pre_ref[...] = pre
    xhat, _ = normed_of(pre)
    hb = (xhat * g_ref[...] + b_ref[...]).astype(bf16)
    hb_ref[...] = hb
    hb_t_ref[...] = hb.T


def slopes_of():
    steps = jnp.arange(HEADS, dtype=f32)
    return jnp.exp2(-8.0 * (steps + 1.0) / HEADS)


def of_layer(weight, layer):
    return pl.BlockSpec((1,) + weight.shape[1:], lambda i: (layer,) + (0,) * (weight.ndim - 1))


def attn_fwd(layer, x, wqkv, wo, gain, bias, dist, slopes):
    rows, width = x.shape
    return pl.pallas_call(
        attn_fwd_kernel,
        name="attn_fwd",
        grid=(1,),
        out_shape=(
            shape((rows, 3 * width), bf16),
            shape((rows, 128), f32),
            shape((rows, width), bf16),
            shape((width, rows), bf16),
            shape((rows, width), f32),
            shape((rows, width), bf16),
            shape((width, rows), bf16),
        ),
        in_specs=[SMEM_SPEC, VMEM_SPEC, of_layer(wqkv, layer), of_layer(wo, layer)]
        + [VMEM_SPEC] * 3,
        out_specs=(VMEM_SPEC,) * 7,
        compiler_params=params(40),
        cost_estimate=cost(2 * rows * width * width * 8, 16 << 20),
    )(slopes, x, wqkv, wo, gain[None], bias[None], dist)


def attn_bwd_kernel(slopes, dab_ref, qkv_ref, lse_ref, wo_ref, dist_ref, out_ref, *scratch):
    dctx_ref, p_ref, ds_ref = scratch
    rows, width = dab_ref.shape
    scale = HEAD_DIM ** (-0.5)
    dctx_ref[...] = mm(dab_ref[...], wo_ref[0], NT).astype(bf16)
    tile = 128

    def pair(p, _):
        def at(c):
            return pl.ds(pl.multiple_of(c * width + p * 128, 128), 128)

        key, val, query = qkv_ref[:, at(1)], qkv_ref[:, at(2)], qkv_ref[:, at(0)]
        dctx = dctx_ref[:, at(0)]
        lane = lax.broadcasted_iota(jnp.int32, (tile, 128), 1)
        wide = lax.broadcasted_iota(jnp.int32, (rows, 128), 1)
        d_q, d_k, d_v = [], [], []
        for side in range(2):
            mine = (lane < HEAD_DIM) == (side == 0)
            for r in range(rows // tile):
                here = pl.ds(r * tile, tile)
                q = jnp.where(mine, qkv_ref[here, at(0)] * bf16(scale), bf16(0))
                dc = jnp.where(mine, dctx_ref[here, at(0)], bf16(0))
                lse = jnp.sum(
                    jnp.where(lane == 2 * p + side, lse_ref[here, :], 0.0), axis=-1, keepdims=True
                )
                s = mm(q, key, NT) - slopes[2 * p + side] * dist_ref[here, :]
                prob = jnp.exp(s - lse)
                d_prob = mm(dc, val, NT)
                mean = jnp.sum(prob * d_prob, axis=-1, keepdims=True)
                p_ref[here, :] = prob.astype(bf16)
                ds_ref[here, :] = (prob * (d_prob - mean)).astype(bf16)
            d_s = ds_ref[...]
            d_q.append(mm(d_s, key))
            d_k.append(mm(d_s, query, TN))
            d_v.append(mm(p_ref[...], dctx, TN))
        low = wide < HEAD_DIM
        out_ref[:, at(0)] = (jnp.where(low, d_q[0], d_q[1]) * scale).astype(bf16)
        out_ref[:, at(1)] = (jnp.where(low, d_k[0], d_k[1]) * scale).astype(bf16)
        out_ref[:, at(2)] = jnp.where(low, d_v[0], d_v[1]).astype(bf16)
        return 0

    lax.fori_loop(0, width // 128, pair, 0)


def attn_bwd(layer, dab, qkv, lse, wo, dist, slopes):
    rows, width = dab.shape
    return pl.pallas_call(
        attn_bwd_kernel,
        name="attn_bwd",
        grid=(1,),
        out_shape=shape((rows, 3 * width), bf16),
        in_specs=[SMEM_SPEC] + [VMEM_SPEC] * 3 + [of_layer(wo, layer), VMEM_SPEC],
        out_specs=VMEM_SPEC,
        scratch_shapes=[
            pltpu.VMEM((rows, width), bf16),
            pltpu.VMEM((rows, rows), bf16),
            pltpu.VMEM((rows, rows), bf16),
        ],
        compiler_params=params(40),
        cost_estimate=cost(2 * rows * width * width * 12, 12 << 20),
    )(slopes, dab, qkv, lse, wo, dist)


def load_groups(groups, d, refs, w_ref, sems):
    copies = []
    at = 0
    shared = None
    for s, group in enumerate(groups):
        mine = []
        if group is None:
            up_ref, down_ref = refs[at : at + 2]
            at += 2
            split = up_ref.shape[1]
            mine = [
                pltpu.make_async_copy(up_ref, w_ref.at[s, :, pl.ds(0, split)], sems.at[s, 0]),
                pltpu.make_async_copy(
                    down_ref, w_ref.at[s, :, pl.ds(split, down_ref.shape[1])], sems.at[s, 1]
                ),
            ]
        else:
            if group == 0:
                shared = refs[at : at + 4]
                at += 4
            half = shared[0].shape[2]
            for c in range(4):
                for i, j in enumerate(order_of(c // 2)):
                    row = jnp.bitwise_xor(d, j ^ (c % 2)) * (2 * half) + (c // 2) * half
                    to = w_ref.at[s, pl.ds(pl.multiple_of(row, half), half)]
                    sem = sems.at[s, 4 * c + i]
                    mine.append(pltpu.make_async_copy(shared[c].at[i, group], to, sem))
        copies.append(mine)
    for mine in copies:
        for copy in mine:
            copy.start()
    return copies


def gelu_parts(gate):
    square = gate * gate
    t = jnp.tanh(gelu_coef * gate * (1.0 + 0.044715 * square))
    half = 0.5 * (1.0 + t)
    slope = half + 0.5 * gate * (1.0 - t * t) * gelu_coef * (1.0 + 3 * 0.044715 * square)
    return gate * half, slope


TILE = 256


def ff_fwd_kernel(groups, n_refs, first, last, at_ref, hb_ref, *refs):
    acc_refs, refs = refs[: 3 if first else 1], refs[3 if first else 1 :]
    weight_refs, refs = refs[:n_refs], refs[n_refs:]
    if last:
        g_ref, b_ref, pre_ref, out_ref, out_t_ref, w_ref, sems = refs
    else:
        pre_ref, w_ref, sems = refs
    width = hb_ref.shape[1]
    copies = load_groups(groups, at_ref[0], weight_refs, w_ref, sems)
    if first:
        xhat, _ = normed_of(acc_refs[0][...])
        pre_ref[...] = xhat * acc_refs[1][...] + acc_refs[2][...]
    else:
        pre_ref[...] = acc_refs[0][...]
    for s in range(len(groups)):
        for copy in copies[s]:
            copy.wait()

        def step(n, _, s=s):
            def at(c):
                return pl.ds(pl.multiple_of(c * width + n * TILE, TILE), TILE)

            hb = hb_ref[...]
            gate, value = mm(hb, w_ref[s, :, at(0)]), mm(hb, w_ref[s, :, at(1)])
            act = (gelu_parts(gate)[0] * value).astype(bf16)
            pre_ref[...] += mm(act, w_ref[s, at(0), pl.ds(2 * width, width)])
            return 0

        lax.fori_loop(0, width // TILE, step, 0)
    if last:
        xhat, _ = normed_of(pre_ref[...])
        out = (xhat * g_ref[...] + b_ref[...]).astype(bf16)
        out_ref[...] = out
        out_t_ref[...] = out.T


def ff_fwd(groups, d, hb, acc, weights, norm=None):
    rows, width = hb.shape
    last = norm is not None
    acc = acc if isinstance(acc, tuple) else (acc,)
    outs = [shape((rows, width), f32)]
    if last:
        outs += [shape((rows, width), bf16), shape((width, rows), bf16)]
    extra = list(norm) if last else []
    n = len(groups)
    return pl.pallas_call(
        functools.partial(ff_fwd_kernel, groups, len(weights), len(acc) == 3, last),
        name="ff_fwd",
        out_shape=tuple(outs),
        in_specs=[SMEM_SPEC, VMEM_SPEC]
        + [VMEM_SPEC] * len(acc)
        + [ANY_SPEC] * len(weights)
        + [VMEM_SPEC] * len(extra),
        out_specs=(VMEM_SPEC,) * len(outs),
        scratch_shapes=[
            pltpu.VMEM((n, width, 3 * width), bf16),
            pltpu.SemaphoreType.DMA((n, 16)),
        ],
        compiler_params=params(44),
        cost_estimate=cost(6 * rows * width * width * n, 5 * n << 20),
    )(d, hb, *acc, *weights, *extra)


def ff_bwd_kernel(groups, at_ref, hb_ref, dyb_ref, acc_ref, *refs):
    weight_refs, (r_ref, dh_ref, w_ref, sems) = refs[:-4], refs[-4:]
    width = hb_ref.shape[1]
    copies = load_groups(groups, at_ref[0], weight_refs, w_ref, sems)
    dh_ref[...] = acc_ref[...]
    for s in range(len(groups)):
        for copy in copies[s]:
            copy.wait()

        def step(n, _, s=s):
            def at(c):
                return pl.ds(pl.multiple_of(c * width + n * TILE, TILE), TILE)

            hb = hb_ref[...]
            gate, value = mm(hb, w_ref[s, :, at(0)]), mm(hb, w_ref[s, :, at(1)])
            d_act = mm(dyb_ref[...], w_ref[s, at(0), pl.ds(2 * width, width)], NT)
            gelu, slope = gelu_parts(gate)
            d_gate = (d_act * value * slope).astype(bf16)
            d_value = (d_act * gelu).astype(bf16)
            r_ref[s, :, at(0)] = d_gate
            r_ref[s, :, at(1)] = d_value
            r_ref[s, :, at(2)] = (gelu * value).astype(bf16)
            dh_ref[...] += mm(d_gate, w_ref[s, :, at(0)], NT) + mm(d_value, w_ref[s, :, at(1)], NT)
            return 0

        lax.fori_loop(0, width // TILE, step, 0)


def ff_bwd(groups, d, hb, dyb, acc, weights):
    rows, width = hb.shape
    n = len(groups)
    return pl.pallas_call(
        functools.partial(ff_bwd_kernel, groups),
        name="ff_bwd",
        out_shape=(shape((n, rows, 3 * width), bf16), shape((rows, width), f32)),
        in_specs=[SMEM_SPEC] + [VMEM_SPEC] * 3 + [ANY_SPEC] * len(weights),
        out_specs=(VMEM_SPEC, VMEM_SPEC),
        scratch_shapes=[
            pltpu.VMEM((n, width, 3 * width), bf16),
            pltpu.SemaphoreType.DMA((n, 16)),
        ],
        compiler_params=params(48),
        cost_estimate=cost(12 * rows * width * width * n, 8 * n << 20),
    )(d, hb, dyb, acc, *weights)


def norm2_bwd_kernel(grad_ref, pre_ref, g_ref, dpre_ref, dyb_ref, dyb_t_ref, small_ref):
    grad = grad_ref[...].astype(f32)
    xhat, rstd = normed_of(pre_ref[...])
    small_ref[0:1] = jnp.sum(grad * xhat, axis=0, keepdims=True)
    small_ref[1:2] = jnp.sum(grad, axis=0, keepdims=True)
    d_pre = norm_back(grad, xhat, rstd, g_ref[...])
    dpre_ref[...] = d_pre
    dyb = d_pre.astype(bf16)
    dyb_ref[...] = dyb
    dyb_t_ref[...] = dyb.T


def norm_bwd(grad, pre, gain):
    rows, width = pre.shape
    return pl.pallas_call(
        norm2_bwd_kernel,
        name="norm_bwd",
        out_shape=(
            shape((rows, width), f32),
            shape((rows, width), bf16),
            shape((width, rows), bf16),
            shape((2, width), f32),
        ),
        in_specs=[VMEM_SPEC] * 3,
        out_specs=(VMEM_SPEC,) * 4,
        compiler_params=params(24),
        cost_estimate=cost(rows * width * 20, 6 << 20),
    )(grad, pre, gain[None])


def pick_rows(d, order, from_ref, to_ref):
    rows = from_ref.shape[0] // 8
    for i, j in enumerate(order):
        at = pl.multiple_of(jnp.bitwise_xor(d, j) * rows, rows)
        to_ref[pl.ds(i * rows, rows), :] = from_ref[pl.ds(at, rows), :]


def send_kernel(order, at_ref, hb_t_ref, dyb_t_ref, r_ref, out_ref, h_ref, y_ref):
    @pl.when((pl.program_id(0) == 0) & (pl.program_id(1) == 0))
    def _():
        pick_rows(at_ref[0], order, hb_t_ref, h_ref)
        pick_rows(at_ref[0], order, dyb_t_ref, y_ref)

    part = pl.program_id(1)

    @pl.when(part < 2)
    def _():
        out_ref[0] = mm(h_ref[...], r_ref[0]).astype(bf16)

    @pl.when(part == 2)
    def _():
        out_ref[0] = mm(y_ref[...], r_ref[0]).astype(bf16)


def keep_kernel(order, at_ref, hb_t_ref, dyb_t_ref, r_ref, got_ref, one_ref, two_ref, h_ref, y_ref):
    @pl.when((pl.program_id(0) == 0) & (pl.program_id(1) == 0))
    def _():
        pick_rows(at_ref[0], order, hb_t_ref, h_ref)
        pick_rows(at_ref[0], order, dyb_t_ref, y_ref)

    part = pl.program_id(1)

    def put(lhs_ref):
        total = (mm(lhs_ref[...], r_ref[0]) + got_ref[0].astype(f32)).astype(bf16)
        half = total.shape[0] // 2
        one_ref[0] = total[:half]
        two_ref[0] = total[half:]

    @pl.when(part < 2)
    def _():
        put(h_ref)

    @pl.when(part == 2)
    def _():
        put(y_ref)


def ff_send(colour, d, hb_t, dyb_t, r):
    width, rows = hb_t.shape
    half = width // 2
    order = [j ^ 1 for j in fold_order(colour)]
    whole = pl.BlockSpec((width, rows), lambda s, c: (0, 0))
    return pl.pallas_call(
        functools.partial(send_kernel, order),
        name="ff_send",
        grid=(2, 3),
        out_shape=shape((2, half, 3 * width), bf16),
        in_specs=[SMEM_SPEC, whole, whole, pl.BlockSpec((1, rows, width), lambda s, c: (s, 0, c))],
        out_specs=pl.BlockSpec((1, half, width), lambda s, c: (s, 0, c)),
        scratch_shapes=[pltpu.VMEM((half, rows), bf16)] * 2,
        compiler_params=params(24),
        cost_estimate=cost(2 * rows * half * width * 6, 10 << 20),
    )(d, hb_t, dyb_t, r)


def ff_keep(colour, d, hb_t, dyb_t, r, got):
    width, rows = hb_t.shape
    half = width // 2
    order = fold_order(colour)
    whole = pl.BlockSpec((width, rows), lambda s, c: (0, 0))
    out = pl.BlockSpec((1, half // 2, width), lambda s, c: (s, 0, c))
    return pl.pallas_call(
        functools.partial(keep_kernel, order),
        name="ff_keep",
        grid=(2, 3),
        out_shape=(shape((2, half // 2, 3 * width), bf16),) * 2,
        in_specs=[
            SMEM_SPEC,
            whole,
            whole,
            pl.BlockSpec((1, rows, width), lambda s, c: (s, 0, c)),
            pl.BlockSpec((1, half, width), lambda s, c: (s, 0, c)),
        ],
        out_specs=(out, out),
        scratch_shapes=[pltpu.VMEM((half, rows), bf16)] * 2,
        compiler_params=params(24),
        cost_estimate=cost(2 * rows * half * width * 6, 12 << 20),
    )(d, hb_t, dyb_t, r, got)


def add_low(a, b):
    return (a.astype(f32) + b.astype(f32)).astype(bf16)


class Fold:
    def __init__(self, net, line, colour, sent, keep):
        self.net, self.line, self.bits = net, line, COLOURS[colour]
        self.keep = keep
        self.got = net.flip(sent, 1)

    def first(self):
        self.kept, sent = self.line.run(self.keep, self.got)
        self.got = self.net.flip(sent, self.bits[0])

    def second(self):
        half = self.kept.shape[1] // 2
        got = self.line.after(self.got)
        sent = add_low(self.kept[:, half:], got[:, half:])
        self.kept = add_low(self.kept[:, :half], got[:, :half])
        self.got = self.net.flip(sent, self.bits[1])

    def done(self):
        return add_low(self.kept, self.line.after(self.got))


def attn_send_kernel(colour, at_ref, x_t_ref, c_t_ref, r_ref, dab_ref, out_ref, h_ref):
    width = x_t_ref.shape[0]
    order = [j ^ 1 for j in fold_order(colour)]
    pick_rows(at_ref[0], order, x_t_ref, h_ref)
    for s in range(2):
        block = 2 * colour + s
        if block < 3:
            out_ref[s] = mm(h_ref[...], r_ref[:, pl.ds(block * width, width)]).astype(bf16)
        else:
            pick_rows(at_ref[0], order, c_t_ref, h_ref)
            out_ref[s] = mm(h_ref[...], dab_ref[...]).astype(bf16)


def attn_keep_kernel(
    colour, at_ref, x_t_ref, c_t_ref, r_ref, dab_ref, got_ref, one_ref, two_ref, h_ref
):
    width = x_t_ref.shape[0]
    order = fold_order(colour)
    pick_rows(at_ref[0], order, x_t_ref, h_ref)
    for s in range(2):
        block = 2 * colour + s
        if block < 3:
            total = mm(h_ref[...], r_ref[:, pl.ds(block * width, width)])
        else:
            pick_rows(at_ref[0], order, c_t_ref, h_ref)
            total = mm(h_ref[...], dab_ref[...])
        total = (total + got_ref[s].astype(f32)).astype(bf16)
        half = total.shape[0] // 2
        one_ref[s] = total[:half]
        two_ref[s] = total[half:]


def attn_send(colour, d, d_qkv, x_t, ctx_t, dab):
    width, rows = x_t.shape
    half = width // 2
    return pl.pallas_call(
        functools.partial(attn_send_kernel, colour),
        name="attn_send",
        out_shape=shape((2, half, width), bf16),
        in_specs=[SMEM_SPEC] + [VMEM_SPEC] * 4,
        out_specs=VMEM_SPEC,
        scratch_shapes=[pltpu.VMEM((half, rows), bf16)],
        compiler_params=params(24),
        cost_estimate=cost(4 * rows * half * width, 6 << 20),
    )(d, x_t, ctx_t, d_qkv, dab)


def attn_keep(colour, d, d_qkv, x_t, ctx_t, dab, got):
    width, rows = x_t.shape
    half = width // 2
    return pl.pallas_call(
        functools.partial(attn_keep_kernel, colour),
        name="attn_keep",
        out_shape=(shape((2, half // 2, width), bf16),) * 2,
        in_specs=[SMEM_SPEC] + [VMEM_SPEC] * 5,
        out_specs=(VMEM_SPEC, VMEM_SPEC),
        scratch_shapes=[pltpu.VMEM((half, rows), bf16)],
        compiler_params=params(24),
        cost_estimate=cost(4 * rows * half * width, 7 << 20),
    )(d, x_t, ctx_t, d_qkv, dab, got)


class Share:
    def __init__(self, net, line, d, z, d_qkv, x_t, ctx_t, dab):
        self.net, self.line, self.z = net, line, z
        self.folds = []
        for colour in range(2):
            sent = line.run(functools.partial(attn_send, colour, d), d_qkv, x_t, ctx_t, dab)

            def keep(got, colour=colour):
                return attn_keep(colour, d, d_qkv, x_t, ctx_t, dab, got)

            self.folds.append(Fold(net, line, colour, sent, keep))

    def first(self):
        for one in self.folds:
            one.first()

    def second(self):
        for one in self.folds:
            one.second()

    def far(self):
        n = self.net.n_t
        stacked = jnp.concatenate([one.done() for one in self.folds], axis=0)
        parts = [
            lax.dynamic_index_in_dim(stacked, lax.rem(self.z - k + n, n), 0, keepdims=False)
            for k in range(n)
        ]
        self.parts = [parts[0]] + [self.net.shift(parts[k], -k) for k in range(1, n)]

    def far_back(self):
        total = self.parts[0].astype(f32)
        for part in self.parts[1:]:
            total = total + self.line.after(part).astype(f32)
        total = total.astype(bf16)
        self.slices = [total] + [self.net.shift(total, k) for k in range(1, self.net.n_t)]

    def gather(self):
        self.gathered = Gather(self.net, self.line, self.slices)


def spread_kernel(layer, at_ref, *refs):
    held = refs[:4]
    qkv_out, wo_out, qkv_buf, wo_buf, sems = refs[-5:]
    d, z = at_ref[0], at_ref[1]
    rows, cols = held[0].shape[2:]
    for k in range(4):
        block = lax.rem(z - k + 4, 4)
        for c in range(4):
            for i, j in enumerate(order_of(c // 2)):
                value = held[c][i, k].astype(f32)
                row = jnp.bitwise_xor(d, j ^ (c % 2)) * (2 * rows) + (c // 2) * rows
                row = pl.multiple_of(row, rows)

                @pl.when(block < 3)
                def _(value=value, row=row, block=block):
                    col = pl.multiple_of(block * cols, cols)
                    qkv_buf[pl.ds(row, rows), pl.ds(col, cols)] = value

                @pl.when(block == 3)
                def _(value=value, row=row):
                    wo_buf[pl.ds(row, rows), :] = value

    one = pltpu.make_async_copy(qkv_buf, qkv_out.at[layer], sems.at[0])
    two = pltpu.make_async_copy(wo_buf, wo_out.at[layer], sems.at[1])
    one.start()
    two.start()
    one.wait()
    two.wait()


def spread_out(layer, where, pieces, before):
    rows, cols = pieces[0].shape[2:]
    width = 16 * rows
    extra = [] if before is None else list(before)
    return pl.pallas_call(
        functools.partial(spread_kernel, layer),
        name="spread_out",
        out_shape=(shape((LAYERS, width, 3 * cols), f32), shape((LAYERS, width, cols), f32)),
        in_specs=[SMEM_SPEC] + [VMEM_SPEC] * 4 + [ANY_SPEC] * len(extra),
        out_specs=(ANY_SPEC, ANY_SPEC),
        scratch_shapes=[
            pltpu.VMEM((width, 3 * cols), f32),
            pltpu.VMEM((width, cols), f32),
            pltpu.SemaphoreType.DMA((2,)),
        ],
        input_output_aliases={5: 0, 6: 1} if extra else {},
        compiler_params=params(32),
        cost_estimate=cost(0, 14 << 20),
    )(where, *pieces, *extra)


class Small:
    def __init__(self, net, line, z, value):
        self.net, self.line, self.z = net, line, z
        self.value, self.got = value, net.flip(value, 1)

    def flip(self, bit):
        self.value = self.value + self.line.after(self.got)
        self.got = self.net.flip(self.value, bit)

    def far(self):
        self.value = self.value + self.line.after(self.got)
        self.got = [self.net.shift(self.value, k) for k in range(1, self.net.n_t)]

    def done(self):
        n = self.net.n_t
        stacked = jnp.stack([self.value] + self.got)
        total = None
        for q in range(n):
            one = lax.dynamic_index_in_dim(stacked, lax.rem(self.z - q + n, n), 0, keepdims=False)
            total = one if total is None else total + one
        return total


def quick_program(
    net,
    x_in,
    bucket,
    lengths,
    qkv_weight,
    out_weight,
    norm_gain1,
    norm_bias1,
    up_weight,
    down_weight,
    norm_gain2,
    norm_bias2,
    cotangent,
):
    rows, width = x_in.shape
    d, z = lax.axis_index("dp").astype(jnp.int32), lax.axis_index("tensor").astype(jnp.int32)
    d_at, dz_at = jnp.reshape(d, (1,)), jnp.stack([d, z])
    part = width // net.n_dp
    line = Line()
    gains1, biases1 = norm_gain1[:, None], norm_bias1[:, None]
    gains2, biases2 = norm_gain2[:, None], norm_bias2[:, None]

    def own_slice(l):
        up = lax.dynamic_slice(up_weight, (l, d * part, 0, 0), (1, part, 2, width))
        down = lax.dynamic_slice(down_weight, (l, d * part, 0), (1, part, width))
        return jnp.concatenate([up.reshape(part, 2 * width), down[0]], axis=1)

    def far_slices(own):
        return {k: net.shift(own, k) for k in (1, 3, 2)}

    own = [own_slice(l) for l in range(LAYERS)]
    far = [far_slices(own[0]), None]
    seg = segments(bucket[0], lengths[0], rows, SHORT)
    same = seg[:, None] == seg[None, :]
    place = jnp.arange(rows, dtype=f32)
    dist = jnp.where(same, jnp.abs(place[:, None] - place[None, :]), 1e34)
    slopes = slopes_of()
    outputs, kept, weights = [], [], []
    x, x_t = x_in, x_in.T

    def run_attn(l, x):
        def call(x):
            return attn_fwd(l, x, qkv_weight, out_weight, norm_gain1[l], norm_bias1[l], dist, slopes)

        return line.run(call, x)

    def run_ff(groups, hb, acc, weights, norm=None):
        return line.run(lambda hb: ff_fwd(groups, d_at, hb, acc, weights, norm), hb)

    def own_weights(l):
        return [up_weight[l].reshape(width, 2 * width), down_weight[l]]

    saved = run_attn(0, x)
    qkv, lse, ctx, ctx_t, pre1, hb, hb_t = saved
    near = Gather(net, line, [far[0][1], far[0][3]])
    far[1] = far_slices(line.after(own[1]))
    mine = own_weights(0)
    acc = run_ff((None,), hb, (pre1, gains1[0], biases1[0]), mine)[0]
    near.second()
    back = Gather(net, line, [far[0][2]])
    near.core()
    back.second()
    acc = run_ff((0, 1), hb, acc, near.pieces())[0]
    back.core()
    near2 = Gather(net, line, [far[1][1], far[1][3]])
    pre2, out, out_t = run_ff((0,), hb, acc, back.pieces(), (gains2[0], biases2[0]))
    weights.append((mine + back.pieces(), near.pieces()))
    kept.append((x_t, qkv, lse, ctx_t, pre1, hb, hb_t, pre2))
    outputs.append(out)
    near2.second()
    back2 = Gather(net, line, [far[1][2]])
    qkv, lse, ctx, ctx_t, pre1, hb, hb_t = run_attn(1, out)
    near2.core()
    back2.second()
    mine = own_weights(1)
    acc = run_ff((None, 0, 1), hb, (pre1, gains1[1], biases1[1]), mine + near2.pieces())[0]
    back2.core()
    pre2, out, _ = run_ff((0,), hb, acc, back2.pieces(), (gains2[1], biases2[1]))
    weights.append((mine + back2.pieces(), near2.pieces()))
    kept.append((out_t, qkv, lse, ctx_t, pre1, hb, hb_t, pre2))
    outputs.append(out)

    def run_norm(grad, pre, gain):
        return line.run(lambda grad: norm_bwd(grad, pre, gain), grad)

    def run_ff_bwd(groups, hb, dyb, acc, weights):
        return line.run(lambda hb: ff_bwd(groups, d_at, hb, dyb, acc, weights), hb)

    def run_send(colour, r, hb_t, dyb_t):
        sent = line.run(lambda r: ff_send(colour, d_at, hb_t, dyb_t, r), r)
        return Fold(
            net, line, colour, sent, lambda got: ff_keep(colour, d_at, hb_t, dyb_t, r, got)
        )

    def to_owners(folded, shifts):
        return [
            folded[i] if k == 0 else net.shift(folded[i], -k) for i, k in enumerate(shifts)
        ]

    def run_grad(l, d_qkv, d_pre1):
        return line.run(lambda d_qkv: d_pre1 + dot(d_qkv, qkv_weight[l].T), d_qkv)

    ff_parts = {}
    x_t, qkv, lse, ctx_t, pre1, hb, hb_t, pre2 = kept[1]
    d_pre2, dyb, dyb_t, small2 = run_norm(cotangent, pre2, norm_gain2[1])
    r, d_h = run_ff_bwd((None, 0), hb, dyb, d_pre2, weights[1][0])
    fold0 = run_send(0, r, hb_t, dyb_t)
    r, d_h = run_ff_bwd((0, 1), hb, dyb, d_h, weights[1][1])
    fold1 = run_send(1, r, hb_t, dyb_t)
    fold0.first()
    d_pre1, dab, _, small1 = run_norm(d_h, pre1, norm_gain1[1])
    small = {1: jnp.concatenate([small1, small2], axis=0)}
    fold1.first()
    d_qkv = line.run(
        lambda dab: attn_bwd(1, dab, qkv, lse, out_weight, dist, slopes), dab
    )
    fold0.second()
    share = Share(net, line, d_at, z, d_qkv, x_t, ctx_t, dab)
    fold1.second()
    grad = run_grad(1, d_qkv, d_pre1)
    share.first()
    ff_parts[1] = to_owners(fold0.done(), (0, 2))
    x_t, qkv, lse, ctx_t, pre1, hb, hb_t, pre2 = kept[0]
    d_pre2, dyb, dyb_t, small2 = run_norm(grad, pre2, norm_gain2[0])
    ff_parts[1] += to_owners(fold1.done(), (1, 3))
    r, d_h = run_ff_bwd((None, 0), hb, dyb, d_pre2, weights[0][0])
    share.second()
    fold0 = run_send(0, r, hb_t, dyb_t)
    r, d_h = run_ff_bwd((0, 1), hb, dyb, d_h, weights[0][1])
    share.far()
    fold1 = run_send(1, r, hb_t, dyb_t)
    fold0.first()
    d_pre1, dab, _, small1 = run_norm(d_h, pre1, norm_gain1[0])
    small[0] = jnp.concatenate([small1, small2], axis=0)
    few = Small(net, line, z, jnp.concatenate([small[0], small[1]], axis=0))
    share.far_back()
    fold1.first()
    few.flip(2)
    d_qkv = line.run(
        lambda dab: attn_bwd(0, dab, qkv, lse, out_weight, dist, slopes), dab
    )
    share.gather()
    fold0.second()
    few.flip(4)
    last_share = Share(net, line, d_at, z, d_qkv, x_t, ctx_t, dab)
    fold1.second()
    few.far()
    share.gathered.second()
    last_share.first()
    ff_parts[0] = to_owners(fold0.done(), (0, 2))
    share.gathered.core()
    last_share.second()
    ff_parts[0] += to_owners(fold1.done(), (1, 3))
    last_share.far()
    grad = run_grad(0, d_qkv, d_pre1)
    last_share.far_back()
    attention_grads = line.run(
        lambda first: spread_out(1, dz_at, [first] + share.gathered.pieces()[1:], None),
        share.gathered.pieces()[0],
    )
    last_share.gather()
    last_share.gathered.second()
    last_share.gathered.core()
    attention_grads = spread_out(0, dz_at, last_share.gathered.pieces(), attention_grads)
    small = few.done().reshape(LAYERS, 4, width)
    up_grads, down_grads = [], []
    for l in range(LAYERS):
        total = ff_parts[l][0].astype(f32)
        for one in ff_parts[l][1:]:
            total = total + one.astype(f32)
        up_grads.append(total[:, : 2 * width].reshape(part, 2, width))
        down_grads.append(total[:, 2 * width :].T)
    return (
        jnp.stack(outputs),
        grad,
        attention_grads[0],
        attention_grads[1],
        small[:, 0],
        small[:, 1],
        jnp.stack(up_grads),
        jnp.stack(down_grads),
        small[:, 2],
        small[:, 3],
    )


def attention_forward(x_low, wqkv, wo, g1, b1, same, decay):
    rows, width = x_low.shape
    qkv_low = dot(x_low, wqkv).astype(bf16)
    query, keys, values = split_heads(qkv_low, width)
    scores = scores_of(query, keys, same, decay)
    top = jnp.max(scores, axis=-1, keepdims=True)
    log_total = top + jnp.log(jnp.sum(jnp.exp(scores - top), axis=-1, keepdims=True))
    probs_low = jnp.exp(scores - log_total).astype(bf16)
    ctx_low = (
        jnp.einsum("hqk,khe->qhe", probs_low, values, preferred_element_type=f32)
        .reshape(rows, width)
        .astype(bf16)
    )
    pre_first = x_low.astype(f32) + dot(ctx_low, wo)
    normed = layer_norm(pre_first, g1, b1)
    return normed, (qkv_low, log_total, ctx_low, pre_first)


def attention_backward(d_attn_low, qkv_low, log_total, ctx_low, wo, same, decay):
    rows, width = d_attn_low.shape
    d_ctx = dot(d_attn_low, wo.T).astype(bf16).reshape(rows, HEADS, HEAD_DIM)
    query, keys, values = split_heads(qkv_low, width)
    probs = jnp.exp(scores_of(query, keys, same, decay) - log_total)
    probs_low = probs.astype(bf16)
    d_values = jnp.einsum("hqk,qhe->khe", probs_low, d_ctx, preferred_element_type=f32)
    d_probs = jnp.einsum("qhe,khe->hqk", d_ctx, values, preferred_element_type=f32)
    d_scores = (probs * (d_probs - jnp.sum(probs * d_probs, axis=-1, keepdims=True))).astype(bf16)
    d_query = jnp.einsum("hqk,khe->qhe", d_scores, keys, preferred_element_type=f32)
    d_keys = jnp.einsum("hqk,qhe->khe", d_scores, query, preferred_element_type=f32)
    scale = HEAD_DIM ** (-0.5)
    return jnp.concatenate(
        [
            (d_query * scale).reshape(rows, width),
            (d_keys * scale).reshape(rows, width),
            d_values.reshape(rows, width),
        ],
        axis=1,
    ).astype(bf16)


def plain_program(
    net,
    x_in,
    bucket,
    lengths,
    qkv_weight,
    out_weight,
    norm_gain1,
    norm_bias1,
    up_weight,
    down_weight,
    norm_gain2,
    norm_bias2,
    cotangent,
):
    rows, width = x_in.shape
    n_t = net.n_t
    hidden = down_weight.shape[1]
    seg = segments(bucket[0], lengths[0], rows, SHORT)
    same = seg[:, None] == seg[None, :]
    decay = alibi(rows, HEADS)
    ups = lax.all_gather(up_weight, "tensor", axis=0)
    downs = lax.all_gather(down_weight, "tensor", axis=0)
    groups = [
        [(ups[k, l].reshape(width, -1), downs[k, l]) for k in range(n_t)] for l in range(LAYERS)
    ]
    layer_in = x_in
    outputs, kept = [], []
    for l in range(LAYERS):
        x_low = layer_in
        normed, keep = attention_forward(
            x_low, qkv_weight[l], out_weight[l], norm_gain1[l], norm_bias1[l], same, decay
        )
        hb = normed.astype(bf16)
        pre_second = normed
        joined, act = [], []
        for up, down in groups[l]:
            joined.append(dot(hb, up))
            act.append(geglu(joined[-1]).astype(bf16))
            pre_second = pre_second + dot(act[-1], down)
        layer_in = layer_norm(pre_second, norm_gain2[l], norm_bias2[l]).astype(bf16)
        outputs.append(layer_in)
        kept.append((x_low, *keep, hb, pre_second, joined, act))
    grad = cotangent.astype(f32)
    attention_grads, small, up_grads, down_grads = ([None] * LAYERS for _ in range(4))
    for l in reversed(range(LAYERS)):
        x_low, qkv_low, log_total, ctx_low, pre_first, hb, pre_second, joined, act = kept[l]
        pull = jax.vjp(layer_norm, pre_second, norm_gain2[l], norm_bias2[l])[1]
        d_pre2, d_gain2, d_bias2 = pull(grad)
        dyb = d_pre2.astype(bf16)
        d_h = d_pre2
        d_joined = []
        for k, (up, down) in enumerate(groups[l]):
            d_act = dot(dyb, down.T)
            d_joined.append(jax.vjp(geglu, joined[k])[1](d_act)[0].astype(bf16))
            d_h = d_h + dot(d_joined[k], up.T)
        d_up = jnp.stack([dot(hb.T, one) for one in d_joined]).astype(bf16)
        d_down = jnp.stack([dot(dyb.T, one) for one in act]).astype(bf16)
        d_up = lax.psum_scatter(d_up, "tensor", scatter_dimension=0)
        d_down = lax.psum_scatter(d_down, "tensor", scatter_dimension=0)
        d_up = lax.psum_scatter(d_up, "dp", scatter_dimension=0, tiled=True)
        d_down = lax.psum_scatter(d_down, "dp", scatter_dimension=0, tiled=True)
        up_grads[l], down_grads[l] = d_up.astype(f32), d_down.astype(f32)
        pull = jax.vjp(layer_norm, pre_first, norm_gain1[l], norm_bias1[l])[1]
        d_pre1, d_gain1, d_bias1 = pull(d_h)
        small[l] = [d_gain1, d_bias1, d_gain2, d_bias2]
        dab = d_pre1.astype(bf16)
        d_qkv = attention_backward(dab, qkv_low, log_total, ctx_low, out_weight[l], same, decay)
        found = lax.psum(
            (dot(x_low.T, d_qkv).astype(bf16), dot(ctx_low.T, dab).astype(bf16)), BOTH
        )
        attention_grads[l] = [one.astype(f32) for one in found]
        grad = d_pre1 + dot(d_qkv, qkv_weight[l].T)
    small = lax.psum(jnp.stack(small[0] + small[1]), BOTH).reshape(LAYERS, 4, width)
    return (
        jnp.stack(outputs),
        grad,
        jnp.stack([one[0] for one in attention_grads]),
        jnp.stack([one[1] for one in attention_grads]),
        small[:, 0],
        small[:, 1],
        jnp.stack(up_grads).reshape(LAYERS, -1, 2, hidden),
        jnp.stack([one.T for one in down_grads]),
        small[:, 2],
        small[:, 3],
    )


def program(net, *args):
    width, hidden = args[0].shape[1], args[8].shape[1]
    quick = net.n_dp == 8 and net.n_t == 4 and hidden == width and width % 256 == 0
    return (quick_program if quick else plain_program)(net, *args)


def solution(mesh):
    in_specs = (
        P(BOTH, None),
        P(BOTH),
        P(BOTH, None),
        P(),
        P(),
        P(),
        P(),
        P(None, None, None, "tensor"),
        P(None, "tensor", None),
        P(),
        P(),
        P(BOTH, None),
    )
    out_specs = (
        P(None, BOTH, None),
        P(BOTH, None),
        P(),
        P(),
        P(),
        P(),
        P(None, "dp", None, "tensor"),
        P(None, "tensor", "dp"),
        P(),
        P(),
    )
    net = Net(mesh)
    return jax.shard_map(
        functools.partial(program, net),
        mesh=mesh,
        in_specs=in_specs,
        out_specs=out_specs,
        check_vma=False,
    )
```

time: 1220 us -> 649 us (0.53)
  waiting for transfers between devices: 809 us -> 153 us
  Pallas kernels: 0 us -> 270 us
  matrix products: 182 us -> 9.69 us
  starting transfers between devices: 1.89 us -> 101 us
  blocking collectives: 41.8 us -> 0 us
  other arithmetic: 69 us -> 35 us
  local copies, waits for them, and re-layouts: 85.4 us -> 66.9 us
  between operations: 17.3 us -> 3.53 us
    pallas_call x0 -> x35, Pallas kernels: none -> 270 us  [the longest x4 76.4 us: ff_bwd(): pl.pallas_call(functools.partial(ff_bwd_kernel, groups), name='ff_bwd', o...]
    psum x1 -> x0, waiting for transfers between devices: 261 us -> none  [shards(): lax.psum((d_wqkv, d_wo, d_gain1, d_bias1, d_gain2, d_bias2), ('dp', 'tens...]
    all_gather x4 -> x0, waiting for transfers between devices: 244 us -> none  [the longest x2 127 us: backward_layer(): lax.all_gather(d_pre2.astype(jnp.bfloat16), 'tensor', axis=0, tiled=True)]
    reduce_scatter x6 -> x0, waiting for transfers between devices: 215 us -> none  [the longest x2 117 us: forward_layer(): lax.psum_scatter(jnp.dot(act_low, wdown, preferred_element_type=jnp.float...]
    dot_general x36 -> x2, matrix products: 182 us -> 9.69 us  [dot(): return jnp.dot(a, b, preferred_element_type=f32)]
    ppermute x0 -> x90, waiting for transfers between devices: none -> 153 us  [the longest x63 114 us: flip(): return lax.ppermute(value, 'dp', [(i, i ^ bit) for i in range(self.n_dp)])]
    ppermute x0 -> x90, starting transfers between devices: none -> 101 us  [the longest x63 51.3 us: flip(): return lax.ppermute(value, 'dp', [(i, i ^ bit) for i in range(self.n_dp)])]
    unnamed x13 -> x0, waiting for transfers between devices: 88.7 us -> none
  transfers between devices with their start and end apart: 12 -> 90, of which waited for: 11 -> 28; matrix products, arithmetic and copies ran while one was open for 10% -> 11% of each run, Pallas kernels for 0% -> 32%
where the time goes in v1:
time: 649 us; the launch traced here: 638 us
  Pallas kernels  270 us (42%)
  waiting for transfers between devices  153 us (24%)
  starting transfers between devices  101 us (16%)
  local copies, waits for them, and re-layouts  66.9 us (10%)
  other arithmetic  35 us (5%)
  matrix products  9.69 us (1%)
    ppermute x63, waiting for transfers between devices, flip(): return lax.ppermute(value, 'dp', [(i, i ^ bit) for i in range(self.n_dp)])  114 us
    pallas_call x4, Pallas kernels, ff_bwd(): pl.pallas_call(functools.partial(ff_bwd_kernel, groups), name='ff_bwd', o...  76.4 us
    ppermute x63, starting transfers between devices, flip(): return lax.ppermute(value, 'dp', [(i, i ^ bit) for i in range(self.n_dp)])  51.3 us
    ppermute x27, starting transfers between devices, shift(): lax.ppermute(value, 'tensor', [(i, (i + step) % n) for i in range(n)])  49.3 us
    pallas_call x5, Pallas kernels, ff_fwd(): pl.pallas_call(functools.partial(ff_fwd_kernel, groups, len(weights), len...  48.3 us
    pallas_call x2, Pallas kernels, attn_fwd(): pl.pallas_call(attn_fwd_kernel, name='attn_fwd', grid=(1,), out_shape=(sh...  48.1 us
    unnamed x245, local copies, waits for them, and re-layouts  44.1 us
    ppermute x27, waiting for transfers between devices, shift(): lax.ppermute(value, 'tensor', [(i, (i + step) % n) for i in range(n)])  39.2 us
  transfers between devices with their start and end apart: 90, of which 28 were waited for; matrix products, arithmetic and copies ran while one was open for 11% of the time, Pallas kernels for 32%

profile of v1, /device:TPU:0, one launch (start us, length us, event | category | flops | bytes accessed | tf_op | source)
XLA Modules:
  0.0 638.4 jit_solution(2896555779423666946)
XLA Ops:
  0.6 2.2 constant_dynamic-slice_fusion
  5.3 3.0 collective-permute-start
  10.4 7.9 %fusion.44 = (bf16[1,768,2,768]{3,2,1,0:T(2,128)(2,1)}, bf16[1,768,2,768]{3,2,1,0:T(2,128)(2,1)}) fusion(bf16[2,768,2,768]{3,2,1,0:T(2,128)(2,1)} %param.19), kind=kLoop, calls=%fused_computation.184 | loop fusion | bytes 9437184 | tf_op jit(solution)/shard_map/slice | solution.py:849
  22.7 24.1 %attn_fwd.2 = (bf16[512,2304]{1,0:T(8,128)(2,1)S(1)}, f32[512,128]{1,0:T(8,128)S(1)}, bf16[512,768]{1,0:T(8,128)(2,1)}, bf16[768,512]{1,0:T(8,128)(2,1)S(1)}, f3...) custom-call(f32[12]{0:T(128)S(1)} %multiply_exponential_fusion.slopes, ...), custom_call_target="tpu_custom_call" | custom-call | flops 4831838208 | bytes 16777216 | tf_op jit(solution)/shard_map/attn_fwd/pallas_call | solution.py:239
  57.7 3.6 ff_fwd.5.refs_0_
  61.4 4.7 collective-permute-done.5
  70.1 16.3 %collective-permute-done.6 = bf16[2,2,48,2304]{3,2,1,0:T(8,128)(2,1)S(1)} collective-permute-done((bf16[2,2,48,2304]{3,2,1,0:T(8,128)(2,1)S(1)}, bf16[2,2,48,2304]{3,2,1,0:T(8,128)(2,1)S(1)}, u32[]{:S(2)}, u32[]{:S(2)}) %collective-permute-start.6) | collective-permute-done | bytes 884768 | tf_op jit(solution)/shard_map/ppermute | solution.py:83
  87.9 3.8 collective-permute-start.16
  93.4 5.7 collective-permute-done.12
  100.4 5.1 collective-permute-done.9
  107.9 13.3 %ff_fwd.6.refs_0_ = f32[512,768]{1,0:T(8,128)S(1)} custom-call(s32[1]{0:T(128)} %bitcast.at_ref, bf16[512,768]{1,0:T(8,128)(2,1)S(1)} %get-tuple-element.246.hb_ref, f32[512,768]{1,0:T(8,128)S(1)} %ff_fwd.5.refs_0_, bf16[4,2,48,2304]{3,2,1,0:T(8,128)(2,1)S(1)} %pad_maximum_fusion.refs_1_.refs_0_, ...), custom_call_target="tpu_custom_call" | custom-call | flops 3623878656 | bytes 10485760 | tf_op jit(solution)/shard_map/ff_fwd/pallas_call | solution.py:413
  125.1 8.2 %ff_fwd.7 = (f32[512,768]{1,0:T(8,128)S(1)}, bf16[512,768]{1,0:T(8,128)(2,1)S(1)}, bf16[768,512]{1,0:T(8,128)(2,1)S(1)}) custom-call(s32[1]{0:T(128)} %bitcast.at_ref, bf16[512,768]{1,0:T(8,128)(2,1)S(1)} %get-tuple-element.246.hb_ref, f32[512,768]{1,0:T(8,128)S(1)} %ff_fwd.6.refs_0_, bf16[4,1,48,2304]{3,2,1,0:T(8,128)(2,1)S(1)} %pad_maximum_fusion.12.refs_1_.refs_2_, ...), custom_call_target="tpu_custom_call" | custom-call | flops 1811939328 | bytes 5242880 | tf_op jit(solution)/shard_map/ff_fwd/pallas_call | solution.py:413
  137.1 24.0 %attn_fwd.3 = (bf16[512,2304]{1,0:T(8,128)(2,1)S(1)}, f32[512,128]{1,0:T(8,128)S(1)}, bf16[512,768]{1,0:T(8,128)(2,1)}, bf16[768,512]{1,0:T(8,128)(2,1)S(1)}, f3...) custom-call(f32[12]{0:T(128)S(1)} %multiply_exponential_fusion.slopes, ...), custom_call_target="tpu_custom_call" | custom-call | flops 4831838208 | bytes 16777216 | tf_op jit(solution)/shard_map/attn_fwd/pallas_call | solution.py:239
  168.8 2.7 collective-permute-done.27
  172.5 3.2 collective-permute-done.24
  178.2 14.2 %ff_fwd.8.refs_0_ = f32[512,768]{1,0:T(8,128)S(1)} custom-call(s32[1]{0:T(128)} %bitcast.at_ref, bf16[512,768]{1,0:T(8,128)(2,1)S(1)} %get-tuple-element.216.hb_ref, f32[512,768]{1,0:T(8,128)S(1)} %get-tuple-element.191.refs_0_.pre_ref, f32[1,768]{1,0:T(1,128)S(1)} %get-tuple-element.385.g_ref.refs_1_, f32[1,768]{1,0:T(1,128)S(1)} %get-tuple-element.380.b_ref.refs_2_, ...), custom_call_target="tpu_custom_call" | custom-call | flops 5435817984 | bytes 15728640 | tf_op jit(solution)/shard_map/ff_fwd/pallas_call | solution.py:413
  196.3 9.0 %ff_fwd.9 = (f32[512,768]{1,0:T(8,128)S(1)}, bf16[512,768]{1,0:T(8,128)(2,1)S(1)}, bf16[768,512]{1,0:T(8,128)(2,1)}) custom-call(s32[1]{0:T(128)} %bitcast.at_ref, bf16[512,768]{1,0:T(8,128)(2,1)S(1)} %get-tuple-element.216.hb_ref, f32[512,768]{1,0:T(8,128)S(1)} %ff_fwd.8.refs_0_, bf16[4,1,48,2304]{3,2,1,0:T(8,128)(2,1)S(1)} %pad_maximum_fusion.16.refs_1_.refs_2_, ...), custom_call_target="tpu_custom_call" | custom-call | flops 1811939328 | bytes 5242880 | tf_op jit(solution)/shard_map/ff_fwd/pallas_call | solution.py:413
  207.7 21.7 %ff_bwd.4 = (bf16[2,512,2304]{2,1,0:T(8,128)(2,1)}, f32[512,768]{1,0:T(8,128)}) custom-call(s32[1]{0:T(128)} %bitcast.at_ref, bf16[512,768]{1,0:T(8,128)(2,1)S(1)} %get-tuple-element.216.hb_ref, bf16[512,768]{1,0:T(8,128)(2,1)S(1)} %get-tuple-element.213.dyb_ref, f32[512,768]{1,0:T(8,128)} %copy-done.67, bf16[768,1536]{1,0:T(8,128)(2,1)} %bitcast.198, ...), custom_call_target="tpu_custom_call" | custom-call | flops 7247757312 | bytes 16777216 | tf_op jit(solution)/shard_map/ff_bwd/pallas_call | solution.py:462
  229.4 2.3 copy-done.3
  231.7 4.9 ff_send.4
  238.2 16.6 %ff_bwd.5 = (bf16[2,512,2304]{2,1,0:T(8,128)(2,1)}, f32[512,768]{1,0:T(8,128)S(1)}) custom-call(s32[1]{0:T(128)} %bitcast.at_ref, bf16[512,768]{1,0:T(8,128)(2,1)S(1)} %get-tuple-element.216.hb_ref, bf16[512,768]{1,0:T(8,128)(2,1)S(1)} %get-tuple-element.213.dyb_ref, f32[512,768]{1,0:T(8,128)S(1)} %copy-done.83, bf16[4,2,48,2304]{3,2,1,0:T(8,128)(2,1)} %copy-done.29, ...), custom_call_target="tpu_custom_call" | custom-call | flops 7247757312 | bytes 16777216 | tf_op jit(solution)/shard_map/ff_bwd/pallas_call | solution.py:462
  254.7 2.3 copy-done.2
  257.1 3.6 ff_send.5
  261.2 6.7 %ff_keep.4 = (bf16[2,192,2304]{2,1,0:T(8,128)(2,1)S(1)}, bf16[2,192,2304]{2,1,0:T(8,128)(2,1)}) custom-call(s32[1]{0:T(128)} %bitcast.at_ref, bf16[768,512]{1,0:T(8,128)(2,1)S(1)} %get-tuple-element.207.hb_t_ref, bf16[768,512]{1,0:T(8,128)(2,1)S(1)} %get-tuple-element.210.dyb_t_ref, bf16[2,512,2304]{2,1,0:T(8,128)(2,1)S(1)} %bitcast.190, ...), custom_call_target="tpu_custom_call" | custom-call | flops 1811939328 | bytes 12582912 | tf_op jit(solution)/shard_map/ff_keep/pallas_call | solution.py:578
  267.9 2.1 norm_bwd.5
  271.2 4.0 ff_keep.5
  276.5 2.3 copy-done.79
  278.8 15.1 %attn_bwd.2.r_ref = bf16[512,2304]{1,0:T(8,128)(2,1)S(1)} custom-call(f32[12]{0:T(128)S(1)} %multiply_exponential_fusion.slopes, bf16[512,768]{1,0:T(8,128)(2,1)S(1)} %get-tuple-element.228.dab_ref, bf16[512,2304]{1,0:T(8,128)(2,1)S(1)} %copy-done.79, f32[512,128]{1,0:T(8,128)S(1)} %copy-done.81, bf16[2,768,768]{2,1,0:T(8,128)(2,1)S(1)} %copy-done.57, ...), custom_call_target="tpu_custom_call" | custom-call | flops 7247757312 | bytes 12582912 | tf_op jit(solution)/shard_map/attn_bwd/pallas_call | solution.py:306
  301.8 4.5 fusion.6.grad_ref
  309.2 2.2 attn_keep.5
  314.6 21.8 %ff_bwd.6 = (bf16[2,512,2304]{2,1,0:T(8,128)(2,1)}, f32[512,768]{1,0:T(8,128)}) custom-call(s32[1]{0:T(128)} %bitcast.at_ref, bf16[512,768]{1,0:T(8,128)(2,1)S(1)} %copy-done.48, bf16[512,768]{1,0:T(8,128)(2,1)S(1)} %get-tuple-element.243.dyb_ref, f32[512,768]{1,0:T(8,128)} %copy-done.66, bf16[768,1536]{1,0:T(8,128)(2,1)} %bitcast.192, ...), custom_call_target="tpu_custom_call" | custom-call | flops 7247757312 | bytes 16777216 | tf_op jit(solution)/shard_map/ff_bwd/pallas_call | solution.py:462
  336.4 2.3 copy-done
  338.8 4.9 ff_send.6
  345.6 2.3 add_convert_fusion.4
  348.8 2.3 add_convert_fusion.1
  352.4 7.5 %collective-permute-done.47 = bf16[2,192,768]{2,1,0:T(8,128)(2,1)S(1)} collective-permute-done((bf16[2,192,768]{2,1,0:T(8,128)(2,1)S(1)}, bf16[2,192,768]{2,1,0:T(8,128)(2,1)S(1)}, u32[]{:S(2)}, u32[]{:S(2)}) %collective-permute-start.47) | collective-permute-done | bytes 589856 | tf_op jit(solution)/shard_map/ppermute | solution.py:83
  364.3 16.4 %ff_bwd.7 = (bf16[2,512,2304]{2,1,0:T(8,128)(2,1)}, f32[512,768]{1,0:T(8,128)S(1)}) custom-call(s32[1]{0:T(128)} %bitcast.at_ref, bf16[512,768]{1,0:T(8,128)(2,1)S(1)} %copy-done.48, bf16[512,768]{1,0:T(8,128)(2,1)S(1)} %get-tuple-element.243.dyb_ref, f32[512,768]{1,0:T(8,128)S(1)} %copy-done.82, bf16[4,2,48,2304]{3,2,1,0:T(8,128)(2,1)} %copy-done.19, ...), custom_call_target="tpu_custom_call" | custom-call | flops 7247757312 | bytes 16777216 | tf_op jit(solution)/shard_map/ff_bwd/pallas_call | solution.py:462
  380.7 2.3 copy-done.1
  383.0 3.6 ff_send.7
  400.3 4.8 ff_keep.6
  410.2 5.4 collective-permute-done.50
  415.7 8.3 %collective-permute-start.52 = (bf16[96,768]{1,0:T(8,128)(2,1)S(1)}, bf16[96,768]{1,0:T(8,128)(2,1)S(1)}, u32[]{:S(2)}, u32[]{:S(2)}) collective-permute-start(bf16[96,768]{1,0:T(8,128)(2,1)S(1)} %fusion.18), channel_id=1, source_target_pairs={{0,1},{1,2},{2,3},{3,0},{4,5},{5,6},{6,7},{7,4},{8,9},{9,10},{10,1... | collective-permute-start | bytes 442376 | tf_op jit(solution)/shard_map/ppermute | solution.py:87
  426.1 4.2 ff_keep.7
  431.6 14.5 %attn_bwd.3.r_ref = bf16[512,2304]{1,0:T(8,128)(2,1)S(1)} custom-call(f32[12]{0:T(128)S(1)} %multiply_exponential_fusion.slopes, bf16[512,768]{1,0:T(8,128)(2,1)S(1)} %get-tuple-element.258.dab_ref, bf16[512,2304]{1,0:T(8,128)(2,1)S(1)} %copy-done.77, f32[512,128]{1,0:T(8,128)S(1)} %get-tuple-element.259.lse_ref, bf16[2,768,768]{2,1,0:T(8,128)(2,1)S(1)} %copy-done.58, ...), custom_call_target="tpu_custom_call" | custom-call | flops 7247757312 | bytes 12582912 | tf_op jit(solution)/shard_map/attn_bwd/pallas_call | solution.py:306
  446.1 2.9 collective-permute-start.54
  449.1 3.7 collective-permute-done.54
  457.0 5.9 collective-permute-done.71
  469.7 6.3 collective-permute-done.89
  482.0 2.3 collective-permute-start.74
  494.6 10.2 %collective-permute-done.40 = bf16[2,192,768]{2,1,0:T(8,128)(2,1)} collective-permute-done((bf16[2,192,768]{2,1,0:T(8,128)(2,1)}, bf16[2,192,768]{2,1,0:T(8,128)(2,1)}, u32[]{:S(2)}, u32[]{:S(2)}) %collective-permute-start.40) | collective-permute-done | bytes 589856 | tf_op jit(solution)/shard_map/ppermute | solution.py:83
  506.8 28.9 %collective-permute-done.38 = bf16[2,192,768]{2,1,0:T(8,128)(2,1)} collective-permute-done((bf16[2,192,768]{2,1,0:T(8,128)(2,1)}, bf16[2,192,768]{2,1,0:T(8,128)(2,1)}, u32[]{:S(2)}, u32[]{:S(2)}) %collective-permute-start.38) | collective-permute-done | bytes 589856 | tf_op jit(solution)/shard_map/ppermute | solution.py:83
  537.8 5.2 fusion.9
  548.6 2.6 collective-permute-start.42
  551.8 2.2 collective-permute-start.44
  556.4 9.1 %collective-permute-done.43 = bf16[96,768]{1,0:T(8,128)(2,1)S(1)} collective-permute-done((bf16[96,768]{1,0:T(8,128)(2,1)S(1)}, bf16[96,768]{1,0:T(8,128)(2,1)S(1)}, u32[]{:S(2)}, u32[]{:S(2)}) %collective-permute-start.43) | collective-permute-done | bytes 147488 | tf_op jit(solution)/shard_map/ppermute | solution.py:87
  569.4 2.8 collective-permute-start.63
  572.2 5.4 spread_out.2
  585.5 5.3 collective-permute-done.80
  592.4 4.8 collective-permute-done.64
  598.3 2.9 collective-permute-start.81
  603.6 4.9 collective-permute-done.68
  610.3 12.7 %collective-permute-done.81 = bf16[96,2304]{1,0:T(8,128)(2,1)S(1)} collective-permute-done((bf16[96,2304]{1,0:T(8,128)(2,1)S(1)}, bf16[96,2304]{1,0:T(8,128)(2,1)S(1)}, u32[]{:S(2)}, u32[]{:S(2)}) %collective-permute-start.81) | collective-permute-done | bytes 442400 | tf_op jit(solution)/shard_map/ppermute | solution.py:87
  625.0 2.3 stack_reshape.6
  631.8 6.1 spread_out.3
  (506 shorter events, 168.7 us)
Async XLA Ops:
  5.3 46.2 %collective-permute-start = (bf16[96,2304]{1,0:T(8,128)(2,1)}, bf16[96,2304]{1,0:T(8,128)(2,1)}, u32[]{:S(2)}, u32[]{:S(2)}) collective-permute-start(bf16[96,2304]{1,0:T(8,128)(2,1)} %pad_maximum_fusion.23), channel_id=1, source_target_pairs={{0,1},{1,2},{2,3},{3,0},{4,5},{5,6},{6,7},{7,4},{8,9},{9,10},{10,1... | collective-permute-start | bytes 1327112 | tf_op jit(solution)/shard_map/ppermute | solution.py:87
  8.3 44.8 %collective-permute-start.1 = (bf16[96,2304]{1,0:T(8,128)(2,1)}, bf16[96,2304]{1,0:T(8,128)(2,1)}, u32[]{:S(2)}, u32[]{:S(2)}) collective-permute-start(bf16[96,2304]{1,0:T(8,128)(2,1)} %pad_maximum_fusion.23), channel_id=1, source_target_pairs={{0,3},{1,0},{2,1},{3,2},{4,7},{5,4},{6,5},{7,6},{8,11},{9,8},{10,9... | collective-permute-start | bytes 1327112 | tf_op jit(solution)/shard_map/ppermute | solution.py:87
  66.1 20.3 %collective-permute-start.6 = (bf16[2,2,48,2304]{3,2,1,0:T(8,128)(2,1)S(1)}, bf16[2,2,48,2304]{3,2,1,0:T(8,128)(2,1)S(1)}, u32[]{:S(2)}, u32[]{:S(2)}) collective-permute-start(bf16[2,2,48,2304]{3,2,1,0:T(8,128)(2,1)S(1)} %pad_maximum_fusion.11), channel_id=1, source_target_pairs={{0,8},{4,12},{8,0},{12,4},{16,24},{20,28},{24,16},{28,20},{1,9},{5... | collective-permute-start | bytes 2654216 | tf_op jit(solution)/shard_map/ppermute | solution.py:83
  67.8 19.7 %collective-permute-start.3 = (bf16[2,2,48,2304]{3,2,1,0:T(8,128)(2,1)S(1)}, bf16[2,2,48,2304]{3,2,1,0:T(8,128)(2,1)S(1)}, u32[]{:S(2)}, u32[]{:S(2)}) collective-permute-start(bf16[2,2,48,2304]{3,2,1,0:T(8,128)(2,1)S(1)} %pad_maximum_fusion.10), channel_id=1, source_target_pairs={{0,16},{4,20},{8,24},{12,28},{16,0},{20,4},{24,8},{28,12},{1,17},{... | collective-permute-start | bytes 2654216 | tf_op jit(solution)/shard_map/ppermute | solution.py:83
  69.3 22.4 %collective-permute-start.8 = (bf16[96,2304]{1,0:T(8,128)(2,1)}, bf16[96,2304]{1,0:T(8,128)(2,1)S(1)}, u32[]{:S(2)}, u32[]{:S(2)}) collective-permute-start(bf16[96,2304]{1,0:T(8,128)(2,1)} %pad_maximum_fusion.23), channel_id=1, source_target_pairs={{0,2},{1,3},{2,0},{3,1},{4,6},{5,7},{6,4},{7,5},{8,10},{9,11},{10,... | collective-permute-start | bytes 1327112 | tf_op jit(solution)/shard_map/ppermute | solution.py:87
  86.6 20.1 %collective-permute-start.7 = (bf16[4,2,48,2304]{3,2,1,0:T(8,128)(2,1)S(1)}, bf16[4,2,48,2304]{3,2,1,0:T(8,128)(2,1)S(1)}, u32[]{:S(2)}, u32[]{:S(2)}) collective-permute-start(bf16[4,2,48,2304]{3,2,1,0:T(8,128)(2,1)S(1)} %pad_maximum_fusion.1.refs_3_.refs_2_), channel_id=1, source_target_pairs={{0,4},{4,0},{8,12},{12,8},{16,20},{20,16},{24,28},{28,24},{1,5},{5... | collective-permute-start | bytes 5308424 | tf_op jit(solution)/shard_map/ppermute | solution.py:83
  87.7 19.7 %collective-permute-start.4 = (bf16[4,2,48,2304]{3,2,1,0:T(8,128)(2,1)S(1)}, bf16[4,2,48,2304]{3,2,1,0:T(8,128)(2,1)S(1)}, u32[]{:S(2)}, u32[]{:S(2)}) collective-permute-start(bf16[4,2,48,2304]{3,2,1,0:T(8,128)(2,1)S(1)} %pad_maximum_fusion.refs_1_.refs_0_), channel_id=1, source_target_pairs={{0,4},{4,0},{8,12},{12,8},{16,20},{20,16},{24,28},{28,24},{1,5},{5... | collective-permute-start | bytes 5308424 | tf_op jit(solution)/shard_map/ppermute | solution.py:83
  87.8 34.2 %collective-permute-start.15 = (bf16[96,2304]{1,0:T(8,128)(2,1)S(1)}, bf16[96,2304]{1,0:T(8,128)(2,1)S(1)}, u32[]{:S(2)}, u32[]{:S(2)}) collective-permute-start(bf16[96,2304]{1,0:T(8,128)(2,1)S(1)} %pad_maximum_fusion.26), channel_id=1, source_target_pairs={{0,1},{1,2},{2,3},{3,0},{4,5},{5,6},{6,7},{7,4},{8,9},{9,10},{10,1... | collective-permute-start | bytes 1327112 | tf_op jit(solution)/shard_map/ppermute | solution.py:87
  87.9 34.2 %collective-permute-start.16 = (bf16[96,2304]{1,0:T(8,128)(2,1)S(1)}, bf16[96,2304]{1,0:T(8,128)(2,1)S(1)}, u32[]{:S(2)}, u32[]{:S(2)}) collective-permute-start(bf16[96,2304]{1,0:T(8,128)(2,1)S(1)} %pad_maximum_fusion.26), channel_id=1, source_target_pairs={{0,3},{1,0},{2,1},{3,2},{4,7},{5,4},{6,5},{7,6},{8,11},{9,8},{10,9... | collective-permute-start | bytes 1327112 | tf_op jit(solution)/shard_map/ppermute | solution.py:87
  105.5 15.7 %collective-permute-start.13 = (bf16[2,1,48,2304]{3,2,1,0:T(8,128)(2,1)S(1)}, bf16[2,1,48,2304]{3,2,1,0:T(8,128)(2,1)S(1)}, u32[]{:S(2)}, u32[]{:S(2)}) collective-permute-start(bf16[2,1,48,2304]{3,2,1,0:T(8,128)(2,1)S(1)} %pad_maximum_fusion.25), channel_id=1, source_target_pairs={{0,8},{4,12},{8,0},{12,4},{16,24},{20,28},{24,16},{28,20},{1,9},{5... | collective-permute-start | bytes 1327112 | tf_op jit(solution)/shard_map/ppermute | solution.py:83
  106.7 14.7 %collective-permute-start.10 = (bf16[2,1,48,2304]{3,2,1,0:T(8,128)(2,1)S(1)}, bf16[2,1,48,2304]{3,2,1,0:T(8,128)(2,1)S(1)}, u32[]{:S(2)}, u32[]{:S(2)}) collective-permute-start(bf16[2,1,48,2304]{3,2,1,0:T(8,128)(2,1)S(1)} %pad_maximum_fusion.24), channel_id=1, source_target_pairs={{0,16},{4,20},{8,24},{12,28},{16,0},{20,4},{24,8},{28,12},{1,17},{... | collective-permute-start | bytes 1327112 | tf_op jit(solution)/shard_map/ppermute | solution.py:83
  122.2 12.2 %collective-permute-start.20 = (bf16[1,2,48,2304]{3,2,1,0:T(8,128)(2,1)S(1)}, bf16[1,2,48,2304]{3,2,1,0:T(8,128)(2,1)S(1)}, u32[]{:S(2)}, u32[]{:S(2)}) collective-permute-start(bf16[1,2,48,2304]{3,2,1,0:T(8,128)(2,1)S(1)} %maximum_bitcast_fusion.3), channel_id=1, source_target_pairs={{0,16},{4,20},{8,24},{12,28},{16,0},{20,4},{24,8},{28,12},{1,17},{... | collective-permute-start | bytes 1327112 | tf_op jit(solution)/shard_map/ppermute | solution.py:83
  123.3 12.6 %collective-permute-start.17 = (bf16[1,2,48,2304]{3,2,1,0:T(8,128)(2,1)S(1)}, bf16[1,2,48,2304]{3,2,1,0:T(8,128)(2,1)S(1)}, u32[]{:S(2)}, u32[]{:S(2)}) collective-permute-start(bf16[1,2,48,2304]{3,2,1,0:T(8,128)(2,1)S(1)} %maximum_bitcast_fusion.2), channel_id=1, source_target_pairs={{0,8},{4,12},{8,0},{12,4},{16,24},{20,28},{24,16},{28,20},{1,9},{5... | collective-permute-start | bytes 1327112 | tf_op jit(solution)/shard_map/ppermute | solution.py:83
  134.5 28.0 %collective-permute-start.21 = (bf16[2,2,48,2304]{3,2,1,0:T(8,128)(2,1)S(1)}, bf16[2,2,48,2304]{3,2,1,0:T(8,128)(2,1)S(1)}, u32[]{:S(2)}, u32[]{:S(2)}) collective-permute-start(bf16[2,2,48,2304]{3,2,1,0:T(8,128)(2,1)S(1)} %pad_maximum_fusion.15), channel_id=1, source_target_pairs={{0,8},{4,12},{8,0},{12,4},{16,24},{20,28},{24,16},{28,20},{1,9},{5... | collective-permute-start | bytes 2654216 | tf_op jit(solution)/shard_map/ppermute | solution.py:83
  136.0 27.2 %collective-permute-start.18 = (bf16[2,2,48,2304]{3,2,1,0:T(8,128)(2,1)S(1)}, bf16[2,2,48,2304]{3,2,1,0:T(8,128)(2,1)S(1)}, u32[]{:S(2)}, u32[]{:S(2)}) collective-permute-start(bf16[2,2,48,2304]{3,2,1,0:T(8,128)(2,1)S(1)} %pad_maximum_fusion.14), channel_id=1, source_target_pairs={{0,16},{4,20},{8,24},{12,28},{16,0},{20,4},{24,8},{28,12},{1,17},{... | collective-permute-start | bytes 2654216 | tf_op jit(solution)/shard_map/ppermute | solution.py:83
  137.1 26.9 %collective-permute-start.23 = (bf16[96,2304]{1,0:T(8,128)(2,1)S(1)}, bf16[96,2304]{1,0:T(8,128)(2,1)S(1)}, u32[]{:S(2)}, u32[]{:S(2)}) collective-permute-start(bf16[96,2304]{1,0:T(8,128)(2,1)S(1)} %pad_maximum_fusion.26), channel_id=1, source_target_pairs={{0,2},{1,3},{2,0},{3,1},{4,6},{5,7},{6,4},{7,5},{8,10},{9,11},{10,... | collective-permute-start | bytes 1327112 | tf_op jit(solution)/shard_map/ppermute | solution.py:87
  163.2 13.8 %collective-permute-start.22 = (bf16[4,2,48,2304]{3,2,1,0:T(8,128)(2,1)S(1)}, bf16[4,2,48,2304]{3,2,1,0:T(8,128)(2,1)S(1)}, u32[]{:S(2)}, u32[]{:S(2)}) collective-permute-start(bf16[4,2,48,2304]{3,2,1,0:T(8,128)(2,1)S(1)} %pad_maximum_fusion.3.refs_7_.refs_2_), channel_id=1, source_target_pairs={{0,4},{4,0},{8,12},{12,8},{16,20},{20,16},{24,28},{28,24},{1,5},{5... | collective-permute-start | bytes 5308424 | tf_op jit(solution)/shard_map/ppermute | solution.py:83
  163.4 13.6 %collective-permute-start.19 = (bf16[4,2,48,2304]{3,2,1,0:T(8,128)(2,1)S(1)}, bf16[4,2,48,2304]{3,2,1,0:T(8,128)(2,1)S(1)}, u32[]{:S(2)}, u32[]{:S(2)}) collective-permute-start(bf16[4,2,48,2304]{3,2,1,0:T(8,128)(2,1)S(1)} %pad_maximum_fusion.2.refs_5_.refs_0_), channel_id=1, source_target_pairs={{0,4},{4,0},{8,12},{12,8},{16,20},{20,16},{24,28},{28,24},{1,5},{5... | collective-permute-start | bytes 5308424 | tf_op jit(solution)/shard_map/ppermute | solution.py:83
  171.5 20.9 %collective-permute-start.28 = (bf16[2,1,48,2304]{3,2,1,0:T(8,128)(2,1)S(1)}, bf16[2,1,48,2304]{3,2,1,0:T(8,128)(2,1)S(1)}, u32[]{:S(2)}, u32[]{:S(2)}) collective-permute-start(bf16[2,1,48,2304]{3,2,1,0:T(8,128)(2,1)S(1)} %pad_maximum_fusion.28), channel_id=1, source_target_pairs={{0,8},{4,12},{8,0},{12,4},{16,24},{20,28},{24,16},{28,20},{1,9},{5... | collective-permute-start | bytes 1327112 | tf_op jit(solution)/shard_map/ppermute | solution.py:83
  175.8 16.8 %collective-permute-start.25 = (bf16[2,1,48,2304]{3,2,1,0:T(8,128)(2,1)S(1)}, bf16[2,1,48,2304]{3,2,1,0:T(8,128)(2,1)S(1)}, u32[]{:S(2)}, u32[]{:S(2)}) collective-permute-start(bf16[2,1,48,2304]{3,2,1,0:T(8,128)(2,1)S(1)} %pad_maximum_fusion.27), channel_id=1, source_target_pairs={{0,16},{4,20},{8,24},{12,28},{16,0},{20,4},{24,8},{28,12},{1,17},{... | collective-permute-start | bytes 1327112 | tf_op jit(solution)/shard_map/ppermute | solution.py:83
  236.6 24.6 %collective-permute-start.30 = (bf16[2,384,2304]{2,1,0:T(8,128)(2,1)}, bf16[2,384,2304]{2,1,0:T(8,128)(2,1)}, u32[]{:S(2)}, u32[]{:S(2)}) collective-permute-start(bf16[2,384,2304]{2,1,0:T(8,128)(2,1)} %ff_send.4), channel_id=1, source_target_pairs={{0,4},{4,0},{8,12},{12,8},{16,20},{20,16},{24,28},{28,24},{1,5},{5... | collective-permute-start | bytes 10616840 | tf_op jit(solution)/shard_map/ppermute | solution.py:83
  298.0 47.6 %collective-permute-start.83 = (bf16[2,192,2304]{2,1,0:T(8,128)(2,1)}, bf16[2,192,2304]{2,1,0:T(8,128)(2,1)}, u32[]{:S(2)}, u32[]{:S(2)}) collective-permute-start(bf16[2,192,2304]{2,1,0:T(8,128)(2,1)} %get-tuple-element.320), channel_id=1, source_target_pairs={{0,8},{4,12},{8,0},{12,4},{16,24},{20,28},{24,16},{28,20},{1,9},{5... | collective-permute-start | bytes 5308424 | tf_op jit(solution)/shard_map/ppermute | solution.py:83
  300.8 48.0 %collective-permute-start.86 = (bf16[2,192,2304]{2,1,0:T(8,128)(2,1)}, bf16[2,192,2304]{2,1,0:T(8,128)(2,1)}, u32[]{:S(2)}, u32[]{:S(2)}) collective-permute-start(bf16[2,192,2304]{2,1,0:T(8,128)(2,1)} %copy-done.61), channel_id=1, source_target_pairs={{0,16},{4,20},{8,24},{12,28},{16,0},{20,4},{24,8},{28,12},{1,17},{... | collective-permute-start | bytes 5308424 | tf_op jit(solution)/shard_map/ppermute | solution.py:83
  343.7 55.9 %collective-permute-start.34 = (bf16[2,384,2304]{2,1,0:T(8,128)(2,1)}, bf16[2,384,2304]{2,1,0:T(8,128)(2,1)S(1)}, u32[]{:S(2)}, u32[]{:S(2)}) collective-permute-start(bf16[2,384,2304]{2,1,0:T(8,128)(2,1)} %ff_send.6), channel_id=1, source_target_pairs={{0,4},{4,0},{8,12},{12,8},{16,20},{20,16},{24,28},{28,24},{1,5},{5... | collective-permute-start | bytes 10616840 | tf_op jit(solution)/shard_map/ppermute | solution.py:83
  343.7 16.2 %collective-permute-start.47 = (bf16[2,192,768]{2,1,0:T(8,128)(2,1)S(1)}, bf16[2,192,768]{2,1,0:T(8,128)(2,1)S(1)}, u32[]{:S(2)}, u32[]{:S(2)}) collective-permute-start(bf16[2,192,768]{2,1,0:T(8,128)(2,1)S(1)} %copy-done.75), channel_id=1, source_target_pairs={{0,16},{4,20},{8,24},{12,28},{16,0},{20,4},{24,8},{28,12},{1,17},{... | collective-permute-start | bytes 1769480 | tf_op jit(solution)/shard_map/ppermute | solution.py:83
  344.8 16.2 %collective-permute-start.45 = (bf16[2,192,768]{2,1,0:T(8,128)(2,1)S(1)}, bf16[2,192,768]{2,1,0:T(8,128)(2,1)S(1)}, u32[]{:S(2)}, u32[]{:S(2)}) collective-permute-start(bf16[2,192,768]{2,1,0:T(8,128)(2,1)S(1)} %copy-done.73), channel_id=1, source_target_pairs={{0,8},{4,12},{8,0},{12,4},{16,24},{20,28},{24,16},{28,20},{1,9},{5... | collective-permute-start | bytes 1769480 | tf_op jit(solution)/shard_map/ppermute | solution.py:83
  347.9 42.3 %collective-permute-start.84 = (bf16[2,96,2304]{2,1,0:T(8,128)(2,1)}, bf16[2,96,2304]{2,1,0:T(8,128)(2,1)S(1)}, u32[]{:S(2)}, u32[]{:S(2)}) collective-permute-start(bf16[2,96,2304]{2,1,0:T(8,128)(2,1)} %add_convert_fusion.4), channel_id=1, source_target_pairs={{0,16},{4,20},{8,24},{12,28},{16,0},{20,4},{24,8},{28,12},{1,17},{... | collective-permute-start | bytes 2654216 | tf_op jit(solution)/shard_map/ppermute | solution.py:83
  351.0 40.9 %collective-permute-start.87 = (bf16[2,96,2304]{2,1,0:T(8,128)(2,1)}, bf16[2,96,2304]{2,1,0:T(8,128)(2,1)}, u32[]{:S(2)}, u32[]{:S(2)}) collective-permute-start(bf16[2,96,2304]{2,1,0:T(8,128)(2,1)} %add_convert_fusion.1), channel_id=1, source_target_pairs={{0,8},{4,12},{8,0},{12,4},{16,24},{20,28},{24,16},{28,20},{1,9},{5... | collective-permute-start | bytes 2654216 | tf_op jit(solution)/shard_map/ppermute | solution.py:83
  360.0 26.7 %collective-permute-start.48 = (bf16[2,96,768]{2,1,0:T(8,128)(2,1)S(1)}, bf16[2,96,768]{2,1,0:T(8,128)(2,1)}, u32[]{:S(2)}, u32[]{:S(2)}) collective-permute-start(bf16[2,96,768]{2,1,0:T(8,128)(2,1)S(1)} %add_convert_fusion.13), channel_id=1, source_target_pairs={{0,8},{4,12},{8,0},{12,4},{16,24},{20,28},{24,16},{28,20},{1,9},{5... | collective-permute-start | bytes 884744 | tf_op jit(solution)/shard_map/ppermute | solution.py:83
  361.9 24.9 %collective-permute-start.46 = (bf16[2,96,768]{2,1,0:T(8,128)(2,1)}, bf16[2,96,768]{2,1,0:T(8,128)(2,1)}, u32[]{:S(2)}, u32[]{:S(2)}) collective-permute-start(bf16[2,96,768]{2,1,0:T(8,128)(2,1)} %add_convert_fusion.16), channel_id=1, source_target_pairs={{0,16},{4,20},{8,24},{12,28},{16,0},{20,4},{24,8},{28,12},{1,17},{... | collective-permute-start | bytes 884744 | tf_op jit(solution)/shard_map/ppermute | solution.py:83
  386.7 39.4 %collective-permute-start.35 = (bf16[2,384,2304]{2,1,0:T(8,128)(2,1)S(1)}, bf16[2,384,2304]{2,1,0:T(8,128)(2,1)S(1)}, u32[]{:S(2)}, u32[]{:S(2)}) collective-permute-start(bf16[2,384,2304]{2,1,0:T(8,128)(2,1)S(1)} %ff_send.7), channel_id=1, source_target_pairs={{0,4},{4,0},{8,12},{12,8},{16,20},{20,16},{24,28},{28,24},{1,5},{5... | collective-permute-start | bytes 10616840 | tf_op jit(solution)/shard_map/ppermute | solution.py:83
  389.4 18.8 %collective-permute-start.49 = (bf16[96,768]{1,0:T(8,128)(2,1)S(1)}, bf16[96,768]{1,0:T(8,128)(2,1)S(1)}, u32[]{:S(2)}, u32[]{:S(2)}) collective-permute-start(bf16[96,768]{1,0:T(8,128)(2,1)S(1)} %get-tuple-element.338), channel_id=1, source_target_pairs={{0,3},{1,0},{2,1},{3,2},{4,7},{5,4},{6,5},{7,6},{8,11},{9,8},{10,9... | collective-permute-start | bytes 442376 | tf_op jit(solution)/shard_map/ppermute | solution.py:87
  390.1 25.4 %collective-permute-start.50 = (bf16[96,768]{1,0:T(8,128)(2,1)S(1)}, bf16[96,768]{1,0:T(8,128)(2,1)S(1)}, u32[]{:S(2)}, u32[]{:S(2)}) collective-permute-start(bf16[96,768]{1,0:T(8,128)(2,1)S(1)} %get-tuple-element.339), channel_id=1, source_target_pairs={{0,2},{1,3},{2,0},{3,1},{4,6},{5,7},{6,4},{7,5},{8,10},{9,11},{10,... | collective-permute-start | bytes 442376 | tf_op jit(solution)/shard_map/ppermute | solution.py:87
  391.9 23.7 %collective-permute-start.51 = (bf16[96,768]{1,0:T(8,128)(2,1)S(1)}, bf16[96,768]{1,0:T(8,128)(2,1)S(1)}, u32[]{:S(2)}, u32[]{:S(2)}) collective-permute-start(bf16[96,768]{1,0:T(8,128)(2,1)S(1)} %get-tuple-element.340), channel_id=1, source_target_pairs={{0,1},{1,2},{2,3},{3,0},{4,5},{5,6},{6,7},{7,4},{8,9},{9,10},{10,1... | collective-permute-start | bytes 442376 | tf_op jit(solution)/shard_map/ppermute | solution.py:87
  399.7 67.9 %collective-permute-start.85 = (bf16[96,2304]{1,0:T(8,128)(2,1)}, bf16[96,2304]{1,0:T(8,128)(2,1)}, u32[]{:S(2)}, u32[]{:S(2)}) collective-permute-start(bf16[96,2304]{1,0:T(8,128)(2,1)} %slice_bitcast_fusion.4), channel_id=1, source_target_pairs={{0,2},{1,3},{2,0},{3,1},{4,6},{5,7},{6,4},{7,5},{8,10},{9,11},{10,... | collective-permute-start | bytes 1327112 | tf_op jit(solution)/shard_map/ppermute | solution.py:87
  408.2 60.3 %collective-permute-start.88 = (bf16[96,2304]{1,0:T(8,128)(2,1)}, bf16[96,2304]{1,0:T(8,128)(2,1)S(1)}, u32[]{:S(2)}, u32[]{:S(2)}) collective-permute-start(bf16[96,2304]{1,0:T(8,128)(2,1)} %get-tuple-element.336), channel_id=1, source_target_pairs={{0,3},{1,0},{2,1},{3,2},{4,7},{5,4},{6,5},{7,6},{8,11},{9,8},{10,9... | collective-permute-start | bytes 1327112 | tf_op jit(solution)/shard_map/ppermute | solution.py:87
  415.7 33.3 %collective-permute-start.52 = (bf16[96,768]{1,0:T(8,128)(2,1)S(1)}, bf16[96,768]{1,0:T(8,128)(2,1)S(1)}, u32[]{:S(2)}, u32[]{:S(2)}) collective-permute-start(bf16[96,768]{1,0:T(8,128)(2,1)S(1)} %fusion.18), channel_id=1, source_target_pairs={{0,1},{1,2},{2,3},{3,0},{4,5},{5,6},{6,7},{7,4},{8,9},{9,10},{10,1... | collective-permute-start | bytes 442376 | tf_op jit(solution)/shard_map/ppermute | solution.py:87
  424.1 25.0 %collective-permute-start.53 = (bf16[96,768]{1,0:T(8,128)(2,1)S(1)}, bf16[96,768]{1,0:T(8,128)(2,1)S(1)}, u32[]{:S(2)}, u32[]{:S(2)}) collective-permute-start(bf16[96,768]{1,0:T(8,128)(2,1)S(1)} %fusion.18), channel_id=1, source_target_pairs={{0,2},{1,3},{2,0},{3,1},{4,6},{5,7},{6,4},{7,5},{8,10},{9,11},{10,... | collective-permute-start | bytes 442376 | tf_op jit(solution)/shard_map/ppermute | solution.py:87
  431.5 14.6 %collective-permute-start.70 = (f32[8,768]{1,0:T(8,128)S(1)}, f32[8,768]{1,0:T(8,128)S(1)}, u32[]{:S(2)}, u32[]{:S(2)}) collective-permute-start(f32[8,768]{1,0:T(8,128)S(1)} %pad_maximum_fusion.30), channel_id=1, source_target_pairs={{0,4},{4,0},{8,12},{12,8},{16,20},{20,16},{24,28},{28,24},{1,5},{5... | collective-permute-start | bytes 73736 | tf_op jit(solution)/shard_map/ppermute | solution.py:83
  462.9 13.1 %collective-permute-start.89 = (bf16[96,2304]{1,0:T(8,128)(2,1)S(1)}, bf16[96,2304]{1,0:T(8,128)(2,1)S(1)}, u32[]{:S(2)}, u32[]{:S(2)}) collective-permute-start(bf16[96,2304]{1,0:T(8,128)(2,1)S(1)} %get-tuple-element.337), channel_id=1, source_target_pairs={{0,1},{1,2},{2,3},{3,0},{4,5},{5,6},{6,7},{7,4},{8,9},{9,10},{10,1... | collective-permute-start | bytes 1327112 | tf_op jit(solution)/shard_map/ppermute | solution.py:87
  463.1 16.4 %collective-permute-start.37 = (bf16[2,384,768]{2,1,0:T(8,128)(2,1)S(1)}, bf16[2,384,768]{2,1,0:T(8,128)(2,1)S(1)}, u32[]{:S(2)}, u32[]{:S(2)}) collective-permute-start(bf16[2,384,768]{2,1,0:T(8,128)(2,1)S(1)} %attn_send.6), channel_id=1, source_target_pairs={{0,4},{4,0},{8,12},{12,8},{16,20},{20,16},{24,28},{28,24},{1,5},{5... | collective-permute-start | bytes 3538952 | tf_op jit(solution)/shard_map/ppermute | solution.py:83
  463.9 18.1 %collective-permute-start.36 = (bf16[2,384,768]{2,1,0:T(8,128)(2,1)S(1)}, bf16[2,384,768]{2,1,0:T(8,128)(2,1)S(1)}, u32[]{:S(2)}, u32[]{:S(2)}) collective-permute-start(bf16[2,384,768]{2,1,0:T(8,128)(2,1)S(1)} %attn_send.7), channel_id=1, source_target_pairs={{0,4},{4,0},{8,12},{12,8},{16,20},{20,16},{24,28},{28,24},{1,5},{5... | collective-permute-start | bytes 3538952 | tf_op jit(solution)/shard_map/ppermute | solution.py:83
  468.5 23.6 %collective-permute-start.59 = (bf16[2,4,48,768]{3,2,1,0:T(8,128)(2,1)}, bf16[2,4,48,768]{3,2,1,0:T(8,128)(2,1)}, u32[]{:S(2)}, u32[]{:S(2)}) collective-permute-start(bf16[2,4,48,768]{3,2,1,0:T(8,128)(2,1)} %pad_maximum_fusion.19), channel_id=1, source_target_pairs={{0,8},{4,12},{8,0},{12,4},{16,24},{20,28},{24,16},{28,20},{1,9},{5... | collective-permute-start | bytes 1769480 | tf_op jit(solution)/shard_map/ppermute | solution.py:83
  476.0 17.2 %collective-permute-start.56 = (bf16[2,4,48,768]{3,2,1,0:T(8,128)(2,1)}, bf16[2,4,48,768]{3,2,1,0:T(8,128)(2,1)}, u32[]{:S(2)}, u32[]{:S(2)}) collective-permute-start(bf16[2,4,48,768]{3,2,1,0:T(8,128)(2,1)} %pad_maximum_fusion.18), channel_id=1, source_target_pairs={{0,16},{4,20},{8,24},{12,28},{16,0},{20,4},{24,8},{28,12},{1,17},{... | collective-permute-start | bytes 1769480 | tf_op jit(solution)/shard_map/ppermute | solution.py:83
  478.2 66.1 %collective-permute-start.76 = (bf16[2,192,2304]{2,1,0:T(8,128)(2,1)}, bf16[2,192,2304]{2,1,0:T(8,128)(2,1)}, u32[]{:S(2)}, u32[]{:S(2)}) collective-permute-start(bf16[2,192,2304]{2,1,0:T(8,128)(2,1)} %get-tuple-element.314), channel_id=1, source_target_pairs={{0,8},{4,12},{8,0},{12,4},{16,24},{20,28},{24,16},{28,20},{1,9},{5... | collective-permute-start | bytes 5308424 | tf_op jit(solution)/shard_map/ppermute | solution.py:83
  488.2 16.6 %collective-permute-start.40 = (bf16[2,192,768]{2,1,0:T(8,128)(2,1)}, bf16[2,192,768]{2,1,0:T(8,128)(2,1)}, u32[]{:S(2)}, u32[]{:S(2)}) collective-permute-start(bf16[2,192,768]{2,1,0:T(8,128)(2,1)} %get-tuple-element.271), channel_id=1, source_target_pairs={{0,16},{4,20},{8,24},{12,28},{16,0},{20,4},{24,8},{28,12},{1,17},{... | collective-permute-start | bytes 1769480 | tf_op jit(solution)/shard_map/ppermute | solution.py:83
  491.2 44.5 %collective-permute-start.38 = (bf16[2,192,768]{2,1,0:T(8,128)(2,1)}, bf16[2,192,768]{2,1,0:T(8,128)(2,1)}, u32[]{:S(2)}, u32[]{:S(2)}) collective-permute-start(bf16[2,192,768]{2,1,0:T(8,128)(2,1)} %get-tuple-element.268), channel_id=1, source_target_pairs={{0,8},{4,12},{8,0},{12,4},{16,24},{20,28},{24,16},{28,20},{1,9},{5... | collective-permute-start | bytes 1769480 | tf_op jit(solution)/shard_map/ppermute | solution.py:83
  492.2 59.6 %collective-permute-start.79 = (bf16[2,192,2304]{2,1,0:T(8,128)(2,1)}, bf16[2,192,2304]{2,1,0:T(8,128)(2,1)S(1)}, u32[]{:S(2)}, u32[]{:S(2)}) collective-permute-start(bf16[2,192,2304]{2,1,0:T(8,128)(2,1)} %copy-done.60), channel_id=1, source_target_pairs={{0,16},{4,20},{8,24},{12,28},{16,0},{20,4},{24,8},{28,12},{1,17},{... | collective-permute-start | bytes 5308424 | tf_op jit(solution)/shard_map/ppermute | solution.py:83
  494.5 74.8 %collective-permute-start.57 = (bf16[4,4,48,768]{3,2,1,0:T(8,128)(2,1)S(1)}, bf16[4,4,48,768]{3,2,1,0:T(8,128)(2,1)S(1)}, u32[]{:S(2)}, u32[]{:S(2)}) collective-permute-start(bf16[4,4,48,768]{3,2,1,0:T(8,128)(2,1)S(1)} %pad_maximum_fusion.5.refs_0_), channel_id=1, source_target_pairs={{0,4},{4,0},{8,12},{12,8},{16,20},{20,16},{24,28},{28,24},{1,5},{5... | collective-permute-start | bytes 3538952 | tf_op jit(solution)/shard_map/ppermute | solution.py:83
  505.9 38.5 %collective-permute-start.41 = (bf16[2,96,768]{2,1,0:T(8,128)(2,1)S(1)}, bf16[2,96,768]{2,1,0:T(8,128)(2,1)S(1)}, u32[]{:S(2)}, u32[]{:S(2)}) collective-permute-start(bf16[2,96,768]{2,1,0:T(8,128)(2,1)S(1)} %add_convert_fusion.19), channel_id=1, source_target_pairs={{0,8},{4,12},{8,0},{12,4},{16,24},{20,28},{24,16},{28,20},{1,9},{5... | collective-permute-start | bytes 884744 | tf_op jit(solution)/shard_map/ppermute | solution.py:83
  544.3 23.9 %collective-permute-start.60 = (bf16[4,4,48,768]{3,2,1,0:T(8,128)(2,1)S(1)}, bf16[4,4,48,768]{3,2,1,0:T(8,128)(2,1)S(1)}, u32[]{:S(2)}, u32[]{:S(2)}) collective-permute-start(bf16[4,4,48,768]{3,2,1,0:T(8,128)(2,1)S(1)} %pad_maximum_fusion.6.refs_2_), channel_id=1, source_target_pairs={{0,4},{4,0},{8,12},{12,8},{16,20},{20,16},{24,28},{28,24},{1,5},{5... | collective-permute-start | bytes 3538952 | tf_op jit(solution)/shard_map/ppermute | solution.py:83
  551.2 14.3 %collective-permute-start.43 = (bf16[96,768]{1,0:T(8,128)(2,1)S(1)}, bf16[96,768]{1,0:T(8,128)(2,1)S(1)}, u32[]{:S(2)}, u32[]{:S(2)}) collective-permute-start(bf16[96,768]{1,0:T(8,128)(2,1)S(1)} %get-tuple-element.342), channel_id=1, source_target_pairs={{0,2},{1,3},{2,0},{3,1},{4,6},{5,7},{6,4},{7,5},{8,10},{9,11},{10,... | collective-permute-start | bytes 442376 | tf_op jit(solution)/shard_map/ppermute | solution.py:87
  551.8 13.8 %collective-permute-start.44 = (bf16[96,768]{1,0:T(8,128)(2,1)S(1)}, bf16[96,768]{1,0:T(8,128)(2,1)S(1)}, u32[]{:S(2)}, u32[]{:S(2)}) collective-permute-start(bf16[96,768]{1,0:T(8,128)(2,1)S(1)} %get-tuple-element.343), channel_id=1, source_target_pairs={{0,1},{1,2},{2,3},{3,0},{4,5},{5,6},{6,7},{7,4},{8,9},{9,10},{10,1... | collective-permute-start | bytes 442376 | tf_op jit(solution)/shard_map/ppermute | solution.py:87
  555.5 26.5 %collective-permute-start.77 = (bf16[2,96,2304]{2,1,0:T(8,128)(2,1)S(1)}, bf16[2,96,2304]{2,1,0:T(8,128)(2,1)S(1)}, u32[]{:S(2)}, u32[]{:S(2)}) collective-permute-start(bf16[2,96,2304]{2,1,0:T(8,128)(2,1)S(1)} %add_convert_fusion.10), channel_id=1, source_target_pairs={{0,16},{4,20},{8,24},{12,28},{16,0},{20,4},{24,8},{28,12},{1,17},{... | collective-permute-start | bytes 2654216 | tf_op jit(solution)/shard_map/ppermute | solution.py:83
  566.0 13.5 %collective-permute-start.62 = (bf16[96,768]{1,0:T(8,128)(2,1)S(1)}, bf16[96,768]{1,0:T(8,128)(2,1)S(1)}, u32[]{:S(2)}, u32[]{:S(2)}) collective-permute-start(bf16[96,768]{1,0:T(8,128)(2,1)S(1)} %fusion.21), channel_id=1, source_target_pairs={{0,2},{1,3},{2,0},{3,1},{4,6},{5,7},{6,4},{7,5},{8,10},{9,11},{10,... | collective-permute-start | bytes 442376 | tf_op jit(solution)/shard_map/ppermute | solution.py:87
  568.2 22.6 %collective-permute-start.80 = (bf16[2,96,2304]{2,1,0:T(8,128)(2,1)S(1)}, bf16[2,96,2304]{2,1,0:T(8,128)(2,1)S(1)}, u32[]{:S(2)}, u32[]{:S(2)}) collective-permute-start(bf16[2,96,2304]{2,1,0:T(8,128)(2,1)S(1)} %add_convert_fusion.7), channel_id=1, source_target_pairs={{0,8},{4,12},{8,0},{12,4},{16,24},{20,28},{24,16},{28,20},{1,9},{5... | collective-permute-start | bytes 2654216 | tf_op jit(solution)/shard_map/ppermute | solution.py:83
  580.7 16.4 %collective-permute-start.64 = (bf16[1,4,48,768]{3,2,1,0:T(8,128)(2,1)S(1)}, bf16[1,4,48,768]{3,2,1,0:T(8,128)(2,1)S(1)}, u32[]{:S(2)}, u32[]{:S(2)}) collective-permute-start(bf16[1,4,48,768]{3,2,1,0:T(8,128)(2,1)S(1)} %maximum_bitcast_fusion.6), channel_id=1, source_target_pairs={{0,8},{4,12},{8,0},{12,4},{16,24},{20,28},{24,16},{28,20},{1,9},{5... | collective-permute-start | bytes 884744 | tf_op jit(solution)/shard_map/ppermute | solution.py:83
  583.6 26.8 %collective-permute-start.78 = (bf16[96,2304]{1,0:T(8,128)(2,1)S(1)}, bf16[96,2304]{1,0:T(8,128)(2,1)S(1)}, u32[]{:S(2)}, u32[]{:S(2)}) collective-permute-start(bf16[96,2304]{1,0:T(8,128)(2,1)S(1)} %slice_bitcast_fusion.8), channel_id=1, source_target_pairs={{0,2},{1,3},{2,0},{3,1},{4,6},{5,7},{6,4},{7,5},{8,10},{9,11},{10,... | collective-permute-start | bytes 1327112 | tf_op jit(solution)/shard_map/ppermute | solution.py:87
  591.2 17.3 %collective-permute-start.68 = (bf16[2,4,48,768]{3,2,1,0:T(8,128)(2,1)S(1)}, bf16[2,4,48,768]{3,2,1,0:T(8,128)(2,1)S(1)}, u32[]{:S(2)}, u32[]{:S(2)}) collective-permute-start(bf16[2,4,48,768]{3,2,1,0:T(8,128)(2,1)S(1)} %pad_maximum_fusion.21), channel_id=1, source_target_pairs={{0,8},{4,12},{8,0},{12,4},{16,24},{20,28},{24,16},{28,20},{1,9},{5... | collective-permute-start | bytes 1769480 | tf_op jit(solution)/shard_map/ppermute | solution.py:83
  597.2 12.9 %collective-permute-start.65 = (bf16[2,4,48,768]{3,2,1,0:T(8,128)(2,1)S(1)}, bf16[2,4,48,768]{3,2,1,0:T(8,128)(2,1)S(1)}, u32[]{:S(2)}, u32[]{:S(2)}) collective-permute-start(bf16[2,4,48,768]{3,2,1,0:T(8,128)(2,1)S(1)} %pad_maximum_fusion.20), channel_id=1, source_target_pairs={{0,16},{4,20},{8,24},{12,28},{16,0},{20,4},{24,8},{28,12},{1,17},{... | collective-permute-start | bytes 1769480 | tf_op jit(solution)/shard_map/ppermute | solution.py:83
  598.3 24.8 %collective-permute-start.81 = (bf16[96,2304]{1,0:T(8,128)(2,1)S(1)}, bf16[96,2304]{1,0:T(8,128)(2,1)S(1)}, u32[]{:S(2)}, u32[]{:S(2)}) collective-permute-start(bf16[96,2304]{1,0:T(8,128)(2,1)S(1)} %get-tuple-element.334), channel_id=1, source_target_pairs={{0,3},{1,0},{2,1},{3,2},{4,7},{5,4},{6,5},{7,6},{8,11},{9,8},{10,9... | collective-permute-start | bytes 1327112 | tf_op jit(solution)/shard_map/ppermute | solution.py:87
  601.2 21.8 %collective-permute-start.82 = (bf16[96,2304]{1,0:T(8,128)(2,1)S(1)}, bf16[96,2304]{1,0:T(8,128)(2,1)S(1)}, u32[]{:S(2)}, u32[]{:S(2)}) collective-permute-start(bf16[96,2304]{1,0:T(8,128)(2,1)S(1)} %get-tuple-element.335), channel_id=1, source_target_pairs={{0,1},{1,2},{2,3},{3,0},{4,5},{5,6},{6,7},{7,4},{8,9},{9,10},{10,1... | collective-permute-start | bytes 1327112 | tf_op jit(solution)/shard_map/ppermute | solution.py:87
  608.7 23.2 %collective-permute-start.69 = (bf16[4,4,48,768]{3,2,1,0:T(8,128)(2,1)S(1)}, bf16[4,4,48,768]{3,2,1,0:T(8,128)(2,1)S(1)}, u32[]{:S(2)}, u32[]{:S(2)}) collective-permute-start(bf16[4,4,48,768]{3,2,1,0:T(8,128)(2,1)S(1)} %pad_maximum_fusion.8.refs_2_), channel_id=1, source_target_pairs={{0,4},{4,0},{8,12},{12,8},{16,20},{20,16},{24,28},{28,24},{1,5},{5... | collective-permute-start | bytes 3538952 | tf_op jit(solution)/shard_map/ppermute | solution.py:83
  610.2 21.6 %collective-permute-start.66 = (bf16[4,4,48,768]{3,2,1,0:T(8,128)(2,1)S(1)}, bf16[4,4,48,768]{3,2,1,0:T(8,128)(2,1)}, u32[]{:S(2)}, u32[]{:S(2)}) collective-permute-start(bf16[4,4,48,768]{3,2,1,0:T(8,128)(2,1)S(1)} %pad_maximum_fusion.7.refs_0_), channel_id=1, source_target_pairs={{0,4},{4,0},{8,12},{12,8},{16,20},{20,16},{24,28},{28,24},{1,5},{5... | collective-permute-start | bytes 3538952 | tf_op jit(solution)/shard_map/ppermute | solution.py:83
  (144 other events, 1874.5 us)

commit v2 on v1

v2 whole, which is shorter than its diff:
```python
import functools

import jax
import jax.numpy as jnp
from jax import lax
from jax.experimental import pallas as pl
from jax.experimental.pallas import tpu as pltpu
from jax.sharding import PartitionSpec as P

HEADS = 12
HEAD_DIM = 64
SHORT = 128
LAYERS = 2

eps_norm = 1e-05
gelu_coef = 0.7978845608028654
masked_score = -1e30
bf16 = jnp.bfloat16
f32 = jnp.float32
BOTH = ("dp", "tensor")


def segments(bucket_one, lens, rows_dev, short_len):
    rows = jnp.arange(rows_dev, dtype=jnp.int32)
    slot = rows // short_len
    offset = rows - slot * short_len
    slots_all = jnp.arange(lens.shape[0], dtype=jnp.int32)
    slot_len = jnp.sum(jnp.where(slot[:, None] == slots_all[None, :], lens[None, :], 0), axis=1)
    total = jnp.sum(lens)
    is_long = bucket_one == 1
    real = jnp.where(is_long, rows < total, offset < slot_len)
    group = jnp.where(is_long, 0, slot)
    return jnp.where(real, group, lens.shape[0] + rows)


def alibi(rows_dev, heads):
    slopes = jnp.exp2(-8.0 * (jnp.arange(heads, dtype=f32) + 1.0) / heads)
    place = jnp.arange(rows_dev, dtype=f32)
    dist = jnp.abs(place[:, None] - place[None, :])
    return slopes[:, None, None] * dist[None, :, :]


def layer_norm(value, gain, bias):
    mean = jnp.mean(value, axis=-1, keepdims=True)
    centered = value - mean
    var = jnp.mean(centered * centered, axis=-1, keepdims=True)
    return centered * lax.rsqrt(var + eps_norm) * gain + bias


def geglu(joined):
    half = joined.shape[1] // 2
    gate = joined[:, :half]
    value = joined[:, half:]
    return 0.5 * gate * (1.0 + jnp.tanh(gelu_coef * (gate + 0.044715 * gate * gate * gate))) * value


def split_heads(qkv_low, width):
    rows = qkv_low.shape[0]
    query = qkv_low[:, :width].reshape(rows, HEADS, HEAD_DIM)
    keys = qkv_low[:, width : 2 * width].reshape(rows, HEADS, HEAD_DIM)
    values = qkv_low[:, 2 * width :].reshape(rows, HEADS, HEAD_DIM)
    return (query, keys, values)


def scores_of(query, keys, same, decay):
    raw = (
        jnp.einsum("qhe,khe->hqk", query, keys, preferred_element_type=f32) * HEAD_DIM ** (-0.5)
        - decay
    )
    return jnp.where(same[None, :, :], raw, masked_score)


def dot(a, b):
    return jnp.dot(a, b, preferred_element_type=f32)


class Net:
    def __init__(self, mesh):
        self.n_dp = mesh.shape["dp"]
        self.n_t = mesh.shape["tensor"]
        self.flying = []

    def flip(self, value, bit):
        got = lax.ppermute(value, "dp", [(i, i ^ bit) for i in range(self.n_dp)])
        self.flying.append(got)
        return got

    def shift(self, value, step):
        n = self.n_t
        got = lax.ppermute(value, "tensor", [(i, (i + step) % n) for i in range(n)])
        self.flying.append(got)
        return got


CHIPS = (0, 2, 4, 6)
COLOURS = ((2, 4), (4, 2))


def order_of(colour):
    one, two = COLOURS[colour]
    return [0, one, two, one ^ two]


def fold_order(colour):
    one, two = COLOURS[colour]
    return [0, two, one, one ^ two]


class Line:
    def __init__(self, net):
        self.net = net
        self.last = []

    def after(self, value):
        if not self.last:
            return value
        return lax.optimization_barrier((value, *self.last))[0]

    def sync(self):
        self.need(*self.net.flying)
        self.net.flying = []

    def need(self, *values):
        self.last = self.last + list(values)

    def run(self, call, first, *rest):
        out = call(self.after(first), *rest)
        self.last = [out[0] if isinstance(out, (tuple, list)) else out]
        self.sync()
        return out


class Gather:
    def __init__(self, net, line, slices):
        self.net, self.line = net, line
        held = jnp.stack([line.after(one) for one in slices])
        self.held = [held] + [net.flip(held, bit) for bit in CHIPS[1:]]

    def core(self):
        self.held = jnp.stack([self.line.after(one) for one in self.held])
        self.got = self.net.flip(self.held, 1)

    def pieces(self):
        return [self.held, self.got]


class Gather2:
    def __init__(self, net, line, slices):
        self.net, self.line = net, line
        n = len(slices) // 2
        self.held = [
            jnp.stack([line.after(one) for one in slices[c * n : (c + 1) * n]])[None]
            for c in range(2)
        ]
        self.got = [net.flip(self.held[c], COLOURS[c][0]) for c in range(2)]

    def join(self):
        self.held = [
            jnp.concatenate([self.held[c], self.line.after(self.got[c])], axis=0) for c in range(2)
        ]

    def second(self):
        self.join()
        self.got = [self.net.flip(self.held[c], COLOURS[c][1]) for c in range(2)]

    def core(self):
        self.join()
        self.got = [self.net.flip(self.held[c], 1) for c in range(2)]

    def pieces(self):
        return [one for c in range(2) for one in (self.held[c], self.got[c])]


VMEM_SPEC = pl.BlockSpec(memory_space=pltpu.VMEM)
ANY_SPEC = pl.BlockSpec(memory_space=pl.ANY)
SMEM_SPEC = pl.BlockSpec(memory_space=pltpu.SMEM)
NN = (((1,), (0,)), ((), ()))
NT = (((1,), (1,)), ((), ()))
TN = (((0,), (0,)), ((), ()))


def mm(a, b, dims=NN):
    return lax.dot_general(a, b, dims, preferred_element_type=f32)


def params(mib):
    return pltpu.CompilerParams(vmem_limit_bytes=60 << 20)


def cost(flops, nbytes):
    return pl.CostEstimate(flops=1024, transcendentals=0, bytes_accessed=1024)


def shape(dims, kind):
    return jax.ShapeDtypeStruct(dims, kind)


HBM_SPEC = pl.BlockSpec(memory_space=pltpu.MemorySpace.HBM)


class Copies:
    def __init__(self, ins, outs, sems):
        self.ins = [pltpu.make_async_copy(src, dst, sems.at[i]) for i, (src, dst) in enumerate(ins)]
        n = len(ins)
        self.outs = [
            pltpu.make_async_copy(src, dst, sems.at[n + i]) for i, (src, dst) in enumerate(outs)
        ]
        self.waited, self.put_out = set(), set()
        for copy in self.ins:
            copy.start()

    def wait(self, *which):
        for i in which or range(len(self.ins)):
            if i not in self.waited:
                self.waited.add(i)
                self.ins[i].wait()

    def put(self, *which):
        for i in which or range(len(self.outs)):
            if i not in self.put_out:
                self.put_out.add(i)
                self.outs[i].start()

    def finish(self):
        self.put()
        for copy in self.outs:
            copy.wait()


def staged_kernel(body, layers, n_smem, n_raw, n_out, n_raw_out, *refs):
    n_in = len(layers)
    smem, refs = refs[:n_smem], refs[n_smem:]
    ins, refs = refs[:n_in], refs[n_in:]
    raw, refs = refs[:n_raw], refs[n_raw:]
    outs, refs = refs[:n_out], refs[n_out:]
    raw_outs, refs = refs[:n_raw_out], refs[n_raw_out:]
    held, refs = refs[:n_in], refs[n_in:]
    made, refs = refs[:n_out], refs[n_out:]
    sems, scratch = refs[0], refs[1:]
    copies = Copies(
        [
            (ref if layer is None else ref.at[layer], to)
            for ref, layer, to in zip(ins, layers, held)
        ],
        list(zip(made, outs)),
        sems,
    )
    body(copies, smem, held, raw, made, raw_outs, scratch)
    copies.finish()


def staged(body, name, smem, ins, raw, outs, raw_outs, scratch, mib, work, aliases=None):
    pairs = [one if isinstance(one, tuple) else (one, None) for one in ins]
    layers = [layer for _, layer in pairs]
    held = [
        pltpu.VMEM(one.shape if layer is None else one.shape[1:], one.dtype) for one, layer in pairs
    ]
    made = [pltpu.VMEM(one.shape, one.dtype) for one in outs]
    n_copies = len(pairs) + len(outs)
    found = pl.pallas_call(
        functools.partial(
            staged_kernel, body, layers, len(smem), len(raw), len(outs), len(raw_outs)
        ),
        name=name,
        out_shape=tuple(outs) + tuple(raw_outs),
        in_specs=[SMEM_SPEC] * len(smem) + [HBM_SPEC] * (len(pairs) + len(raw)),
        out_specs=(HBM_SPEC,) * (len(outs) + len(raw_outs)),
        scratch_shapes=held + made + [pltpu.SemaphoreType.DMA((n_copies,))] + scratch,
        input_output_aliases=aliases or {},
        compiler_params=params(mib),
        cost_estimate=work,
    )(*smem, *[one for one, _ in pairs], *raw)
    return found


def normed_of(value):
    mean = jnp.mean(value, axis=-1, keepdims=True)
    centered = value - mean
    var = jnp.mean(centered * centered, axis=-1, keepdims=True)
    rstd = lax.rsqrt(var + eps_norm)
    return centered * rstd, rstd


def norm_back(grad, xhat, rstd, gain):
    scaled = grad * gain
    first = jnp.mean(scaled, axis=-1, keepdims=True)
    second = jnp.mean(scaled * xhat, axis=-1, keepdims=True)
    return rstd * (scaled - first - xhat * second)


def attn_fwd_kernel(copies, smem, ins, raw, outs, raw_outs, scratch):
    (slopes,) = smem
    x_ref, wqkv_ref, dist_ref, wo_ref, g_ref, b_ref = ins
    qkv_ref, lse_ref, ctx_ref, ctx_t_ref, pre_ref, hb_ref, hb_t_ref = outs
    rows, width = x_ref.shape
    copies.wait(0, 1)
    x = x_ref[...]
    for c in range(3):
        cols = pl.ds(c * width, width)
        qkv_ref[:, cols] = mm(x, wqkv_ref[:, cols]).astype(bf16)
    copies.put(0)
    copies.wait()
    lse_ref[...] = jnp.zeros_like(lse_ref)
    s_ref, p_ref = scratch

    def pair(p, _):
        def at(c):
            return pl.ds(pl.multiple_of(c * width + p * 128, 128), 128)

        key, val = qkv_ref[:, at(1)], qkv_ref[:, at(2)]
        query = qkv_ref[:, at(0)] * bf16(HEAD_DIM ** (-0.5))
        wide = lax.broadcasted_iota(jnp.int32, (rows, 128), 1)
        for side in range(2):
            mine = (wide < HEAD_DIM) == (side == 0)
            s_ref[side] = mm(jnp.where(mine, query, bf16(0)), key, NT)

        dist = dist_ref[...]
        total_lse = lse_ref[...]
        for side in range(2):
            s = s_ref[side] - slopes[2 * p + side] * dist
            top = jnp.max(s, axis=-1, keepdims=True)
            e = jnp.exp(s - top)
            total = jnp.sum(e, axis=-1, keepdims=True)
            p_ref[side] = (e * (1.0 / total)).astype(bf16)
            total_lse += jnp.where(wide == 2 * p + side, top + jnp.log(total), 0.0)
        lse_ref[...] = total_lse
        found = [mm(p_ref[side], val) for side in range(2)]
        ctx_ref[:, at(0)] = jnp.where(wide < HEAD_DIM, found[0], found[1]).astype(bf16)
        return 0

    lax.fori_loop(0, width // 128, pair, 0)
    copies.put(1, 2)
    ctx = ctx_ref[...]
    pre = x.astype(f32) + mm(ctx, wo_ref[...])
    pre_ref[...] = pre
    ctx_t_ref[...] = ctx.T
    copies.put(3, 4)
    xhat, _ = normed_of(pre)
    hb = (xhat * g_ref[...] + b_ref[...]).astype(bf16)
    hb_ref[...] = hb
    hb_t_ref[...] = hb.T


def slopes_of():
    steps = jnp.arange(HEADS, dtype=f32)
    return jnp.exp2(-8.0 * (steps + 1.0) / HEADS)


def attn_fwd(layer, x, wqkv, wo, gain, bias, dist, slopes):
    rows, width = x.shape
    return staged(
        attn_fwd_kernel,
        "attn_fwd",
        [slopes],
        [x, (wqkv, layer), dist, (wo, layer), gain, bias],
        [],
        [
            shape((rows, 3 * width), bf16),
            shape((rows, 128), f32),
            shape((rows, width), bf16),
            shape((width, rows), bf16),
            shape((rows, width), f32),
            shape((rows, width), bf16),
            shape((width, rows), bf16),
        ],
        [],
        [pltpu.VMEM((2, rows, rows), f32), pltpu.VMEM((2, rows, rows), bf16)],
        36,
        cost(0, 0),
    )


def attn_bwd_kernel(copies, smem, ins, raw, outs, raw_outs, scratch):
    slopes, at_ref = smem
    dab_ref, wo_ref, qkv_ref, lse_ref, dist_ref, x_t_ref, c_t_ref, wqkv_ref, dpre_ref = ins[:9]
    small_refs = ins[9:]
    dctx_ref, s_ref, dp_ref, p_ref, ds_ref, out_ref, rows_ref = scratch
    sent_ref, kept_ref, grad_ref = outs
    rows, width = dab_ref.shape
    scale = HEAD_DIM ** (-0.5)
    copies.wait(0, 1)
    dctx_ref[...] = mm(dab_ref[...], wo_ref[...], NT).astype(bf16)
    copies.wait(2, 3, 4)
    def pair(p, _):
        def at(c):
            return pl.ds(pl.multiple_of(c * width + p * 128, 128), 128)

        key, val, query = qkv_ref[:, at(1)], qkv_ref[:, at(2)], qkv_ref[:, at(0)]
        dctx = dctx_ref[:, at(0)]
        wide = lax.broadcasted_iota(jnp.int32, (rows, 128), 1)
        low = wide < HEAD_DIM
        for side in range(2):
            mine = low == (side == 0)
            s_ref[side] = mm(jnp.where(mine, query * bf16(scale), bf16(0)), key, NT)
            dp_ref[side] = mm(jnp.where(mine, dctx, bf16(0)), val, NT)

        dist = dist_ref[...]
        for side in range(2):
            lse = jnp.sum(jnp.where(wide == 2 * p + side, lse_ref[...], 0.0), axis=-1, keepdims=True)
            prob = jnp.exp(s_ref[side] - slopes[2 * p + side] * dist - lse)
            d_prob = dp_ref[side]
            mean = jnp.sum(prob * d_prob, axis=-1, keepdims=True)
            p_ref[side] = prob.astype(bf16)
            ds_ref[side] = (prob * (d_prob - mean)).astype(bf16)
        d_q = [mm(ds_ref[side], key) for side in range(2)]
        query_t, dctx_t = query.T, dctx.T
        d_k = [mm(query_t, ds_ref[side]).T for side in range(2)]
        d_v = [mm(dctx_t, p_ref[side]).T for side in range(2)]
        out_ref[:, at(0)] = (jnp.where(low, d_q[0], d_q[1]) * scale).astype(bf16)
        out_ref[:, at(1)] = (jnp.where(low, d_k[0], d_k[1]) * scale).astype(bf16)
        out_ref[:, at(2)] = jnp.where(low, d_v[0], d_v[1]).astype(bf16)
        return 0

    lax.fori_loop(0, width // 128, pair, 0)
    part = width // 8
    copies.wait()
    for colour in range(2):
        order = fold_order(colour)
        order = order + [j ^ 1 for j in order]
        pick_rows(at_ref[0], order, x_t_ref, rows_ref)
        for block in (2 * colour, 2 * colour + 1):
            if block < 3:
                rhs = out_ref[:, pl.ds(block * width, width)]
            else:
                rhs = dab_ref[...]
                pick_rows(at_ref[0], order, c_t_ref, rows_ref)
            total = mm(rows_ref[...], rhs).astype(bf16)
            few = small_refs[block // 2][block % 2 : block % 2 + 1]
            for i, j in enumerate(order):
                to = (kept_ref, sent_ref)[i // 4].at[block, i % 4]
                to[pl.ds(0, part)] = total[i * part : (i + 1) * part]
                here = jnp.where(jnp.bitwise_xor(at_ref[0], j) == 0, few, 0.0)
                to[pl.ds(part, FEW)] = jnp.broadcast_to(here, (FEW, width)).astype(bf16)
    copies.put(0, 1)
    grad_ref[...] = dpre_ref[...] + mm(out_ref[...], wqkv_ref[...], NT)


FEW = 8


def attn_bwd(layer, d, dab, qkv, lse, wo, dist, slopes, d_pre, x_t, ctx_t, wqkv, small):
    rows, width = dab.shape
    part = shape((4, 4, width // 8 + FEW, width), bf16)
    return staged(
        attn_bwd_kernel,
        "attn_bwd",
        [slopes, d],
        [dab, (wo, layer), qkv, lse, dist, x_t, ctx_t, (wqkv, layer), d_pre, *small],
        [],
        [part, part, shape((rows, width), f32)],
        [],
        [
            pltpu.VMEM((rows, width), bf16),
            pltpu.VMEM((2, rows, rows), f32),
            pltpu.VMEM((2, rows, rows), f32),
            pltpu.VMEM((2, rows, rows), bf16),
            pltpu.VMEM((2, rows, rows), bf16),
            pltpu.VMEM((rows, 3 * width), bf16),
            pltpu.VMEM((width, rows), bf16),
        ],
        40,
        cost(0, 0),
    )


def load_groups(groups, d, refs, w_ref, sems, slots):
    loads = []
    at = 0
    sources = {}
    for g, (kind, index) in enumerate(groups):
        mine = []
        s = g % slots
        count = {"own": 2, "pair": 2, "two": 4, "all": 1}[kind]
        if kind not in sources:
            sources[kind] = refs[at : at + count]
            at += count
        source = sources[kind]
        if kind == "own":
            split = source[0].shape[1]
            rest = source[1].shape[1]
            pairs = [
                (source[0], w_ref.at[s, :, pl.ds(0, split)]),
                (source[1], w_ref.at[s, :, pl.ds(split, rest)]),
            ]
        elif kind == "all":
            part = source[0].shape[2]
            pairs = [(source[0].at[j, index], w_ref.at[s, pl.ds(j * part, part)]) for j in range(8)]
        else:
            colour, place = index if kind == "two" else (0, index)
            chips = order_of(colour) if kind == "two" else CHIPS
            part = source[0].shape[2]
            pairs = []
            for c in range(2):
                for i, j in enumerate(chips):
                    row = pl.multiple_of(jnp.bitwise_xor(d, j ^ c) * part, part)
                    pairs.append(
                        (source[2 * colour + c].at[i, place], w_ref.at[s, pl.ds(row, part)])
                    )
        for i, (one, to) in enumerate(pairs):
            mine.append(pltpu.make_async_copy(one, to, sems.at[g, i]))
        loads.append(mine)
    return loads


def gelu_parts(gate):
    square = gate * gate
    t = jnp.tanh(gelu_coef * gate * (1.0 + 0.044715 * square))
    half = 0.5 * (1.0 + t)
    slope = half + 0.5 * gate * (1.0 - t * t) * gelu_coef * (1.0 + 3 * 0.044715 * square)
    return gate * half, slope


TILE = 768


def ff_fwd_kernel(groups, first, last, copies, smem, ins, raw, outs, raw_outs, scratch):
    (at_ref,) = smem
    hb_ref, acc_refs, norm_refs = ins[0], ins[1 : 4 if first else 2], ins[4 if first else 2 :]
    pre_ref = outs[0]
    w_ref, sems = scratch
    width = hb_ref.shape[1]
    loads = load_groups(groups, at_ref[0], raw, w_ref, sems, len(groups))
    for load in loads:
        for copy in load:
            copy.start()
    copies.wait()
    if first:
        xhat, _ = normed_of(acc_refs[0][...])
        pre_ref[...] = xhat * acc_refs[1][...] + acc_refs[2][...]
    else:
        pre_ref[...] = acc_refs[0][...]
    for s in range(len(groups)):
        for copy in loads[s]:
            copy.wait()

        def step(n, _, s=s):
            def at(c):
                return pl.ds(pl.multiple_of(c * width + n * TILE, TILE), TILE)

            hb = hb_ref[...]
            gate, value = mm(hb, w_ref[s, :, at(0)]), mm(hb, w_ref[s, :, at(1)])
            act = (gelu_parts(gate)[0] * value).astype(bf16)
            pre_ref[...] += mm(act, w_ref[s, at(0), pl.ds(2 * width, width)])
            return 0

        step(0, 0)
    if last:
        copies.put(0)
        xhat, _ = normed_of(pre_ref[...])
        out = (xhat * norm_refs[0][...] + norm_refs[1][...]).astype(bf16)
        outs[1][...] = out
        outs[2][...] = out.T


def ff_fwd(groups, d, hb, acc, weights, norm=None):
    rows, width = hb.shape
    last = norm is not None
    acc = acc if isinstance(acc, tuple) else (acc,)
    outs = [shape((rows, width), f32)]
    if last:
        outs += [shape((rows, width), bf16), shape((width, rows), bf16)]
    n = len(groups)
    return staged(
        functools.partial(ff_fwd_kernel, groups, len(acc) == 3, last),
        "ff_fwd",
        [d],
        [hb, *acc, *(norm if last else ())],
        weights,
        outs,
        [],
        [
            pltpu.VMEM((n, width, 3 * width), bf16),
            pltpu.SemaphoreType.DMA((n, 16)),
        ],
        36,
        cost(0, 0),
    )


def pick_rows(d, order, from_ref, to_ref):
    rows = from_ref.shape[0] // 8
    for i, j in enumerate(order):
        at = pl.multiple_of(jnp.bitwise_xor(d, j) * rows, rows)
        to_ref[pl.ds(i * rows, rows), :] = from_ref[pl.ds(at, rows), :]


def norm_bwd(grad, pre, gain_ref, small_ref):
    xhat, rstd = normed_of(pre)
    small_ref[0:1] = jnp.sum(grad * xhat, axis=0, keepdims=True)
    small_ref[1:2] = jnp.sum(grad, axis=0, keepdims=True)
    return norm_back(grad, xhat, rstd, gain_ref[...])


def ff_bwd_kernel(groups, first, last, slot, copies, smem, ins, raw, outs, raw_outs, scratch):
    (at_ref,) = smem
    hb_ref, hb_t_ref, *ins = ins
    w_ref, g_ref, sems, out_sems = scratch
    width = hb_ref.shape[1]
    part = width // 8
    n = len(groups)
    loads = load_groups(groups, at_ref[0], raw, w_ref, sems, 2)
    for copy in loads[0]:
        copy.start()
    copies.wait()
    dh_ref, *outs = outs
    if first:
        grad_ref, pre_ref, gain_ref, *ins = ins
        dyb_ref, dyb_t_ref, small2_ref, *outs = outs
        d_pre = norm_bwd(grad_ref[...].astype(f32), pre_ref[...], gain_ref, small2_ref)
        dh_ref[...] = d_pre
        dyb_ref[...] = d_pre.astype(bf16)
        dyb_t_ref[...] = dyb_ref[...].T
    else:
        dyb_ref, dyb_t_ref, acc_ref, *ins = ins
        dh_ref[...] = acc_ref[...]
    out = []
    for s in range(n):
        if s + 1 < n:
            for copy in loads[s + 1]:
                copy.start()
        for copy in loads[s]:
            copy.wait()
        if s >= 2:
            out[s - 2].wait()
        weights = w_ref.at[s % 2]
        grads = g_ref.at[s % 2]

        def at(c):
            return pl.ds(c * width, width)

        hb = hb_ref[...]
        gate, value = mm(hb, weights[:, at(0)]), mm(hb, weights[:, at(1)])
        d_act = mm(dyb_ref[...], weights[:, at(2)], NT)
        gelu, slope = gelu_parts(gate)
        d_gate = (d_act * value * slope).astype(bf16)
        d_value = (d_act * gelu).astype(bf16)
        act = (gelu * value).astype(bf16)
        dh_ref[...] += mm(d_gate, weights[:, at(0)], NT) + mm(d_value, weights[:, at(1)], NT)
        for c, (lhs, rhs) in enumerate(((hb_t_ref, d_gate), (hb_t_ref, d_value), (dyb_t_ref, act))):
            total = mm(lhs[...], rhs).astype(bf16)
            for j in range(8):
                grads[j, :, at(c)] = total[j * part : (j + 1) * part]
        out.append(pltpu.make_async_copy(grads, raw_outs[0].at[:, slot + s], out_sems.at[s]))
        out[s].start()
    if last:
        pre_ref, gain_ref = ins
        dab_ref, small1_ref = outs
        d_pre = norm_bwd(dh_ref[...], pre_ref[...], gain_ref, small1_ref)
        dh_ref[...] = d_pre
        dab_ref[...] = d_pre.astype(bf16)
    for one in out[-2:]:
        one.wait()


def ff_bwd(groups, slot, d, hb, hb_t, ins, weights, first=False, last=False, into=None):
    rows, width = hb.shape
    n = len(groups)
    low, few = shape((rows, width), bf16), shape((2, width), f32)
    outs = [shape((rows, width), f32)]
    outs += [low, shape((width, rows), bf16), few] if first else []
    outs += [low, few] if last else []
    extra = [] if into is None else [into]
    n_in = 3 + len(ins) + len(weights)
    return staged(
        functools.partial(ff_bwd_kernel, groups, first, last, slot),
        "ff_bwd",
        [d],
        [hb, hb_t, *ins],
        weights + extra,
        outs,
        [shape((8, 4, width // 8, 3 * width), bf16)],
        [
            pltpu.VMEM((2, width, 3 * width), bf16),
            pltpu.VMEM((2, 8, width // 8, 3 * width), bf16),
            pltpu.SemaphoreType.DMA((n, 16)),
            pltpu.SemaphoreType.DMA((n,)),
        ],
        60,
        cost(0, 0),
        {n_in: len(outs)} if extra else {},
    )


def add_low(a, b):
    return (a.astype(f32) + b.astype(f32)).astype(bf16)


class Share:
    def __init__(self, net, line, z, sent, kept):
        self.net, self.line, self.z = net, line, z
        self.kept, self.got = kept, net.flip(line.after(sent), 1)

    def first(self):
        got = self.line.after(self.got)
        half = [(self.kept[2 * c : 2 * c + 2], got[2 * c : 2 * c + 2]) for c in range(2)]
        self.got = [
            self.net.flip(add_low(kept[:, 2:], got[:, 2:]), COLOURS[c][0])
            for c, (kept, got) in enumerate(half)
        ]
        self.kept = [add_low(kept[:, :2], got[:, :2]) for kept, got in half]

    def second(self):
        got = [self.line.after(one) for one in self.got]
        self.got = [
            self.net.flip(add_low(self.kept[c][:, 1], got[c][:, 1]), COLOURS[c][1])
            for c in range(2)
        ]
        self.kept = [add_low(self.kept[c][:, 0], got[c][:, 0]) for c in range(2)]

    def far(self):
        n = self.net.n_t
        total = [add_low(self.kept[c], self.line.after(self.got[c])) for c in range(2)]
        total = jnp.concatenate(total, axis=0)
        parts = [
            lax.dynamic_index_in_dim(total, lax.rem(self.z - k + n, n), 0, keepdims=False)
            for k in range(n)
        ]
        self.parts = [parts[0]] + [self.net.shift(parts[k], -k) for k in range(1, n)]

    def far_back(self):
        total = self.parts[0].astype(f32)
        for part in self.parts[1:]:
            total = total + self.line.after(part).astype(f32)
        total = total.astype(bf16)
        self.slices = [total] + [self.net.shift(total, k) for k in range(1, self.net.n_t)]

    def gather(self):
        self.gathered = Gather2(self.net, self.line, self.slices)


def spread_kernel(layer, copies, smem, ins, raw, outs, raw_outs, scratch):
    (at_ref,) = smem
    held = ins
    (small_ref,) = outs
    qkv_out, wo_out = raw_outs
    qkv_buf, wo_buf, sems = scratch
    d, z = at_ref[0], at_ref[1]
    rows, cols = held[0].shape[2:]
    rows = rows - FEW
    copies.wait()
    for k in range(4):
        block = lax.rem(z - k + 4, 4)
        for c in range(2):
            for i, j in enumerate(order_of(k // 2)):
                ref = held[2 * (k // 2) + c].at[i, k % 2]
                value = ref[pl.ds(0, rows)].astype(f32)
                slot = jnp.bitwise_xor(d, j ^ c)
                row = pl.multiple_of(slot * rows, rows)

                @pl.when(block < 3)
                def _(value=value, row=row, block=block):
                    col = pl.multiple_of(block * cols, cols)
                    qkv_buf[pl.ds(row, rows), pl.ds(col, cols)] = value

                @pl.when(block == 3)
                def _(value=value, row=row):
                    wo_buf[pl.ds(row, rows), :] = value

                @pl.when(slot == 0)
                def _(ref=ref, block=block):
                    small_ref[block] = ref[pl.ds(rows, FEW)].astype(f32)

    one = pltpu.make_async_copy(qkv_buf, qkv_out.at[layer], sems.at[0])
    two = pltpu.make_async_copy(wo_buf, wo_out.at[layer], sems.at[1])
    one.start()
    two.start()
    one.wait()
    two.wait()


def spread_out(layer, where, pieces, before):
    rows, cols = pieces[0].shape[2:]
    width = 8 * (rows - FEW)
    return staged(
        functools.partial(spread_kernel, layer),
        "spread_out",
        [where],
        pieces,
        [] if before is None else list(before),
        [shape((4, FEW, cols), f32)],
        [shape((LAYERS, width, 3 * cols), f32), shape((LAYERS, width, cols), f32)],
        [
            pltpu.VMEM((width, 3 * cols), f32),
            pltpu.VMEM((width, cols), f32),
            pltpu.SemaphoreType.DMA((2,)),
        ],
        24,
        cost(0, 0),
        {} if before is None else {5: 1, 6: 2},
    )


def quick_program(
    net,
    x_in,
    bucket,
    lengths,
    qkv_weight,
    out_weight,
    norm_gain1,
    norm_bias1,
    up_weight,
    down_weight,
    norm_gain2,
    norm_bias2,
    cotangent,
):
    rows, width = x_in.shape
    d, z = lax.axis_index("dp").astype(jnp.int32), lax.axis_index("tensor").astype(jnp.int32)
    d_at, dz_at = jnp.reshape(d, (1,)), jnp.stack([d, z])
    part = width // net.n_dp
    net.flying = []
    line = Line(net)
    gains1, biases1 = norm_gain1[:, None], norm_bias1[:, None]
    gains2, biases2 = norm_gain2[:, None], norm_bias2[:, None]

    def own_slice(l):
        up = lax.dynamic_slice(up_weight, (l, d * part, 0, 0), (1, part, 2, width))
        down = lax.dynamic_slice(down_weight, (l, d * part, 0), (1, part, width))
        return jnp.concatenate([up.reshape(part, 2 * width), down[0]], axis=1)

    def own_weights(l):
        return [up_weight[l].reshape(width, 2 * width), down_weight[l]]

    seg = segments(bucket[0], lengths[0], rows, SHORT)
    same = seg[:, None] == seg[None, :]
    place = jnp.arange(rows, dtype=f32)
    dist = jnp.where(same, jnp.abs(place[:, None] - place[None, :]), 1e34)
    slopes = slopes_of()
    outputs, kept = [], []

    def run_attn(l, x):
        def call(x):
            return attn_fwd(l, x, qkv_weight, out_weight, gains1[l], biases1[l], dist, slopes)

        return line.run(call, x)

    def run_ff(groups, hb, acc, weights, norm=None):
        return line.run(lambda hb: ff_fwd(groups, d_at, hb, acc, weights, norm), hb)

    OWN, PAIR, TWO, ALL = "own", "pair", "two", "all"
    own = own_slice(0)
    far = {k: net.shift(own, k) for k in (1, 3)}
    x_t = x_in.T
    qkv, lse, ctx, ctx_t, pre1, hb, hb_t = run_attn(0, x_in)
    planes = lax.all_gather(line.after(own_slice(1)), "tensor")
    near = Gather2(net, line, [far[1], far[3]])
    far[2] = net.shift(line.after(own), 2)
    mine = own_weights(0)
    acc = run_ff(((OWN, 0),), hb, (pre1, gains1[0], biases1[0]), mine)[0]
    near.second()
    back = Gather(net, line, [far[2]])
    line.sync()
    near.core()
    line.need(planes)
    planes = line.after(planes)
    others = jnp.stack(
        [
            lax.dynamic_index_in_dim(planes, lax.rem(z - k + net.n_t, net.n_t), 0, keepdims=False)
            for k in range(1, net.n_t)
        ]
    )
    others = lax.all_gather(others, "dp")
    back.core()
    line.sync()
    pre2, out, out_t = run_ff(
        ((TWO, (0, 0)), (TWO, (1, 0)), (PAIR, 0)),
        hb,
        acc,
        near.pieces() + back.pieces(),
        (gains2[0], biases2[0]),
    )
    kept.append((x_t, qkv, lse, ctx_t, pre1, hb, hb_t, pre2))
    outputs.append(out)
    weights = [
        [
            (((OWN, 0), (PAIR, 0)), mine + back.pieces()),
            (((TWO, (0, 0)), (TWO, (1, 0))), near.pieces()),
        ]
    ]
    qkv, lse, ctx, ctx_t, pre1, hb, hb_t = run_attn(1, out)
    mine = own_weights(1)
    acc = run_ff(((OWN, 0),), hb, (pre1, gains1[1], biases1[1]), mine)[0]
    pre2, out, _ = run_ff(
        ((ALL, 0), (ALL, 1), (ALL, 2)), hb, acc, [others], (gains2[1], biases2[1])
    )
    weights.append([(((OWN, 0), (ALL, 1), (ALL, 0), (ALL, 2)), mine + [others])])
    kept.append((out_t, qkv, lse, ctx_t, pre1, hb, hb_t, pre2))
    outputs.append(out)

    order = (0, 2, 1, 3)

    def run_ff_bwd(l, at, ins, **how):
        groups, arrays = weights[l][at]
        hb, hb_t = kept[l][5:7]
        return line.run(lambda hb: ff_bwd(groups, 2 * at, d_at, hb, hb_t, ins, arrays, **how), hb)

    def run_attn_bwd(l, dab, d_pre, small):
        x_t, qkv, lse, ctx_t = kept[l][:4]
        return line.run(
            lambda dab: attn_bwd(
                l,
                d_at,
                dab,
                qkv,
                lse,
                out_weight,
                dist,
                slopes,
                d_pre,
                x_t,
                ctx_t,
                qkv_weight,
                small,
            ),
            dab,
        )

    def over_dp(grads):
        return lax.psum_scatter(line.after(grads), "dp", scatter_dimension=0, tiled=True)[0]

    def to_owner(l, i):
        return net.shift(line.after(ff[l][i]), -order[i])

    pre1, pre2 = kept[1][4], kept[1][7]
    d_pre1, _, _, small2, dab, small1, g = run_ff_bwd(
        1, 0, (cotangent, pre2, gains2[1], pre1, gains1[1]), first=True, last=True
    )
    ff = {1: over_dp(g)}
    sent, keep, grad = run_attn_bwd(1, dab, d_pre1, (small1, small2))
    pre1, pre2 = kept[0][4], kept[0][7]
    share = Share(net, line, z, sent, keep)
    d_h, dyb, dyb_t, small2, g = run_ff_bwd(0, 0, (grad, pre2, gains2[0]), first=True)
    share.first()
    d_pre1, dab, small1, g = run_ff_bwd(
        0, 1, (dyb, dyb_t, d_h, pre1, gains1[0]), into=g, last=True
    )
    ff[0] = over_dp(g)
    share.second()
    sent, keep, grad = run_attn_bwd(0, dab, d_pre1, (small1, small2))
    last_share = Share(net, line, z, sent, keep)
    line.sync()
    last_share.first()
    share.far()
    line.sync()
    last_share.second()
    share.far_back()
    line.sync()
    last_share.far()
    share.gather()
    line.sync()
    last_share.far_back()
    share.gathered.second()
    line.sync()
    line.need(ff[1])
    last_share.gather()
    share.gathered.core()
    ff_parts = {1: [ff[1][0], to_owner(1, 1)]}
    line.sync()
    last_share.gathered.second()
    ff_parts[1] += [to_owner(1, 2), to_owner(1, 3)]
    found = line.run(
        lambda first: spread_out(1, dz_at, [first] + share.gathered.pieces()[1:], None),
        share.gathered.pieces()[0],
    )
    last_share.gathered.core()
    line.need(ff[0])
    ff_parts[0] = [ff[0][0]] + [to_owner(0, i) for i in (1, 2, 3)]
    small = {1: found[0]}
    found = spread_out(0, dz_at, last_share.gathered.pieces(), found[1:])
    small[0] = found[0]
    attention_grads = found[1:]
    small = jnp.stack([small[l][:, 0] for l in range(LAYERS)])
    up_grads, down_grads = [], []
    for l in range(LAYERS):
        total = ff_parts[l][0].astype(f32)
        for one in ff_parts[l][1:]:
            total = total + one.astype(f32)
        up_grads.append(total[:, : 2 * width].reshape(part, 2, width))
        down_grads.append(total[:, 2 * width :].T)
    return (
        jnp.stack(outputs),
        grad,
        attention_grads[0],
        attention_grads[1],
        small[:, 0],
        small[:, 1],
        jnp.stack(up_grads),
        jnp.stack(down_grads),
        small[:, 2],
        small[:, 3],
    )


def attention_forward(x_low, wqkv, wo, g1, b1, same, decay):
    rows, width = x_low.shape
    qkv_low = dot(x_low, wqkv).astype(bf16)
    query, keys, values = split_heads(qkv_low, width)
    scores = scores_of(query, keys, same, decay)
    top = jnp.max(scores, axis=-1, keepdims=True)
    log_total = top + jnp.log(jnp.sum(jnp.exp(scores - top), axis=-1, keepdims=True))
    probs_low = jnp.exp(scores - log_total).astype(bf16)
    ctx_low = (
        jnp.einsum("hqk,khe->qhe", probs_low, values, preferred_element_type=f32)
        .reshape(rows, width)
        .astype(bf16)
    )
    pre_first = x_low.astype(f32) + dot(ctx_low, wo)
    normed = layer_norm(pre_first, g1, b1)
    return normed, (qkv_low, log_total, ctx_low, pre_first)


def attention_backward(d_attn_low, qkv_low, log_total, ctx_low, wo, same, decay):
    rows, width = d_attn_low.shape
    d_ctx = dot(d_attn_low, wo.T).astype(bf16).reshape(rows, HEADS, HEAD_DIM)
    query, keys, values = split_heads(qkv_low, width)
    probs = jnp.exp(scores_of(query, keys, same, decay) - log_total)
    probs_low = probs.astype(bf16)
    d_values = jnp.einsum("hqk,qhe->khe", probs_low, d_ctx, preferred_element_type=f32)
    d_probs = jnp.einsum("qhe,khe->hqk", d_ctx, values, preferred_element_type=f32)
    d_scores = (probs * (d_probs - jnp.sum(probs * d_probs, axis=-1, keepdims=True))).astype(bf16)
    d_query = jnp.einsum("hqk,khe->qhe", d_scores, keys, preferred_element_type=f32)
    d_keys = jnp.einsum("hqk,qhe->khe", d_scores, query, preferred_element_type=f32)
    scale = HEAD_DIM ** (-0.5)
    return jnp.concatenate(
        [
            (d_query * scale).reshape(rows, width),
            (d_keys * scale).reshape(rows, width),
            d_values.reshape(rows, width),
        ],
        axis=1,
    ).astype(bf16)


def plain_program(
    net,
    x_in,
    bucket,
    lengths,
    qkv_weight,
    out_weight,
    norm_gain1,
    norm_bias1,
    up_weight,
    down_weight,
    norm_gain2,
    norm_bias2,
    cotangent,
):
    rows, width = x_in.shape
    n_t = net.n_t
    hidden = down_weight.shape[1]
    seg = segments(bucket[0], lengths[0], rows, SHORT)
    same = seg[:, None] == seg[None, :]
    decay = alibi(rows, HEADS)
    ups = lax.all_gather(up_weight, "tensor", axis=0)
    downs = lax.all_gather(down_weight, "tensor", axis=0)
    groups = [
        [(ups[k, l].reshape(width, -1), downs[k, l]) for k in range(n_t)] for l in range(LAYERS)
    ]
    layer_in = x_in
    outputs, kept = [], []
    for l in range(LAYERS):
        x_low = layer_in
        normed, keep = attention_forward(
            x_low, qkv_weight[l], out_weight[l], norm_gain1[l], norm_bias1[l], same, decay
        )
        hb = normed.astype(bf16)
        pre_second = normed
        joined, act = [], []
        for up, down in groups[l]:
            joined.append(dot(hb, up))
            act.append(geglu(joined[-1]).astype(bf16))
            pre_second = pre_second + dot(act[-1], down)
        layer_in = layer_norm(pre_second, norm_gain2[l], norm_bias2[l]).astype(bf16)
        outputs.append(layer_in)
        kept.append((x_low, *keep, hb, pre_second, joined, act))
    grad = cotangent.astype(f32)
    attention_grads, small, up_grads, down_grads = ([None] * LAYERS for _ in range(4))
    for l in reversed(range(LAYERS)):
        x_low, qkv_low, log_total, ctx_low, pre_first, hb, pre_second, joined, act = kept[l]
        pull = jax.vjp(layer_norm, pre_second, norm_gain2[l], norm_bias2[l])[1]
        d_pre2, d_gain2, d_bias2 = pull(grad)
        dyb = d_pre2.astype(bf16)
        d_h = d_pre2
        d_joined = []
        for k, (up, down) in enumerate(groups[l]):
            d_act = dot(dyb, down.T)
            d_joined.append(jax.vjp(geglu, joined[k])[1](d_act)[0].astype(bf16))
            d_h = d_h + dot(d_joined[k], up.T)
        d_up = jnp.stack([dot(hb.T, one) for one in d_joined]).astype(bf16)
        d_down = jnp.stack([dot(dyb.T, one) for one in act]).astype(bf16)
        d_up = lax.psum_scatter(d_up, "tensor", scatter_dimension=0)
        d_down = lax.psum_scatter(d_down, "tensor", scatter_dimension=0)
        d_up = lax.psum_scatter(d_up, "dp", scatter_dimension=0, tiled=True)
        d_down = lax.psum_scatter(d_down, "dp", scatter_dimension=0, tiled=True)
        up_grads[l], down_grads[l] = d_up.astype(f32), d_down.astype(f32)
        pull = jax.vjp(layer_norm, pre_first, norm_gain1[l], norm_bias1[l])[1]
        d_pre1, d_gain1, d_bias1 = pull(d_h)
        small[l] = [d_gain1, d_bias1, d_gain2, d_bias2]
        dab = d_pre1.astype(bf16)
        d_qkv = attention_backward(dab, qkv_low, log_total, ctx_low, out_weight[l], same, decay)
        found = lax.psum(
            (dot(x_low.T, d_qkv).astype(bf16), dot(ctx_low.T, dab).astype(bf16)), BOTH
        )
        attention_grads[l] = [one.astype(f32) for one in found]
        grad = d_pre1 + dot(d_qkv, qkv_weight[l].T)
    small = lax.psum(jnp.stack(small[0] + small[1]), BOTH).reshape(LAYERS, 4, width)
    return (
        jnp.stack(outputs),
        grad,
        jnp.stack([one[0] for one in attention_grads]),
        jnp.stack([one[1] for one in attention_grads]),
        small[:, 0],
        small[:, 1],
        jnp.stack(up_grads).reshape(LAYERS, -1, 2, hidden),
        jnp.stack([one.T for one in down_grads]),
        small[:, 2],
        small[:, 3],
    )


def program(net, *args):
    width, hidden = args[0].shape[1], args[8].shape[1]
    quick = net.n_dp == 8 and net.n_t == 4 and hidden == width and width % 256 == 0
    return (quick_program if quick else plain_program)(net, *args)


def solution(mesh):
    in_specs = (
        P(BOTH, None),
        P(BOTH),
        P(BOTH, None),
        P(),
        P(),
        P(),
        P(),
        P(None, None, None, "tensor"),
        P(None, "tensor", None),
        P(),
        P(),
        P(BOTH, None),
    )
    out_specs = (
        P(None, BOTH, None),
        P(BOTH, None),
        P(),
        P(),
        P(),
        P(),
        P(None, "dp", None, "tensor"),
        P(None, "tensor", "dp"),
        P(),
        P(),
    )
    net = Net(mesh)
    return jax.shard_map(
        functools.partial(program, net),
        mesh=mesh,
        in_specs=in_specs,
        out_specs=out_specs,
        check_vma=False,
    )
```

time: 649 us -> 555 us (0.86)
  the two profiles are of different devices: /device:TPU:0 before, /device:TPU:17 now
where the time goes in v2:
time: 555 us; the launch traced here: 550 us
  waiting for transfers between devices  211 us (38%)
  Pallas kernels  200 us (36%)
  starting transfers between devices  56.8 us (10%)
  local copies, waits for them, and re-layouts  35.8 us (6%)
  other arithmetic  30.1 us (5%)
  between operations  15.6 us (3%)
    pallas_call x13, Pallas kernels, staged(): pl.pallas_call(functools.partial(staged_kernel, body, layers, len(smem),...  200 us
    ppermute x21, waiting for transfers between devices, shift(): got = lax.ppermute(value, 'tensor', [(i, (i + step) % n) for i in range(n)])  109 us
    ppermute x32, waiting for transfers between devices, flip(): got = lax.ppermute(value, 'dp', [(i, i ^ bit) for i in range(self.n_dp)])  80.6 us
    ppermute x32, starting transfers between devices, flip(): got = lax.ppermute(value, 'dp', [(i, i ^ bit) for i in range(self.n_dp)])  34.6 us
    all_gather x1, waiting for transfers between devices, quick_program(): others = lax.all_gather(others, 'dp')  21.9 us
    ppermute x21, starting transfers between devices, shift(): got = lax.ppermute(value, 'tensor', [(i, (i + step) % n) for i in range(n)])  21.7 us
  transfers between devices with their start and end apart: 57, of which 31 were waited for; matrix products, arithmetic and copies ran while one was open for 9% of the time, Pallas kernels for 28%

profile of v2, /device:TPU:17, one launch (start us, length us, event | category | flops | bytes accessed | tf_op | source)
XLA Modules:
  0.0 549.8 jit_solution(17699272089112461945)
XLA Ops:
  8.2 1.5 constant_dynamic-slice_fusion.3
  15.8 14.4 %attn_fwd.2 = (bf16[512,2304]{1,0:T(8,128)(2,1)}, f32[512,128]{1,0:T(8,128)}, bf16[512,768]{1,0:T(8,128)(2,1)}, bf16[768,512]{1,0:T(8,128)(2,1)}, f32[512,768]{1...) custom-call(f32[12]{0:T(128)} %multiply_exponential_fusion.refs_0_, bf16[512,768]{1,0:T(8,128)(2,1)} %refs_1_.1, ...), custom_call_target="tpu_custom_call" | custom-call | flops 1024 | bytes 1024 | tf_op jit(solution)/shard_map/attn_fwd/pallas_call | solution.py:260
  33.8 1.9 collective-permute-start.4
  35.7 7.0 %fusion.50 = (bf16[1,768,2,768]{3,2,1,0:T(2,128)(2,1)}, bf16[1,768,2,768]{3,2,1,0:T(2,128)(2,1)S(1)}) fusion(bf16[2,768,2,768]{3,2,1,0:T(2,128)(2,1)} %param.19), kind=kLoop, calls=%fused_computation.153 | loop fusion | bytes 9437184 | tf_op jit(solution)/shard_map/slice | solution.py:823
  42.7 1.9 copy.59
  45.2 1.6 slice_bitcast_fusion
  46.8 6.2 %ff_fwd.4.refs_2_ = f32[512,768]{1,0:T(8,128)} custom-call(s32[1]{0:T(128)} %bitcast.refs_0_.refs_1_, bf16[512,768]{1,0:T(8,128)(2,1)} %get-tuple-element.165.refs_1_, f32[512,768]{1,0:T(8,128)} %get-tuple-element.123.refs_2_.refs_6_, f32[1,768]{1,0:T(1,128)} %get-tuple-element.273.refs_5_.refs_3_.refs_7_, f32[1,768]{1,0:T(1,128)} %get-tuple-element.270.refs_6_.refs_4_, ...), custom_call_target="tpu_custom_call" | custom-call | flops 1024 | bytes 1024 | tf_op jit(solution)/shard_map/ff_fwd/pallas_call | solution.py:260
  53.0 20.5 %collective-permute-done.4 = bf16[96,2304]{1,0:T(8,128)(2,1)} collective-permute-done((bf16[96,2304]{1,0:T(8,128)(2,1)S(1)}, bf16[96,2304]{1,0:T(8,128)(2,1)}, u32[]{:S(2)}, u32[]{:S(2)}) %collective-permute-start.4) | collective-permute-done | bytes 442400 | tf_op jit(solution)/shard_map/ppermute | solution.py:90
  76.2 2.0 collective-permute-start.9
  78.8 22.6 %collective-permute-done.9 = bf16[1,96,2304]{2,1,0:T(8,128)(2,1)} collective-permute-done((bf16[1,96,2304]{2,1,0:T(8,128)(2,1)}, bf16[1,96,2304]{2,1,0:T(8,128)(2,1)}, u32[]{:S(2)}, u32[]{:S(2)}) %collective-permute-start.9) | collective-permute-done | bytes 442400 | tf_op jit(solution)/shard_map/ppermute | solution.py:84
  101.4 8.7 %collective-permute-done.8 = bf16[1,96,2304]{2,1,0:T(8,128)(2,1)} collective-permute-done((bf16[1,96,2304]{2,1,0:T(8,128)(2,1)}, bf16[1,96,2304]{2,1,0:T(8,128)(2,1)}, u32[]{:S(2)}, u32[]{:S(2)}) %collective-permute-start.8) | collective-permute-done | bytes 442400 | tf_op jit(solution)/shard_map/ppermute | solution.py:84
  114.3 6.1 %collective-permute-start.11 = (bf16[4,1,96,2304]{3,2,1,0:T(8,128)(2,1)S(1)}, bf16[4,1,96,2304]{3,2,1,0:T(8,128)(2,1)S(1)}, u32[]{:S(2)}, u32[]{:S(2)}) collective-permute-start(bf16[4,1,96,2304]{3,2,1,0:T(8,128)(2,1)S(1)} %pad_maximum_fusion.1.refs_7_.refs_10_), channel_id=1, source_target_pairs={{0,4},{4,0},{8,12},{12,8},{16,20},{20,16},{24,28},{28,24},{1,5},{5... | collective-permute-start | bytes 5308424 | tf_op jit(solution)/shard_map/ppermute | solution.py:84
  121.6 1.8 pad_maximum_fusion.2.refs_9_.refs_8_
  124.0 1.8 copy.61
  126.5 2.3 collective-permute-done.12.refs_10_.refs_9_
  130.0 14.7 %ff_fwd.5 = (f32[512,768]{1,0:T(8,128)}, bf16[512,768]{1,0:T(8,128)(2,1)}, bf16[768,512]{1,0:T(8,128)(2,1)}) custom-call(s32[1]{0:T(128)} %bitcast.refs_0_.refs_1_, bf16[512,768]{1,0:T(8,128)(2,1)} %get-tuple-element.165.refs_1_, f32[512,768]{1,0:T(8,128)} %ff_fwd.4.refs_2_, f32[1,768]{1,0:T(1,128)} %get-tuple-element.275.refs_3_.refs_5_, ...), custom_call_target="tpu_custom_call" | custom-call | flops 1024 | bytes 1024 | tf_op jit(solution)/shard_map/ff_fwd/pallas_call | solution.py:260
  144.8 14.9 %attn_fwd.3 = (bf16[512,2304]{1,0:T(8,128)(2,1)}, f32[512,128]{1,0:T(8,128)}, bf16[512,768]{1,0:T(8,128)(2,1)}, bf16[768,512]{1,0:T(8,128)(2,1)}, f32[512,768]{1...) custom-call(f32[12]{0:T(128)} %multiply_exponential_fusion.refs_0_, ...), custom_call_target="tpu_custom_call" | custom-call | flops 1024 | bytes 1024 | tf_op jit(solution)/shard_map/attn_fwd/pallas_call | solution.py:260
  159.7 6.3 %ff_fwd.6.refs_2_ = f32[512,768]{1,0:T(8,128)} custom-call(s32[1]{0:T(128)} %bitcast.refs_0_.refs_1_, bf16[512,768]{1,0:T(8,128)(2,1)} %get-tuple-element.149.refs_1_, f32[512,768]{1,0:T(8,128)} %get-tuple-element.144.refs_2_.refs_6_, f32[1,768]{1,0:T(1,128)} %get-tuple-element.274.refs_5_.refs_3_.refs_7_, f32[1,768]{1,0:T(1,128)} %get-tuple-element.269.refs_6_.refs_4_, ...), custom_call_target="tpu_custom_call" | custom-call | flops 1024 | bytes 1024 | tf_op jit(solution)/shard_map/ff_fwd/pallas_call | solution.py:260
  165.9 21.9 %all-gather.7.cloned.1.call-done = bf16[24,96,2304]{2,1,0:T(8,128)(2,1)} async-done(((bf16[3,96,2304]{2,1,0:T(8,128)(2,1)}), bf16[24,96,2304]{2,1,0:T(8,128)(2,1)}) %all-gather.7.cloned.1.call-update) | async-done | bytes 10616848 | tf_op jit(solution)/shard_map/all_gather | solution.py:863
  187.8 13.4 %ff_fwd.7 = (f32[512,768]{1,0:T(8,128)}, bf16[512,768]{1,0:T(8,128)(2,1)}, bf16[768,512]{1,0:T(8,128)(2,1)}) custom-call(s32[1]{0:T(128)} %bitcast.refs_0_.refs_1_, bf16[512,768]{1,0:T(8,128)(2,1)} %get-tuple-element.149.refs_1_, f32[512,768]{1,0:T(8,128)} %ff_fwd.6.refs_2_, f32[1,768]{1,0:T(1,128)} %get-tuple-element.276.refs_3_.refs_5_, ...), custom_call_target="tpu_custom_call" | custom-call | flops 1024 | bytes 1024 | tf_op jit(solution)/shard_map/ff_fwd/pallas_call | solution.py:260
  201.2 31.8 %ff_bwd.3 = (f32[512,768]{1,0:T(8,128)}, bf16[512,768]{1,0:T(8,128)(2,1)}, bf16[768,512]{1,0:T(8,128)(2,1)}, f32[2,768]{1,0:T(2,128)}, bf16[512,768]{1,0:T(8,128...) custom-call(s32[1]{0:T(128)} %bitcast.refs_0_.refs_1_, bf16[512,768]{1,0:T(8,128)(2,1)} %get-tuple-element.149.refs_1_, ...), custom_call_target="tpu_custom_call" | custom-call | flops 1024 | bytes 1024 | tf_op jit(solution)/shard_map/ff_bwd/pallas_call | solution.py:260
  233.2 21.5 %attn_bwd.2 = (bf16[4,4,104,768]{3,2,1,0:T(8,128)(2,1)}, bf16[4,4,104,768]{3,2,1,0:T(8,128)(2,1)}, f32[512,768]{1,0:T(8,128)}) custom-call(f32[12]{0:T(128)} %multiply_exponential_fusion.refs_0_, s32[1]{0:T(128)} %bitcast.refs_0_.refs_1_, bf16[512,768]{1,0:T(8,128)(2,1)} %get-tuple-element.153.refs_2_, bf16[2,768,768]{2,1,0:T(8,128)(2,1)} %refs_3_.5, ...), custom_call_target="tpu_custom_call" | custom-call | flops 1024 | bytes 1024 | tf_op jit(solution)/shard_map/attn_bwd/pallas_call | solution.py:260
  254.7 2.1 copy.47
  257.0 19.2 %ff_bwd.4 = (f32[512,768]{1,0:T(8,128)}, bf16[512,768]{1,0:T(8,128)(2,1)}, bf16[768,512]{1,0:T(8,128)(2,1)}, f32[2,768]{1,0:T(2,128)}, bf16[8,4,96,2304]{3,2,1,0:T(8,128)(2,1)}) custom-call(s32[1]{0:T(128)} %bitcast.refs_0_.refs_1_, bf16[512,768]{1,0:T(8,128)(2,1)} %get-tuple-element.165.refs_1_, bf16[768,512]{1,0:T(8,128)(2,1)} %get-tuple-element.161.refs_2_, ...), custom_call_target="tpu_custom_call" | custom-call | flops 1024 | bytes 1024 | tf_op jit(solution)/shard_map/ff_bwd/pallas_call | solution.py:260
  276.3 4.1 add_convert_fusion.4
  282.1 19.2 %ff_bwd.5 = (f32[512,768]{1,0:T(8,128)}, bf16[512,768]{1,0:T(8,128)(2,1)}, f32[2,768]{1,0:T(2,128)}, bf16[8,4,96,2304]{3,2,1,0:T(8,128)(2,1)}) custom-call(s32[1]{0:T(128)} %bitcast.refs_0_.refs_1_, bf16[512,768]{1,0:T(8,128)(2,1)} %get-tuple-element.165.refs_1_, bf16[768,512]{1,0:T(8,128)(2,1)} %get-tuple-element.161.refs_2_, ...), custom_call_target="tpu_custom_call", output_to_operand_aliasing={{3}: (12, {})} | custom-call | flops 1024 | bytes 1024 | tf_op jit(solution)/shard_map/ff_bwd/pallas_call | solution.py:260
  301.3 9.2 %collective-permute-done.15 = bf16[2,2,104,768]{3,2,0,1:T(8,128)(2,1)S(1)} collective-permute-done((bf16[2,2,104,768]{3,2,0,1:T(8,128)(2,1)}, bf16[2,2,104,768]{3,2,0,1:T(8,128)(2,1)S(1)}, u32[]{:S(2)}, u32[]{:S(2)}) %collective-permute-start.15) | collective-permute-done | bytes 639008 | tf_op jit(solution)/shard_map/ppermute | solution.py:84
  315.1 21.0 %attn_bwd.3 = (bf16[4,4,104,768]{3,2,1,0:T(8,128)(2,1)}, bf16[4,4,104,768]{3,2,1,0:T(8,128)(2,1)}, f32[512,768]{1,0:T(8,128)}) custom-call(f32[12]{0:T(128)} %multiply_exponential_fusion.refs_0_, s32[1]{0:T(128)} %bitcast.refs_0_.refs_1_, bf16[512,768]{1,0:T(8,128)(2,1)} %get-tuple-element.173.refs_2_, bf16[2,768,768]{2,1,0:T(8,128)(2,1)} %refs_3_.5, ...), custom_call_target="tpu_custom_call" | custom-call | flops 1024 | bytes 1024 | tf_op jit(solution)/shard_map/attn_bwd/pallas_call | solution.py:260
  336.1 2.0 copy.54
  338.2 2.0 collective-permute-start.18
  340.2 4.4 collective-permute-done.18
  344.7 1.7 add_convert_fusion
  350.2 2.0 collective-permute-start.22
  353.6 4.7 collective-permute-done.21
  358.3 6.0 %collective-permute-done.22 = bf16[104,768]{1,0:T(8,128)(2,1)} collective-permute-done((bf16[104,768]{1,0:T(8,128)(2,1)}, bf16[104,768]{1,0:T(8,128)(2,1)}, u32[]{:S(2)}, u32[]{:S(2)}) %collective-permute-start.22) | collective-permute-done | bytes 159776 | tf_op jit(solution)/shard_map/ppermute | solution.py:90
  367.5 3.2 collective-permute-start.27
  370.7 1.4 collective-permute-start.26
  372.1 8.0 %collective-permute-done.27 = bf16[104,768]{1,0:T(8,128)(2,1)S(1)} collective-permute-done((bf16[104,768]{1,0:T(8,128)(2,1)S(1)}, bf16[104,768]{1,0:T(8,128)(2,1)S(1)}, u32[]{:S(2)}, u32[]{:S(2)}) %collective-permute-start.27) | collective-permute-done | bytes 159776 | tf_op jit(solution)/shard_map/ppermute | solution.py:90
  380.1 5.4 collective-permute-done.26
  387.8 1.7 collective-permute-start.31
  389.4 6.0 %collective-permute-done.30 = bf16[104,768]{1,0:T(8,128)(2,1)S(1)} collective-permute-done((bf16[104,768]{1,0:T(8,128)(2,1)S(1)}, bf16[104,768]{1,0:T(8,128)(2,1)S(1)}, u32[]{:S(2)}, u32[]{:S(2)}) %collective-permute-start.30) | collective-permute-done | bytes 159776 | tf_op jit(solution)/shard_map/ppermute | solution.py:90
  395.4 6.3 %collective-permute-done.29 = bf16[104,768]{1,0:T(8,128)(2,1)S(1)} collective-permute-done((bf16[104,768]{1,0:T(8,128)(2,1)S(1)}, bf16[104,768]{1,0:T(8,128)(2,1)S(1)}, u32[]{:S(2)}, u32[]{:S(2)}) %collective-permute-start.29) | collective-permute-done | bytes 159776 | tf_op jit(solution)/shard_map/ppermute | solution.py:90
  404.2 1.7 collective-permute-start.36
  407.2 2.5 collective-permute-done.36
  409.7 9.0 %collective-permute-done.35 = bf16[104,768]{1,0:T(8,128)(2,1)S(1)} collective-permute-done((bf16[104,768]{1,0:T(8,128)(2,1)S(1)}, bf16[104,768]{1,0:T(8,128)(2,1)S(1)}, u32[]{:S(2)}, u32[]{:S(2)}) %collective-permute-start.35) | collective-permute-done | bytes 159776 | tf_op jit(solution)/shard_map/ppermute | solution.py:90
  419.6 12.7 %collective-permute-done.38 = bf16[2,2,104,768]{3,2,1,0:T(8,128)(2,1)S(1)} collective-permute-done((bf16[2,2,104,768]{3,2,1,0:T(8,128)(2,1)S(1)}, bf16[2,2,104,768]{3,2,1,0:T(8,128)(2,1)S(1)}, u32[]{:S(2)}, u32[]{:S(2)}) %collective-permute-start.38) | collective-permute-done | bytes 639008 | tf_op jit(solution)/shard_map/ppermute | solution.py:84
  433.0 2.6 collective-permute-start.42
  438.7 11.4 %collective-permute-done.40 = bf16[1,2,104,768]{3,2,1,0:T(8,128)(2,1)S(1)} collective-permute-done((bf16[1,2,104,768]{3,2,1,0:T(8,128)(2,1)S(1)}, bf16[1,2,104,768]{3,2,1,0:T(8,128)(2,1)S(1)}, u32[]{:S(2)}, u32[]{:S(2)}) %collective-permute-start.40) | collective-permute-done | bytes 319520 | tf_op jit(solution)/shard_map/ppermute | solution.py:84
  450.1 4.1 collective-permute-done.43
  459.2 1.9 collective-permute-start.47
  463.0 8.7 %spread_out.2 = (f32[4,8,768]{2,1,0:T(8,128)}, f32[2,768,2304]{2,1,0:T(8,128)}, f32[2,768,768]{2,1,0:T(8,128)}) custom-call(s32[2]{0:T(128)} %pad_add_fusion.refs_0_, bf16[4,2,104,768]{3,2,1,0:T(8,128)(2,1)} %copy-done.8, bf16[4,2,104,768]{3,2,1,0:T(8,128)(2,1)} %copy-done.21, bf16[4,2,104,768]{3,2,1,0:T(8,128)(2,1)} %copy-done.7, ...), custom_call_target="tpu_custom_call" | custom-call | flops 1024 | bytes 1024 | tf_op jit(solution)/shard_map/spread_out/pallas_call | solution.py:260
  472.7 7.9 %collective-permute-done.47 = bf16[96,2304]{1,0:T(8,128)(2,1)} collective-permute-done((bf16[96,2304]{1,0:T(8,128)(2,1)}, bf16[96,2304]{1,0:T(8,128)(2,1)}, u32[]{:S(2)}, u32[]{:S(2)}) %collective-permute-start.47) | collective-permute-done | bytes 442400 | tf_op jit(solution)/shard_map/ppermute | solution.py:90
  480.6 5.1 collective-permute-done.45
  488.0 2.7 collective-permute-start.49
  492.6 1.5 fusion.1
  494.1 2.4 slice_bitcast_fusion.5
  496.8 2.2 collective-permute-start.51
  500.6 1.4 stack_reshape.7
  502.0 8.7 %spread_out.3 = (f32[4,8,768]{2,1,0:T(8,128)}, f32[2,768,2304]{2,1,0:T(8,128)}, f32[2,768,768]{2,1,0:T(8,128)}) custom-call(s32[2]{0:T(128)} %pad_add_fusion.refs_0_, bf16[4,2,104,768]{3,2,1,0:T(8,128)(2,1)} %copy-done.10, bf16[4,2,104,768]{3,2,1,0:T(8,128)(2,1)} %collective-permute-done.48.refs_2_, ...), custom_call_target="tpu_custom_call", output_to_operand_aliasing={{1}: (5, {}), {2}: (6, {})} | custom-call | flops 1024 | bytes 1024 | tf_op jit(solution)/shard_map/spread_out/pallas_call | solution.py:260
  512.3 3.5 collective-permute-done.50
  515.8 19.0 %collective-permute-done.51 = bf16[96,2304]{1,0:T(8,128)(2,1)} collective-permute-done((bf16[96,2304]{1,0:T(8,128)(2,1)}, bf16[96,2304]{1,0:T(8,128)(2,1)}, u32[]{:S(2)}, u32[]{:S(2)}) %collective-permute-start.51) | collective-permute-done | bytes 442400 | tf_op jit(solution)/shard_map/ppermute | solution.py:90
  534.7 3.6 collective-permute-done.52
  538.3 1.6 fusion.3
  540.4 1.6 pad_maximum_fusion.9
  (226 shorter events, 63.9 us)
Async XLA Ops:
  7.2 104.0 %all-gather.5.cloned.1.call-start = ((), (), s32[]{:S(2)}) async-start(), calls=%async_computation.4 | async-start | bytes 2211840 | tf_op jit(solution)/shard_map/all_gather | solution.py:846
  9.8 21.2 %collective-permute-start.1 = (bf16[96,2304]{1,0:T(8,128)(2,1)S(1)}, bf16[96,2304]{1,0:T(8,128)(2,1)S(1)}, u32[]{:S(2)}, u32[]{:S(2)}) collective-permute-start(bf16[96,2304]{1,0:T(8,128)(2,1)S(1)} %pad_maximum_fusion.17), channel_id=1, source_target_pairs={{0,3},{1,0},{2,1},{3,2},{4,7},{5,4},{6,5},{7,6},{8,11},{9,8},{10,9... | collective-permute-start | bytes 1327112 | tf_op jit(solution)/shard_map/ppermute | solution.py:90
  10.0 21.0 %collective-permute-start = (bf16[96,2304]{1,0:T(8,128)(2,1)S(1)}, bf16[96,2304]{1,0:T(8,128)(2,1)S(1)}, u32[]{:S(2)}, u32[]{:S(2)}) collective-permute-start(bf16[96,2304]{1,0:T(8,128)(2,1)S(1)} %pad_maximum_fusion.17), channel_id=1, source_target_pairs={{0,1},{1,2},{2,3},{3,0},{4,5},{5,6},{6,7},{7,4},{8,9},{9,10},{10,1... | collective-permute-start | bytes 1327112 | tf_op jit(solution)/shard_map/ppermute | solution.py:90
  31.0 156.8 %all-gather.7.cloned.1.call-start = ((), (), s32[]{:S(2)}) async-start(), calls=%async_computation.5 | async-start | bytes 11943936 | tf_op jit(solution)/shard_map/all_gather | solution.py:863
  31.3 21.7 %collective-permute-start.2 = (bf16[1,1,96,2304]{3,2,1,0:T(8,128)(2,1)S(1)}, bf16[1,1,96,2304]{3,2,1,0:T(8,128)(2,1)S(1)}, u32[]{:S(2)}, u32[]{:S(2)}) collective-permute-start(bf16[1,1,96,2304]{3,2,1,0:T(8,128)(2,1)S(1)} %bitcast.156), channel_id=1, source_target_pairs={{0,8},{4,12},{8,0},{12,4},{16,24},{20,28},{24,16},{28,20},{1,9},{5... | collective-permute-start | bytes 1327112 | tf_op jit(solution)/shard_map/ppermute | solution.py:84
  32.6 20.4 %collective-permute-start.3 = (bf16[1,1,96,2304]{3,2,1,0:T(8,128)(2,1)S(1)}, bf16[1,1,96,2304]{3,2,1,0:T(8,128)(2,1)S(1)}, u32[]{:S(2)}, u32[]{:S(2)}) collective-permute-start(bf16[1,1,96,2304]{3,2,1,0:T(8,128)(2,1)S(1)} %bitcast.159), channel_id=1, source_target_pairs={{0,16},{4,20},{8,24},{12,28},{16,0},{20,4},{24,8},{28,12},{1,17},{... | collective-permute-start | bytes 1327112 | tf_op jit(solution)/shard_map/ppermute | solution.py:84
  33.8 39.7 %collective-permute-start.4 = (bf16[96,2304]{1,0:T(8,128)(2,1)S(1)}, bf16[96,2304]{1,0:T(8,128)(2,1)}, u32[]{:S(2)}, u32[]{:S(2)}) collective-permute-start(bf16[96,2304]{1,0:T(8,128)(2,1)S(1)} %pad_maximum_fusion.17), channel_id=1, source_target_pairs={{0,2},{1,3},{2,0},{3,1},{4,6},{5,7},{6,4},{7,5},{8,10},{9,11},{10,... | collective-permute-start | bytes 1327112 | tf_op jit(solution)/shard_map/ppermute | solution.py:90
  75.5 35.6 %collective-permute-start.6 = (bf16[2,1,96,2304]{3,2,1,0:T(8,128)(2,1)}, bf16[2,1,96,2304]{3,2,1,0:T(8,128)(2,1)S(1)}, u32[]{:S(2)}, u32[]{:S(2)}) collective-permute-start(bf16[2,1,96,2304]{3,2,1,0:T(8,128)(2,1)} %pad_maximum_fusion.11), channel_id=1, source_target_pairs={{0,8},{4,12},{8,0},{12,4},{16,24},{20,28},{24,16},{28,20},{1,9},{5... | collective-permute-start | bytes 2654216 | tf_op jit(solution)/shard_map/ppermute | solution.py:84
  75.8 35.3 %collective-permute-start.5 = (bf16[2,1,96,2304]{3,2,1,0:T(8,128)(2,1)}, bf16[2,1,96,2304]{3,2,1,0:T(8,128)(2,1)S(1)}, u32[]{:S(2)}, u32[]{:S(2)}) collective-permute-start(bf16[2,1,96,2304]{3,2,1,0:T(8,128)(2,1)} %pad_maximum_fusion.10), channel_id=1, source_target_pairs={{0,16},{4,20},{8,24},{12,28},{16,0},{20,4},{24,8},{28,12},{1,17},{... | collective-permute-start | bytes 2654216 | tf_op jit(solution)/shard_map/ppermute | solution.py:84
  76.2 25.2 %collective-permute-start.9 = (bf16[1,96,2304]{2,1,0:T(8,128)(2,1)}, bf16[1,96,2304]{2,1,0:T(8,128)(2,1)}, u32[]{:S(2)}, u32[]{:S(2)}) collective-permute-start(bf16[1,96,2304]{2,1,0:T(8,128)(2,1)} %bitcast.7), channel_id=1, source_target_pairs={{0,24},{4,28},{8,16},{12,20},{16,8},{20,12},{24,0},{28,4},{1,25},{... | collective-permute-start | bytes 1327112 | tf_op jit(solution)/shard_map/ppermute | solution.py:84
  78.2 31.9 %collective-permute-start.8 = (bf16[1,96,2304]{2,1,0:T(8,128)(2,1)}, bf16[1,96,2304]{2,1,0:T(8,128)(2,1)}, u32[]{:S(2)}, u32[]{:S(2)}) collective-permute-start(bf16[1,96,2304]{2,1,0:T(8,128)(2,1)} %bitcast.7), channel_id=1, source_target_pairs={{0,16},{4,20},{8,24},{12,28},{16,0},{20,4},{24,8},{28,12},{1,17},{... | collective-permute-start | bytes 1327112 | tf_op jit(solution)/shard_map/ppermute | solution.py:84
  78.5 32.7 %collective-permute-start.7 = (bf16[1,96,2304]{2,1,0:T(8,128)(2,1)}, bf16[1,96,2304]{2,1,0:T(8,128)(2,1)}, u32[]{:S(2)}, u32[]{:S(2)}) collective-permute-start(bf16[1,96,2304]{2,1,0:T(8,128)(2,1)} %bitcast.7), channel_id=1, source_target_pairs={{0,8},{4,12},{8,0},{12,4},{16,24},{20,28},{24,16},{28,20},{1,9},{5... | collective-permute-start | bytes 1327112 | tf_op jit(solution)/shard_map/ppermute | solution.py:84
  113.8 319.0 %reduce-scatter.3.cloned.1.call-start = ((), (), s32[]{:S(2)}) async-start(), calls=%async_computation.2 | async-start | bytes 15925248 | tf_op jit(solution)/shard_map/reduce_scatter | solution.py:920
  114.3 12.1 %collective-permute-start.11 = (bf16[4,1,96,2304]{3,2,1,0:T(8,128)(2,1)S(1)}, bf16[4,1,96,2304]{3,2,1,0:T(8,128)(2,1)S(1)}, u32[]{:S(2)}, u32[]{:S(2)}) collective-permute-start(bf16[4,1,96,2304]{3,2,1,0:T(8,128)(2,1)S(1)} %pad_maximum_fusion.1.refs_7_.refs_10_), channel_id=1, source_target_pairs={{0,4},{4,0},{8,12},{12,8},{16,20},{20,16},{24,28},{28,24},{1,5},{5... | collective-permute-start | bytes 5308424 | tf_op jit(solution)/shard_map/ppermute | solution.py:84
  120.6 5.8 %collective-permute-start.10 = (bf16[4,1,96,2304]{3,2,1,0:T(8,128)(2,1)S(1)}, bf16[4,1,96,2304]{3,2,1,0:T(8,128)(2,1)S(1)}, u32[]{:S(2)}, u32[]{:S(2)}) collective-permute-start(bf16[4,1,96,2304]{3,2,1,0:T(8,128)(2,1)S(1)} %pad_maximum_fusion.refs_5_.refs_8_), channel_id=1, source_target_pairs={{0,4},{4,0},{8,12},{12,8},{16,20},{20,16},{24,28},{28,24},{1,5},{5... | collective-permute-start | bytes 5308424 | tf_op jit(solution)/shard_map/ppermute | solution.py:84
  123.4 5.4 collective-permute-start.12
  233.1 261.0 %reduce-scatter.5.cloned.1.call-start = ((), (), s32[]{:S(2)}) async-start(), calls=%async_computation.3 | async-start | bytes 15925248 | tf_op jit(solution)/shard_map/reduce_scatter | solution.py:920
  256.7 19.5 %collective-permute-start.13 = (bf16[4,4,104,768]{3,2,0,1:T(8,128)(2,1)S(1)}, bf16[4,4,104,768]{3,2,0,1:T(8,128)(2,1)}, u32[]{:S(2)}, u32[]{:S(2)}) collective-permute-start(bf16[4,4,104,768]{3,2,0,1:T(8,128)(2,1)S(1)} %copy.47), channel_id=1, source_target_pairs={{0,4},{4,0},{8,12},{12,8},{16,20},{20,16},{24,28},{28,24},{1,5},{5... | collective-permute-start | bytes 7667720 | tf_op jit(solution)/shard_map/ppermute | solution.py:84
  280.4 30.7 %copy-start.17 = (bf16[2,2,104,768]{3,2,0,1:T(8,128)(2,1)}, bf16[2,2,104,768]{3,2,0,1:T(8,128)(2,1)S(1)}, u32[]{:S(2)}) copy-start(bf16[2,2,104,768]{3,2,0,1:T(8,128)(2,1)S(1)} %get-tuple-element.234) | copy-start | bytes 1916932
  280.4 32.8 %copy-start.15 = (bf16[2,2,104,768]{3,2,0,1:T(8,128)(2,1)}, bf16[2,2,104,768]{3,2,0,1:T(8,128)(2,1)S(1)}, u32[]{:S(2)}) copy-start(bf16[2,2,104,768]{3,2,0,1:T(8,128)(2,1)S(1)} %get-tuple-element.235) | copy-start | bytes 1916932
  280.4 30.1 %collective-permute-start.15 = (bf16[2,2,104,768]{3,2,0,1:T(8,128)(2,1)}, bf16[2,2,104,768]{3,2,0,1:T(8,128)(2,1)S(1)}, u32[]{:S(2)}, u32[]{:S(2)}) collective-permute-start(bf16[2,2,104,768]{3,2,0,1:T(8,128)(2,1)} %get-tuple-element.236), channel_id=1, source_target_pairs={{0,16},{4,20},{8,24},{12,28},{16,0},{20,4},{24,8},{28,12},{1,17},{... | collective-permute-start | bytes 1916936 | tf_op jit(solution)/shard_map/ppermute | solution.py:84
  281.3 29.8 %collective-permute-start.14 = (bf16[2,2,104,768]{3,2,0,1:T(8,128)(2,1)S(1)}, bf16[2,2,104,768]{3,2,0,1:T(8,128)(2,1)S(1)}, u32[]{:S(2)}, u32[]{:S(2)}) collective-permute-start(bf16[2,2,104,768]{3,2,0,1:T(8,128)(2,1)S(1)} %get-tuple-element.237), channel_id=1, source_target_pairs={{0,8},{4,12},{8,0},{12,4},{16,24},{20,28},{24,16},{28,20},{1,9},{5... | collective-permute-start | bytes 1916936 | tf_op jit(solution)/shard_map/ppermute | solution.py:84
  312.1 24.0 %collective-permute-start.17 = (bf16[2,104,768]{2,1,0:T(8,128)(2,1)}, bf16[2,104,768]{2,1,0:T(8,128)(2,1)S(1)}, u32[]{:S(2)}, u32[]{:S(2)}) collective-permute-start(bf16[2,104,768]{2,1,0:T(8,128)(2,1)} %fusion.9), channel_id=1, source_target_pairs={{0,8},{4,12},{8,0},{12,4},{16,24},{20,28},{24,16},{28,20},{1,9},{5... | collective-permute-start | bytes 958472 | tf_op jit(solution)/shard_map/ppermute | solution.py:84
  313.3 22.8 %collective-permute-start.16 = (bf16[2,104,768]{2,1,0:T(8,128)(2,1)S(1)}, bf16[2,104,768]{2,1,0:T(8,128)(2,1)S(1)}, u32[]{:S(2)}, u32[]{:S(2)}) collective-permute-start(bf16[2,104,768]{2,1,0:T(8,128)(2,1)S(1)} %fusion.8), channel_id=1, source_target_pairs={{0,16},{4,20},{8,24},{12,28},{16,0},{20,4},{24,8},{28,12},{1,17},{... | collective-permute-start | bytes 958472 | tf_op jit(solution)/shard_map/ppermute | solution.py:84
  338.2 6.5 %collective-permute-start.18 = (bf16[4,4,104,768]{3,2,0,1:T(8,128)(2,1)S(1)}, bf16[4,4,104,768]{3,2,0,1:T(8,128)(2,1)S(1)}, u32[]{:S(2)}, u32[]{:S(2)}) collective-permute-start(bf16[4,4,104,768]{3,2,0,1:T(8,128)(2,1)S(1)} %copy.54), channel_id=1, source_target_pairs={{0,4},{4,0},{8,12},{12,8},{16,20},{20,16},{24,28},{28,24},{1,5},{5... | collective-permute-start | bytes 7667720 | tf_op jit(solution)/shard_map/ppermute | solution.py:84
  346.3 17.9 %collective-permute-start.20 = (bf16[2,2,104,768]{3,2,0,1:T(8,128)(2,1)}, bf16[2,2,104,768]{3,2,0,1:T(8,128)(2,1)S(1)}, u32[]{:S(2)}, u32[]{:S(2)}) collective-permute-start(bf16[2,2,104,768]{3,2,0,1:T(8,128)(2,1)} %get-tuple-element.231), channel_id=1, source_target_pairs={{0,16},{4,20},{8,24},{12,28},{16,0},{20,4},{24,8},{28,12},{1,17},{... | collective-permute-start | bytes 1916936 | tf_op jit(solution)/shard_map/ppermute | solution.py:84
  347.1 17.1 %collective-permute-start.19 = (bf16[2,2,104,768]{3,2,0,1:T(8,128)(2,1)}, bf16[2,2,104,768]{3,2,0,1:T(8,128)(2,1)S(1)}, u32[]{:S(2)}, u32[]{:S(2)}) collective-permute-start(bf16[2,2,104,768]{3,2,0,1:T(8,128)(2,1)} %get-tuple-element.232), channel_id=1, source_target_pairs={{0,8},{4,12},{8,0},{12,4},{16,24},{20,28},{24,16},{28,20},{1,9},{5... | collective-permute-start | bytes 1916936 | tf_op jit(solution)/shard_map/ppermute | solution.py:84
  348.7 4.9 collective-permute-start.23
  349.9 8.3 %collective-permute-start.21 = (bf16[104,768]{1,0:T(8,128)(2,1)}, bf16[104,768]{1,0:T(8,128)(2,1)S(1)}, u32[]{:S(2)}, u32[]{:S(2)}) collective-permute-start(bf16[104,768]{1,0:T(8,128)(2,1)} %get-tuple-element.259), channel_id=1, source_target_pairs={{0,3},{1,0},{2,1},{3,2},{4,7},{5,4},{6,5},{7,6},{8,11},{9,8},{10,9... | collective-permute-start | bytes 479240 | tf_op jit(solution)/shard_map/ppermute | solution.py:90
  350.2 14.1 %collective-permute-start.22 = (bf16[104,768]{1,0:T(8,128)(2,1)}, bf16[104,768]{1,0:T(8,128)(2,1)}, u32[]{:S(2)}, u32[]{:S(2)}) collective-permute-start(bf16[104,768]{1,0:T(8,128)(2,1)} %get-tuple-element.260), channel_id=1, source_target_pairs={{0,2},{1,3},{2,0},{3,1},{4,6},{5,7},{6,4},{7,5},{8,10},{9,11},{10,... | collective-permute-start | bytes 479240 | tf_op jit(solution)/shard_map/ppermute | solution.py:90
  364.4 21.2 %collective-permute-start.25 = (bf16[2,104,768]{2,1,0:T(8,128)(2,1)S(1)}, bf16[2,104,768]{2,1,0:T(8,128)(2,1)S(1)}, u32[]{:S(2)}, u32[]{:S(2)}) collective-permute-start(bf16[2,104,768]{2,1,0:T(8,128)(2,1)S(1)} %fusion.14), channel_id=1, source_target_pairs={{0,8},{4,12},{8,0},{12,4},{16,24},{20,28},{24,16},{28,20},{1,9},{5... | collective-permute-start | bytes 958472 | tf_op jit(solution)/shard_map/ppermute | solution.py:84
  365.6 19.9 %collective-permute-start.24 = (bf16[2,104,768]{2,1,0:T(8,128)(2,1)S(1)}, bf16[2,104,768]{2,1,0:T(8,128)(2,1)S(1)}, u32[]{:S(2)}, u32[]{:S(2)}) collective-permute-start(bf16[2,104,768]{2,1,0:T(8,128)(2,1)S(1)} %fusion.13), channel_id=1, source_target_pairs={{0,16},{4,20},{8,24},{12,28},{16,0},{20,4},{24,8},{28,12},{1,17},{... | collective-permute-start | bytes 958472 | tf_op jit(solution)/shard_map/ppermute | solution.py:84
  367.4 19.9 %copy-start.25 = (bf16[2,2,104,768]{3,2,0,1:T(8,128)(2,1)S(1)}, bf16[2,2,104,768]{3,2,0,1:T(8,128)(2,1)}, u32[]{:S(2)}) copy-start(bf16[2,2,104,768]{3,2,0,1:T(8,128)(2,1)} %copy-done.24) | copy-start | bytes 1916932
  367.4 4.7 collective-permute-start.28
  367.5 12.6 %collective-permute-start.27 = (bf16[104,768]{1,0:T(8,128)(2,1)S(1)}, bf16[104,768]{1,0:T(8,128)(2,1)S(1)}, u32[]{:S(2)}, u32[]{:S(2)}) collective-permute-start(bf16[104,768]{1,0:T(8,128)(2,1)S(1)} %fusion.21), channel_id=1, source_target_pairs={{0,2},{1,3},{2,0},{3,1},{4,6},{5,7},{6,4},{7,5},{8,10},{9,11},{10,... | collective-permute-start | bytes 479240 | tf_op jit(solution)/shard_map/ppermute | solution.py:90
  370.7 14.9 %collective-permute-start.26 = (bf16[104,768]{1,0:T(8,128)(2,1)S(1)}, bf16[104,768]{1,0:T(8,128)(2,1)S(1)}, u32[]{:S(2)}, u32[]{:S(2)}) collective-permute-start(bf16[104,768]{1,0:T(8,128)(2,1)S(1)} %fusion.21), channel_id=1, source_target_pairs={{0,1},{1,2},{2,3},{3,0},{4,5},{5,6},{6,7},{7,4},{8,9},{9,10},{10,1... | collective-permute-start | bytes 479240 | tf_op jit(solution)/shard_map/ppermute | solution.py:90
  385.6 16.2 %collective-permute-start.33 = (bf16[1,2,104,768]{3,2,1,0:T(8,128)(2,1)S(1)}, bf16[1,2,104,768]{3,2,1,0:T(8,128)(2,1)S(1)}, u32[]{:S(2)}, u32[]{:S(2)}) collective-permute-start(bf16[1,2,104,768]{3,2,1,0:T(8,128)(2,1)S(1)} %maximum_bitcast_fusion.1), channel_id=1, source_target_pairs={{0,16},{4,20},{8,24},{12,28},{16,0},{20,4},{24,8},{28,12},{1,17},{... | collective-permute-start | bytes 958472 | tf_op jit(solution)/shard_map/ppermute | solution.py:84
  386.5 16.1 %collective-permute-start.32 = (bf16[1,2,104,768]{3,2,1,0:T(8,128)(2,1)S(1)}, bf16[1,2,104,768]{3,2,1,0:T(8,128)(2,1)S(1)}, u32[]{:S(2)}, u32[]{:S(2)}) collective-permute-start(bf16[1,2,104,768]{3,2,1,0:T(8,128)(2,1)S(1)} %maximum_bitcast_fusion), channel_id=1, source_target_pairs={{0,8},{4,12},{8,0},{12,4},{16,24},{20,28},{24,16},{28,20},{1,9},{5... | collective-permute-start | bytes 958472 | tf_op jit(solution)/shard_map/ppermute | solution.py:84
  387.6 7.8 %collective-permute-start.30 = (bf16[104,768]{1,0:T(8,128)(2,1)S(1)}, bf16[104,768]{1,0:T(8,128)(2,1)S(1)}, u32[]{:S(2)}, u32[]{:S(2)}) collective-permute-start(bf16[104,768]{1,0:T(8,128)(2,1)S(1)} %get-tuple-element.255), channel_id=1, source_target_pairs={{0,2},{1,3},{2,0},{3,1},{4,6},{5,7},{6,4},{7,5},{8,10},{9,11},{10,... | collective-permute-start | bytes 479240 | tf_op jit(solution)/shard_map/ppermute | solution.py:90
  387.7 14.0 %collective-permute-start.29 = (bf16[104,768]{1,0:T(8,128)(2,1)S(1)}, bf16[104,768]{1,0:T(8,128)(2,1)S(1)}, u32[]{:S(2)}, u32[]{:S(2)}) collective-permute-start(bf16[104,768]{1,0:T(8,128)(2,1)S(1)} %get-tuple-element.256), channel_id=1, source_target_pairs={{0,3},{1,0},{2,1},{3,2},{4,7},{5,4},{6,5},{7,6},{8,11},{9,8},{10,9... | collective-permute-start | bytes 479240 | tf_op jit(solution)/shard_map/ppermute | solution.py:90
  387.8 14.1 %collective-permute-start.31 = (bf16[104,768]{1,0:T(8,128)(2,1)S(1)}, bf16[104,768]{1,0:T(8,128)(2,1)S(1)}, u32[]{:S(2)}, u32[]{:S(2)}) collective-permute-start(bf16[104,768]{1,0:T(8,128)(2,1)S(1)} %get-tuple-element.257), channel_id=1, source_target_pairs={{0,1},{1,2},{2,3},{3,0},{4,5},{5,6},{6,7},{7,4},{8,9},{9,10},{10,1... | collective-permute-start | bytes 479240 | tf_op jit(solution)/shard_map/ppermute | solution.py:90
  402.8 29.6 %collective-permute-start.38 = (bf16[2,2,104,768]{3,2,1,0:T(8,128)(2,1)S(1)}, bf16[2,2,104,768]{3,2,1,0:T(8,128)(2,1)S(1)}, u32[]{:S(2)}, u32[]{:S(2)}) collective-permute-start(bf16[2,2,104,768]{3,2,1,0:T(8,128)(2,1)S(1)} %pad_maximum_fusion.13), channel_id=1, source_target_pairs={{0,8},{4,12},{8,0},{12,4},{16,24},{20,28},{24,16},{28,20},{1,9},{5... | collective-permute-start | bytes 1916936 | tf_op jit(solution)/shard_map/ppermute | solution.py:84
  403.4 29.4 %collective-permute-start.37 = (bf16[2,2,104,768]{3,2,1,0:T(8,128)(2,1)S(1)}, bf16[2,2,104,768]{3,2,1,0:T(8,128)(2,1)S(1)}, u32[]{:S(2)}, u32[]{:S(2)}) collective-permute-start(bf16[2,2,104,768]{3,2,1,0:T(8,128)(2,1)S(1)} %pad_maximum_fusion.12), channel_id=1, source_target_pairs={{0,16},{4,20},{8,24},{12,28},{16,0},{20,4},{24,8},{28,12},{1,17},{... | collective-permute-start | bytes 1916936 | tf_op jit(solution)/shard_map/ppermute | solution.py:84
  404.2 5.6 %collective-permute-start.36 = (bf16[104,768]{1,0:T(8,128)(2,1)S(1)}, bf16[104,768]{1,0:T(8,128)(2,1)S(1)}, u32[]{:S(2)}, u32[]{:S(2)}) collective-permute-start(bf16[104,768]{1,0:T(8,128)(2,1)S(1)} %fusion.18), channel_id=1, source_target_pairs={{0,3},{1,0},{2,1},{3,2},{4,7},{5,4},{6,5},{7,6},{8,11},{9,8},{10,9... | collective-permute-start | bytes 479240 | tf_op jit(solution)/shard_map/ppermute | solution.py:90
  405.9 12.8 %collective-permute-start.35 = (bf16[104,768]{1,0:T(8,128)(2,1)S(1)}, bf16[104,768]{1,0:T(8,128)(2,1)S(1)}, u32[]{:S(2)}, u32[]{:S(2)}) collective-permute-start(bf16[104,768]{1,0:T(8,128)(2,1)S(1)} %fusion.18), channel_id=1, source_target_pairs={{0,2},{1,3},{2,0},{3,1},{4,6},{5,7},{6,4},{7,5},{8,10},{9,11},{10,... | collective-permute-start | bytes 479240 | tf_op jit(solution)/shard_map/ppermute | solution.py:90
  405.9 13.7 %collective-permute-start.34 = (bf16[104,768]{1,0:T(8,128)(2,1)S(1)}, bf16[104,768]{1,0:T(8,128)(2,1)S(1)}, u32[]{:S(2)}, u32[]{:S(2)}) collective-permute-start(bf16[104,768]{1,0:T(8,128)(2,1)S(1)} %fusion.18), channel_id=1, source_target_pairs={{0,1},{1,2},{2,3},{3,0},{4,5},{5,6},{6,7},{7,4},{8,9},{9,10},{10,1... | collective-permute-start | bytes 479240 | tf_op jit(solution)/shard_map/ppermute | solution.py:90
  418.8 14.2 %copy-start.37 = (bf16[104,768]{1,0:T(8,128)(2,1)}, bf16[104,768]{1,0:T(8,128)(2,1)S(1)}, u32[]{:S(2)}) copy-start(bf16[104,768]{1,0:T(8,128)(2,1)S(1)} %collective-permute-done.35) | copy-start | bytes 479236
  433.0 21.2 %collective-permute-start.42 = (bf16[4,2,104,768]{3,2,1,0:T(8,128)(2,1)S(1)}, bf16[4,2,104,768]{3,2,1,0:T(8,128)(2,1)S(1)}, u32[]{:S(2)}, u32[]{:S(2)}) collective-permute-start(bf16[4,2,104,768]{3,2,1,0:T(8,128)(2,1)S(1)} %pad_maximum_fusion.6.refs_3_), channel_id=1, source_target_pairs={{0,4},{4,0},{8,12},{12,8},{16,20},{20,16},{24,28},{28,24},{1,5},{5... | collective-permute-start | bytes 3833864 | tf_op jit(solution)/shard_map/ppermute | solution.py:84
  435.8 18.4 %collective-permute-start.41 = (bf16[4,2,104,768]{3,2,1,0:T(8,128)(2,1)S(1)}, bf16[4,2,104,768]{3,2,1,0:T(8,128)(2,1)S(1)}, u32[]{:S(2)}, u32[]{:S(2)}) collective-permute-start(bf16[4,2,104,768]{3,2,1,0:T(8,128)(2,1)S(1)} %pad_maximum_fusion.5.refs_1_), channel_id=1, source_target_pairs={{0,4},{4,0},{8,12},{12,8},{16,20},{20,16},{24,28},{28,24},{1,5},{5... | collective-permute-start | bytes 3833864 | tf_op jit(solution)/shard_map/ppermute | solution.py:84
  436.9 17.3 %collective-permute-start.43 = (bf16[96,2304]{1,0:T(8,128)(2,1)S(1)}, bf16[96,2304]{1,0:T(8,128)(2,1)S(1)}, u32[]{:S(2)}, u32[]{:S(2)}) collective-permute-start(bf16[96,2304]{1,0:T(8,128)(2,1)S(1)} %get-tuple-element.211), channel_id=1, source_target_pairs={{0,2},{1,3},{2,0},{3,1},{4,6},{5,7},{6,4},{7,5},{8,10},{9,11},{10,... | collective-permute-start | bytes 1327112 | tf_op jit(solution)/shard_map/ppermute | solution.py:90
  437.1 13.0 %collective-permute-start.40 = (bf16[1,2,104,768]{3,2,1,0:T(8,128)(2,1)S(1)}, bf16[1,2,104,768]{3,2,1,0:T(8,128)(2,1)S(1)}, u32[]{:S(2)}, u32[]{:S(2)}) collective-permute-start(bf16[1,2,104,768]{3,2,1,0:T(8,128)(2,1)S(1)} %maximum_bitcast_fusion.3), channel_id=1, source_target_pairs={{0,16},{4,20},{8,24},{12,28},{16,0},{20,4},{24,8},{28,12},{1,17},{... | collective-permute-start | bytes 958472 | tf_op jit(solution)/shard_map/ppermute | solution.py:84
  437.7 24.0 %copy-start.12 = (bf16[512,768]{1,0:T(8,128)(2,1)S(1)}, bf16[512,768]{1,0:T(8,128)(2,1)}, u32[]{:S(2)}) copy-start(bf16[512,768]{1,0:T(8,128)(2,1)} %get-tuple-element.140.refs_1_) | copy-start | bytes 2359300
  437.7 24.0 %copy-start.23 = (bf16[512,768]{1,0:T(8,128)(2,1)S(1)}, bf16[512,768]{1,0:T(8,128)(2,1)}, u32[]{:S(2)}) copy-start(bf16[512,768]{1,0:T(8,128)(2,1)} %get-tuple-element.147) | copy-start | bytes 2359300
  437.8 12.3 %collective-permute-start.39 = (bf16[1,2,104,768]{3,2,1,0:T(8,128)(2,1)S(1)}, bf16[1,2,104,768]{3,2,1,0:T(8,128)(2,1)S(1)}, u32[]{:S(2)}, u32[]{:S(2)}) collective-permute-start(bf16[1,2,104,768]{3,2,1,0:T(8,128)(2,1)S(1)} %maximum_bitcast_fusion.2), channel_id=1, source_target_pairs={{0,8},{4,12},{8,0},{12,4},{16,24},{20,28},{24,16},{28,20},{1,9},{5... | collective-permute-start | bytes 958472 | tf_op jit(solution)/shard_map/ppermute | solution.py:84
  456.4 29.2 %collective-permute-start.45 = (bf16[2,2,104,768]{3,2,1,0:T(8,128)(2,1)S(1)}, bf16[2,2,104,768]{3,2,1,0:T(8,128)(2,1)}, u32[]{:S(2)}, u32[]{:S(2)}) collective-permute-start(bf16[2,2,104,768]{3,2,1,0:T(8,128)(2,1)S(1)} %pad_maximum_fusion.15), channel_id=1, source_target_pairs={{0,8},{4,12},{8,0},{12,4},{16,24},{20,28},{24,16},{28,20},{1,9},{5... | collective-permute-start | bytes 1916936 | tf_op jit(solution)/shard_map/ppermute | solution.py:84
  457.6 29.2 %collective-permute-start.44 = (bf16[2,2,104,768]{3,2,1,0:T(8,128)(2,1)S(1)}, bf16[2,2,104,768]{3,2,1,0:T(8,128)(2,1)}, u32[]{:S(2)}, u32[]{:S(2)}) collective-permute-start(bf16[2,2,104,768]{3,2,1,0:T(8,128)(2,1)S(1)} %pad_maximum_fusion.14), channel_id=1, source_target_pairs={{0,16},{4,20},{8,24},{12,28},{16,0},{20,4},{24,8},{28,12},{1,17},{... | collective-permute-start | bytes 1916936 | tf_op jit(solution)/shard_map/ppermute | solution.py:84
  458.3 14.3 %collective-permute-start.46 = (bf16[96,2304]{1,0:T(8,128)(2,1)}, bf16[96,2304]{1,0:T(8,128)(2,1)S(1)}, u32[]{:S(2)}, u32[]{:S(2)}) collective-permute-start(bf16[96,2304]{1,0:T(8,128)(2,1)} %get-tuple-element.216), channel_id=1, source_target_pairs={{0,3},{1,0},{2,1},{3,2},{4,7},{5,4},{6,5},{7,6},{8,11},{9,8},{10,9... | collective-permute-start | bytes 1327112 | tf_op jit(solution)/shard_map/ppermute | solution.py:90
  459.2 21.3 %collective-permute-start.47 = (bf16[96,2304]{1,0:T(8,128)(2,1)}, bf16[96,2304]{1,0:T(8,128)(2,1)}, u32[]{:S(2)}, u32[]{:S(2)}) collective-permute-start(bf16[96,2304]{1,0:T(8,128)(2,1)} %get-tuple-element.217), channel_id=1, source_target_pairs={{0,1},{1,2},{2,3},{3,0},{4,5},{5,6},{6,7},{7,4},{8,9},{9,10},{10,1... | collective-permute-start | bytes 1327112 | tf_op jit(solution)/shard_map/ppermute | solution.py:90
  472.7 19.3 %copy-start.32 = (bf16[96,2304]{1,0:T(8,128)(2,1)}, bf16[96,2304]{1,0:T(8,128)(2,1)S(1)}, u32[]{:S(2)}) copy-start(bf16[96,2304]{1,0:T(8,128)(2,1)S(1)} %collective-permute-done.46) | copy-start | bytes 1327108
  488.0 14.0 %collective-permute-start.49 = (bf16[4,2,104,768]{3,2,1,0:T(8,128)(2,1)S(1)}, bf16[4,2,104,768]{3,2,1,0:T(8,128)(2,1)}, u32[]{:S(2)}, u32[]{:S(2)}) collective-permute-start(bf16[4,2,104,768]{3,2,1,0:T(8,128)(2,1)S(1)} %pad_maximum_fusion.8.refs_3_), channel_id=1, source_target_pairs={{0,4},{4,0},{8,12},{12,8},{16,20},{20,16},{24,28},{28,24},{1,5},{5... | collective-permute-start | bytes 3833864 | tf_op jit(solution)/shard_map/ppermute | solution.py:84
  492.0 10.0 %collective-permute-start.48 = (bf16[4,2,104,768]{3,2,1,0:T(8,128)(2,1)S(1)}, bf16[4,2,104,768]{3,2,1,0:T(8,128)(2,1)}, u32[]{:S(2)}, u32[]{:S(2)}) collective-permute-start(bf16[4,2,104,768]{3,2,1,0:T(8,128)(2,1)S(1)} %pad_maximum_fusion.7.refs_1_), channel_id=1, source_target_pairs={{0,4},{4,0},{8,12},{12,8},{16,20},{20,16},{24,28},{28,24},{1,5},{5... | collective-permute-start | bytes 3833864 | tf_op jit(solution)/shard_map/ppermute | solution.py:84
  496.5 19.3 %collective-permute-start.50 = (bf16[96,2304]{1,0:T(8,128)(2,1)}, bf16[96,2304]{1,0:T(8,128)(2,1)}, u32[]{:S(2)}, u32[]{:S(2)}) collective-permute-start(bf16[96,2304]{1,0:T(8,128)(2,1)} %get-tuple-element.227), channel_id=1, source_target_pairs={{0,2},{1,3},{2,0},{3,1},{4,6},{5,7},{6,4},{7,5},{8,10},{9,11},{10,... | collective-permute-start | bytes 1327112 | tf_op jit(solution)/shard_map/ppermute | solution.py:90
  496.8 37.9 %collective-permute-start.51 = (bf16[96,2304]{1,0:T(8,128)(2,1)}, bf16[96,2304]{1,0:T(8,128)(2,1)}, u32[]{:S(2)}, u32[]{:S(2)}) collective-permute-start(bf16[96,2304]{1,0:T(8,128)(2,1)} %get-tuple-element.228), channel_id=1, source_target_pairs={{0,3},{1,0},{2,1},{3,2},{4,7},{5,4},{6,5},{7,6},{8,11},{9,8},{10,9... | collective-permute-start | bytes 1327112 | tf_op jit(solution)/shard_map/ppermute | solution.py:90
  498.9 39.4 %collective-permute-start.52 = (bf16[96,2304]{1,0:T(8,128)(2,1)}, bf16[96,2304]{1,0:T(8,128)(2,1)}, u32[]{:S(2)}, u32[]{:S(2)}) collective-permute-start(bf16[96,2304]{1,0:T(8,128)(2,1)} %get-tuple-element.229), channel_id=1, source_target_pairs={{0,1},{1,2},{2,3},{3,0},{4,5},{5,6},{6,7},{7,4},{8,9},{9,10},{10,1... | collective-permute-start | bytes 1327112 | tf_op jit(solution)/shard_map/ppermute | solution.py:90
  (37 other events, 120.9 us)
Sparse Core Ops, SparseCore 0:
  31.1 52.7 all-gather.4
  113.9 73.8 all-gather.6
  233.2 116.0 reduce-scatter.2
  352.7 137.7 reduce-scatter.4

commit v3 on v2

--- a/solution.py
+++ b/solution.py
@@ -80,9 +80,10 @@
         self.n_t = mesh.shape["tensor"]
         self.flying = []
 
-    def flip(self, value, bit):
+    def flip(self, value, bit, wait=True):
         got = lax.ppermute(value, "dp", [(i, i ^ bit) for i in range(self.n_dp)])
-        self.flying.append(got)
+        if wait:
+            self.flying.append(got)
         return got
 
     def shift(self, value, step):
@@ -131,20 +132,6 @@
 
 
 class Gather:
-    def __init__(self, net, line, slices):
-        self.net, self.line = net, line
-        held = jnp.stack([line.after(one) for one in slices])
-        self.held = [held] + [net.flip(held, bit) for bit in CHIPS[1:]]
-
-    def core(self):
-        self.held = jnp.stack([self.line.after(one) for one in self.held])
-        self.got = self.net.flip(self.held, 1)
-
-    def pieces(self):
-        return [self.held, self.got]
-
-
-class Gather2:
     def __init__(self, net, line, slices):
         self.net, self.line = net, line
         n = len(slices) // 2
@@ -165,10 +152,11 @@
 
     def core(self):
         self.join()
-        self.got = [self.net.flip(self.held[c], 1) for c in range(2)]
+        self.held = jnp.concatenate(self.held, axis=0)
+        self.got = self.net.flip(self.held, 1)
 
     def pieces(self):
-        return [one for c in range(2) for one in (self.held[c], self.got[c])]
+        return [self.held, self.got]
 
 
 VMEM_SPEC = pl.BlockSpec(memory_space=pltpu.VMEM)
@@ -470,11 +458,12 @@
     for g, (kind, index) in enumerate(groups):
         mine = []
         s = g % slots
-        count = {"own": 2, "pair": 2, "two": 4, "all": 1}[kind]
         if kind not in sources:
+            count = 1 if kind == "all" else 2
             sources[kind] = refs[at : at + count]
             at += count
         source = sources[kind]
+        part = source[0].shape[2] if kind != "own" else 0
         if kind == "own":
             split = source[0].shape[1]
             rest = source[1].shape[1]
@@ -483,19 +472,20 @@
                 (source[1], w_ref.at[s, :, pl.ds(split, rest)]),
             ]
         elif kind == "all":
-            part = source[0].shape[2]
             pairs = [(source[0].at[j, index], w_ref.at[s, pl.ds(j * part, part)]) for j in range(8)]
         else:
-            colour, place = index if kind == "two" else (0, index)
-            chips = order_of(colour) if kind == "two" else CHIPS
-            part = source[0].shape[2]
             pairs = []
-            for c in range(2):
-                for i, j in enumerate(chips):
-                    row = pl.multiple_of(jnp.bitwise_xor(d, j ^ c) * part, part)
-                    pairs.append(
-                        (source[2 * colour + c].at[i, place], w_ref.at[s, pl.ds(row, part)])
-                    )
+            for colour in (index,) if kind == "two" else (0, 1):
+                for c in range(2):
+                    for i, j in enumerate(order_of(colour)):
+                        slot = jnp.bitwise_xor(d, j ^ c)
+                        if kind == "two":
+                            row = slot * part
+                        else:
+                            row = slot * (2 * part) + colour * part
+                        row = pl.multiple_of(row, part)
+                        one = source[c].at[4 * colour + i, 0]
+                        pairs.append((one, w_ref.at[s, pl.ds(row, part)]))
         for i, (one, to) in enumerate(pairs):
             mine.append(pltpu.make_async_copy(one, to, sems.at[g, i]))
         loads.append(mine)
@@ -591,10 +581,15 @@
     return norm_back(grad, xhat, rstd, gain_ref[...])
 
 
-def ff_bwd_kernel(groups, first, last, slot, copies, smem, ins, raw, outs, raw_outs, scratch):
+def ff_bwd_kernel(
+    groups, first, last, slot, with_grads, copies, smem, ins, raw, outs, raw_outs, scratch
+):
     (at_ref,) = smem
-    hb_ref, hb_t_ref, *ins = ins
-    w_ref, g_ref, sems, out_sems = scratch
+    hb_ref, *ins = ins
+    w_ref, sems, *scratch = scratch
+    if with_grads:
+        hb_t_ref, *ins = ins
+        g_ref, out_sems = scratch
     width = hb_ref.shape[1]
     part = width // 8
     n = len(groups)
@@ -620,10 +615,7 @@
                 copy.start()
         for copy in loads[s]:
             copy.wait()
-        if s >= 2:
-            out[s - 2].wait()
         weights = w_ref.at[s % 2]
-        grads = g_ref.at[s % 2]
 
         def at(c):
             return pl.ds(c * width, width)
@@ -636,6 +628,11 @@
         d_value = (d_act * gelu).astype(bf16)
         act = (gelu * value).astype(bf16)
         dh_ref[...] += mm(d_gate, weights[:, at(0)], NT) + mm(d_value, weights[:, at(1)], NT)
+        if not with_grads:
+            continue
+        if s >= 2:
+            out[s - 2].wait()
+        grads = g_ref.at[s % 2]
         for c, (lhs, rhs) in enumerate(((hb_t_ref, d_gate), (hb_t_ref, d_value), (dyb_t_ref, act))):
             total = mm(lhs[...], rhs).astype(bf16)
             for j in range(8):
@@ -652,7 +649,7 @@
         one.wait()
 
 
-def ff_bwd(groups, slot, d, hb, hb_t, ins, weights, first=False, last=False, into=None):
+def ff_bwd(groups, slot, d, hb, hb_t, ins, weights, first=False, last=False, into=None, grads=True):
     rows, width = hb.shape
     n = len(groups)
     low, few = shape((rows, width), bf16), shape((2, width), f32)
@@ -661,28 +658,96 @@
     outs += [low, few] if last else []
     extra = [] if into is None else [into]
     n_in = 3 + len(ins) + len(weights)
+    scratch = [pltpu.VMEM((2, width, 3 * width), bf16), pltpu.SemaphoreType.DMA((n, 16))]
+    if grads:
+        scratch += [
+            pltpu.VMEM((2, 8, width // 8, 3 * width), bf16),
+            pltpu.SemaphoreType.DMA((n,)),
+        ]
     return staged(
-        functools.partial(ff_bwd_kernel, groups, first, last, slot),
+        functools.partial(ff_bwd_kernel, groups, first, last, slot, grads),
         "ff_bwd",
         [d],
-        [hb, hb_t, *ins],
+        [hb, *([hb_t] if grads else []), *ins],
         weights + extra,
         outs,
-        [shape((8, 4, width // 8, 3 * width), bf16)],
-        [
-            pltpu.VMEM((2, width, 3 * width), bf16),
-            pltpu.VMEM((2, 8, width // 8, 3 * width), bf16),
-            pltpu.SemaphoreType.DMA((n, 16)),
-            pltpu.SemaphoreType.DMA((n,)),
-        ],
+        [shape((8, 4, width // 8, 3 * width), bf16)] if grads else [],
+        scratch,
         60,
         cost(0, 0),
         {n_in: len(outs)} if extra else {},
     )
 
 
+def ff_grads_kernel(n, copies, smem, ins, raw, outs, raw_outs, scratch):
+    up_ref, down_ref, *rows_refs = ins
+    (total_ref,) = scratch
+    (at_ref,) = smem
+    sent_ref, kept_ref = outs
+    width = up_ref.shape[0]
+    part = width // 8
+    copies.wait(0, 1)
+    for s in range(n):
+        copies.wait(2 + 2 * s, 3 + 2 * s)
+        hb, dyb = rows_refs[2 * s][...], rows_refs[2 * s + 1][...]
+        gate, value = mm(hb, up_ref[:, pl.ds(0, width)]), mm(hb, up_ref[:, pl.ds(width, width)])
+        d_act = mm(dyb, down_ref[...], NT)
+        gelu, slope = gelu_parts(gate)
+        d_gate = (d_act * value * slope).astype(bf16)
+        d_value = (d_act * gelu).astype(bf16)
+        act = (gelu * value).astype(bf16)
+        hb_t, dyb_t = hb.T, dyb.T
+        for c, (lhs, rhs) in enumerate(((hb_t, d_gate), (hb_t, d_value), (dyb_t, act))):
+            at = pl.ds(c * width, width)
+            total = mm(lhs, rhs)
+            total_ref[:, at] = total if s == 0 else total + total_ref[:, at]
+    order = fold_order(0)
+    for to_ref, flip in ((sent_ref, 1), (kept_ref, 0)):
+        for i, j in enumerate(order):
+            row = pl.multiple_of(jnp.bitwise_xor(at_ref[0], j ^ flip) * part, part)
+            to_ref[i] = total_ref[pl.ds(row, part), :].astype(bf16)
+        copies.put(flip ^ 1)
+
+
+def ff_grads(d, up, down, all_hb, all_dyb):
+    width = up.shape[0]
+    return staged(
+        functools.partial(ff_grads_kernel, all_hb.shape[0]),
+        "ff_grads",
+        [d],
+        [up, down, *[(one, s) for s in range(all_hb.shape[0]) for one in (all_hb, all_dyb)]],
+        [],
+        [shape((4, width // 8, 3 * width), bf16)] * 2,
+        [],
+        [pltpu.VMEM((width, 3 * width), f32)],
+        60,
+        cost(0, 0),
+    )
+
+
 def add_low(a, b):
     return (a.astype(f32) + b.astype(f32)).astype(bf16)
+
+
+class Fold:
+    def __init__(self, net, line, sent, kept):
+        self.net, self.line = net, line
+        self.kept, self.got = kept, net.flip(line.after(sent), 1)
+
+    def step(self, bit):
+        got = self.line.after(self.got)
+        half = self.kept.shape[0] // 2
+        self.got = self.net.flip(add_low(self.kept[half:], got[half:]), bit, wait=False)
+        self.kept = add_low(self.kept[:half], got[:half])
+
+    def first(self):
+        self.step(COLOURS[0][0])
+
+    def second(self):
+        self.step(COLOURS[0][1])
+
+    def done(self):
+        return self.kept[0].astype(f32) + self.line.after(self.got)[0].astype(f32)
 
 
 class Share:
@@ -725,7 +790,7 @@
         self.slices = [total] + [self.net.shift(total, k) for k in range(1, self.net.n_t)]
 
     def gather(self):
-        self.gathered = Gather2(self.net, self.line, self.slices)
+        self.gathered = Gather(self.net, self.line, self.slices)
 
 
 def spread_kernel(layer, copies, smem, ins, raw, outs, raw_outs, scratch):
@@ -733,39 +798,59 @@
     held = ins
     (small_ref,) = outs
     qkv_out, wo_out = raw_outs
-    qkv_buf, wo_buf, sems = scratch
+    buf, sems = scratch
     d, z = at_ref[0], at_ref[1]
     rows, cols = held[0].shape[2:]
     rows = rows - FEW
-    copies.wait()
-    for k in range(4):
-        block = lax.rem(z - k + 4, 4)
+
+    def each(act):
         for c in range(2):
-            for i, j in enumerate(order_of(k // 2)):
-                ref = held[2 * (k // 2) + c].at[i, k % 2]
-                value = ref[pl.ds(0, rows)].astype(f32)
-                slot = jnp.bitwise_xor(d, j ^ c)
-                row = pl.multiple_of(slot * rows, rows)
-
-                @pl.when(block < 3)
-                def _(value=value, row=row, block=block):
-                    col = pl.multiple_of(block * cols, cols)
-                    qkv_buf[pl.ds(row, rows), pl.ds(col, cols)] = value
-
-                @pl.when(block == 3)
-                def _(value=value, row=row):
-                    wo_buf[pl.ds(row, rows), :] = value
-
-                @pl.when(slot == 0)
-                def _(ref=ref, block=block):
-                    small_ref[block] = ref[pl.ds(rows, FEW)].astype(f32)
-
-    one = pltpu.make_async_copy(qkv_buf, qkv_out.at[layer], sems.at[0])
-    two = pltpu.make_async_copy(wo_buf, wo_out.at[layer], sems.at[1])
-    one.start()
-    two.start()
-    one.wait()
-    two.wait()
+            for k in range(4):
+                block = lax.rem(z - k + 4, 4)
+                for i, j in enumerate(order_of(k // 2)):
+                    act(c, k, i, j, block, 16 * c + 4 * k + i)
+
+    def copy_of(n, slot, block, to_qkv):
+        row = pl.ds(pl.multiple_of(slot * rows, rows), rows)
+        if to_qkv:
+            col = pl.ds(pl.multiple_of(block * cols, cols), cols)
+            to = qkv_out.at[layer, row, col]
+        else:
+            to = wo_out.at[layer, row, :]
+        return pltpu.make_async_copy(buf.at[n], to, sems.at[n])
+
+    def begin(c, k, i, j, block, n):
+        if k == 0 and i == 0:
+            copies.wait(c)
+        ref = held[c].at[4 * (k // 2) + i, k % 2]
+        slot = jnp.bitwise_xor(d, j ^ c)
+        buf[n] = ref[pl.ds(0, rows)].astype(f32)
+
+        @pl.when(block < 3)
+        def _():
+            copy_of(n, slot, block, True).start()
+
+        @pl.when(block == 3)
+        def _():
+            copy_of(n, slot, block, False).start()
+
+        @pl.when(slot == 0)
+        def _():
+            small_ref[block] = ref[pl.ds(rows, FEW)].astype(f32)
+
+    def end(c, k, i, j, block, n):
+        slot = jnp.bitwise_xor(d, j ^ c)
+
+        @pl.when(block < 3)
+        def _():
+            copy_of(n, slot, block, True).wait()
+
+        @pl.when(block == 3)
+        def _():
+            copy_of(n, slot, block, False).wait()
+
+    each(begin)
+    each(end)
 
 
 def spread_out(layer, where, pieces, before):
@@ -779,14 +864,10 @@
         [] if before is None else list(before),
         [shape((4, FEW, cols), f32)],
         [shape((LAYERS, width, 3 * cols), f32), shape((LAYERS, width, cols), f32)],
-        [
-            pltpu.VMEM((width, 3 * cols), f32),
-            pltpu.VMEM((width, cols), f32),
-            pltpu.SemaphoreType.DMA((2,)),
-        ],
+        [pltpu.VMEM((32, rows - FEW, cols), f32), pltpu.SemaphoreType.DMA((32,))],
         24,
         cost(0, 0),
-        {} if before is None else {5: 1, 6: 2},
+        {} if before is None else {3: 1, 4: 2},
     )
 
 
@@ -838,20 +919,19 @@
     def run_ff(groups, hb, acc, weights, norm=None):
         return line.run(lambda hb: ff_fwd(groups, d_at, hb, acc, weights, norm), hb)
 
-    OWN, PAIR, TWO, ALL = "own", "pair", "two", "all"
+    OWN, HALF, TWO, ALL = "own", "half", "two", "all"
     own = own_slice(0)
     far = {k: net.shift(own, k) for k in (1, 3)}
     x_t = x_in.T
     qkv, lse, ctx, ctx_t, pre1, hb, hb_t = run_attn(0, x_in)
-    planes = lax.all_gather(line.after(own_slice(1)), "tensor")
-    near = Gather2(net, line, [far[1], far[3]])
+    near = Gather(net, line, [far[1], far[3]])
     far[2] = net.shift(line.after(own), 2)
     mine = own_weights(0)
     acc = run_ff(((OWN, 0),), hb, (pre1, gains1[0], biases1[0]), mine)[0]
+    planes = lax.all_gather(line.after(own_slice(1)), "tensor")
     near.second()
-    back = Gather(net, line, [far[2]])
+    back = Gather(net, line, [far[2][: part // 2], far[2][part // 2 :]])
     line.sync()
-    near.core()
     line.need(planes)
     planes = line.after(planes)
     others = jnp.stack(
@@ -861,10 +941,13 @@
         ]
     )
     others = lax.all_gather(others, "dp")
+    near.core()
+    back.second()
+    line.sync()
     back.core()
     line.sync()
     pre2, out, out_t = run_ff(
-        ((TWO, (0, 0)), (TWO, (1, 0)), (PAIR, 0)),
+        ((TWO, 0), (TWO, 1), (HALF, 0)),
         hb,
         acc,
         near.pieces() + back.pieces(),
@@ -874,13 +957,15 @@
     outputs.append(out)
     weights = [
         [
-            (((OWN, 0), (PAIR, 0)), mine + back.pieces()),
-            (((TWO, (0, 0)), (TWO, (1, 0))), near.pieces()),
+            (((OWN, 0),), mine),
+            (((HALF, 0), (TWO, 0), (TWO, 1)), back.pieces() + near.pieces()),
         ]
     ]
     qkv, lse, ctx, ctx_t, pre1, hb, hb_t = run_attn(1, out)
     mine = own_weights(1)
     acc = run_ff(((OWN, 0),), hb, (pre1, gains1[1], biases1[1]), mine)[0]
+    line.need(others)
+    all_hb = lax.all_gather(line.after(hb), "tensor")
     pre2, out, _ = run_ff(
         ((ALL, 0), (ALL, 1), (ALL, 2)), hb, acc, [others], (gains2[1], biases2[1])
     )
@@ -893,7 +978,7 @@
     def run_ff_bwd(l, at, ins, **how):
         groups, arrays = weights[l][at]
         hb, hb_t = kept[l][5:7]
-        return line.run(lambda hb: ff_bwd(groups, 2 * at, d_at, hb, hb_t, ins, arrays, **how), hb)
+        return line.run(lambda hb: ff_bwd(groups, at, d_at, hb, hb_t, ins, arrays, **how), hb)
 
     def run_attn_bwd(l, dab, d_pre, small):
         x_t, qkv, lse, ctx_t = kept[l][:4]
@@ -923,11 +1008,12 @@
         return net.shift(line.after(ff[l][i]), -order[i])
 
     pre1, pre2 = kept[1][4], kept[1][7]
-    d_pre1, _, _, small2, dab, small1, g = run_ff_bwd(
-        1, 0, (cotangent, pre2, gains2[1], pre1, gains1[1]), first=True, last=True
-    )
-    ff = {1: over_dp(g)}
+    d_pre1, dyb, _, small2, dab, small1 = run_ff_bwd(
+        1, 0, (cotangent, pre2, gains2[1], pre1, gains1[1]), first=True, last=True, grads=False
+    )
     sent, keep, grad = run_attn_bwd(1, dab, d_pre1, (small1, small2))
+    line.need(all_hb)
+    all_dyb = lax.all_gather(line.after(dyb), "tensor")
     pre1, pre2 = kept[0][4], kept[0][7]
     share = Share(net, line, z, sent, keep)
     d_h, dyb, dyb_t, small2, g = run_ff_bwd(0, 0, (grad, pre2, gains2[0]), first=True)
@@ -935,39 +1021,48 @@
     d_pre1, dab, small1, g = run_ff_bwd(
         0, 1, (dyb, dyb_t, d_h, pre1, gains1[0]), into=g, last=True
     )
-    ff[0] = over_dp(g)
     share.second()
     sent, keep, grad = run_attn_bwd(0, dab, d_pre1, (small1, small2))
+    line.need(all_dyb)
+    ff = {0: over_dp(g)}
     last_share = Share(net, line, z, sent, keep)
+    share.far()
     line.sync()
     last_share.first()
-    share.far()
-    line.sync()
+    share.far_back()
+    own_up, own_down = weights[1][0][1][:2]
+    sent, keep = line.run(lambda up: ff_grads(d_at, up, own_down, all_hb, all_dyb), own_up)
     last_share.second()
-    share.far_back()
+    share.gather()
+    fold = Fold(net, line, sent, keep)
     line.sync()
     last_share.far()
-    share.gather()
+    share.gathered.second()
     line.sync()
     last_share.far_back()
-    share.gathered.second()
+    share.gathered.core()
+    fold.first()
     line.sync()
-    line.need(ff[1])
     last_share.gather()
-    share.gathered.core()
-    ff_parts = {1: [ff[1][0], to_owner(1, 1)]}
-    line.sync()
-    last_share.gathered.second()
-    ff_parts[1] += [to_owner(1, 2), to_owner(1, 3)]
     found = line.run(
         lambda first: spread_out(1, dz_at, [first] + share.gathered.pieces()[1:], None),
         share.gathered.pieces()[0],
     )
+    small = {1: found[0]}
+    line.need(ff[0], fold.got)
+    last_share.gathered.second()
+    ff_parts = {0: [ff[0][0], to_owner(0, 1), to_owner(0, 2)]}
+    fold.second()
+    line.sync()
     last_share.gathered.core()
-    line.need(ff[0])
-    ff_parts[0] = [ff[0][0]] + [to_owner(0, i) for i in (1, 2, 3)]
-    small = {1: found[0]}
-    found = spread_out(0, dz_at, last_share.gathered.pieces(), found[1:])
+    line.sync()
+    ff_parts[0].append(to_owner(0, 3))
+    rest = found[1:]
+    found = line.run(
+        lambda first: spread_out(0, dz_at, [first] + last_share.gathered.pieces()[1:], rest),
+        last_share.gathered.pieces()[0],
+    )
+    ff_parts[1] = [fold.done()]
     small[0] = found[0]
     attention_grads = found[1:]
     small = jnp.stack([small[l][:, 0] for l in range(LAYERS)])

time: 555 us -> 537 us (0.968)
  the two profiles are of different devices: /device:TPU:17 before, /device:TPU:0 now
where the time goes in v3:
time: 537 us; the launch traced here: 528 us
  Pallas kernels  208 us (39%)
  waiting for transfers between devices  176 us (33%)
  starting transfers between devices  61.3 us (11%)
  local copies, waits for them, and re-layouts  39.2 us (7%)
  other arithmetic  27 us (5%)
  between operations  15.8 us (3%)
    pallas_call x14, Pallas kernels, staged(): pl.pallas_call(functools.partial(staged_kernel, body, layers, len(smem),...  208 us
    ppermute x33, waiting for transfers between devices, flip(): got = lax.ppermute(value, 'dp', [(i, i ^ bit) for i in range(self.n_dp)])  85.7 us
    ppermute x18, waiting for transfers between devices, shift(): got = lax.ppermute(value, 'tensor', [(i, (i + step) % n) for i in range(n)])  68.8 us
    ppermute x33, starting transfers between devices, flip(): got = lax.ppermute(value, 'dp', [(i, i ^ bit) for i in range(self.n_dp)])  31.8 us
    ppermute x18, starting transfers between devices, shift(): got = lax.ppermute(value, 'tensor', [(i, (i + step) % n) for i in range(n)])  28.6 us
    unnamed x121, local copies, waits for them, and re-layouts  18.4 us
  transfers between devices with their start and end apart: 56, of which 24 were waited for; matrix products, arithmetic and copies ran while one was open for 9% of the time, Pallas kernels for 39%

profile of v3, /device:TPU:0, one launch (start us, length us, event | category | flops | bytes accessed | tf_op | source)
XLA Modules:
  0.0 527.9 jit_solution(17303863535562591)
XLA Ops:
  9.8 3.1 collective-permute-start
  12.9 2.1 collective-permute-start.1
  19.4 14.4 %attn_fwd.2 = (bf16[512,2304]{1,0:T(8,128)(2,1)}, f32[512,128]{1,0:T(8,128)}, bf16[512,768]{1,0:T(8,128)(2,1)}, bf16[768,512]{1,0:T(8,128)(2,1)}, f32[512,768]{1...) custom-call(f32[12]{0:T(128)} %multiply_exponential_fusion.refs_0_, bf16[512,768]{1,0:T(8,128)(2,1)} %refs_1_.1, ...), custom_call_target="tpu_custom_call" | custom-call | flops 1024 | bytes 1024 | tf_op jit(solution)/shard_map/attn_fwd/pallas_call | solution.py:248
  33.9 7.1 %fusion.48 = (bf16[1,768,2,768]{3,2,1,0:T(2,128)(2,1)}, bf16[1,768,2,768]{3,2,1,0:T(2,128)(2,1)S(1)}) fusion(bf16[2,768,2,768]{3,2,1,0:T(2,128)(2,1)} %param.19), kind=kLoop, calls=%fused_computation.170 | loop fusion | bytes 9437184 | tf_op jit(solution)/shard_map/slice | solution.py:904
  43.5 1.5 collective-permute-start.3
  45.0 1.6 slice_bitcast_fusion
  46.6 1.8 copy.59
  49.2 6.2 %ff_fwd.4.refs_2_ = f32[512,768]{1,0:T(8,128)} custom-call(s32[1]{0:T(128)} %bitcast.refs_0_.refs_1_, bf16[512,768]{1,0:T(8,128)(2,1)} %get-tuple-element.170.refs_1_, f32[512,768]{1,0:T(8,128)} %get-tuple-element.128.refs_2_.refs_6_, f32[1,768]{1,0:T(1,128)} %get-tuple-element.284.refs_5_.refs_3_.refs_7_, f32[1,768]{1,0:T(1,128)} %get-tuple-element.281.refs_6_.refs_4_, ...), custom_call_target="tpu_custom_call" | custom-call | flops 1024 | bytes 1024 | tf_op jit(solution)/shard_map/ff_fwd/pallas_call | solution.py:248
  55.4 6.7 %collective-permute-done.4 = bf16[96,2304]{1,0:T(8,128)(2,1)S(1)} collective-permute-done((bf16[96,2304]{1,0:T(8,128)(2,1)S(1)}, bf16[96,2304]{1,0:T(8,128)(2,1)S(1)}, u32[]{:S(2)}, u32[]{:S(2)}) %collective-permute-start.4) | collective-permute-done | bytes 442400 | tf_op jit(solution)/shard_map/ppermute | solution.py:91
  70.1 22.5 %collective-permute-done.8 = bf16[1,1,48,2304]{3,2,1,0:T(8,128)(2,1)S(1)} collective-permute-done((bf16[1,1,48,2304]{3,2,1,0:T(8,128)(2,1)S(1)}, bf16[1,1,48,2304]{3,2,1,0:T(8,128)(2,1)S(1)}, u32[]{:S(2)}, u32[]{:S(2)}) %collective-permute-start.8) | collective-permute-done | bytes 221216 | tf_op jit(solution)/shard_map/ppermute | solution.py:84
  92.6 10.1 %all-gather.9.cloned.1.call-done = bf16[384,2304]{1,0:T(8,128)(2,1)} async-done(((bf16[96,2304]{1,0:T(8,128)(2,1)}), bf16[384,2304]{1,0:T(8,128)(2,1)}) %all-gather.9.cloned.1.call-update) | async-done | bytes 1769488 | tf_op jit(solution)/shard_map/all_gather | solution.py:931
  107.4 1.5 collective-permute-start.11
  109.0 1.5 collective-permute-start.10
  110.6 14.7 %collective-permute-done.11 = bf16[2,1,48,2304]{3,2,1,0:T(8,128)(2,1)S(1)} collective-permute-done((bf16[2,1,48,2304]{3,2,1,0:T(8,128)(2,1)S(1)}, bf16[2,1,48,2304]{3,2,1,0:T(8,128)(2,1)S(1)}, u32[]{:S(2)}, u32[]{:S(2)}) %collective-permute-start.11) | collective-permute-done | bytes 442400 | tf_op jit(solution)/shard_map/ppermute | solution.py:84
  125.2 2.4 collective-permute-done.10
  127.8 1.6 copy-done.1
  129.4 1.8 copy.61
  133.1 13.7 %ff_fwd.5 = (f32[512,768]{1,0:T(8,128)}, bf16[512,768]{1,0:T(8,128)(2,1)}, bf16[768,512]{1,0:T(8,128)(2,1)}) custom-call(s32[1]{0:T(128)} %bitcast.refs_0_.refs_1_, bf16[512,768]{1,0:T(8,128)(2,1)} %get-tuple-element.170.refs_1_, f32[512,768]{1,0:T(8,128)} %ff_fwd.4.refs_2_, f32[1,768]{1,0:T(1,128)} %get-tuple-element.286.refs_3_.refs_5_, ...), custom_call_target="tpu_custom_call" | custom-call | flops 1024 | bytes 1024 | tf_op jit(solution)/shard_map/ff_fwd/pallas_call | solution.py:248
  146.9 14.4 %attn_fwd.3 = (bf16[512,2304]{1,0:T(8,128)(2,1)}, f32[512,128]{1,0:T(8,128)}, bf16[512,768]{1,0:T(8,128)(2,1)}, bf16[768,512]{1,0:T(8,128)(2,1)}, f32[512,768]{1...) custom-call(f32[12]{0:T(128)} %multiply_exponential_fusion.refs_0_, ...), custom_call_target="tpu_custom_call" | custom-call | flops 1024 | bytes 1024 | tf_op jit(solution)/shard_map/attn_fwd/pallas_call | solution.py:248
  161.2 6.2 %ff_fwd.6.refs_2_ = f32[512,768]{1,0:T(8,128)} custom-call(s32[1]{0:T(128)} %bitcast.refs_0_.refs_1_, bf16[512,768]{1,0:T(8,128)(2,1)} %get-tuple-element.155.refs_1_, f32[512,768]{1,0:T(8,128)} %get-tuple-element.150.refs_2_.refs_5_, f32[1,768]{1,0:T(1,128)} %get-tuple-element.285.refs_5_.refs_3_.refs_6_, f32[1,768]{1,0:T(1,128)} %get-tuple-element.280.refs_6_.refs_4_, ...), custom_call_target="tpu_custom_call" | custom-call | flops 1024 | bytes 1024 | tf_op jit(solution)/shard_map/ff_fwd/pallas_call | solution.py:248
  167.4 4.3 all-gather.11.cloned.1.call-done
  172.0 13.4 %ff_fwd.7 = (f32[512,768]{1,0:T(8,128)}, bf16[512,768]{1,0:T(8,128)(2,1)}, bf16[768,512]{1,0:T(8,128)(2,1)}) custom-call(s32[1]{0:T(128)} %bitcast.refs_0_.refs_1_, bf16[512,768]{1,0:T(8,128)(2,1)} %get-tuple-element.155.refs_1_, f32[512,768]{1,0:T(8,128)} %ff_fwd.6.refs_2_, f32[1,768]{1,0:T(1,128)} %get-tuple-element.287.refs_3_.refs_4_, ...), custom_call_target="tpu_custom_call" | custom-call | flops 1024 | bytes 1024 | tf_op jit(solution)/shard_map/ff_fwd/pallas_call | solution.py:248
  185.4 23.3 %ff_bwd.3 = (f32[512,768]{1,0:T(8,128)}, bf16[512,768]{1,0:T(8,128)(2,1)}, bf16[768,512]{1,0:T(8,128)(2,1)}, f32[2,768]{1,0:T(2,128)}, bf16[512,768]{1,0:T(8,128)(2,1)}, /*index=5*/f32[2,768]{1,0:T(2,128)}) custom-call(s32[1]{0:T(128)} %bitcast.refs_0_.refs_1_, bf16[512,768]{1,0:T(8,128)(2,1)} %get-tuple-element.155.refs_1_, bf16[512,768]{1,0:T(8,128)(2,1)} %refs_2_.5, ...), custom_call_target="tpu_custom_call" | custom-call | flops 1024 | bytes 1024 | tf_op jit(solution)/shard_map/ff_bwd/pallas_call | solution.py:248
  208.7 21.0 %attn_bwd.2 = (bf16[4,4,104,768]{3,2,1,0:T(8,128)(2,1)}, bf16[4,4,104,768]{3,2,1,0:T(8,128)(2,1)}, f32[512,768]{1,0:T(8,128)}) custom-call(f32[12]{0:T(128)} %multiply_exponential_fusion.refs_0_, s32[1]{0:T(128)} %bitcast.refs_0_.refs_1_, bf16[512,768]{1,0:T(8,128)(2,1)} %get-tuple-element.158.refs_2_, bf16[2,768,768]{2,1,0:T(8,128)(2,1)} %refs_3_.3, ...), custom_call_target="tpu_custom_call" | custom-call | flops 1024 | bytes 1024 | tf_op jit(solution)/shard_map/attn_bwd/pallas_call | solution.py:248
  229.8 7.1 %all-gather.13.cloned.1.call-done = bf16[2048,768]{1,0:T(8,128)(2,1)} async-done(((bf16[512,768]{1,0:T(8,128)(2,1)}), bf16[2048,768]{1,0:T(8,128)(2,1)}) %all-gather.13.cloned.1.call-update) | async-done | bytes 3145744 | tf_op jit(solution)/shard_map/all_gather | solution.py:968
  237.1 1.9 copy.47
  239.1 13.3 %ff_bwd.4 = (f32[512,768]{1,0:T(8,128)}, bf16[512,768]{1,0:T(8,128)(2,1)}, bf16[768,512]{1,0:T(8,128)(2,1)}, f32[2,768]{1,0:T(2,128)}, bf16[8,4,96,2304]{3,2,1,0:T(8,128)(2,1)}) custom-call(s32[1]{0:T(128)} %bitcast.refs_0_.refs_1_, bf16[512,768]{1,0:T(8,128)(2,1)} %get-tuple-element.170.refs_1_, bf16[768,512]{1,0:T(8,128)(2,1)} %get-tuple-element.166.refs_2_, ...), custom_call_target="tpu_custom_call" | custom-call | flops 1024 | bytes 1024 | tf_op jit(solution)/shard_map/ff_bwd/pallas_call | solution.py:248
  252.4 4.1 add_convert_fusion.6
  259.4 25.8 %ff_bwd.5 = (f32[512,768]{1,0:T(8,128)}, bf16[512,768]{1,0:T(8,128)(2,1)}, f32[2,768]{1,0:T(2,128)}, bf16[8,4,96,2304]{3,2,1,0:T(8,128)(2,1)}) custom-call(s32[1]{0:T(128)} %bitcast.refs_0_.refs_1_, bf16[512,768]{1,0:T(8,128)(2,1)} %get-tuple-element.170.refs_1_, bf16[768,512]{1,0:T(8,128)(2,1)} %get-tuple-element.166.refs_2_, ...), custom_call_target="tpu_custom_call", output_to_operand_aliasing={{3}: (12, {})} | custom-call | flops 1024 | bytes 1024 | tf_op jit(solution)/shard_map/ff_bwd/pallas_call | solution.py:248
  289.2 21.1 %attn_bwd.3 = (bf16[4,4,104,768]{3,2,1,0:T(8,128)(2,1)}, bf16[4,4,104,768]{3,2,1,0:T(8,128)(2,1)}, f32[512,768]{1,0:T(8,128)}) custom-call(f32[12]{0:T(128)} %multiply_exponential_fusion.refs_0_, s32[1]{0:T(128)} %bitcast.refs_0_.refs_1_, bf16[512,768]{1,0:T(8,128)(2,1)} %get-tuple-element.178.refs_2_, bf16[2,768,768]{2,1,0:T(8,128)(2,1)} %refs_3_.3, ...), custom_call_target="tpu_custom_call" | custom-call | flops 1024 | bytes 1024 | tf_op jit(solution)/shard_map/attn_bwd/pallas_call | solution.py:248
  311.2 1.7 copy-done.10
  316.1 1.9 collective-permute-start.21
  318.0 3.3 collective-permute-done.19
  321.3 8.6 %collective-permute-done.20 = bf16[104,768]{1,0:T(8,128)(2,1)S(1)} collective-permute-done((bf16[104,768]{1,0:T(8,128)(2,1)S(1)}, bf16[104,768]{1,0:T(8,128)(2,1)S(1)}, u32[]{:S(2)}, u32[]{:S(2)}) %collective-permute-start.20) | collective-permute-done | bytes 159776 | tf_op jit(solution)/shard_map/ppermute | solution.py:91
  330.0 1.7 add_convert_fusion.2
  336.3 2.0 collective-permute-start.25
  338.2 3.0 collective-permute-start.26
  341.2 21.7 %ff_grads.1 = (bf16[4,96,2304]{2,1,0:T(8,128)(2,1)}, bf16[4,96,2304]{2,1,0:T(8,128)(2,1)}) custom-call(s32[1]{0:T(128)} %bitcast.refs_0_.refs_1_, bf16[768,1536]{1,0:T(8,128)(2,1)} %bitcast.159, bf16[768,768]{1,0:T(8,128)(2,1)} %get-tuple-element.254.refs_6_.refs_8_.refs_2_, bf16[4,512,768]{2,1,0:T(8,128)(2,1)} %bitcast.147, bf16[4,512,768]{2,1,0:T(8,128)(2,1)} %bitcast.151, ...), custom_call_target="tpu_custom_call" | custom-call | flops 1024 | bytes 1024 | tf_op jit(solution)/shard_map/ff_grads/pallas_call | solution.py:248
  365.2 1.7 collective-permute-start.28
  367.6 12.8 %collective-permute-done.30 = bf16[1,2,104,768]{3,2,1,0:T(8,128)(2,1)S(1)} collective-permute-done((bf16[1,2,104,768]{3,2,1,0:T(8,128)(2,1)S(1)}, bf16[1,2,104,768]{3,2,1,0:T(8,128)(2,1)S(1)}, u32[]{:S(2)}, u32[]{:S(2)}) %collective-permute-start.30) | collective-permute-done | bytes 319520 | tf_op jit(solution)/shard_map/ppermute | solution.py:84
  381.8 13.4 %collective-permute-done.28 = bf16[2,104,768]{2,1,0:T(8,128)(2,1)S(1)} collective-permute-done((bf16[2,104,768]{2,1,0:T(8,128)(2,1)S(1)}, bf16[2,104,768]{2,1,0:T(8,128)(2,1)S(1)}, u32[]{:S(2)}, u32[]{:S(2)}) %collective-permute-start.28) | collective-permute-done | bytes 319520 | tf_op jit(solution)/shard_map/ppermute | solution.py:84
  395.9 1.6 collective-permute-start.35
  398.2 1.9 collective-permute-start.34
  400.3 4.0 collective-permute-done.32
  404.3 7.6 %collective-permute-done.33 = bf16[104,768]{1,0:T(8,128)(2,1)S(1)} collective-permute-done((bf16[104,768]{1,0:T(8,128)(2,1)S(1)}, bf16[104,768]{1,0:T(8,128)(2,1)S(1)}, u32[]{:S(2)}, u32[]{:S(2)}) %collective-permute-start.33) | collective-permute-done | bytes 159776 | tf_op jit(solution)/shard_map/ppermute | solution.py:91
  413.9 1.7 add_convert_fusion
  416.0 1.7 collective-permute-start.37
  417.7 2.7 collective-permute-start.38
  420.4 2.8 collective-permute-start.39
  424.0 6.7 %collective-permute-done.38 = bf16[104,768]{1,0:T(8,128)(2,1)S(1)} collective-permute-done((bf16[104,768]{1,0:T(8,128)(2,1)S(1)}, bf16[104,768]{1,0:T(8,128)(2,1)S(1)}, u32[]{:S(2)}, u32[]{:S(2)}) %collective-permute-start.38) | collective-permute-done | bytes 159776 | tf_op jit(solution)/shard_map/ppermute | solution.py:91
  432.3 2.5 collective-permute-start.42
  434.8 1.8 collective-permute-start.41
  437.3 6.9 %spread_out.2 = (f32[4,8,768]{2,1,0:T(8,128)}, f32[2,768,2304]{2,1,0:T(8,128)}, f32[2,768,768]{2,1,0:T(8,128)}) custom-call(s32[2]{0:T(128)} %pad_add_fusion.refs_0_, bf16[8,2,104,768]{3,2,1,0:T(8,128)(2,1)} %copy-done.5, bf16[8,2,104,768]{3,2,1,0:T(8,128)(2,1)} %copy-done.11), custom_call_target="tpu_custom_call" | custom-call | flops 1024 | bytes 1024 | tf_op jit(solution)/shard_map/spread_out/pallas_call | solution.py:248
  444.2 8.0 %collective-permute-done.43 = bf16[2,96,2304]{2,1,0:T(8,128)(2,1)S(1)} collective-permute-done((bf16[2,96,2304]{2,1,0:T(8,128)(2,1)}, bf16[2,96,2304]{2,1,0:T(8,128)(2,1)S(1)}, u32[]{:S(2)}, u32[]{:S(2)}) %collective-permute-start.43) | collective-permute-done | bytes 884768 | tf_op jit(solution)/shard_map/ppermute | solution.py:84
  452.2 6.6 %collective-permute-done.41 = bf16[1,2,104,768]{3,2,1,0:T(8,128)(2,1)S(1)} collective-permute-done((bf16[1,2,104,768]{3,2,1,0:T(8,128)(2,1)S(1)}, bf16[1,2,104,768]{3,2,1,0:T(8,128)(2,1)S(1)}, u32[]{:S(2)}, u32[]{:S(2)}) %collective-permute-start.41) | collective-permute-done | bytes 319520 | tf_op jit(solution)/shard_map/ppermute | solution.py:84
  459.4 1.8 collective-permute-start.44
  462.0 3.4 collective-permute-start.47
  466.6 9.5 %collective-permute-done.47 = bf16[96,2304]{1,0:T(8,128)(2,1)S(1)} collective-permute-done((bf16[96,2304]{1,0:T(8,128)(2,1)S(1)}, bf16[96,2304]{1,0:T(8,128)(2,1)S(1)}, u32[]{:S(2)}, u32[]{:S(2)}) %collective-permute-start.47) | collective-permute-done | bytes 442400 | tf_op jit(solution)/shard_map/ppermute | solution.py:91
  476.0 17.5 %collective-permute-done.46 = bf16[96,2304]{1,0:T(8,128)(2,1)S(1)} collective-permute-done((bf16[96,2304]{1,0:T(8,128)(2,1)S(1)}, bf16[96,2304]{1,0:T(8,128)(2,1)S(1)}, u32[]{:S(2)}, u32[]{:S(2)}) %collective-permute-start.46) | collective-permute-done | bytes 442400 | tf_op jit(solution)/shard_map/ppermute | solution.py:91
  496.6 2.0 collective-permute-done.48.refs_2_
  502.2 6.9 %spread_out.3 = (f32[4,8,768]{2,1,0:T(8,128)}, f32[2,768,2304]{2,1,0:T(8,128)}, f32[2,768,768]{2,1,0:T(8,128)}) custom-call(s32[2]{0:T(128)} %pad_add_fusion.refs_0_, bf16[8,2,104,768]{3,2,1,0:T(8,128)(2,1)} %copy-done.6, bf16[8,2,104,768]{3,2,1,0:T(8,128)(2,1)} %copy-done.15, ...), custom_call_target="tpu_custom_call", output_to_operand_aliasing={{1}: (3, {}), {2}: (4, {})} | custom-call | flops 1024 | bytes 1024 | tf_op jit(solution)/shard_map/spread_out/pallas_call | solution.py:248
  510.7 4.1 collective-permute-done.49
  514.8 1.6 fusion.1
  519.4 1.6 pad_maximum_fusion.2
  (259 shorter events, 64.9 us)
Async XLA Ops:
  7.2 95.5 %all-gather.9.cloned.1.call-start = ((), (), s32[]{:S(2)}) async-start(), calls=%async_computation.2 | async-start | bytes 2211840 | tf_op jit(solution)/shard_map/all_gather | solution.py:931
  9.8 31.2 %collective-permute-start = (bf16[96,2304]{1,0:T(8,128)(2,1)S(1)}, bf16[96,2304]{1,0:T(8,128)(2,1)S(1)}, u32[]{:S(2)}, u32[]{:S(2)}) collective-permute-start(bf16[96,2304]{1,0:T(8,128)(2,1)S(1)} %pad_maximum_fusion.10), channel_id=1, source_target_pairs={{0,1},{1,2},{2,3},{3,0},{4,5},{5,6},{6,7},{7,4},{8,9},{9,10},{10,1... | collective-permute-start | bytes 1327112 | tf_op jit(solution)/shard_map/ppermute | solution.py:91
  12.9 28.1 %collective-permute-start.1 = (bf16[96,2304]{1,0:T(8,128)(2,1)S(1)}, bf16[96,2304]{1,0:T(8,128)(2,1)S(1)}, u32[]{:S(2)}, u32[]{:S(2)}) collective-permute-start(bf16[96,2304]{1,0:T(8,128)(2,1)S(1)} %pad_maximum_fusion.10), channel_id=1, source_target_pairs={{0,3},{1,0},{2,1},{3,2},{4,7},{5,4},{6,5},{7,6},{8,11},{9,8},{10,9... | collective-permute-start | bytes 1327112 | tf_op jit(solution)/shard_map/ppermute | solution.py:91
  41.0 21.1 %collective-permute-start.4 = (bf16[96,2304]{1,0:T(8,128)(2,1)S(1)}, bf16[96,2304]{1,0:T(8,128)(2,1)S(1)}, u32[]{:S(2)}, u32[]{:S(2)}) collective-permute-start(bf16[96,2304]{1,0:T(8,128)(2,1)S(1)} %pad_maximum_fusion.10), channel_id=1, source_target_pairs={{0,2},{1,3},{2,0},{3,1},{4,6},{5,7},{6,4},{7,5},{8,10},{9,11},{10,... | collective-permute-start | bytes 1327112 | tf_op jit(solution)/shard_map/ppermute | solution.py:91
  42.0 20.2 %collective-permute-start.2 = (bf16[1,1,96,2304]{3,2,1,0:T(8,128)(2,1)S(1)}, bf16[1,1,96,2304]{3,2,1,0:T(8,128)(2,1)S(1)}, u32[]{:S(2)}, u32[]{:S(2)}) collective-permute-start(bf16[1,1,96,2304]{3,2,1,0:T(8,128)(2,1)S(1)} %bitcast.172), channel_id=1, source_target_pairs={{0,8},{4,12},{8,0},{12,4},{16,24},{20,28},{24,16},{28,20},{1,9},{5... | collective-permute-start | bytes 1327112 | tf_op jit(solution)/shard_map/ppermute | solution.py:84
  43.5 18.7 %collective-permute-start.3 = (bf16[1,1,96,2304]{3,2,1,0:T(8,128)(2,1)S(1)}, bf16[1,1,96,2304]{3,2,1,0:T(8,128)(2,1)S(1)}, u32[]{:S(2)}, u32[]{:S(2)}) collective-permute-start(bf16[1,1,96,2304]{3,2,1,0:T(8,128)(2,1)S(1)} %bitcast.170), channel_id=1, source_target_pairs={{0,16},{4,20},{8,24},{12,28},{16,0},{20,4},{24,8},{28,12},{1,17},{... | collective-permute-start | bytes 1327112 | tf_op jit(solution)/shard_map/ppermute | solution.py:84
  62.2 109.6 %all-gather.11.cloned.1.call-start = ((), (), s32[]{:S(2)}) async-start(), calls=%async_computation.3 | async-start | bytes 11943936 | tf_op jit(solution)/shard_map/all_gather | solution.py:943
  63.9 28.7 %collective-permute-start.6 = (bf16[2,1,96,2304]{3,2,1,0:T(8,128)(2,1)}, bf16[2,1,96,2304]{3,2,1,0:T(8,128)(2,1)S(1)}, u32[]{:S(2)}, u32[]{:S(2)}) collective-permute-start(bf16[2,1,96,2304]{3,2,1,0:T(8,128)(2,1)} %pad_maximum_fusion.4), channel_id=1, source_target_pairs={{0,8},{4,12},{8,0},{12,4},{16,24},{20,28},{24,16},{28,20},{1,9},{5... | collective-permute-start | bytes 2654216 | tf_op jit(solution)/shard_map/ppermute | solution.py:84
  66.3 26.2 %collective-permute-start.5 = (bf16[2,1,96,2304]{3,2,1,0:T(8,128)(2,1)}, bf16[2,1,96,2304]{3,2,1,0:T(8,128)(2,1)}, u32[]{:S(2)}, u32[]{:S(2)}) collective-permute-start(bf16[2,1,96,2304]{3,2,1,0:T(8,128)(2,1)} %pad_maximum_fusion.3), channel_id=1, source_target_pairs={{0,16},{4,20},{8,24},{12,28},{16,0},{20,4},{24,8},{28,12},{1,17},{... | collective-permute-start | bytes 2654216 | tf_op jit(solution)/shard_map/ppermute | solution.py:84
  69.0 23.6 %collective-permute-start.8 = (bf16[1,1,48,2304]{3,2,1,0:T(8,128)(2,1)S(1)}, bf16[1,1,48,2304]{3,2,1,0:T(8,128)(2,1)S(1)}, u32[]{:S(2)}, u32[]{:S(2)}) collective-permute-start(bf16[1,1,48,2304]{3,2,1,0:T(8,128)(2,1)S(1)} %bitcast.166), channel_id=1, source_target_pairs={{0,16},{4,20},{8,24},{12,28},{16,0},{20,4},{24,8},{28,12},{1,17},{... | collective-permute-start | bytes 663560 | tf_op jit(solution)/shard_map/ppermute | solution.py:84
  69.5 23.1 %collective-permute-start.7 = (bf16[1,1,48,2304]{3,2,1,0:T(8,128)(2,1)S(1)}, bf16[1,1,48,2304]{3,2,1,0:T(8,128)(2,1)S(1)}, u32[]{:S(2)}, u32[]{:S(2)}) collective-permute-start(bf16[1,1,48,2304]{3,2,1,0:T(8,128)(2,1)S(1)} %bitcast.168), channel_id=1, source_target_pairs={{0,8},{4,12},{8,0},{12,4},{16,24},{20,28},{24,16},{28,20},{1,9},{5... | collective-permute-start | bytes 663560 | tf_op jit(solution)/shard_map/ppermute | solution.py:84
  105.4 131.5 %all-gather.13.cloned.1.call-start = ((), (), s32[]{:S(2)}) async-start(), calls=%async_computation.4 | async-start | bytes 3932160 | tf_op jit(solution)/shard_map/all_gather | solution.py:968
  107.3 20.4 %collective-permute-start.9 = (bf16[8,1,96,2304]{3,2,1,0:T(8,128)(2,1)S(1)}, bf16[8,1,96,2304]{3,2,1,0:T(8,128)(2,1)S(1)}, u32[]{:S(2)}, u32[]{:S(2)}) collective-permute-start(bf16[8,1,96,2304]{3,2,1,0:T(8,128)(2,1)S(1)} %constant_dynamic-update-slice_fusion.refs_5_.refs_10_), channel_id=1, source_target_pairs={{0,4},{4,0},{8,12},{12,8},{16,20},{20,16},{24,28},{28,24},{1,5},{5... | collective-permute-start | bytes 10616840 | tf_op jit(solution)/shard_map/ppermute | solution.py:84
  107.4 17.8 %collective-permute-start.11 = (bf16[2,1,48,2304]{3,2,1,0:T(8,128)(2,1)S(1)}, bf16[2,1,48,2304]{3,2,1,0:T(8,128)(2,1)S(1)}, u32[]{:S(2)}, u32[]{:S(2)}) collective-permute-start(bf16[2,1,48,2304]{3,2,1,0:T(8,128)(2,1)S(1)} %pad_maximum_fusion.13), channel_id=1, source_target_pairs={{0,8},{4,12},{8,0},{12,4},{16,24},{20,28},{24,16},{28,20},{1,9},{5... | collective-permute-start | bytes 1327112 | tf_op jit(solution)/shard_map/ppermute | solution.py:84
  109.0 18.6 %collective-permute-start.10 = (bf16[2,1,48,2304]{3,2,1,0:T(8,128)(2,1)S(1)}, bf16[2,1,48,2304]{3,2,1,0:T(8,128)(2,1)S(1)}, u32[]{:S(2)}, u32[]{:S(2)}) collective-permute-start(bf16[2,1,48,2304]{3,2,1,0:T(8,128)(2,1)S(1)} %pad_maximum_fusion.12), channel_id=1, source_target_pairs={{0,16},{4,20},{8,24},{12,28},{16,0},{20,4},{24,8},{28,12},{1,17},{... | collective-permute-start | bytes 1327112 | tf_op jit(solution)/shard_map/ppermute | solution.py:84
  127.8 4.1 collective-permute-start.12
  171.8 138.6 %all-gather.15.cloned.1.call-start = ((), (), s32[]{:S(2)}) async-start(), calls=%async_computation.5 | async-start | bytes 3932160 | tf_op jit(solution)/shard_map/all_gather | solution.py:1016
  236.9 221.9 %reduce-scatter.2.cloned.1.call-start = ((), (), s32[]{:S(2)}) async-start(), calls=%async_computation.1 | async-start | bytes 15925248 | tf_op jit(solution)/shard_map/reduce_scatter | solution.py:1005
  239.0 13.4 %collective-permute-start.13 = (bf16[4,4,104,768]{3,2,0,1:T(8,128)(2,1)S(1)}, bf16[4,4,104,768]{3,2,0,1:T(8,128)(2,1)}, u32[]{:S(2)}, u32[]{:S(2)}) collective-permute-start(bf16[4,4,104,768]{3,2,0,1:T(8,128)(2,1)S(1)} %copy.47), channel_id=1, source_target_pairs={{0,4},{4,0},{8,12},{12,8},{16,20},{20,16},{24,28},{28,24},{1,5},{5... | collective-permute-start | bytes 7667720 | tf_op jit(solution)/shard_map/ppermute | solution.py:84
  256.5 28.8 %copy-start.13 = (bf16[2,2,104,768]{3,2,0,1:T(8,128)(2,1)}, bf16[2,2,104,768]{3,2,0,1:T(8,128)(2,1)S(1)}, u32[]{:S(2)}) copy-start(bf16[2,2,104,768]{3,2,0,1:T(8,128)(2,1)S(1)} %get-tuple-element.244) | copy-start | bytes 1916932
  256.5 28.7 %collective-permute-start.14 = (bf16[2,2,104,768]{3,2,0,1:T(8,128)(2,1)}, bf16[2,2,104,768]{3,2,0,1:T(8,128)(2,1)S(1)}, u32[]{:S(2)}, u32[]{:S(2)}) collective-permute-start(bf16[2,2,104,768]{3,2,0,1:T(8,128)(2,1)} %get-tuple-element.247), channel_id=1, source_target_pairs={{0,8},{4,12},{8,0},{12,4},{16,24},{20,28},{24,16},{28,20},{1,9},{5... | collective-permute-start | bytes 1916936 | tf_op jit(solution)/shard_map/ppermute | solution.py:84
  257.9 27.3 %collective-permute-start.15 = (bf16[2,2,104,768]{3,2,0,1:T(8,128)(2,1)}, bf16[2,2,104,768]{3,2,0,1:T(8,128)(2,1)S(1)}, u32[]{:S(2)}, u32[]{:S(2)}) collective-permute-start(bf16[2,2,104,768]{3,2,0,1:T(8,128)(2,1)} %get-tuple-element.246), channel_id=1, source_target_pairs={{0,16},{4,20},{8,24},{12,28},{16,0},{20,4},{24,8},{28,12},{1,17},{... | collective-permute-start | bytes 1916936 | tf_op jit(solution)/shard_map/ppermute | solution.py:84
  285.2 25.1 %copy-start.33 = (bf16[2,2,104,768]{3,2,0,1:T(8,128)(2,1)}, bf16[2,2,104,768]{3,2,0,1:T(8,128)(2,1)S(1)}, u32[]{:S(2)}) copy-start(bf16[2,2,104,768]{3,2,0,1:T(8,128)(2,1)S(1)} %collective-permute-done.14) | copy-start | bytes 1916932
  285.2 25.1 %copy-start.35 = (bf16[2,2,104,768]{3,2,0,1:T(8,128)(2,1)}, bf16[2,2,104,768]{3,2,0,1:T(8,128)(2,1)S(1)}, u32[]{:S(2)}) copy-start(bf16[2,2,104,768]{3,2,0,1:T(8,128)(2,1)S(1)} %collective-permute-done.15) | copy-start | bytes 1916932
  286.0 24.3 %collective-permute-start.17 = (bf16[2,104,768]{2,1,0:T(8,128)(2,1)}, bf16[2,104,768]{2,1,0:T(8,128)(2,1)S(1)}, u32[]{:S(2)}, u32[]{:S(2)}) collective-permute-start(bf16[2,104,768]{2,1,0:T(8,128)(2,1)} %fusion.7), channel_id=1, source_target_pairs={{0,8},{4,12},{8,0},{12,4},{16,24},{20,28},{24,16},{28,20},{1,9},{5... | collective-permute-start | bytes 958472 | tf_op jit(solution)/shard_map/ppermute | solution.py:84
  287.4 23.0 %collective-permute-start.16 = (bf16[2,104,768]{2,1,0:T(8,128)(2,1)}, bf16[2,104,768]{2,1,0:T(8,128)(2,1)S(1)}, u32[]{:S(2)}, u32[]{:S(2)}) collective-permute-start(bf16[2,104,768]{2,1,0:T(8,128)(2,1)} %fusion.6), channel_id=1, source_target_pairs={{0,16},{4,20},{8,24},{12,28},{16,0},{20,4},{24,8},{28,12},{1,17},{... | collective-permute-start | bytes 958472 | tf_op jit(solution)/shard_map/ppermute | solution.py:84
  313.1 16.8 %collective-permute-start.18 = (bf16[4,4,104,768]{3,2,0,1:T(8,128)(2,1)S(1)}, bf16[4,4,104,768]{3,2,0,1:T(8,128)(2,1)S(1)}, u32[]{:S(2)}, u32[]{:S(2)}) collective-permute-start(bf16[4,4,104,768]{3,2,0,1:T(8,128)(2,1)S(1)} %copy.54), channel_id=1, source_target_pairs={{0,4},{4,0},{8,12},{12,8},{16,20},{20,16},{24,28},{28,24},{1,5},{5... | collective-permute-start | bytes 7667720 | tf_op jit(solution)/shard_map/ppermute | solution.py:84
  314.9 6.4 %collective-permute-start.19 = (bf16[104,768]{1,0:T(8,128)(2,1)S(1)}, bf16[104,768]{1,0:T(8,128)(2,1)S(1)}, u32[]{:S(2)}, u32[]{:S(2)}) collective-permute-start(bf16[104,768]{1,0:T(8,128)(2,1)S(1)} %get-tuple-element.268), channel_id=1, source_target_pairs={{0,3},{1,0},{2,1},{3,2},{4,7},{5,4},{6,5},{7,6},{8,11},{9,8},{10,9... | collective-permute-start | bytes 479240 | tf_op jit(solution)/shard_map/ppermute | solution.py:91
  315.7 14.3 %collective-permute-start.20 = (bf16[104,768]{1,0:T(8,128)(2,1)S(1)}, bf16[104,768]{1,0:T(8,128)(2,1)S(1)}, u32[]{:S(2)}, u32[]{:S(2)}) collective-permute-start(bf16[104,768]{1,0:T(8,128)(2,1)S(1)} %get-tuple-element.269), channel_id=1, source_target_pairs={{0,2},{1,3},{2,0},{3,1},{4,6},{5,7},{6,4},{7,5},{8,10},{9,11},{10,... | collective-permute-start | bytes 479240 | tf_op jit(solution)/shard_map/ppermute | solution.py:91
  316.1 13.9 %collective-permute-start.21 = (bf16[104,768]{1,0:T(8,128)(2,1)S(1)}, bf16[104,768]{1,0:T(8,128)(2,1)S(1)}, u32[]{:S(2)}, u32[]{:S(2)}) collective-permute-start(bf16[104,768]{1,0:T(8,128)(2,1)S(1)} %get-tuple-element.267), channel_id=1, source_target_pairs={{0,1},{1,2},{2,3},{3,0},{4,5},{5,6},{6,7},{7,4},{8,9},{9,10},{10,1... | collective-permute-start | bytes 479240 | tf_op jit(solution)/shard_map/ppermute | solution.py:91
  331.6 31.3 %collective-permute-start.22 = (bf16[2,2,104,768]{3,2,0,1:T(8,128)(2,1)}, bf16[2,2,104,768]{3,2,0,1:T(8,128)(2,1)S(1)}, u32[]{:S(2)}, u32[]{:S(2)}) collective-permute-start(bf16[2,2,104,768]{3,2,0,1:T(8,128)(2,1)} %get-tuple-element.242), channel_id=1, source_target_pairs={{0,8},{4,12},{8,0},{12,4},{16,24},{20,28},{24,16},{28,20},{1,9},{5... | collective-permute-start | bytes 1916936 | tf_op jit(solution)/shard_map/ppermute | solution.py:84
  333.1 29.9 %collective-permute-start.23 = (bf16[2,2,104,768]{3,2,0,1:T(8,128)(2,1)}, bf16[2,2,104,768]{3,2,0,1:T(8,128)(2,1)S(1)}, u32[]{:S(2)}, u32[]{:S(2)}) collective-permute-start(bf16[2,2,104,768]{3,2,0,1:T(8,128)(2,1)} %get-tuple-element.241), channel_id=1, source_target_pairs={{0,16},{4,20},{8,24},{12,28},{16,0},{20,4},{24,8},{28,12},{1,17},{... | collective-permute-start | bytes 1916936 | tf_op jit(solution)/shard_map/ppermute | solution.py:84
  335.6 27.3 %collective-permute-start.24 = (bf16[104,768]{1,0:T(8,128)(2,1)S(1)}, bf16[104,768]{1,0:T(8,128)(2,1)S(1)}, u32[]{:S(2)}, u32[]{:S(2)}) collective-permute-start(bf16[104,768]{1,0:T(8,128)(2,1)S(1)} %fusion.19), channel_id=1, source_target_pairs={{0,1},{1,2},{2,3},{3,0},{4,5},{5,6},{6,7},{7,4},{8,9},{9,10},{10,1... | collective-permute-start | bytes 479240 | tf_op jit(solution)/shard_map/ppermute | solution.py:91
  336.3 26.7 %collective-permute-start.25 = (bf16[104,768]{1,0:T(8,128)(2,1)S(1)}, bf16[104,768]{1,0:T(8,128)(2,1)S(1)}, u32[]{:S(2)}, u32[]{:S(2)}) collective-permute-start(bf16[104,768]{1,0:T(8,128)(2,1)S(1)} %fusion.19), channel_id=1, source_target_pairs={{0,2},{1,3},{2,0},{3,1},{4,6},{5,7},{6,4},{7,5},{8,10},{9,11},{10,... | collective-permute-start | bytes 479240 | tf_op jit(solution)/shard_map/ppermute | solution.py:91
  338.2 24.7 %collective-permute-start.26 = (bf16[104,768]{1,0:T(8,128)(2,1)S(1)}, bf16[104,768]{1,0:T(8,128)(2,1)S(1)}, u32[]{:S(2)}, u32[]{:S(2)}) collective-permute-start(bf16[104,768]{1,0:T(8,128)(2,1)S(1)} %fusion.19), channel_id=1, source_target_pairs={{0,3},{1,0},{2,1},{3,2},{4,7},{5,4},{6,5},{7,6},{8,11},{9,8},{10,9... | collective-permute-start | bytes 479240 | tf_op jit(solution)/shard_map/ppermute | solution.py:91
  363.0 32.3 %collective-permute-start.31 = (bf16[4,96,2304]{2,1,0:T(8,128)(2,1)}, bf16[4,96,2304]{2,1,0:T(8,128)(2,1)S(1)}, u32[]{:S(2)}, u32[]{:S(2)}) collective-permute-start(bf16[4,96,2304]{2,1,0:T(8,128)(2,1)} %get-tuple-element.205), channel_id=1, source_target_pairs={{0,4},{4,0},{8,12},{12,8},{16,20},{20,16},{24,28},{28,24},{1,5},{5... | collective-permute-start | bytes 5308424 | tf_op jit(solution)/shard_map/ppermute | solution.py:84
  363.1 17.3 %collective-permute-start.30 = (bf16[1,2,104,768]{3,2,1,0:T(8,128)(2,1)S(1)}, bf16[1,2,104,768]{3,2,1,0:T(8,128)(2,1)S(1)}, u32[]{:S(2)}, u32[]{:S(2)}) collective-permute-start(bf16[1,2,104,768]{3,2,1,0:T(8,128)(2,1)S(1)} %maximum_bitcast_fusion.1), channel_id=1, source_target_pairs={{0,16},{4,20},{8,24},{12,28},{16,0},{20,4},{24,8},{28,12},{1,17},{... | collective-permute-start | bytes 958472 | tf_op jit(solution)/shard_map/ppermute | solution.py:84
  364.6 17.3 %collective-permute-start.29 = (bf16[1,2,104,768]{3,2,1,0:T(8,128)(2,1)S(1)}, bf16[1,2,104,768]{3,2,1,0:T(8,128)(2,1)S(1)}, u32[]{:S(2)}, u32[]{:S(2)}) collective-permute-start(bf16[1,2,104,768]{3,2,1,0:T(8,128)(2,1)S(1)} %maximum_bitcast_fusion), channel_id=1, source_target_pairs={{0,8},{4,12},{8,0},{12,4},{16,24},{20,28},{24,16},{28,20},{1,9},{5... | collective-permute-start | bytes 958472 | tf_op jit(solution)/shard_map/ppermute | solution.py:84
  365.2 30.1 %collective-permute-start.28 = (bf16[2,104,768]{2,1,0:T(8,128)(2,1)S(1)}, bf16[2,104,768]{2,1,0:T(8,128)(2,1)S(1)}, u32[]{:S(2)}, u32[]{:S(2)}) collective-permute-start(bf16[2,104,768]{2,1,0:T(8,128)(2,1)S(1)} %fusion.12), channel_id=1, source_target_pairs={{0,8},{4,12},{8,0},{12,4},{16,24},{20,28},{24,16},{28,20},{1,9},{5... | collective-permute-start | bytes 958472 | tf_op jit(solution)/shard_map/ppermute | solution.py:84
  366.9 28.4 %collective-permute-start.27 = (bf16[2,104,768]{2,1,0:T(8,128)(2,1)S(1)}, bf16[2,104,768]{2,1,0:T(8,128)(2,1)S(1)}, u32[]{:S(2)}, u32[]{:S(2)}) collective-permute-start(bf16[2,104,768]{2,1,0:T(8,128)(2,1)S(1)} %fusion.11), channel_id=1, source_target_pairs={{0,16},{4,20},{8,24},{12,28},{16,0},{20,4},{24,8},{28,12},{1,17},{... | collective-permute-start | bytes 958472 | tf_op jit(solution)/shard_map/ppermute | solution.py:84
  395.4 16.9 %collective-permute-start.36 = (bf16[2,2,104,768]{3,2,1,0:T(8,128)(2,1)S(1)}, bf16[2,2,104,768]{3,2,1,0:T(8,128)(2,1)S(1)}, u32[]{:S(2)}, u32[]{:S(2)}) collective-permute-start(bf16[2,2,104,768]{3,2,1,0:T(8,128)(2,1)S(1)} %pad_maximum_fusion.6), channel_id=1, source_target_pairs={{0,8},{4,12},{8,0},{12,4},{16,24},{20,28},{24,16},{28,20},{1,9},{5... | collective-permute-start | bytes 1916936 | tf_op jit(solution)/shard_map/ppermute | solution.py:84
  395.9 17.7 %collective-permute-start.35 = (bf16[2,2,104,768]{3,2,1,0:T(8,128)(2,1)S(1)}, bf16[2,2,104,768]{3,2,1,0:T(8,128)(2,1)S(1)}, u32[]{:S(2)}, u32[]{:S(2)}) collective-permute-start(bf16[2,2,104,768]{3,2,1,0:T(8,128)(2,1)S(1)} %pad_maximum_fusion.5), channel_id=1, source_target_pairs={{0,16},{4,20},{8,24},{12,28},{16,0},{20,4},{24,8},{28,12},{1,17},{... | collective-permute-start | bytes 1916936 | tf_op jit(solution)/shard_map/ppermute | solution.py:84
  398.0 6.2 %collective-permute-start.32 = (bf16[104,768]{1,0:T(8,128)(2,1)S(1)}, bf16[104,768]{1,0:T(8,128)(2,1)S(1)}, u32[]{:S(2)}, u32[]{:S(2)}) collective-permute-start(bf16[104,768]{1,0:T(8,128)(2,1)S(1)} %get-tuple-element.265), channel_id=1, source_target_pairs={{0,3},{1,0},{2,1},{3,2},{4,7},{5,4},{6,5},{7,6},{8,11},{9,8},{10,9... | collective-permute-start | bytes 479240 | tf_op jit(solution)/shard_map/ppermute | solution.py:91
  398.1 13.8 %collective-permute-start.33 = (bf16[104,768]{1,0:T(8,128)(2,1)S(1)}, bf16[104,768]{1,0:T(8,128)(2,1)S(1)}, u32[]{:S(2)}, u32[]{:S(2)}) collective-permute-start(bf16[104,768]{1,0:T(8,128)(2,1)S(1)} %get-tuple-element.264), channel_id=1, source_target_pairs={{0,2},{1,3},{2,0},{3,1},{4,6},{5,7},{6,4},{7,5},{8,10},{9,11},{10,... | collective-permute-start | bytes 479240 | tf_op jit(solution)/shard_map/ppermute | solution.py:91
  398.2 13.7 %collective-permute-start.34 = (bf16[104,768]{1,0:T(8,128)(2,1)S(1)}, bf16[104,768]{1,0:T(8,128)(2,1)S(1)}, u32[]{:S(2)}, u32[]{:S(2)}) collective-permute-start(bf16[104,768]{1,0:T(8,128)(2,1)S(1)} %get-tuple-element.266), channel_id=1, source_target_pairs={{0,1},{1,2},{2,3},{3,0},{4,5},{5,6},{6,7},{7,4},{8,9},{9,10},{10,1... | collective-permute-start | bytes 479240 | tf_op jit(solution)/shard_map/ppermute | solution.py:91
  413.8 16.9 %collective-permute-start.40 = (bf16[8,2,104,768]{3,2,1,0:T(8,128)(2,1)S(1)}, bf16[8,2,104,768]{3,2,1,0:T(8,128)(2,1)S(1)}, u32[]{:S(2)}, u32[]{:S(2)}) collective-permute-start(bf16[8,2,104,768]{3,2,1,0:T(8,128)(2,1)S(1)} %constant_dynamic-update-slice_fusion.12.refs_1_), channel_id=1, source_target_pairs={{0,4},{4,0},{8,12},{12,8},{16,20},{20,16},{24,28},{28,24},{1,5},{5... | collective-permute-start | bytes 7667720 | tf_op jit(solution)/shard_map/ppermute | solution.py:84
  415.6 36.7 %collective-permute-start.43 = (bf16[2,96,2304]{2,1,0:T(8,128)(2,1)}, bf16[2,96,2304]{2,1,0:T(8,128)(2,1)S(1)}, u32[]{:S(2)}, u32[]{:S(2)}) collective-permute-start(bf16[2,96,2304]{2,1,0:T(8,128)(2,1)} %get-tuple-element.253), channel_id=1, source_target_pairs={{0,8},{4,12},{8,0},{12,4},{16,24},{20,28},{24,16},{28,20},{1,9},{5... | collective-permute-start | bytes 2654216 | tf_op jit(solution)/shard_map/ppermute | solution.py:84
  416.0 8.0 %collective-permute-start.37 = (bf16[104,768]{1,0:T(8,128)(2,1)S(1)}, bf16[104,768]{1,0:T(8,128)(2,1)S(1)}, u32[]{:S(2)}, u32[]{:S(2)}) collective-permute-start(bf16[104,768]{1,0:T(8,128)(2,1)S(1)} %fusion.16), channel_id=1, source_target_pairs={{0,1},{1,2},{2,3},{3,0},{4,5},{5,6},{6,7},{7,4},{8,9},{9,10},{10,1... | collective-permute-start | bytes 479240 | tf_op jit(solution)/shard_map/ppermute | solution.py:91
  417.7 13.0 %collective-permute-start.38 = (bf16[104,768]{1,0:T(8,128)(2,1)S(1)}, bf16[104,768]{1,0:T(8,128)(2,1)S(1)}, u32[]{:S(2)}, u32[]{:S(2)}) collective-permute-start(bf16[104,768]{1,0:T(8,128)(2,1)S(1)} %fusion.16), channel_id=1, source_target_pairs={{0,2},{1,3},{2,0},{3,1},{4,6},{5,7},{6,4},{7,5},{8,10},{9,11},{10,... | collective-permute-start | bytes 479240 | tf_op jit(solution)/shard_map/ppermute | solution.py:91
  420.4 10.3 %collective-permute-start.39 = (bf16[104,768]{1,0:T(8,128)(2,1)S(1)}, bf16[104,768]{1,0:T(8,128)(2,1)S(1)}, u32[]{:S(2)}, u32[]{:S(2)}) collective-permute-start(bf16[104,768]{1,0:T(8,128)(2,1)S(1)} %fusion.16), channel_id=1, source_target_pairs={{0,3},{1,0},{2,1},{3,2},{4,7},{5,4},{6,5},{7,6},{8,11},{9,8},{10,9... | collective-permute-start | bytes 479240 | tf_op jit(solution)/shard_map/ppermute | solution.py:91
  432.3 19.9 %collective-permute-start.42 = (bf16[1,2,104,768]{3,2,1,0:T(8,128)(2,1)S(1)}, bf16[1,2,104,768]{3,2,1,0:T(8,128)(2,1)S(1)}, u32[]{:S(2)}, u32[]{:S(2)}) collective-permute-start(bf16[1,2,104,768]{3,2,1,0:T(8,128)(2,1)S(1)} %maximum_bitcast_fusion.3), channel_id=1, source_target_pairs={{0,16},{4,20},{8,24},{12,28},{16,0},{20,4},{24,8},{28,12},{1,17},{... | collective-permute-start | bytes 958472 | tf_op jit(solution)/shard_map/ppermute | solution.py:84
  434.8 24.0 %collective-permute-start.41 = (bf16[1,2,104,768]{3,2,1,0:T(8,128)(2,1)S(1)}, bf16[1,2,104,768]{3,2,1,0:T(8,128)(2,1)S(1)}, u32[]{:S(2)}, u32[]{:S(2)}) collective-permute-start(bf16[1,2,104,768]{3,2,1,0:T(8,128)(2,1)S(1)} %maximum_bitcast_fusion.2), channel_id=1, source_target_pairs={{0,8},{4,12},{8,0},{12,4},{16,24},{20,28},{24,16},{28,20},{1,9},{5... | collective-permute-start | bytes 958472 | tf_op jit(solution)/shard_map/ppermute | solution.py:84
  458.9 34.7 %collective-permute-start.45 = (bf16[2,2,104,768]{3,2,1,0:T(8,128)(2,1)S(1)}, bf16[2,2,104,768]{3,2,1,0:T(8,128)(2,1)S(1)}, u32[]{:S(2)}, u32[]{:S(2)}) collective-permute-start(bf16[2,2,104,768]{3,2,1,0:T(8,128)(2,1)S(1)} %pad_maximum_fusion.8), channel_id=1, source_target_pairs={{0,8},{4,12},{8,0},{12,4},{16,24},{20,28},{24,16},{28,20},{1,9},{5... | collective-permute-start | bytes 1916936 | tf_op jit(solution)/shard_map/ppermute | solution.py:84
  459.3 34.3 %copy-start.28 = (bf16[104,768]{1,0:T(8,128)(2,1)S(1)}, bf16[104,768]{1,0:T(8,128)(2,1)}, u32[]{:S(2)}) copy-start(bf16[104,768]{1,0:T(8,128)(2,1)} %copy-done.27) | copy-start | bytes 479236
  459.4 34.3 %copy-start.30 = (bf16[104,768]{1,0:T(8,128)(2,1)S(1)}, bf16[104,768]{1,0:T(8,128)(2,1)}, u32[]{:S(2)}) copy-start(bf16[104,768]{1,0:T(8,128)(2,1)} %copy-done.29) | copy-start | bytes 479236
  459.4 34.2 %collective-permute-start.44 = (bf16[2,2,104,768]{3,2,1,0:T(8,128)(2,1)S(1)}, bf16[2,2,104,768]{3,2,1,0:T(8,128)(2,1)S(1)}, u32[]{:S(2)}, u32[]{:S(2)}) collective-permute-start(bf16[2,2,104,768]{3,2,1,0:T(8,128)(2,1)S(1)} %pad_maximum_fusion.7), channel_id=1, source_target_pairs={{0,16},{4,20},{8,24},{12,28},{16,0},{20,4},{24,8},{28,12},{1,17},{... | collective-permute-start | bytes 1916936 | tf_op jit(solution)/shard_map/ppermute | solution.py:84
  462.0 31.7 %copy-start.21 = (bf16[1,2,104,768]{3,2,1,0:T(8,128)(2,1)S(1)}, bf16[1,2,104,768]{3,2,1,0:T(8,128)(2,1)}, u32[]{:S(2)}) copy-start(bf16[1,2,104,768]{3,2,1,0:T(8,128)(2,1)} %copy-done.20) | copy-start | bytes 958468
  462.0 14.0 %collective-permute-start.47 = (bf16[96,2304]{1,0:T(8,128)(2,1)S(1)}, bf16[96,2304]{1,0:T(8,128)(2,1)S(1)}, u32[]{:S(2)}, u32[]{:S(2)}) collective-permute-start(bf16[96,2304]{1,0:T(8,128)(2,1)S(1)} %get-tuple-element.228), channel_id=1, source_target_pairs={{0,3},{1,0},{2,1},{3,2},{4,7},{5,4},{6,5},{7,6},{8,11},{9,8},{10,9... | collective-permute-start | bytes 1327112 | tf_op jit(solution)/shard_map/ppermute | solution.py:91
  465.4 28.2 %collective-permute-start.46 = (bf16[96,2304]{1,0:T(8,128)(2,1)S(1)}, bf16[96,2304]{1,0:T(8,128)(2,1)S(1)}, u32[]{:S(2)}, u32[]{:S(2)}) collective-permute-start(bf16[96,2304]{1,0:T(8,128)(2,1)S(1)} %get-tuple-element.227), channel_id=1, source_target_pairs={{0,2},{1,3},{2,0},{3,1},{4,6},{5,7},{6,4},{7,5},{8,10},{9,11},{10,... | collective-permute-start | bytes 1327112 | tf_op jit(solution)/shard_map/ppermute | solution.py:91
  465.4 28.9 %copy-start.8 = (bf16[512,768]{1,0:T(8,128)(2,1)S(1)}, bf16[512,768]{1,0:T(8,128)(2,1)}, u32[]{:S(2)}) copy-start(bf16[512,768]{1,0:T(8,128)(2,1)} %get-tuple-element.146.refs_1_) | copy-start | bytes 2359300
  465.4 28.9 %copy-start.26 = (bf16[512,768]{1,0:T(8,128)(2,1)S(1)}, bf16[512,768]{1,0:T(8,128)(2,1)}, u32[]{:S(2)}) copy-start(bf16[512,768]{1,0:T(8,128)(2,1)} %get-tuple-element.153) | copy-start | bytes 2359300
  493.8 4.9 collective-permute-start.48
  500.2 14.6 %collective-permute-start.49 = (bf16[96,2304]{1,0:T(8,128)(2,1)}, bf16[96,2304]{1,0:T(8,128)(2,1)}, u32[]{:S(2)}, u32[]{:S(2)}) collective-permute-start(bf16[96,2304]{1,0:T(8,128)(2,1)} %get-tuple-element.237), channel_id=1, source_target_pairs={{0,1},{1,2},{2,3},{3,0},{4,5},{5,6},{6,7},{7,4},{8,9},{9,10},{10,1... | collective-permute-start | bytes 1327112 | tf_op jit(solution)/shard_map/ppermute | solution.py:91
  501.3 15.2 %collective-permute-start.50 = (bf16[1,96,2304]{2,1,0:T(8,128)(2,1)S(1)}, bf16[1,96,2304]{2,1,0:T(8,128)(2,1)}, u32[]{:S(2)}, u32[]{:S(2)}) collective-permute-start(bf16[1,96,2304]{2,1,0:T(8,128)(2,1)S(1)} %add_convert_fusion.10), channel_id=1, source_target_pairs={{0,16},{4,20},{8,24},{12,28},{16,0},{20,4},{24,8},{28,12},{1,17},{... | collective-permute-start | bytes 1327112 | tf_op jit(solution)/shard_map/ppermute | solution.py:84
  (42 other events, 259.5 us)
Sparse Core Ops, SparseCore 0:
  62.3 40.4 all-gather.8
  105.5 66.2 all-gather.10
  173.3 63.4 all-gather.12
  238.3 62.1 all-gather.14
  311.3 137.9 reduce-scatter.1

commit v4 on v3

--- a/solution.py
+++ b/solution.py
@@ -86,10 +86,11 @@
             self.flying.append(got)
         return got
 
-    def shift(self, value, step):
+    def shift(self, value, step, wait=True):
         n = self.n_t
         got = lax.ppermute(value, "tensor", [(i, (i + step) % n) for i in range(n)])
-        self.flying.append(got)
+        if wait:
+            self.flying.append(got)
         return got
 
 
@@ -921,14 +922,14 @@
 
     OWN, HALF, TWO, ALL = "own", "half", "two", "all"
     own = own_slice(0)
-    far = {k: net.shift(own, k) for k in (1, 3)}
+    far = {k: net.shift(own, k, wait=k != 2) for k in (1, 3, 2)}
     x_t = x_in.T
     qkv, lse, ctx, ctx_t, pre1, hb, hb_t = run_attn(0, x_in)
+    planes = lax.all_gather(line.after(own_slice(1)), "tensor")
     near = Gather(net, line, [far[1], far[3]])
-    far[2] = net.shift(line.after(own), 2)
     mine = own_weights(0)
     acc = run_ff(((OWN, 0),), hb, (pre1, gains1[0], biases1[0]), mine)[0]
-    planes = lax.all_gather(line.after(own_slice(1)), "tensor")
+    line.need(far[2])
     near.second()
     back = Gather(net, line, [far[2][: part // 2], far[2][part // 2 :]])
     line.sync()
@@ -945,14 +946,8 @@
     back.second()
     line.sync()
     back.core()
-    line.sync()
-    pre2, out, out_t = run_ff(
-        ((TWO, 0), (TWO, 1), (HALF, 0)),
-        hb,
-        acc,
-        near.pieces() + back.pieces(),
-        (gains2[0], biases2[0]),
-    )
+    acc = run_ff(((TWO, 0), (TWO, 1)), hb, acc, near.pieces())[0]
+    pre2, out, out_t = run_ff(((HALF, 0),), hb, acc, back.pieces(), (gains2[0], biases2[0]))
     kept.append((x_t, qkv, lse, ctx_t, pre1, hb, hb_t, pre2))
     outputs.append(out)
     weights = [

time: 537 us -> 515 us (0.959)
  waiting for transfers between devices: 176 us -> 154 us
    all_gather x1, waiting for transfers between devices: 10.1 us -> 1.67 us  [quick_program(): planes = lax.all_gather(line.after(own_slice(1)), 'tensor')]
    ppermute x18, waiting for transfers between devices: 68.8 us -> 62.5 us  [shift(): got = lax.ppermute(value, 'tensor', [(i, (i + step) % n) for i in range(n)])]
    pallas_call x14 -> x15, Pallas kernels: 208 us -> 211 us  [staged(): pl.pallas_call(functools.partial(staged_kernel, body, layers, len(smem),...]
    unnamed x121 -> x115, local copies, waits for them, and re-layouts: 18.4 us -> 19.5 us
  transfers between devices with their start and end apart: 56 -> 56, of which waited for: 24 -> 22; matrix products, arithmetic and copies ran while one was open for 9% -> 10% of each run, Pallas kernels for 39% -> 41%
where the time goes in v4:
time: 515 us; the launch traced here: 510 us
  Pallas kernels  211 us (41%)
  waiting for transfers between devices  154 us (30%)
  starting transfers between devices  62.4 us (12%)
  local copies, waits for them, and re-layouts  39.9 us (8%)
  other arithmetic  27 us (5%)
  between operations  15.6 us (3%)
    pallas_call x15, Pallas kernels, staged(): pl.pallas_call(functools.partial(staged_kernel, body, layers, len(smem),...  211 us
    ppermute x33, waiting for transfers between devices, flip(): got = lax.ppermute(value, 'dp', [(i, i ^ bit) for i in range(self.n_dp)])  81.3 us
    ppermute x18, waiting for transfers between devices, shift(): got = lax.ppermute(value, 'tensor', [(i, (i + step) % n) for i in range(n)])  62.5 us
    ppermute x33, starting transfers between devices, flip(): got = lax.ppermute(value, 'dp', [(i, i ^ bit) for i in range(self.n_dp)])  31.6 us
    ppermute x18, starting transfers between devices, shift(): got = lax.ppermute(value, 'tensor', [(i, (i + step) % n) for i in range(n)])  29.2 us
    unnamed x115, local copies, waits for them, and re-layouts  19.5 us
  transfers between devices with their start and end apart: 56, of which 22 were waited for; matrix products, arithmetic and copies ran while one was open for 10% of the time, Pallas kernels for 41%

profile of v4, /device:TPU:0, one launch (start us, length us, event | category | flops | bytes accessed | tf_op | source)
XLA Modules:
  0.0 509.6 jit_solution(6371527190738840529)
XLA Ops:
  9.8 3.1 collective-permute-start
  12.9 2.1 collective-permute-start.1
  20.3 14.4 %attn_fwd.2 = (bf16[512,2304]{1,0:T(8,128)(2,1)}, f32[512,128]{1,0:T(8,128)}, bf16[512,768]{1,0:T(8,128)(2,1)}, bf16[768,512]{1,0:T(8,128)(2,1)}, f32[512,768]{1...) custom-call(f32[12]{0:T(128)} %multiply_exponential_fusion.refs_0_, bf16[512,768]{1,0:T(8,128)(2,1)} %refs_1_.1, ...), custom_call_target="tpu_custom_call" | custom-call | flops 1024 | bytes 1024 | tf_op jit(solution)/shard_map/attn_fwd/pallas_call | solution.py:249
  37.1 1.5 collective-permute-start.3
  39.1 7.1 %fusion.48 = (bf16[1,768,2,768]{3,2,1,0:T(2,128)(2,1)}, bf16[1,768,2,768]{3,2,1,0:T(2,128)(2,1)S(1)}) fusion(bf16[2,768,2,768]{3,2,1,0:T(2,128)(2,1)} %param.19), kind=kLoop, calls=%fused_computation.170 | loop fusion | bytes 9437184 | tf_op jit(solution)/shard_map/slice | solution.py:905
  46.2 1.9 copy.59
  48.5 1.6 slice_bitcast_fusion
  50.1 6.5 %ff_fwd.5.refs_2_ = f32[512,768]{1,0:T(8,128)} custom-call(s32[1]{0:T(128)} %bitcast.refs_0_.refs_1_, bf16[512,768]{1,0:T(8,128)(2,1)} %get-tuple-element.170.refs_1_, f32[512,768]{1,0:T(8,128)} %get-tuple-element.128.refs_2_.refs_6_, f32[1,768]{1,0:T(1,128)} %get-tuple-element.284.refs_5_.refs_3_.refs_7_, f32[1,768]{1,0:T(1,128)} %get-tuple-element.281.refs_6_.refs_4_, ...), custom_call_target="tpu_custom_call" | custom-call | flops 1024 | bytes 1024 | tf_op jit(solution)/shard_map/ff_fwd/pallas_call | solution.py:249
  59.4 1.6 collective-permute-start.8
  61.0 1.7 collective-permute-start.7
  62.8 20.7 %collective-permute-done.8 = bf16[1,1,48,2304]{3,2,1,0:T(8,128)(2,1)S(1)} collective-permute-done((bf16[1,1,48,2304]{3,2,1,0:T(8,128)(2,1)S(1)}, bf16[1,1,48,2304]{3,2,1,0:T(8,128)(2,1)S(1)}, u32[]{:S(2)}, u32[]{:S(2)}) %collective-permute-start.8) | collective-permute-done | bytes 221216 | tf_op jit(solution)/shard_map/ppermute | solution.py:84
  83.5 1.7 all-gather.9.cloned.1.call-done
  89.6 1.5 collective-permute-start.11
  91.2 1.5 collective-permute-start.10
  94.2 13.2 %collective-permute-done.11 = bf16[2,1,48,2304]{3,2,1,0:T(8,128)(2,1)S(1)} collective-permute-done((bf16[2,1,48,2304]{3,2,1,0:T(8,128)(2,1)S(1)}, bf16[2,1,48,2304]{3,2,1,0:T(8,128)(2,1)S(1)}, u32[]{:S(2)}, u32[]{:S(2)}) %collective-permute-start.11) | collective-permute-done | bytes 442400 | tf_op jit(solution)/shard_map/ppermute | solution.py:84
  107.3 2.4 collective-permute-done.10
  113.3 1.9 copy.61
  115.8 9.8 %ff_fwd.6.refs_2_ = f32[512,768]{1,0:T(8,128)} custom-call(s32[1]{0:T(128)} %bitcast.refs_0_.refs_1_, bf16[512,768]{1,0:T(8,128)(2,1)} %get-tuple-element.170.refs_1_, f32[512,768]{1,0:T(8,128)} %ff_fwd.5.refs_2_, bf16[8,1,96,2304]{3,2,1,0:T(8,128)(2,1)} %copy-done, bf16[8,1,96,2304]{3,2,1,0:T(8,128)(2,1)} %copy-done.1), custom_call_target="tpu_custom_call" | custom-call | flops 1024 | bytes 1024 | tf_op jit(solution)/shard_map/ff_fwd/pallas_call | solution.py:249
  125.6 6.8 %ff_fwd.7 = (f32[512,768]{1,0:T(8,128)}, bf16[512,768]{1,0:T(8,128)(2,1)}, bf16[768,512]{1,0:T(8,128)(2,1)}) custom-call(s32[1]{0:T(128)} %bitcast.refs_0_.refs_1_, bf16[512,768]{1,0:T(8,128)(2,1)} %get-tuple-element.170.refs_1_, f32[512,768]{1,0:T(8,128)} %ff_fwd.6.refs_2_, f32[1,768]{1,0:T(1,128)} %get-tuple-element.286.refs_3_.refs_5_, ...), custom_call_target="tpu_custom_call" | custom-call | flops 1024 | bytes 1024 | tf_op jit(solution)/shard_map/ff_fwd/pallas_call | solution.py:249
  132.5 14.4 %attn_fwd.3 = (bf16[512,2304]{1,0:T(8,128)(2,1)}, f32[512,128]{1,0:T(8,128)}, bf16[512,768]{1,0:T(8,128)(2,1)}, bf16[768,512]{1,0:T(8,128)(2,1)}, f32[512,768]{1...) custom-call(f32[12]{0:T(128)} %multiply_exponential_fusion.refs_0_, ...), custom_call_target="tpu_custom_call" | custom-call | flops 1024 | bytes 1024 | tf_op jit(solution)/shard_map/attn_fwd/pallas_call | solution.py:249
  146.9 6.2 %ff_fwd.8.refs_2_ = f32[512,768]{1,0:T(8,128)} custom-call(s32[1]{0:T(128)} %bitcast.refs_0_.refs_1_, bf16[512,768]{1,0:T(8,128)(2,1)} %get-tuple-element.155.refs_1_, f32[512,768]{1,0:T(8,128)} %get-tuple-element.150.refs_2_.refs_5_, f32[1,768]{1,0:T(1,128)} %get-tuple-element.285.refs_5_.refs_3_.refs_6_, f32[1,768]{1,0:T(1,128)} %get-tuple-element.280.refs_6_.refs_4_, ...), custom_call_target="tpu_custom_call" | custom-call | flops 1024 | bytes 1024 | tf_op jit(solution)/shard_map/ff_fwd/pallas_call | solution.py:249
  154.5 13.4 %ff_fwd.9 = (f32[512,768]{1,0:T(8,128)}, bf16[512,768]{1,0:T(8,128)(2,1)}, bf16[768,512]{1,0:T(8,128)(2,1)}) custom-call(s32[1]{0:T(128)} %bitcast.refs_0_.refs_1_, bf16[512,768]{1,0:T(8,128)(2,1)} %get-tuple-element.155.refs_1_, f32[512,768]{1,0:T(8,128)} %ff_fwd.8.refs_2_, f32[1,768]{1,0:T(1,128)} %get-tuple-element.287.refs_3_.refs_4_, ...), custom_call_target="tpu_custom_call" | custom-call | flops 1024 | bytes 1024 | tf_op jit(solution)/shard_map/ff_fwd/pallas_call | solution.py:249
  167.9 23.1 %ff_bwd.3 = (f32[512,768]{1,0:T(8,128)}, bf16[512,768]{1,0:T(8,128)(2,1)}, bf16[768,512]{1,0:T(8,128)(2,1)}, f32[2,768]{1,0:T(2,128)}, bf16[512,768]{1,0:T(8,128)(2,1)}, /*index=5*/f32[2,768]{1,0:T(2,128)}) custom-call(s32[1]{0:T(128)} %bitcast.refs_0_.refs_1_, bf16[512,768]{1,0:T(8,128)(2,1)} %get-tuple-element.155.refs_1_, bf16[512,768]{1,0:T(8,128)(2,1)} %refs_2_.5, ...), custom_call_target="tpu_custom_call" | custom-call | flops 1024 | bytes 1024 | tf_op jit(solution)/shard_map/ff_bwd/pallas_call | solution.py:249
  191.0 20.9 %attn_bwd.2 = (bf16[4,4,104,768]{3,2,1,0:T(8,128)(2,1)}, bf16[4,4,104,768]{3,2,1,0:T(8,128)(2,1)}, f32[512,768]{1,0:T(8,128)}) custom-call(f32[12]{0:T(128)} %multiply_exponential_fusion.refs_0_, s32[1]{0:T(128)} %bitcast.refs_0_.refs_1_, bf16[512,768]{1,0:T(8,128)(2,1)} %get-tuple-element.158.refs_2_, bf16[2,768,768]{2,1,0:T(8,128)(2,1)} %refs_3_.3, ...), custom_call_target="tpu_custom_call" | custom-call | flops 1024 | bytes 1024 | tf_op jit(solution)/shard_map/attn_bwd/pallas_call | solution.py:249
  211.9 7.3 %all-gather.13.cloned.1.call-done = bf16[2048,768]{1,0:T(8,128)(2,1)} async-done(((bf16[512,768]{1,0:T(8,128)(2,1)}), bf16[2048,768]{1,0:T(8,128)(2,1)}) %all-gather.13.cloned.1.call-update) | async-done | bytes 3145744 | tf_op jit(solution)/shard_map/all_gather | solution.py:963
  219.6 1.9 copy.47
  221.6 13.3 %ff_bwd.4 = (f32[512,768]{1,0:T(8,128)}, bf16[512,768]{1,0:T(8,128)(2,1)}, bf16[768,512]{1,0:T(8,128)(2,1)}, f32[2,768]{1,0:T(2,128)}, bf16[8,4,96,2304]{3,2,1,0:T(8,128)(2,1)}) custom-call(s32[1]{0:T(128)} %bitcast.refs_0_.refs_1_, bf16[512,768]{1,0:T(8,128)(2,1)} %get-tuple-element.170.refs_1_, bf16[768,512]{1,0:T(8,128)(2,1)} %get-tuple-element.166.refs_2_, ...), custom_call_target="tpu_custom_call" | custom-call | flops 1024 | bytes 1024 | tf_op jit(solution)/shard_map/ff_bwd/pallas_call | solution.py:249
  234.8 4.1 add_convert_fusion.6
  241.9 25.7 %ff_bwd.5 = (f32[512,768]{1,0:T(8,128)}, bf16[512,768]{1,0:T(8,128)(2,1)}, f32[2,768]{1,0:T(2,128)}, bf16[8,4,96,2304]{3,2,1,0:T(8,128)(2,1)}) custom-call(s32[1]{0:T(128)} %bitcast.refs_0_.refs_1_, bf16[512,768]{1,0:T(8,128)(2,1)} %get-tuple-element.170.refs_1_, bf16[768,512]{1,0:T(8,128)(2,1)} %get-tuple-element.166.refs_2_, ...), custom_call_target="tpu_custom_call", output_to_operand_aliasing={{3}: (12, {})} | custom-call | flops 1024 | bytes 1024 | tf_op jit(solution)/shard_map/ff_bwd/pallas_call | solution.py:249
  271.6 21.0 %attn_bwd.3 = (bf16[4,4,104,768]{3,2,1,0:T(8,128)(2,1)}, bf16[4,4,104,768]{3,2,1,0:T(8,128)(2,1)}, f32[512,768]{1,0:T(8,128)}) custom-call(f32[12]{0:T(128)} %multiply_exponential_fusion.refs_0_, s32[1]{0:T(128)} %bitcast.refs_0_.refs_1_, bf16[512,768]{1,0:T(8,128)(2,1)} %get-tuple-element.178.refs_2_, bf16[2,768,768]{2,1,0:T(8,128)(2,1)} %refs_3_.3, ...), custom_call_target="tpu_custom_call" | custom-call | flops 1024 | bytes 1024 | tf_op jit(solution)/shard_map/attn_bwd/pallas_call | solution.py:249
  293.5 1.7 copy-done.8
  298.4 1.9 collective-permute-start.21
  300.3 3.3 collective-permute-done.19
  303.6 8.6 %collective-permute-done.20 = bf16[104,768]{1,0:T(8,128)(2,1)S(1)} collective-permute-done((bf16[104,768]{1,0:T(8,128)(2,1)S(1)}, bf16[104,768]{1,0:T(8,128)(2,1)S(1)}, u32[]{:S(2)}, u32[]{:S(2)}) %collective-permute-start.20) | collective-permute-done | bytes 159776 | tf_op jit(solution)/shard_map/ppermute | solution.py:91
  312.2 1.7 add_convert_fusion.2
  318.5 2.0 collective-permute-start.25
  320.5 3.2 collective-permute-start.26
  323.8 21.6 %ff_grads.1 = (bf16[4,96,2304]{2,1,0:T(8,128)(2,1)}, bf16[4,96,2304]{2,1,0:T(8,128)(2,1)}) custom-call(s32[1]{0:T(128)} %bitcast.refs_0_.refs_1_, bf16[768,1536]{1,0:T(8,128)(2,1)} %bitcast.159, bf16[768,768]{1,0:T(8,128)(2,1)} %get-tuple-element.254.refs_6_.refs_8_.refs_2_, bf16[4,512,768]{2,1,0:T(8,128)(2,1)} %bitcast.147, bf16[4,512,768]{2,1,0:T(8,128)(2,1)} %bitcast.151, ...), custom_call_target="tpu_custom_call" | custom-call | flops 1024 | bytes 1024 | tf_op jit(solution)/shard_map/ff_grads/pallas_call | solution.py:249
  350.1 12.8 %collective-permute-done.30 = bf16[1,2,104,768]{3,2,1,0:T(8,128)(2,1)S(1)} collective-permute-done((bf16[1,2,104,768]{3,2,1,0:T(8,128)(2,1)S(1)}, bf16[1,2,104,768]{3,2,1,0:T(8,128)(2,1)S(1)}, u32[]{:S(2)}, u32[]{:S(2)}) %collective-permute-start.30) | collective-permute-done | bytes 319520 | tf_op jit(solution)/shard_map/ppermute | solution.py:84
  364.1 13.4 %collective-permute-done.28 = bf16[2,104,768]{2,1,0:T(8,128)(2,1)S(1)} collective-permute-done((bf16[2,104,768]{2,1,0:T(8,128)(2,1)S(1)}, bf16[2,104,768]{2,1,0:T(8,128)(2,1)S(1)}, u32[]{:S(2)}, u32[]{:S(2)}) %collective-permute-start.28) | collective-permute-done | bytes 319520 | tf_op jit(solution)/shard_map/ppermute | solution.py:84
  380.9 1.9 collective-permute-start.34
  382.9 3.5 collective-permute-done.32
  386.5 8.1 %collective-permute-done.33 = bf16[104,768]{1,0:T(8,128)(2,1)S(1)} collective-permute-done((bf16[104,768]{1,0:T(8,128)(2,1)S(1)}, bf16[104,768]{1,0:T(8,128)(2,1)S(1)}, u32[]{:S(2)}, u32[]{:S(2)}) %collective-permute-start.33) | collective-permute-done | bytes 159776 | tf_op jit(solution)/shard_map/ppermute | solution.py:91
  394.6 1.7 collective-permute-done.35
  396.6 1.7 add_convert_fusion
  398.4 1.6 collective-permute-start.37
  400.0 3.0 collective-permute-start.38
  403.0 2.8 collective-permute-start.39
  406.7 6.7 %collective-permute-done.38 = bf16[104,768]{1,0:T(8,128)(2,1)S(1)} collective-permute-done((bf16[104,768]{1,0:T(8,128)(2,1)S(1)}, bf16[104,768]{1,0:T(8,128)(2,1)S(1)}, u32[]{:S(2)}, u32[]{:S(2)}) %collective-permute-start.38) | collective-permute-done | bytes 159776 | tf_op jit(solution)/shard_map/ppermute | solution.py:91
  413.4 1.5 copy-done.9
  415.0 2.5 collective-permute-start.42
  417.6 1.8 collective-permute-start.41
  420.0 7.0 %spread_out.2 = (f32[4,8,768]{2,1,0:T(8,128)}, f32[2,768,2304]{2,1,0:T(8,128)}, f32[2,768,768]{2,1,0:T(8,128)}) custom-call(s32[2]{0:T(128)} %pad_add_fusion.refs_0_, bf16[8,2,104,768]{3,2,1,0:T(8,128)(2,1)} %copy-done.3, bf16[8,2,104,768]{3,2,1,0:T(8,128)(2,1)} %copy-done.9), custom_call_target="tpu_custom_call" | custom-call | flops 1024 | bytes 1024 | tf_op jit(solution)/shard_map/spread_out/pallas_call | solution.py:249
  427.0 7.1 %collective-permute-done.43 = bf16[2,96,2304]{2,1,0:T(8,128)(2,1)S(1)} collective-permute-done((bf16[2,96,2304]{2,1,0:T(8,128)(2,1)}, bf16[2,96,2304]{2,1,0:T(8,128)(2,1)S(1)}, u32[]{:S(2)}, u32[]{:S(2)}) %collective-permute-start.43) | collective-permute-done | bytes 884768 | tf_op jit(solution)/shard_map/ppermute | solution.py:84
  434.1 6.6 %collective-permute-done.41 = bf16[1,2,104,768]{3,2,1,0:T(8,128)(2,1)S(1)} collective-permute-done((bf16[1,2,104,768]{3,2,1,0:T(8,128)(2,1)S(1)}, bf16[1,2,104,768]{3,2,1,0:T(8,128)(2,1)S(1)}, u32[]{:S(2)}, u32[]{:S(2)}) %collective-permute-start.41) | collective-permute-done | bytes 319520 | tf_op jit(solution)/shard_map/ppermute | solution.py:84
  441.2 1.8 collective-permute-start.44
  443.9 3.4 collective-permute-start.47
  448.4 9.5 %collective-permute-done.47 = bf16[96,2304]{1,0:T(8,128)(2,1)S(1)} collective-permute-done((bf16[96,2304]{1,0:T(8,128)(2,1)S(1)}, bf16[96,2304]{1,0:T(8,128)(2,1)S(1)}, u32[]{:S(2)}, u32[]{:S(2)}) %collective-permute-start.47) | collective-permute-done | bytes 442400 | tf_op jit(solution)/shard_map/ppermute | solution.py:91
  457.9 17.9 %collective-permute-done.46 = bf16[96,2304]{1,0:T(8,128)(2,1)S(1)} collective-permute-done((bf16[96,2304]{1,0:T(8,128)(2,1)S(1)}, bf16[96,2304]{1,0:T(8,128)(2,1)S(1)}, u32[]{:S(2)}, u32[]{:S(2)}) %collective-permute-start.46) | collective-permute-done | bytes 442400 | tf_op jit(solution)/shard_map/ppermute | solution.py:91
  479.0 2.0 collective-permute-done.48.refs_2_
  484.2 6.9 %spread_out.3 = (f32[4,8,768]{2,1,0:T(8,128)}, f32[2,768,2304]{2,1,0:T(8,128)}, f32[2,768,768]{2,1,0:T(8,128)}) custom-call(s32[2]{0:T(128)} %pad_add_fusion.refs_0_, bf16[8,2,104,768]{3,2,1,0:T(8,128)(2,1)} %copy-done.4, bf16[8,2,104,768]{3,2,1,0:T(8,128)(2,1)} %copy-done.13, ...), custom_call_target="tpu_custom_call", output_to_operand_aliasing={{1}: (3, {}), {2}: (4, {})} | custom-call | flops 1024 | bytes 1024 | tf_op jit(solution)/shard_map/spread_out/pallas_call | solution.py:249
  492.7 4.0 collective-permute-done.49
  496.8 1.6 fusion.1
  501.4 1.6 pad_maximum_fusion.2
  (254 shorter events, 65.1 us)
Async XLA Ops:
  7.2 78.0 %all-gather.9.cloned.1.call-start = ((), (), s32[]{:S(2)}) async-start(), calls=%async_computation.2 | async-start | bytes 2211840 | tf_op jit(solution)/shard_map/all_gather | solution.py:928
  9.8 25.7 %collective-permute-start = (bf16[96,2304]{1,0:T(8,128)(2,1)S(1)}, bf16[96,2304]{1,0:T(8,128)(2,1)S(1)}, u32[]{:S(2)}, u32[]{:S(2)}) collective-permute-start(bf16[96,2304]{1,0:T(8,128)(2,1)S(1)} %pad_maximum_fusion.10), channel_id=1, source_target_pairs={{0,1},{1,2},{2,3},{3,0},{4,5},{5,6},{6,7},{7,4},{8,9},{9,10},{10,1... | collective-permute-start | bytes 1327112 | tf_op jit(solution)/shard_map/ppermute | solution.py:91
  12.9 22.7 %collective-permute-start.1 = (bf16[96,2304]{1,0:T(8,128)(2,1)S(1)}, bf16[96,2304]{1,0:T(8,128)(2,1)S(1)}, u32[]{:S(2)}, u32[]{:S(2)}) collective-permute-start(bf16[96,2304]{1,0:T(8,128)(2,1)S(1)} %pad_maximum_fusion.10), channel_id=1, source_target_pairs={{0,3},{1,0},{2,1},{3,2},{4,7},{5,4},{6,5},{7,6},{8,11},{9,8},{10,9... | collective-permute-start | bytes 1327112 | tf_op jit(solution)/shard_map/ppermute | solution.py:91
  15.0 41.6 %collective-permute-start.4 = (bf16[96,2304]{1,0:T(8,128)(2,1)S(1)}, bf16[96,2304]{1,0:T(8,128)(2,1)S(1)}, u32[]{:S(2)}, u32[]{:S(2)}) collective-permute-start(bf16[96,2304]{1,0:T(8,128)(2,1)S(1)} %pad_maximum_fusion.10), channel_id=1, source_target_pairs={{0,2},{1,3},{2,0},{3,1},{4,6},{5,7},{6,4},{7,5},{8,10},{9,11},{10,... | collective-permute-start | bytes 1327112 | tf_op jit(solution)/shard_map/ppermute | solution.py:91
  35.6 21.1 %collective-permute-start.2 = (bf16[1,1,96,2304]{3,2,1,0:T(8,128)(2,1)S(1)}, bf16[1,1,96,2304]{3,2,1,0:T(8,128)(2,1)S(1)}, u32[]{:S(2)}, u32[]{:S(2)}) collective-permute-start(bf16[1,1,96,2304]{3,2,1,0:T(8,128)(2,1)S(1)} %bitcast.172), channel_id=1, source_target_pairs={{0,8},{4,12},{8,0},{12,4},{16,24},{20,28},{24,16},{28,20},{1,9},{5... | collective-permute-start | bytes 1327112 | tf_op jit(solution)/shard_map/ppermute | solution.py:84
  37.1 19.6 %collective-permute-start.3 = (bf16[1,1,96,2304]{3,2,1,0:T(8,128)(2,1)S(1)}, bf16[1,1,96,2304]{3,2,1,0:T(8,128)(2,1)S(1)}, u32[]{:S(2)}, u32[]{:S(2)}) collective-permute-start(bf16[1,1,96,2304]{3,2,1,0:T(8,128)(2,1)S(1)} %bitcast.170), channel_id=1, source_target_pairs={{0,16},{4,20},{8,24},{12,28},{16,0},{20,4},{24,8},{28,12},{1,17},{... | collective-permute-start | bytes 1327112 | tf_op jit(solution)/shard_map/ppermute | solution.py:84
  38.6 115.4 %all-gather.11.cloned.1.call-start = ((), (), s32[]{:S(2)}) async-start(), calls=%async_computation.3 | async-start | bytes 11943936 | tf_op jit(solution)/shard_map/all_gather | solution.py:944
  57.6 25.9 %collective-permute-start.6 = (bf16[2,1,96,2304]{3,2,1,0:T(8,128)(2,1)}, bf16[2,1,96,2304]{3,2,1,0:T(8,128)(2,1)S(1)}, u32[]{:S(2)}, u32[]{:S(2)}) collective-permute-start(bf16[2,1,96,2304]{3,2,1,0:T(8,128)(2,1)} %pad_maximum_fusion.4), channel_id=1, source_target_pairs={{0,8},{4,12},{8,0},{12,4},{16,24},{20,28},{24,16},{28,20},{1,9},{5... | collective-permute-start | bytes 2654216 | tf_op jit(solution)/shard_map/ppermute | solution.py:84
  58.9 24.6 %collective-permute-start.5 = (bf16[2,1,96,2304]{3,2,1,0:T(8,128)(2,1)}, bf16[2,1,96,2304]{3,2,1,0:T(8,128)(2,1)}, u32[]{:S(2)}, u32[]{:S(2)}) collective-permute-start(bf16[2,1,96,2304]{3,2,1,0:T(8,128)(2,1)} %pad_maximum_fusion.3), channel_id=1, source_target_pairs={{0,16},{4,20},{8,24},{12,28},{16,0},{20,4},{24,8},{28,12},{1,17},{... | collective-permute-start | bytes 2654216 | tf_op jit(solution)/shard_map/ppermute | solution.py:84
  59.4 24.1 %collective-permute-start.8 = (bf16[1,1,48,2304]{3,2,1,0:T(8,128)(2,1)S(1)}, bf16[1,1,48,2304]{3,2,1,0:T(8,128)(2,1)S(1)}, u32[]{:S(2)}, u32[]{:S(2)}) collective-permute-start(bf16[1,1,48,2304]{3,2,1,0:T(8,128)(2,1)S(1)} %bitcast.166), channel_id=1, source_target_pairs={{0,16},{4,20},{8,24},{12,28},{16,0},{20,4},{24,8},{28,12},{1,17},{... | collective-permute-start | bytes 663560 | tf_op jit(solution)/shard_map/ppermute | solution.py:84
  61.0 22.5 %collective-permute-start.7 = (bf16[1,1,48,2304]{3,2,1,0:T(8,128)(2,1)S(1)}, bf16[1,1,48,2304]{3,2,1,0:T(8,128)(2,1)S(1)}, u32[]{:S(2)}, u32[]{:S(2)}) collective-permute-start(bf16[1,1,48,2304]{3,2,1,0:T(8,128)(2,1)S(1)} %bitcast.168), channel_id=1, source_target_pairs={{0,8},{4,12},{8,0},{12,4},{16,24},{20,28},{24,16},{28,20},{1,9},{5... | collective-permute-start | bytes 663560 | tf_op jit(solution)/shard_map/ppermute | solution.py:84
  87.8 131.3 %all-gather.13.cloned.1.call-start = ((), (), s32[]{:S(2)}) async-start(), calls=%async_computation.4 | async-start | bytes 3932160 | tf_op jit(solution)/shard_map/all_gather | solution.py:963
  89.5 20.2 %collective-permute-start.9 = (bf16[8,1,96,2304]{3,2,1,0:T(8,128)(2,1)S(1)}, bf16[8,1,96,2304]{3,2,1,0:T(8,128)(2,1)S(1)}, u32[]{:S(2)}, u32[]{:S(2)}) collective-permute-start(bf16[8,1,96,2304]{3,2,1,0:T(8,128)(2,1)S(1)} %constant_dynamic-update-slice_fusion.refs_3_.refs_10_), channel_id=1, source_target_pairs={{0,4},{4,0},{8,12},{12,8},{16,20},{20,16},{24,28},{28,24},{1,5},{5... | collective-permute-start | bytes 10616840 | tf_op jit(solution)/shard_map/ppermute | solution.py:84
  89.6 17.7 %collective-permute-start.11 = (bf16[2,1,48,2304]{3,2,1,0:T(8,128)(2,1)S(1)}, bf16[2,1,48,2304]{3,2,1,0:T(8,128)(2,1)S(1)}, u32[]{:S(2)}, u32[]{:S(2)}) collective-permute-start(bf16[2,1,48,2304]{3,2,1,0:T(8,128)(2,1)S(1)} %pad_maximum_fusion.13), channel_id=1, source_target_pairs={{0,8},{4,12},{8,0},{12,4},{16,24},{20,28},{24,16},{28,20},{1,9},{5... | collective-permute-start | bytes 1327112 | tf_op jit(solution)/shard_map/ppermute | solution.py:84
  91.2 18.5 %collective-permute-start.10 = (bf16[2,1,48,2304]{3,2,1,0:T(8,128)(2,1)S(1)}, bf16[2,1,48,2304]{3,2,1,0:T(8,128)(2,1)S(1)}, u32[]{:S(2)}, u32[]{:S(2)}) collective-permute-start(bf16[2,1,48,2304]{3,2,1,0:T(8,128)(2,1)S(1)} %pad_maximum_fusion.12), channel_id=1, source_target_pairs={{0,16},{4,20},{8,24},{12,28},{16,0},{20,4},{24,8},{28,12},{1,17},{... | collective-permute-start | bytes 1327112 | tf_op jit(solution)/shard_map/ppermute | solution.py:84
  113.2 12.4 %collective-permute-start.12 = (bf16[8,1,48,2304]{3,2,1,0:T(8,128)(2,1)}, bf16[8,1,48,2304]{3,2,1,0:T(8,128)(2,1)}, u32[]{:S(2)}, u32[]{:S(2)}) collective-permute-start(bf16[8,1,48,2304]{3,2,1,0:T(8,128)(2,1)} %constant_dynamic-update-slice_fusion.6.refs_5_.refs_8_), channel_id=1, source_target_pairs={{0,4},{4,0},{8,12},{12,8},{16,20},{20,16},{24,28},{28,24},{1,5},{5... | collective-permute-start | bytes 5308424 | tf_op jit(solution)/shard_map/ppermute | solution.py:84
  154.0 138.7 %all-gather.15.cloned.1.call-start = ((), (), s32[]{:S(2)}) async-start(), calls=%async_computation.5 | async-start | bytes 3932160 | tf_op jit(solution)/shard_map/all_gather | solution.py:1011
  219.1 221.6 %reduce-scatter.2.cloned.1.call-start = ((), (), s32[]{:S(2)}) async-start(), calls=%async_computation.1 | async-start | bytes 15925248 | tf_op jit(solution)/shard_map/reduce_scatter | solution.py:1000
  221.5 13.3 %collective-permute-start.13 = (bf16[4,4,104,768]{3,2,0,1:T(8,128)(2,1)S(1)}, bf16[4,4,104,768]{3,2,0,1:T(8,128)(2,1)}, u32[]{:S(2)}, u32[]{:S(2)}) collective-permute-start(bf16[4,4,104,768]{3,2,0,1:T(8,128)(2,1)S(1)} %copy.47), channel_id=1, source_target_pairs={{0,4},{4,0},{8,12},{12,8},{16,20},{20,16},{24,28},{28,24},{1,5},{5... | collective-permute-start | bytes 7667720 | tf_op jit(solution)/shard_map/ppermute | solution.py:84
  238.9 28.7 %copy-start.11 = (bf16[2,2,104,768]{3,2,0,1:T(8,128)(2,1)}, bf16[2,2,104,768]{3,2,0,1:T(8,128)(2,1)S(1)}, u32[]{:S(2)}) copy-start(bf16[2,2,104,768]{3,2,0,1:T(8,128)(2,1)S(1)} %get-tuple-element.244) | copy-start | bytes 1916932
  238.9 28.7 %collective-permute-start.14 = (bf16[2,2,104,768]{3,2,0,1:T(8,128)(2,1)}, bf16[2,2,104,768]{3,2,0,1:T(8,128)(2,1)S(1)}, u32[]{:S(2)}, u32[]{:S(2)}) collective-permute-start(bf16[2,2,104,768]{3,2,0,1:T(8,128)(2,1)} %get-tuple-element.247), channel_id=1, source_target_pairs={{0,8},{4,12},{8,0},{12,4},{16,24},{20,28},{24,16},{28,20},{1,9},{5... | collective-permute-start | bytes 1916936 | tf_op jit(solution)/shard_map/ppermute | solution.py:84
  240.4 27.2 %collective-permute-start.15 = (bf16[2,2,104,768]{3,2,0,1:T(8,128)(2,1)}, bf16[2,2,104,768]{3,2,0,1:T(8,128)(2,1)S(1)}, u32[]{:S(2)}, u32[]{:S(2)}) collective-permute-start(bf16[2,2,104,768]{3,2,0,1:T(8,128)(2,1)} %get-tuple-element.246), channel_id=1, source_target_pairs={{0,16},{4,20},{8,24},{12,28},{16,0},{20,4},{24,8},{28,12},{1,17},{... | collective-permute-start | bytes 1916936 | tf_op jit(solution)/shard_map/ppermute | solution.py:84
  267.6 25.0 %copy-start.31 = (bf16[2,2,104,768]{3,2,0,1:T(8,128)(2,1)}, bf16[2,2,104,768]{3,2,0,1:T(8,128)(2,1)S(1)}, u32[]{:S(2)}) copy-start(bf16[2,2,104,768]{3,2,0,1:T(8,128)(2,1)S(1)} %collective-permute-done.14) | copy-start | bytes 1916932
  267.6 25.0 %copy-start.33 = (bf16[2,2,104,768]{3,2,0,1:T(8,128)(2,1)}, bf16[2,2,104,768]{3,2,0,1:T(8,128)(2,1)S(1)}, u32[]{:S(2)}) copy-start(bf16[2,2,104,768]{3,2,0,1:T(8,128)(2,1)S(1)} %collective-permute-done.15) | copy-start | bytes 1916932
  268.5 24.2 %collective-permute-start.17 = (bf16[2,104,768]{2,1,0:T(8,128)(2,1)}, bf16[2,104,768]{2,1,0:T(8,128)(2,1)S(1)}, u32[]{:S(2)}, u32[]{:S(2)}) collective-permute-start(bf16[2,104,768]{2,1,0:T(8,128)(2,1)} %fusion.7), channel_id=1, source_target_pairs={{0,8},{4,12},{8,0},{12,4},{16,24},{20,28},{24,16},{28,20},{1,9},{5... | collective-permute-start | bytes 958472 | tf_op jit(solution)/shard_map/ppermute | solution.py:84
  269.8 22.8 %collective-permute-start.16 = (bf16[2,104,768]{2,1,0:T(8,128)(2,1)}, bf16[2,104,768]{2,1,0:T(8,128)(2,1)S(1)}, u32[]{:S(2)}, u32[]{:S(2)}) collective-permute-start(bf16[2,104,768]{2,1,0:T(8,128)(2,1)} %fusion.6), channel_id=1, source_target_pairs={{0,16},{4,20},{8,24},{12,28},{16,0},{20,4},{24,8},{28,12},{1,17},{... | collective-permute-start | bytes 958472 | tf_op jit(solution)/shard_map/ppermute | solution.py:84
  295.4 16.8 %collective-permute-start.18 = (bf16[4,4,104,768]{3,2,0,1:T(8,128)(2,1)S(1)}, bf16[4,4,104,768]{3,2,0,1:T(8,128)(2,1)S(1)}, u32[]{:S(2)}, u32[]{:S(2)}) collective-permute-start(bf16[4,4,104,768]{3,2,0,1:T(8,128)(2,1)S(1)} %copy.54), channel_id=1, source_target_pairs={{0,4},{4,0},{8,12},{12,8},{16,20},{20,16},{24,28},{28,24},{1,5},{5... | collective-permute-start | bytes 7667720 | tf_op jit(solution)/shard_map/ppermute | solution.py:84
  297.2 6.4 %collective-permute-start.19 = (bf16[104,768]{1,0:T(8,128)(2,1)S(1)}, bf16[104,768]{1,0:T(8,128)(2,1)S(1)}, u32[]{:S(2)}, u32[]{:S(2)}) collective-permute-start(bf16[104,768]{1,0:T(8,128)(2,1)S(1)} %get-tuple-element.268), channel_id=1, source_target_pairs={{0,3},{1,0},{2,1},{3,2},{4,7},{5,4},{6,5},{7,6},{8,11},{9,8},{10,9... | collective-permute-start | bytes 479240 | tf_op jit(solution)/shard_map/ppermute | solution.py:91
  298.0 14.3 %collective-permute-start.20 = (bf16[104,768]{1,0:T(8,128)(2,1)S(1)}, bf16[104,768]{1,0:T(8,128)(2,1)S(1)}, u32[]{:S(2)}, u32[]{:S(2)}) collective-permute-start(bf16[104,768]{1,0:T(8,128)(2,1)S(1)} %get-tuple-element.269), channel_id=1, source_target_pairs={{0,2},{1,3},{2,0},{3,1},{4,6},{5,7},{6,4},{7,5},{8,10},{9,11},{10,... | collective-permute-start | bytes 479240 | tf_op jit(solution)/shard_map/ppermute | solution.py:91
  298.4 13.9 %collective-permute-start.21 = (bf16[104,768]{1,0:T(8,128)(2,1)S(1)}, bf16[104,768]{1,0:T(8,128)(2,1)S(1)}, u32[]{:S(2)}, u32[]{:S(2)}) collective-permute-start(bf16[104,768]{1,0:T(8,128)(2,1)S(1)} %get-tuple-element.267), channel_id=1, source_target_pairs={{0,1},{1,2},{2,3},{3,0},{4,5},{5,6},{6,7},{7,4},{8,9},{9,10},{10,1... | collective-permute-start | bytes 479240 | tf_op jit(solution)/shard_map/ppermute | solution.py:91
  313.9 31.5 %collective-permute-start.22 = (bf16[2,2,104,768]{3,2,0,1:T(8,128)(2,1)}, bf16[2,2,104,768]{3,2,0,1:T(8,128)(2,1)S(1)}, u32[]{:S(2)}, u32[]{:S(2)}) collective-permute-start(bf16[2,2,104,768]{3,2,0,1:T(8,128)(2,1)} %get-tuple-element.242), channel_id=1, source_target_pairs={{0,8},{4,12},{8,0},{12,4},{16,24},{20,28},{24,16},{28,20},{1,9},{5... | collective-permute-start | bytes 1916936 | tf_op jit(solution)/shard_map/ppermute | solution.py:84
  315.4 30.1 %collective-permute-start.23 = (bf16[2,2,104,768]{3,2,0,1:T(8,128)(2,1)}, bf16[2,2,104,768]{3,2,0,1:T(8,128)(2,1)S(1)}, u32[]{:S(2)}, u32[]{:S(2)}) collective-permute-start(bf16[2,2,104,768]{3,2,0,1:T(8,128)(2,1)} %get-tuple-element.241), channel_id=1, source_target_pairs={{0,16},{4,20},{8,24},{12,28},{16,0},{20,4},{24,8},{28,12},{1,17},{... | collective-permute-start | bytes 1916936 | tf_op jit(solution)/shard_map/ppermute | solution.py:84
  317.9 27.5 %collective-permute-start.24 = (bf16[104,768]{1,0:T(8,128)(2,1)S(1)}, bf16[104,768]{1,0:T(8,128)(2,1)S(1)}, u32[]{:S(2)}, u32[]{:S(2)}) collective-permute-start(bf16[104,768]{1,0:T(8,128)(2,1)S(1)} %fusion.19), channel_id=1, source_target_pairs={{0,1},{1,2},{2,3},{3,0},{4,5},{5,6},{6,7},{7,4},{8,9},{9,10},{10,1... | collective-permute-start | bytes 479240 | tf_op jit(solution)/shard_map/ppermute | solution.py:91
  318.5 26.9 %collective-permute-start.25 = (bf16[104,768]{1,0:T(8,128)(2,1)S(1)}, bf16[104,768]{1,0:T(8,128)(2,1)S(1)}, u32[]{:S(2)}, u32[]{:S(2)}) collective-permute-start(bf16[104,768]{1,0:T(8,128)(2,1)S(1)} %fusion.19), channel_id=1, source_target_pairs={{0,2},{1,3},{2,0},{3,1},{4,6},{5,7},{6,4},{7,5},{8,10},{9,11},{10,... | collective-permute-start | bytes 479240 | tf_op jit(solution)/shard_map/ppermute | solution.py:91
  320.5 24.9 %collective-permute-start.26 = (bf16[104,768]{1,0:T(8,128)(2,1)S(1)}, bf16[104,768]{1,0:T(8,128)(2,1)S(1)}, u32[]{:S(2)}, u32[]{:S(2)}) collective-permute-start(bf16[104,768]{1,0:T(8,128)(2,1)S(1)} %fusion.19), channel_id=1, source_target_pairs={{0,3},{1,0},{2,1},{3,2},{4,7},{5,4},{6,5},{7,6},{8,11},{9,8},{10,9... | collective-permute-start | bytes 479240 | tf_op jit(solution)/shard_map/ppermute | solution.py:91
  345.5 32.1 %collective-permute-start.31 = (bf16[4,96,2304]{2,1,0:T(8,128)(2,1)}, bf16[4,96,2304]{2,1,0:T(8,128)(2,1)S(1)}, u32[]{:S(2)}, u32[]{:S(2)}) collective-permute-start(bf16[4,96,2304]{2,1,0:T(8,128)(2,1)} %get-tuple-element.205), channel_id=1, source_target_pairs={{0,4},{4,0},{8,12},{12,8},{16,20},{20,16},{24,28},{28,24},{1,5},{5... | collective-permute-start | bytes 5308424 | tf_op jit(solution)/shard_map/ppermute | solution.py:84
  345.6 17.3 %collective-permute-start.30 = (bf16[1,2,104,768]{3,2,1,0:T(8,128)(2,1)S(1)}, bf16[1,2,104,768]{3,2,1,0:T(8,128)(2,1)S(1)}, u32[]{:S(2)}, u32[]{:S(2)}) collective-permute-start(bf16[1,2,104,768]{3,2,1,0:T(8,128)(2,1)S(1)} %maximum_bitcast_fusion.1), channel_id=1, source_target_pairs={{0,16},{4,20},{8,24},{12,28},{16,0},{20,4},{24,8},{28,12},{1,17},{... | collective-permute-start | bytes 958472 | tf_op jit(solution)/shard_map/ppermute | solution.py:84
  346.8 17.3 %collective-permute-start.29 = (bf16[1,2,104,768]{3,2,1,0:T(8,128)(2,1)S(1)}, bf16[1,2,104,768]{3,2,1,0:T(8,128)(2,1)S(1)}, u32[]{:S(2)}, u32[]{:S(2)}) collective-permute-start(bf16[1,2,104,768]{3,2,1,0:T(8,128)(2,1)S(1)} %maximum_bitcast_fusion), channel_id=1, source_target_pairs={{0,8},{4,12},{8,0},{12,4},{16,24},{20,28},{24,16},{28,20},{1,9},{5... | collective-permute-start | bytes 958472 | tf_op jit(solution)/shard_map/ppermute | solution.py:84
  347.9 29.7 %collective-permute-start.28 = (bf16[2,104,768]{2,1,0:T(8,128)(2,1)S(1)}, bf16[2,104,768]{2,1,0:T(8,128)(2,1)S(1)}, u32[]{:S(2)}, u32[]{:S(2)}) collective-permute-start(bf16[2,104,768]{2,1,0:T(8,128)(2,1)S(1)} %fusion.12), channel_id=1, source_target_pairs={{0,8},{4,12},{8,0},{12,4},{16,24},{20,28},{24,16},{28,20},{1,9},{5... | collective-permute-start | bytes 958472 | tf_op jit(solution)/shard_map/ppermute | solution.py:84
  349.2 28.4 %collective-permute-start.27 = (bf16[2,104,768]{2,1,0:T(8,128)(2,1)S(1)}, bf16[2,104,768]{2,1,0:T(8,128)(2,1)S(1)}, u32[]{:S(2)}, u32[]{:S(2)}) collective-permute-start(bf16[2,104,768]{2,1,0:T(8,128)(2,1)S(1)} %fusion.11), channel_id=1, source_target_pairs={{0,16},{4,20},{8,24},{12,28},{16,0},{20,4},{24,8},{28,12},{1,17},{... | collective-permute-start | bytes 958472 | tf_op jit(solution)/shard_map/ppermute | solution.py:84
  377.6 17.0 %collective-permute-start.36 = (bf16[2,2,104,768]{3,2,1,0:T(8,128)(2,1)S(1)}, bf16[2,2,104,768]{3,2,1,0:T(8,128)(2,1)S(1)}, u32[]{:S(2)}, u32[]{:S(2)}) collective-permute-start(bf16[2,2,104,768]{3,2,1,0:T(8,128)(2,1)S(1)} %pad_maximum_fusion.6), channel_id=1, source_target_pairs={{0,8},{4,12},{8,0},{12,4},{16,24},{20,28},{24,16},{28,20},{1,9},{5... | collective-permute-start | bytes 1916936 | tf_op jit(solution)/shard_map/ppermute | solution.py:84
  378.7 17.7 %collective-permute-start.35 = (bf16[2,2,104,768]{3,2,1,0:T(8,128)(2,1)S(1)}, bf16[2,2,104,768]{3,2,1,0:T(8,128)(2,1)S(1)}, u32[]{:S(2)}, u32[]{:S(2)}) collective-permute-start(bf16[2,2,104,768]{3,2,1,0:T(8,128)(2,1)S(1)} %pad_maximum_fusion.5), channel_id=1, source_target_pairs={{0,16},{4,20},{8,24},{12,28},{16,0},{20,4},{24,8},{28,12},{1,17},{... | collective-permute-start | bytes 1916936 | tf_op jit(solution)/shard_map/ppermute | solution.py:84
  380.3 6.2 %collective-permute-start.32 = (bf16[104,768]{1,0:T(8,128)(2,1)S(1)}, bf16[104,768]{1,0:T(8,128)(2,1)S(1)}, u32[]{:S(2)}, u32[]{:S(2)}) collective-permute-start(bf16[104,768]{1,0:T(8,128)(2,1)S(1)} %get-tuple-element.265), channel_id=1, source_target_pairs={{0,3},{1,0},{2,1},{3,2},{4,7},{5,4},{6,5},{7,6},{8,11},{9,8},{10,9... | collective-permute-start | bytes 479240 | tf_op jit(solution)/shard_map/ppermute | solution.py:91
  380.4 14.2 %collective-permute-start.33 = (bf16[104,768]{1,0:T(8,128)(2,1)S(1)}, bf16[104,768]{1,0:T(8,128)(2,1)S(1)}, u32[]{:S(2)}, u32[]{:S(2)}) collective-permute-start(bf16[104,768]{1,0:T(8,128)(2,1)S(1)} %get-tuple-element.264), channel_id=1, source_target_pairs={{0,2},{1,3},{2,0},{3,1},{4,6},{5,7},{6,4},{7,5},{8,10},{9,11},{10,... | collective-permute-start | bytes 479240 | tf_op jit(solution)/shard_map/ppermute | solution.py:91
  380.9 13.7 %collective-permute-start.34 = (bf16[104,768]{1,0:T(8,128)(2,1)S(1)}, bf16[104,768]{1,0:T(8,128)(2,1)S(1)}, u32[]{:S(2)}, u32[]{:S(2)}) collective-permute-start(bf16[104,768]{1,0:T(8,128)(2,1)S(1)} %get-tuple-element.266), channel_id=1, source_target_pairs={{0,1},{1,2},{2,3},{3,0},{4,5},{5,6},{6,7},{7,4},{8,9},{9,10},{10,1... | collective-permute-start | bytes 479240 | tf_op jit(solution)/shard_map/ppermute | solution.py:91
  396.5 16.9 %collective-permute-start.40 = (bf16[8,2,104,768]{3,2,1,0:T(8,128)(2,1)S(1)}, bf16[8,2,104,768]{3,2,1,0:T(8,128)(2,1)S(1)}, u32[]{:S(2)}, u32[]{:S(2)}) collective-permute-start(bf16[8,2,104,768]{3,2,1,0:T(8,128)(2,1)S(1)} %constant_dynamic-update-slice_fusion.12.refs_1_), channel_id=1, source_target_pairs={{0,4},{4,0},{8,12},{12,8},{16,20},{20,16},{24,28},{28,24},{1,5},{5... | collective-permute-start | bytes 7667720 | tf_op jit(solution)/shard_map/ppermute | solution.py:84
  398.2 35.9 %collective-permute-start.43 = (bf16[2,96,2304]{2,1,0:T(8,128)(2,1)}, bf16[2,96,2304]{2,1,0:T(8,128)(2,1)S(1)}, u32[]{:S(2)}, u32[]{:S(2)}) collective-permute-start(bf16[2,96,2304]{2,1,0:T(8,128)(2,1)} %get-tuple-element.253), channel_id=1, source_target_pairs={{0,8},{4,12},{8,0},{12,4},{16,24},{20,28},{24,16},{28,20},{1,9},{5... | collective-permute-start | bytes 2654216 | tf_op jit(solution)/shard_map/ppermute | solution.py:84
  398.4 8.3 %collective-permute-start.37 = (bf16[104,768]{1,0:T(8,128)(2,1)S(1)}, bf16[104,768]{1,0:T(8,128)(2,1)S(1)}, u32[]{:S(2)}, u32[]{:S(2)}) collective-permute-start(bf16[104,768]{1,0:T(8,128)(2,1)S(1)} %fusion.16), channel_id=1, source_target_pairs={{0,1},{1,2},{2,3},{3,0},{4,5},{5,6},{6,7},{7,4},{8,9},{9,10},{10,1... | collective-permute-start | bytes 479240 | tf_op jit(solution)/shard_map/ppermute | solution.py:91
  400.0 13.3 %collective-permute-start.38 = (bf16[104,768]{1,0:T(8,128)(2,1)S(1)}, bf16[104,768]{1,0:T(8,128)(2,1)S(1)}, u32[]{:S(2)}, u32[]{:S(2)}) collective-permute-start(bf16[104,768]{1,0:T(8,128)(2,1)S(1)} %fusion.16), channel_id=1, source_target_pairs={{0,2},{1,3},{2,0},{3,1},{4,6},{5,7},{6,4},{7,5},{8,10},{9,11},{10,... | collective-permute-start | bytes 479240 | tf_op jit(solution)/shard_map/ppermute | solution.py:91
  403.0 10.3 %collective-permute-start.39 = (bf16[104,768]{1,0:T(8,128)(2,1)S(1)}, bf16[104,768]{1,0:T(8,128)(2,1)S(1)}, u32[]{:S(2)}, u32[]{:S(2)}) collective-permute-start(bf16[104,768]{1,0:T(8,128)(2,1)S(1)} %fusion.16), channel_id=1, source_target_pairs={{0,3},{1,0},{2,1},{3,2},{4,7},{5,4},{6,5},{7,6},{8,11},{9,8},{10,9... | collective-permute-start | bytes 479240 | tf_op jit(solution)/shard_map/ppermute | solution.py:91
  415.0 19.1 %collective-permute-start.42 = (bf16[1,2,104,768]{3,2,1,0:T(8,128)(2,1)S(1)}, bf16[1,2,104,768]{3,2,1,0:T(8,128)(2,1)S(1)}, u32[]{:S(2)}, u32[]{:S(2)}) collective-permute-start(bf16[1,2,104,768]{3,2,1,0:T(8,128)(2,1)S(1)} %maximum_bitcast_fusion.3), channel_id=1, source_target_pairs={{0,16},{4,20},{8,24},{12,28},{16,0},{20,4},{24,8},{28,12},{1,17},{... | collective-permute-start | bytes 958472 | tf_op jit(solution)/shard_map/ppermute | solution.py:84
  417.6 23.1 %collective-permute-start.41 = (bf16[1,2,104,768]{3,2,1,0:T(8,128)(2,1)S(1)}, bf16[1,2,104,768]{3,2,1,0:T(8,128)(2,1)S(1)}, u32[]{:S(2)}, u32[]{:S(2)}) collective-permute-start(bf16[1,2,104,768]{3,2,1,0:T(8,128)(2,1)S(1)} %maximum_bitcast_fusion.2), channel_id=1, source_target_pairs={{0,8},{4,12},{8,0},{12,4},{16,24},{20,28},{24,16},{28,20},{1,9},{5... | collective-permute-start | bytes 958472 | tf_op jit(solution)/shard_map/ppermute | solution.py:84
  440.8 35.1 %collective-permute-start.45 = (bf16[2,2,104,768]{3,2,1,0:T(8,128)(2,1)S(1)}, bf16[2,2,104,768]{3,2,1,0:T(8,128)(2,1)S(1)}, u32[]{:S(2)}, u32[]{:S(2)}) collective-permute-start(bf16[2,2,104,768]{3,2,1,0:T(8,128)(2,1)S(1)} %pad_maximum_fusion.8), channel_id=1, source_target_pairs={{0,8},{4,12},{8,0},{12,4},{16,24},{20,28},{24,16},{28,20},{1,9},{5... | collective-permute-start | bytes 1916936 | tf_op jit(solution)/shard_map/ppermute | solution.py:84
  441.2 34.7 %copy-start.26 = (bf16[104,768]{1,0:T(8,128)(2,1)S(1)}, bf16[104,768]{1,0:T(8,128)(2,1)}, u32[]{:S(2)}) copy-start(bf16[104,768]{1,0:T(8,128)(2,1)} %copy-done.25) | copy-start | bytes 479236
  441.2 34.7 %copy-start.28 = (bf16[104,768]{1,0:T(8,128)(2,1)S(1)}, bf16[104,768]{1,0:T(8,128)(2,1)}, u32[]{:S(2)}) copy-start(bf16[104,768]{1,0:T(8,128)(2,1)} %copy-done.27) | copy-start | bytes 479236
  441.2 34.6 %collective-permute-start.44 = (bf16[2,2,104,768]{3,2,1,0:T(8,128)(2,1)S(1)}, bf16[2,2,104,768]{3,2,1,0:T(8,128)(2,1)S(1)}, u32[]{:S(2)}, u32[]{:S(2)}) collective-permute-start(bf16[2,2,104,768]{3,2,1,0:T(8,128)(2,1)S(1)} %pad_maximum_fusion.7), channel_id=1, source_target_pairs={{0,16},{4,20},{8,24},{12,28},{16,0},{20,4},{24,8},{28,12},{1,17},{... | collective-permute-start | bytes 1916936 | tf_op jit(solution)/shard_map/ppermute | solution.py:84
  443.9 32.1 %copy-start.19 = (bf16[1,2,104,768]{3,2,1,0:T(8,128)(2,1)S(1)}, bf16[1,2,104,768]{3,2,1,0:T(8,128)(2,1)}, u32[]{:S(2)}) copy-start(bf16[1,2,104,768]{3,2,1,0:T(8,128)(2,1)} %copy-done.18) | copy-start | bytes 958468
  443.9 14.0 %collective-permute-start.47 = (bf16[96,2304]{1,0:T(8,128)(2,1)S(1)}, bf16[96,2304]{1,0:T(8,128)(2,1)S(1)}, u32[]{:S(2)}, u32[]{:S(2)}) collective-permute-start(bf16[96,2304]{1,0:T(8,128)(2,1)S(1)} %get-tuple-element.228), channel_id=1, source_target_pairs={{0,3},{1,0},{2,1},{3,2},{4,7},{5,4},{6,5},{7,6},{8,11},{9,8},{10,9... | collective-permute-start | bytes 1327112 | tf_op jit(solution)/shard_map/ppermute | solution.py:91
  447.3 28.6 %collective-permute-start.46 = (bf16[96,2304]{1,0:T(8,128)(2,1)S(1)}, bf16[96,2304]{1,0:T(8,128)(2,1)S(1)}, u32[]{:S(2)}, u32[]{:S(2)}) collective-permute-start(bf16[96,2304]{1,0:T(8,128)(2,1)S(1)} %get-tuple-element.227), channel_id=1, source_target_pairs={{0,2},{1,3},{2,0},{3,1},{4,6},{5,7},{6,4},{7,5},{8,10},{9,11},{10,... | collective-permute-start | bytes 1327112 | tf_op jit(solution)/shard_map/ppermute | solution.py:91
  447.3 29.3 %copy-start.6 = (bf16[512,768]{1,0:T(8,128)(2,1)S(1)}, bf16[512,768]{1,0:T(8,128)(2,1)}, u32[]{:S(2)}) copy-start(bf16[512,768]{1,0:T(8,128)(2,1)} %get-tuple-element.146.refs_1_) | copy-start | bytes 2359300
  447.3 29.3 %copy-start.24 = (bf16[512,768]{1,0:T(8,128)(2,1)S(1)}, bf16[512,768]{1,0:T(8,128)(2,1)}, u32[]{:S(2)}) copy-start(bf16[512,768]{1,0:T(8,128)(2,1)} %get-tuple-element.153) | copy-start | bytes 2359300
  476.1 4.9 collective-permute-start.48
  482.4 14.3 %collective-permute-start.49 = (bf16[96,2304]{1,0:T(8,128)(2,1)}, bf16[96,2304]{1,0:T(8,128)(2,1)}, u32[]{:S(2)}, u32[]{:S(2)}) collective-permute-start(bf16[96,2304]{1,0:T(8,128)(2,1)} %get-tuple-element.237), channel_id=1, source_target_pairs={{0,1},{1,2},{2,3},{3,0},{4,5},{5,6},{6,7},{7,4},{8,9},{9,10},{10,1... | collective-permute-start | bytes 1327112 | tf_op jit(solution)/shard_map/ppermute | solution.py:91
  483.2 15.2 %collective-permute-start.50 = (bf16[1,96,2304]{2,1,0:T(8,128)(2,1)S(1)}, bf16[1,96,2304]{2,1,0:T(8,128)(2,1)}, u32[]{:S(2)}, u32[]{:S(2)}) collective-permute-start(bf16[1,96,2304]{2,1,0:T(8,128)(2,1)S(1)} %add_convert_fusion.10), channel_id=1, source_target_pairs={{0,16},{4,20},{8,24},{12,28},{16,0},{20,4},{24,8},{28,12},{1,17},{... | collective-permute-start | bytes 1327112 | tf_op jit(solution)/shard_map/ppermute | solution.py:84
  (39 other events, 253.2 us)
Sparse Core Ops, SparseCore 0:
  38.7 46.4 all-gather.8
  87.9 66.0 all-gather.10
  155.6 63.4 all-gather.12
  220.5 62.1 all-gather.14
  293.6 136.7 reduce-scatter.1

commit v5 on v4

--- a/solution.py
+++ b/solution.py
@@ -1046,12 +1046,12 @@
     small = {1: found[0]}
     line.need(ff[0], fold.got)
     last_share.gathered.second()
-    ff_parts = {0: [ff[0][0], to_owner(0, 1), to_owner(0, 2)]}
+    ff_parts = {0: [ff[0][0], to_owner(0, 2), to_owner(0, 3)]}
     fold.second()
     line.sync()
     last_share.gathered.core()
     line.sync()
-    ff_parts[0].append(to_owner(0, 3))
+    ff_parts[0].append(to_owner(0, 1))
     rest = found[1:]
     found = line.run(
         lambda first: spread_out(0, dz_at, [first] + last_share.gathered.pieces()[1:], rest),

time: 515 us -> 514 us (level)
  no operation moved by 1% of the time
where the time goes in v5:
time: 514 us; the launch traced here: 509 us
  Pallas kernels  211 us (41%)
  waiting for transfers between devices  152 us (30%)
  starting transfers between devices  63.9 us (12%)
  local copies, waits for them, and re-layouts  39.9 us (8%)
  other arithmetic  27 us (5%)
  between operations  15.6 us (3%)
    pallas_call x15, Pallas kernels, staged(): pl.pallas_call(functools.partial(staged_kernel, body, layers, len(smem),...  211 us
    ppermute x33, waiting for transfers between devices, flip(): got = lax.ppermute(value, 'dp', [(i, i ^ bit) for i in range(self.n_dp)])  81.3 us
    ppermute x18, waiting for transfers between devices, shift(): got = lax.ppermute(value, 'tensor', [(i, (i + step) % n) for i in range(n)])  60.4 us
    ppermute x33, starting transfers between devices, flip(): got = lax.ppermute(value, 'dp', [(i, i ^ bit) for i in range(self.n_dp)])  31.2 us
    ppermute x18, starting transfers between devices, shift(): got = lax.ppermute(value, 'tensor', [(i, (i + step) % n) for i in range(n)])  31 us
    unnamed x115, local copies, waits for them, and re-layouts  19.5 us
  transfers between devices with their start and end apart: 56, of which 22 were waited for; matrix products, arithmetic and copies ran while one was open for 10% of the time, Pallas kernels for 41%

profile of v5, /device:TPU:0, one launch (start us, length us, event | category | flops | bytes accessed | tf_op | source)
XLA Modules:
  0.0 509.0 jit_solution(16445802146636293313)
XLA Ops:
  9.8 3.1 collective-permute-start
  12.9 2.1 collective-permute-start.1
  20.3 14.4 %attn_fwd.2 = (bf16[512,2304]{1,0:T(8,128)(2,1)}, f32[512,128]{1,0:T(8,128)}, bf16[512,768]{1,0:T(8,128)(2,1)}, bf16[768,512]{1,0:T(8,128)(2,1)}, f32[512,768]{1...) custom-call(f32[12]{0:T(128)} %multiply_exponential_fusion.refs_0_, bf16[512,768]{1,0:T(8,128)(2,1)} %refs_1_.1, ...), custom_call_target="tpu_custom_call" | custom-call | flops 1024 | bytes 1024 | tf_op jit(solution)/shard_map/attn_fwd/pallas_call | solution.py:249
  39.1 7.1 %fusion.48 = (bf16[1,768,2,768]{3,2,1,0:T(2,128)(2,1)}, bf16[1,768,2,768]{3,2,1,0:T(2,128)(2,1)S(1)}) fusion(bf16[2,768,2,768]{3,2,1,0:T(2,128)(2,1)} %param.19), kind=kLoop, calls=%fused_computation.170 | loop fusion | bytes 9437184 | tf_op jit(solution)/shard_map/slice | solution.py:905
  46.2 1.9 copy.59
  48.5 1.6 slice_bitcast_fusion
  50.1 6.5 %ff_fwd.5.refs_2_ = f32[512,768]{1,0:T(8,128)} custom-call(s32[1]{0:T(128)} %bitcast.refs_0_.refs_1_, bf16[512,768]{1,0:T(8,128)(2,1)} %get-tuple-element.170.refs_1_, f32[512,768]{1,0:T(8,128)} %get-tuple-element.128.refs_2_.refs_6_, f32[1,768]{1,0:T(1,128)} %get-tuple-element.284.refs_5_.refs_3_.refs_7_, f32[1,768]{1,0:T(1,128)} %get-tuple-element.281.refs_6_.refs_4_, ...), custom_call_target="tpu_custom_call" | custom-call | flops 1024 | bytes 1024 | tf_op jit(solution)/shard_map/ff_fwd/pallas_call | solution.py:249
  59.4 1.6 collective-permute-start.8
  61.0 1.7 collective-permute-start.7
  62.8 20.7 %collective-permute-done.8 = bf16[1,1,48,2304]{3,2,1,0:T(8,128)(2,1)S(1)} collective-permute-done((bf16[1,1,48,2304]{3,2,1,0:T(8,128)(2,1)S(1)}, bf16[1,1,48,2304]{3,2,1,0:T(8,128)(2,1)S(1)}, u32[]{:S(2)}, u32[]{:S(2)}) %collective-permute-start.8) | collective-permute-done | bytes 221216 | tf_op jit(solution)/shard_map/ppermute | solution.py:84
  83.5 1.7 all-gather.9.cloned.1.call-done
  89.6 1.5 collective-permute-start.11
  91.2 1.5 collective-permute-start.10
  94.2 13.2 %collective-permute-done.11 = bf16[2,1,48,2304]{3,2,1,0:T(8,128)(2,1)S(1)} collective-permute-done((bf16[2,1,48,2304]{3,2,1,0:T(8,128)(2,1)S(1)}, bf16[2,1,48,2304]{3,2,1,0:T(8,128)(2,1)S(1)}, u32[]{:S(2)}, u32[]{:S(2)}) %collective-permute-start.11) | collective-permute-done | bytes 442400 | tf_op jit(solution)/shard_map/ppermute | solution.py:84
  107.3 2.4 collective-permute-done.10
  113.3 1.9 copy.61
  115.8 9.8 %ff_fwd.6.refs_2_ = f32[512,768]{1,0:T(8,128)} custom-call(s32[1]{0:T(128)} %bitcast.refs_0_.refs_1_, bf16[512,768]{1,0:T(8,128)(2,1)} %get-tuple-element.170.refs_1_, f32[512,768]{1,0:T(8,128)} %ff_fwd.5.refs_2_, bf16[8,1,96,2304]{3,2,1,0:T(8,128)(2,1)} %copy-done, bf16[8,1,96,2304]{3,2,1,0:T(8,128)(2,1)} %copy-done.1), custom_call_target="tpu_custom_call" | custom-call | flops 1024 | bytes 1024 | tf_op jit(solution)/shard_map/ff_fwd/pallas_call | solution.py:249
  125.6 6.8 %ff_fwd.7 = (f32[512,768]{1,0:T(8,128)}, bf16[512,768]{1,0:T(8,128)(2,1)}, bf16[768,512]{1,0:T(8,128)(2,1)}) custom-call(s32[1]{0:T(128)} %bitcast.refs_0_.refs_1_, bf16[512,768]{1,0:T(8,128)(2,1)} %get-tuple-element.170.refs_1_, f32[512,768]{1,0:T(8,128)} %ff_fwd.6.refs_2_, f32[1,768]{1,0:T(1,128)} %get-tuple-element.286.refs_3_.refs_5_, ...), custom_call_target="tpu_custom_call" | custom-call | flops 1024 | bytes 1024 | tf_op jit(solution)/shard_map/ff_fwd/pallas_call | solution.py:249
  132.5 14.4 %attn_fwd.3 = (bf16[512,2304]{1,0:T(8,128)(2,1)}, f32[512,128]{1,0:T(8,128)}, bf16[512,768]{1,0:T(8,128)(2,1)}, bf16[768,512]{1,0:T(8,128)(2,1)}, f32[512,768]{1...) custom-call(f32[12]{0:T(128)} %multiply_exponential_fusion.refs_0_, ...), custom_call_target="tpu_custom_call" | custom-call | flops 1024 | bytes 1024 | tf_op jit(solution)/shard_map/attn_fwd/pallas_call | solution.py:249
  146.9 6.2 %ff_fwd.8.refs_2_ = f32[512,768]{1,0:T(8,128)} custom-call(s32[1]{0:T(128)} %bitcast.refs_0_.refs_1_, bf16[512,768]{1,0:T(8,128)(2,1)} %get-tuple-element.155.refs_1_, f32[512,768]{1,0:T(8,128)} %get-tuple-element.150.refs_2_.refs_5_, f32[1,768]{1,0:T(1,128)} %get-tuple-element.285.refs_5_.refs_3_.refs_6_, f32[1,768]{1,0:T(1,128)} %get-tuple-element.280.refs_6_.refs_4_, ...), custom_call_target="tpu_custom_call" | custom-call | flops 1024 | bytes 1024 | tf_op jit(solution)/shard_map/ff_fwd/pallas_call | solution.py:249
  154.5 13.4 %ff_fwd.9 = (f32[512,768]{1,0:T(8,128)}, bf16[512,768]{1,0:T(8,128)(2,1)}, bf16[768,512]{1,0:T(8,128)(2,1)}) custom-call(s32[1]{0:T(128)} %bitcast.refs_0_.refs_1_, bf16[512,768]{1,0:T(8,128)(2,1)} %get-tuple-element.155.refs_1_, f32[512,768]{1,0:T(8,128)} %ff_fwd.8.refs_2_, f32[1,768]{1,0:T(1,128)} %get-tuple-element.287.refs_3_.refs_4_, ...), custom_call_target="tpu_custom_call" | custom-call | flops 1024 | bytes 1024 | tf_op jit(solution)/shard_map/ff_fwd/pallas_call | solution.py:249
  167.9 23.1 %ff_bwd.3 = (f32[512,768]{1,0:T(8,128)}, bf16[512,768]{1,0:T(8,128)(2,1)}, bf16[768,512]{1,0:T(8,128)(2,1)}, f32[2,768]{1,0:T(2,128)}, bf16[512,768]{1,0:T(8,128)(2,1)}, /*index=5*/f32[2,768]{1,0:T(2,128)}) custom-call(s32[1]{0:T(128)} %bitcast.refs_0_.refs_1_, bf16[512,768]{1,0:T(8,128)(2,1)} %get-tuple-element.155.refs_1_, bf16[512,768]{1,0:T(8,128)(2,1)} %refs_2_.5, ...), custom_call_target="tpu_custom_call" | custom-call | flops 1024 | bytes 1024 | tf_op jit(solution)/shard_map/ff_bwd/pallas_call | solution.py:249
  191.0 20.9 %attn_bwd.2 = (bf16[4,4,104,768]{3,2,1,0:T(8,128)(2,1)}, bf16[4,4,104,768]{3,2,1,0:T(8,128)(2,1)}, f32[512,768]{1,0:T(8,128)}) custom-call(f32[12]{0:T(128)} %multiply_exponential_fusion.refs_0_, s32[1]{0:T(128)} %bitcast.refs_0_.refs_1_, bf16[512,768]{1,0:T(8,128)(2,1)} %get-tuple-element.158.refs_2_, bf16[2,768,768]{2,1,0:T(8,128)(2,1)} %refs_3_.3, ...), custom_call_target="tpu_custom_call" | custom-call | flops 1024 | bytes 1024 | tf_op jit(solution)/shard_map/attn_bwd/pallas_call | solution.py:249
  211.9 7.3 %all-gather.13.cloned.1.call-done = bf16[2048,768]{1,0:T(8,128)(2,1)} async-done(((bf16[512,768]{1,0:T(8,128)(2,1)}), bf16[2048,768]{1,0:T(8,128)(2,1)}) %all-gather.13.cloned.1.call-update) | async-done | bytes 3145744 | tf_op jit(solution)/shard_map/all_gather | solution.py:963
  219.6 1.9 copy.47
  221.6 13.3 %ff_bwd.4 = (f32[512,768]{1,0:T(8,128)}, bf16[512,768]{1,0:T(8,128)(2,1)}, bf16[768,512]{1,0:T(8,128)(2,1)}, f32[2,768]{1,0:T(2,128)}, bf16[8,4,96,2304]{3,2,1,0:T(8,128)(2,1)}) custom-call(s32[1]{0:T(128)} %bitcast.refs_0_.refs_1_, bf16[512,768]{1,0:T(8,128)(2,1)} %get-tuple-element.170.refs_1_, bf16[768,512]{1,0:T(8,128)(2,1)} %get-tuple-element.166.refs_2_, ...), custom_call_target="tpu_custom_call" | custom-call | flops 1024 | bytes 1024 | tf_op jit(solution)/shard_map/ff_bwd/pallas_call | solution.py:249
  234.8 4.1 add_convert_fusion.6
  241.9 25.7 %ff_bwd.5 = (f32[512,768]{1,0:T(8,128)}, bf16[512,768]{1,0:T(8,128)(2,1)}, f32[2,768]{1,0:T(2,128)}, bf16[8,4,96,2304]{3,2,1,0:T(8,128)(2,1)}) custom-call(s32[1]{0:T(128)} %bitcast.refs_0_.refs_1_, bf16[512,768]{1,0:T(8,128)(2,1)} %get-tuple-element.170.refs_1_, bf16[768,512]{1,0:T(8,128)(2,1)} %get-tuple-element.166.refs_2_, ...), custom_call_target="tpu_custom_call", output_to_operand_aliasing={{3}: (12, {})} | custom-call | flops 1024 | bytes 1024 | tf_op jit(solution)/shard_map/ff_bwd/pallas_call | solution.py:249
  271.6 21.0 %attn_bwd.3 = (bf16[4,4,104,768]{3,2,1,0:T(8,128)(2,1)}, bf16[4,4,104,768]{3,2,1,0:T(8,128)(2,1)}, f32[512,768]{1,0:T(8,128)}) custom-call(f32[12]{0:T(128)} %multiply_exponential_fusion.refs_0_, s32[1]{0:T(128)} %bitcast.refs_0_.refs_1_, bf16[512,768]{1,0:T(8,128)(2,1)} %get-tuple-element.178.refs_2_, bf16[2,768,768]{2,1,0:T(8,128)(2,1)} %refs_3_.3, ...), custom_call_target="tpu_custom_call" | custom-call | flops 1024 | bytes 1024 | tf_op jit(solution)/shard_map/attn_bwd/pallas_call | solution.py:249
  293.5 1.7 copy-done.8
  298.4 1.9 collective-permute-start.21
  300.3 3.3 collective-permute-done.19
  303.6 8.6 %collective-permute-done.20 = bf16[104,768]{1,0:T(8,128)(2,1)S(1)} collective-permute-done((bf16[104,768]{1,0:T(8,128)(2,1)S(1)}, bf16[104,768]{1,0:T(8,128)(2,1)S(1)}, u32[]{:S(2)}, u32[]{:S(2)}) %collective-permute-start.20) | collective-permute-done | bytes 159776 | tf_op jit(solution)/shard_map/ppermute | solution.py:91
  312.2 1.7 add_convert_fusion.2
  318.5 2.0 collective-permute-start.25
  320.5 3.2 collective-permute-start.26
  323.8 21.6 %ff_grads.1 = (bf16[4,96,2304]{2,1,0:T(8,128)(2,1)}, bf16[4,96,2304]{2,1,0:T(8,128)(2,1)}) custom-call(s32[1]{0:T(128)} %bitcast.refs_0_.refs_1_, bf16[768,1536]{1,0:T(8,128)(2,1)} %bitcast.159, bf16[768,768]{1,0:T(8,128)(2,1)} %get-tuple-element.254.refs_6_.refs_8_.refs_2_, bf16[4,512,768]{2,1,0:T(8,128)(2,1)} %bitcast.147, bf16[4,512,768]{2,1,0:T(8,128)(2,1)} %bitcast.151, ...), custom_call_target="tpu_custom_call" | custom-call | flops 1024 | bytes 1024 | tf_op jit(solution)/shard_map/ff_grads/pallas_call | solution.py:249
  350.1 12.8 %collective-permute-done.30 = bf16[1,2,104,768]{3,2,1,0:T(8,128)(2,1)S(1)} collective-permute-done((bf16[1,2,104,768]{3,2,1,0:T(8,128)(2,1)S(1)}, bf16[1,2,104,768]{3,2,1,0:T(8,128)(2,1)S(1)}, u32[]{:S(2)}, u32[]{:S(2)}) %collective-permute-start.30) | collective-permute-done | bytes 319520 | tf_op jit(solution)/shard_map/ppermute | solution.py:84
  364.1 13.4 %collective-permute-done.28 = bf16[2,104,768]{2,1,0:T(8,128)(2,1)S(1)} collective-permute-done((bf16[2,104,768]{2,1,0:T(8,128)(2,1)S(1)}, bf16[2,104,768]{2,1,0:T(8,128)(2,1)S(1)}, u32[]{:S(2)}, u32[]{:S(2)}) %collective-permute-start.28) | collective-permute-done | bytes 319520 | tf_op jit(solution)/shard_map/ppermute | solution.py:84
  380.9 1.9 collective-permute-start.34
  382.9 3.5 collective-permute-done.32
  386.5 8.1 %collective-permute-done.33 = bf16[104,768]{1,0:T(8,128)(2,1)S(1)} collective-permute-done((bf16[104,768]{1,0:T(8,128)(2,1)S(1)}, bf16[104,768]{1,0:T(8,128)(2,1)S(1)}, u32[]{:S(2)}, u32[]{:S(2)}) %collective-permute-start.33) | collective-permute-done | bytes 159776 | tf_op jit(solution)/shard_map/ppermute | solution.py:91
  394.6 1.7 collective-permute-done.35
  396.6 1.7 add_convert_fusion
  398.4 1.6 collective-permute-start.37
  400.0 3.0 collective-permute-start.38
  403.0 2.8 collective-permute-start.39
  406.7 6.7 %collective-permute-done.38 = bf16[104,768]{1,0:T(8,128)(2,1)S(1)} collective-permute-done((bf16[104,768]{1,0:T(8,128)(2,1)S(1)}, bf16[104,768]{1,0:T(8,128)(2,1)S(1)}, u32[]{:S(2)}, u32[]{:S(2)}) %collective-permute-start.38) | collective-permute-done | bytes 159776 | tf_op jit(solution)/shard_map/ppermute | solution.py:91
  415.0 2.5 collective-permute-start.42
  417.6 1.8 collective-permute-start.41
  420.0 7.0 %spread_out.2 = (f32[4,8,768]{2,1,0:T(8,128)}, f32[2,768,2304]{2,1,0:T(8,128)}, f32[2,768,768]{2,1,0:T(8,128)}) custom-call(s32[2]{0:T(128)} %pad_add_fusion.refs_0_, bf16[8,2,104,768]{3,2,1,0:T(8,128)(2,1)} %copy-done.3, bf16[8,2,104,768]{3,2,1,0:T(8,128)(2,1)} %copy-done.9), custom_call_target="tpu_custom_call" | custom-call | flops 1024 | bytes 1024 | tf_op jit(solution)/shard_map/spread_out/pallas_call | solution.py:249
  427.0 7.1 %collective-permute-done.43 = bf16[2,96,2304]{2,1,0:T(8,128)(2,1)S(1)} collective-permute-done((bf16[2,96,2304]{2,1,0:T(8,128)(2,1)}, bf16[2,96,2304]{2,1,0:T(8,128)(2,1)S(1)}, u32[]{:S(2)}, u32[]{:S(2)}) %collective-permute-start.43) | collective-permute-done | bytes 884768 | tf_op jit(solution)/shard_map/ppermute | solution.py:84
  434.1 6.6 %collective-permute-done.41 = bf16[1,2,104,768]{3,2,1,0:T(8,128)(2,1)S(1)} collective-permute-done((bf16[1,2,104,768]{3,2,1,0:T(8,128)(2,1)S(1)}, bf16[1,2,104,768]{3,2,1,0:T(8,128)(2,1)S(1)}, u32[]{:S(2)}, u32[]{:S(2)}) %collective-permute-start.41) | collective-permute-done | bytes 319520 | tf_op jit(solution)/shard_map/ppermute | solution.py:84
  441.2 1.8 collective-permute-start.44
  443.9 1.5 collective-permute-start.47
  445.4 2.3 collective-permute-start.46
  448.9 10.0 %collective-permute-done.47 = bf16[96,2304]{1,0:T(8,128)(2,1)S(1)} collective-permute-done((bf16[96,2304]{1,0:T(8,128)(2,1)S(1)}, bf16[96,2304]{1,0:T(8,128)(2,1)S(1)}, u32[]{:S(2)}, u32[]{:S(2)}) %collective-permute-start.47) | collective-permute-done | bytes 442400 | tf_op jit(solution)/shard_map/ppermute | solution.py:91
  458.9 7.7 %collective-permute-done.46 = bf16[96,2304]{1,0:T(8,128)(2,1)S(1)} collective-permute-done((bf16[96,2304]{1,0:T(8,128)(2,1)S(1)}, bf16[96,2304]{1,0:T(8,128)(2,1)S(1)}, u32[]{:S(2)}, u32[]{:S(2)}) %collective-permute-start.46) | collective-permute-done | bytes 442400 | tf_op jit(solution)/shard_map/ppermute | solution.py:91
  469.8 2.0 collective-permute-done.48.refs_2_
  473.2 2.0 collective-permute-start.49
  475.9 6.9 %spread_out.3 = (f32[4,8,768]{2,1,0:T(8,128)}, f32[2,768,2304]{2,1,0:T(8,128)}, f32[2,768,768]{2,1,0:T(8,128)}) custom-call(s32[2]{0:T(128)} %pad_add_fusion.refs_0_, bf16[8,2,104,768]{3,2,1,0:T(8,128)(2,1)} %copy-done.4, bf16[8,2,104,768]{3,2,1,0:T(8,128)(2,1)} %copy-done.13, ...), custom_call_target="tpu_custom_call", output_to_operand_aliasing={{1}: (3, {}), {2}: (4, {})} | custom-call | flops 1024 | bytes 1024 | tf_op jit(solution)/shard_map/spread_out/pallas_call | solution.py:249
  484.5 11.6 %collective-permute-done.49 = bf16[96,2304]{1,0:T(8,128)(2,1)} collective-permute-done((bf16[96,2304]{1,0:T(8,128)(2,1)}, bf16[96,2304]{1,0:T(8,128)(2,1)}, u32[]{:S(2)}, u32[]{:S(2)}) %collective-permute-start.49) | collective-permute-done | bytes 442400 | tf_op jit(solution)/shard_map/ppermute | solution.py:91
  496.1 1.6 fusion.1
  500.7 1.6 pad_maximum_fusion.2
  (254 shorter events, 67.1 us)
Async XLA Ops:
  7.2 78.0 %all-gather.9.cloned.1.call-start = ((), (), s32[]{:S(2)}) async-start(), calls=%async_computation.2 | async-start | bytes 2211840 | tf_op jit(solution)/shard_map/all_gather | solution.py:928
  9.8 25.7 %collective-permute-start = (bf16[96,2304]{1,0:T(8,128)(2,1)S(1)}, bf16[96,2304]{1,0:T(8,128)(2,1)S(1)}, u32[]{:S(2)}, u32[]{:S(2)}) collective-permute-start(bf16[96,2304]{1,0:T(8,128)(2,1)S(1)} %pad_maximum_fusion.10), channel_id=1, source_target_pairs={{0,1},{1,2},{2,3},{3,0},{4,5},{5,6},{6,7},{7,4},{8,9},{9,10},{10,1... | collective-permute-start | bytes 1327112 | tf_op jit(solution)/shard_map/ppermute | solution.py:91
  12.9 22.7 %collective-permute-start.1 = (bf16[96,2304]{1,0:T(8,128)(2,1)S(1)}, bf16[96,2304]{1,0:T(8,128)(2,1)S(1)}, u32[]{:S(2)}, u32[]{:S(2)}) collective-permute-start(bf16[96,2304]{1,0:T(8,128)(2,1)S(1)} %pad_maximum_fusion.10), channel_id=1, source_target_pairs={{0,3},{1,0},{2,1},{3,2},{4,7},{5,4},{6,5},{7,6},{8,11},{9,8},{10,9... | collective-permute-start | bytes 1327112 | tf_op jit(solution)/shard_map/ppermute | solution.py:91
  15.0 41.6 %collective-permute-start.4 = (bf16[96,2304]{1,0:T(8,128)(2,1)S(1)}, bf16[96,2304]{1,0:T(8,128)(2,1)S(1)}, u32[]{:S(2)}, u32[]{:S(2)}) collective-permute-start(bf16[96,2304]{1,0:T(8,128)(2,1)S(1)} %pad_maximum_fusion.10), channel_id=1, source_target_pairs={{0,2},{1,3},{2,0},{3,1},{4,6},{5,7},{6,4},{7,5},{8,10},{9,11},{10,... | collective-permute-start | bytes 1327112 | tf_op jit(solution)/shard_map/ppermute | solution.py:91
  35.6 21.1 %collective-permute-start.2 = (bf16[1,1,96,2304]{3,2,1,0:T(8,128)(2,1)S(1)}, bf16[1,1,96,2304]{3,2,1,0:T(8,128)(2,1)S(1)}, u32[]{:S(2)}, u32[]{:S(2)}) collective-permute-start(bf16[1,1,96,2304]{3,2,1,0:T(8,128)(2,1)S(1)} %bitcast.172), channel_id=1, source_target_pairs={{0,8},{4,12},{8,0},{12,4},{16,24},{20,28},{24,16},{28,20},{1,9},{5... | collective-permute-start | bytes 1327112 | tf_op jit(solution)/shard_map/ppermute | solution.py:84
  37.1 19.6 %collective-permute-start.3 = (bf16[1,1,96,2304]{3,2,1,0:T(8,128)(2,1)S(1)}, bf16[1,1,96,2304]{3,2,1,0:T(8,128)(2,1)S(1)}, u32[]{:S(2)}, u32[]{:S(2)}) collective-permute-start(bf16[1,1,96,2304]{3,2,1,0:T(8,128)(2,1)S(1)} %bitcast.170), channel_id=1, source_target_pairs={{0,16},{4,20},{8,24},{12,28},{16,0},{20,4},{24,8},{28,12},{1,17},{... | collective-permute-start | bytes 1327112 | tf_op jit(solution)/shard_map/ppermute | solution.py:84
  38.6 115.4 %all-gather.11.cloned.1.call-start = ((), (), s32[]{:S(2)}) async-start(), calls=%async_computation.3 | async-start | bytes 11943936 | tf_op jit(solution)/shard_map/all_gather | solution.py:944
  57.6 25.9 %collective-permute-start.6 = (bf16[2,1,96,2304]{3,2,1,0:T(8,128)(2,1)}, bf16[2,1,96,2304]{3,2,1,0:T(8,128)(2,1)S(1)}, u32[]{:S(2)}, u32[]{:S(2)}) collective-permute-start(bf16[2,1,96,2304]{3,2,1,0:T(8,128)(2,1)} %pad_maximum_fusion.4), channel_id=1, source_target_pairs={{0,8},{4,12},{8,0},{12,4},{16,24},{20,28},{24,16},{28,20},{1,9},{5... | collective-permute-start | bytes 2654216 | tf_op jit(solution)/shard_map/ppermute | solution.py:84
  58.9 24.6 %collective-permute-start.5 = (bf16[2,1,96,2304]{3,2,1,0:T(8,128)(2,1)}, bf16[2,1,96,2304]{3,2,1,0:T(8,128)(2,1)}, u32[]{:S(2)}, u32[]{:S(2)}) collective-permute-start(bf16[2,1,96,2304]{3,2,1,0:T(8,128)(2,1)} %pad_maximum_fusion.3), channel_id=1, source_target_pairs={{0,16},{4,20},{8,24},{12,28},{16,0},{20,4},{24,8},{28,12},{1,17},{... | collective-permute-start | bytes 2654216 | tf_op jit(solution)/shard_map/ppermute | solution.py:84
  59.4 24.1 %collective-permute-start.8 = (bf16[1,1,48,2304]{3,2,1,0:T(8,128)(2,1)S(1)}, bf16[1,1,48,2304]{3,2,1,0:T(8,128)(2,1)S(1)}, u32[]{:S(2)}, u32[]{:S(2)}) collective-permute-start(bf16[1,1,48,2304]{3,2,1,0:T(8,128)(2,1)S(1)} %bitcast.166), channel_id=1, source_target_pairs={{0,16},{4,20},{8,24},{12,28},{16,0},{20,4},{24,8},{28,12},{1,17},{... | collective-permute-start | bytes 663560 | tf_op jit(solution)/shard_map/ppermute | solution.py:84
  61.0 22.5 %collective-permute-start.7 = (bf16[1,1,48,2304]{3,2,1,0:T(8,128)(2,1)S(1)}, bf16[1,1,48,2304]{3,2,1,0:T(8,128)(2,1)S(1)}, u32[]{:S(2)}, u32[]{:S(2)}) collective-permute-start(bf16[1,1,48,2304]{3,2,1,0:T(8,128)(2,1)S(1)} %bitcast.168), channel_id=1, source_target_pairs={{0,8},{4,12},{8,0},{12,4},{16,24},{20,28},{24,16},{28,20},{1,9},{5... | collective-permute-start | bytes 663560 | tf_op jit(solution)/shard_map/ppermute | solution.py:84
  87.8 131.3 %all-gather.13.cloned.1.call-start = ((), (), s32[]{:S(2)}) async-start(), calls=%async_computation.4 | async-start | bytes 3932160 | tf_op jit(solution)/shard_map/all_gather | solution.py:963
  89.5 23.7 %copy-start = (bf16[8,1,96,2304]{3,2,1,0:T(8,128)(2,1)}, bf16[8,1,96,2304]{3,2,1,0:T(8,128)(2,1)S(1)}, u32[]{:S(2)}) copy-start(bf16[8,1,96,2304]{3,2,1,0:T(8,128)(2,1)S(1)} %constant_dynamic-update-slice_fusion.refs_3_.refs_10_) | copy-start | bytes 10616836
  89.5 20.2 %collective-permute-start.9 = (bf16[8,1,96,2304]{3,2,1,0:T(8,128)(2,1)S(1)}, bf16[8,1,96,2304]{3,2,1,0:T(8,128)(2,1)S(1)}, u32[]{:S(2)}, u32[]{:S(2)}) collective-permute-start(bf16[8,1,96,2304]{3,2,1,0:T(8,128)(2,1)S(1)} %constant_dynamic-update-slice_fusion.refs_3_.refs_10_), channel_id=1, source_target_pairs={{0,4},{4,0},{8,12},{12,8},{16,20},{20,16},{24,28},{28,24},{1,5},{5... | collective-permute-start | bytes 10616840 | tf_op jit(solution)/shard_map/ppermute | solution.py:84
  89.6 23.6 %copy-start.2 = (bf16[1,768,2,768]{3,2,1,0:T(2,128)(2,1)S(1)}, bf16[1,768,2,768]{3,2,1,0:T(2,128)(2,1)}, u32[]{:S(2)}) copy-start(bf16[1,768,2,768]{3,2,1,0:T(2,128)(2,1)} %get-tuple-element.248) | copy-start | bytes 7077892
  89.6 17.7 %collective-permute-start.11 = (bf16[2,1,48,2304]{3,2,1,0:T(8,128)(2,1)S(1)}, bf16[2,1,48,2304]{3,2,1,0:T(8,128)(2,1)S(1)}, u32[]{:S(2)}, u32[]{:S(2)}) collective-permute-start(bf16[2,1,48,2304]{3,2,1,0:T(8,128)(2,1)S(1)} %pad_maximum_fusion.13), channel_id=1, source_target_pairs={{0,8},{4,12},{8,0},{12,4},{16,24},{20,28},{24,16},{28,20},{1,9},{5... | collective-permute-start | bytes 1327112 | tf_op jit(solution)/shard_map/ppermute | solution.py:84
  91.2 18.5 %collective-permute-start.10 = (bf16[2,1,48,2304]{3,2,1,0:T(8,128)(2,1)S(1)}, bf16[2,1,48,2304]{3,2,1,0:T(8,128)(2,1)S(1)}, u32[]{:S(2)}, u32[]{:S(2)}) collective-permute-start(bf16[2,1,48,2304]{3,2,1,0:T(8,128)(2,1)S(1)} %pad_maximum_fusion.12), channel_id=1, source_target_pairs={{0,16},{4,20},{8,24},{12,28},{16,0},{20,4},{24,8},{28,12},{1,17},{... | collective-permute-start | bytes 1327112 | tf_op jit(solution)/shard_map/ppermute | solution.py:84
  113.2 12.4 %collective-permute-start.12 = (bf16[8,1,48,2304]{3,2,1,0:T(8,128)(2,1)}, bf16[8,1,48,2304]{3,2,1,0:T(8,128)(2,1)}, u32[]{:S(2)}, u32[]{:S(2)}) collective-permute-start(bf16[8,1,48,2304]{3,2,1,0:T(8,128)(2,1)} %constant_dynamic-update-slice_fusion.6.refs_5_.refs_8_), channel_id=1, source_target_pairs={{0,4},{4,0},{8,12},{12,8},{16,20},{20,16},{24,28},{28,24},{1,5},{5... | collective-permute-start | bytes 5308424 | tf_op jit(solution)/shard_map/ppermute | solution.py:84
  154.0 138.7 %all-gather.15.cloned.1.call-start = ((), (), s32[]{:S(2)}) async-start(), calls=%async_computation.5 | async-start | bytes 3932160 | tf_op jit(solution)/shard_map/all_gather | solution.py:1011
  219.1 221.6 %reduce-scatter.2.cloned.1.call-start = ((), (), s32[]{:S(2)}) async-start(), calls=%async_computation.1 | async-start | bytes 15925248 | tf_op jit(solution)/shard_map/reduce_scatter | solution.py:1000
  221.5 13.3 %collective-permute-start.13 = (bf16[4,4,104,768]{3,2,0,1:T(8,128)(2,1)S(1)}, bf16[4,4,104,768]{3,2,0,1:T(8,128)(2,1)}, u32[]{:S(2)}, u32[]{:S(2)}) collective-permute-start(bf16[4,4,104,768]{3,2,0,1:T(8,128)(2,1)S(1)} %copy.47), channel_id=1, source_target_pairs={{0,4},{4,0},{8,12},{12,8},{16,20},{20,16},{24,28},{28,24},{1,5},{5... | collective-permute-start | bytes 7667720 | tf_op jit(solution)/shard_map/ppermute | solution.py:84
  238.9 28.7 %copy-start.11 = (bf16[2,2,104,768]{3,2,0,1:T(8,128)(2,1)}, bf16[2,2,104,768]{3,2,0,1:T(8,128)(2,1)S(1)}, u32[]{:S(2)}) copy-start(bf16[2,2,104,768]{3,2,0,1:T(8,128)(2,1)S(1)} %get-tuple-element.244) | copy-start | bytes 1916932
  238.9 28.7 %collective-permute-start.14 = (bf16[2,2,104,768]{3,2,0,1:T(8,128)(2,1)}, bf16[2,2,104,768]{3,2,0,1:T(8,128)(2,1)S(1)}, u32[]{:S(2)}, u32[]{:S(2)}) collective-permute-start(bf16[2,2,104,768]{3,2,0,1:T(8,128)(2,1)} %get-tuple-element.247), channel_id=1, source_target_pairs={{0,8},{4,12},{8,0},{12,4},{16,24},{20,28},{24,16},{28,20},{1,9},{5... | collective-permute-start | bytes 1916936 | tf_op jit(solution)/shard_map/ppermute | solution.py:84
  240.4 27.2 %collective-permute-start.15 = (bf16[2,2,104,768]{3,2,0,1:T(8,128)(2,1)}, bf16[2,2,104,768]{3,2,0,1:T(8,128)(2,1)S(1)}, u32[]{:S(2)}, u32[]{:S(2)}) collective-permute-start(bf16[2,2,104,768]{3,2,0,1:T(8,128)(2,1)} %get-tuple-element.246), channel_id=1, source_target_pairs={{0,16},{4,20},{8,24},{12,28},{16,0},{20,4},{24,8},{28,12},{1,17},{... | collective-permute-start | bytes 1916936 | tf_op jit(solution)/shard_map/ppermute | solution.py:84
  267.6 25.0 %copy-start.31 = (bf16[2,2,104,768]{3,2,0,1:T(8,128)(2,1)}, bf16[2,2,104,768]{3,2,0,1:T(8,128)(2,1)S(1)}, u32[]{:S(2)}) copy-start(bf16[2,2,104,768]{3,2,0,1:T(8,128)(2,1)S(1)} %collective-permute-done.14) | copy-start | bytes 1916932
  267.6 25.0 %copy-start.33 = (bf16[2,2,104,768]{3,2,0,1:T(8,128)(2,1)}, bf16[2,2,104,768]{3,2,0,1:T(8,128)(2,1)S(1)}, u32[]{:S(2)}) copy-start(bf16[2,2,104,768]{3,2,0,1:T(8,128)(2,1)S(1)} %collective-permute-done.15) | copy-start | bytes 1916932
  268.5 24.2 %collective-permute-start.17 = (bf16[2,104,768]{2,1,0:T(8,128)(2,1)}, bf16[2,104,768]{2,1,0:T(8,128)(2,1)S(1)}, u32[]{:S(2)}, u32[]{:S(2)}) collective-permute-start(bf16[2,104,768]{2,1,0:T(8,128)(2,1)} %fusion.7), channel_id=1, source_target_pairs={{0,8},{4,12},{8,0},{12,4},{16,24},{20,28},{24,16},{28,20},{1,9},{5... | collective-permute-start | bytes 958472 | tf_op jit(solution)/shard_map/ppermute | solution.py:84
  269.8 22.8 %collective-permute-start.16 = (bf16[2,104,768]{2,1,0:T(8,128)(2,1)}, bf16[2,104,768]{2,1,0:T(8,128)(2,1)S(1)}, u32[]{:S(2)}, u32[]{:S(2)}) collective-permute-start(bf16[2,104,768]{2,1,0:T(8,128)(2,1)} %fusion.6), channel_id=1, source_target_pairs={{0,16},{4,20},{8,24},{12,28},{16,0},{20,4},{24,8},{28,12},{1,17},{... | collective-permute-start | bytes 958472 | tf_op jit(solution)/shard_map/ppermute | solution.py:84
  295.4 16.8 %collective-permute-start.18 = (bf16[4,4,104,768]{3,2,0,1:T(8,128)(2,1)S(1)}, bf16[4,4,104,768]{3,2,0,1:T(8,128)(2,1)S(1)}, u32[]{:S(2)}, u32[]{:S(2)}) collective-permute-start(bf16[4,4,104,768]{3,2,0,1:T(8,128)(2,1)S(1)} %copy.54), channel_id=1, source_target_pairs={{0,4},{4,0},{8,12},{12,8},{16,20},{20,16},{24,28},{28,24},{1,5},{5... | collective-permute-start | bytes 7667720 | tf_op jit(solution)/shard_map/ppermute | solution.py:84
  297.2 6.4 %collective-permute-start.19 = (bf16[104,768]{1,0:T(8,128)(2,1)S(1)}, bf16[104,768]{1,0:T(8,128)(2,1)S(1)}, u32[]{:S(2)}, u32[]{:S(2)}) collective-permute-start(bf16[104,768]{1,0:T(8,128)(2,1)S(1)} %get-tuple-element.268), channel_id=1, source_target_pairs={{0,3},{1,0},{2,1},{3,2},{4,7},{5,4},{6,5},{7,6},{8,11},{9,8},{10,9... | collective-permute-start | bytes 479240 | tf_op jit(solution)/shard_map/ppermute | solution.py:91
  298.0 14.3 %collective-permute-start.20 = (bf16[104,768]{1,0:T(8,128)(2,1)S(1)}, bf16[104,768]{1,0:T(8,128)(2,1)S(1)}, u32[]{:S(2)}, u32[]{:S(2)}) collective-permute-start(bf16[104,768]{1,0:T(8,128)(2,1)S(1)} %get-tuple-element.269), channel_id=1, source_target_pairs={{0,2},{1,3},{2,0},{3,1},{4,6},{5,7},{6,4},{7,5},{8,10},{9,11},{10,... | collective-permute-start | bytes 479240 | tf_op jit(solution)/shard_map/ppermute | solution.py:91
  298.4 13.9 %collective-permute-start.21 = (bf16[104,768]{1,0:T(8,128)(2,1)S(1)}, bf16[104,768]{1,0:T(8,128)(2,1)S(1)}, u32[]{:S(2)}, u32[]{:S(2)}) collective-permute-start(bf16[104,768]{1,0:T(8,128)(2,1)S(1)} %get-tuple-element.267), channel_id=1, source_target_pairs={{0,1},{1,2},{2,3},{3,0},{4,5},{5,6},{6,7},{7,4},{8,9},{9,10},{10,1... | collective-permute-start | bytes 479240 | tf_op jit(solution)/shard_map/ppermute | solution.py:91
  313.9 31.5 %collective-permute-start.22 = (bf16[2,2,104,768]{3,2,0,1:T(8,128)(2,1)}, bf16[2,2,104,768]{3,2,0,1:T(8,128)(2,1)S(1)}, u32[]{:S(2)}, u32[]{:S(2)}) collective-permute-start(bf16[2,2,104,768]{3,2,0,1:T(8,128)(2,1)} %get-tuple-element.242), channel_id=1, source_target_pairs={{0,8},{4,12},{8,0},{12,4},{16,24},{20,28},{24,16},{28,20},{1,9},{5... | collective-permute-start | bytes 1916936 | tf_op jit(solution)/shard_map/ppermute | solution.py:84
  315.4 30.1 %collective-permute-start.23 = (bf16[2,2,104,768]{3,2,0,1:T(8,128)(2,1)}, bf16[2,2,104,768]{3,2,0,1:T(8,128)(2,1)S(1)}, u32[]{:S(2)}, u32[]{:S(2)}) collective-permute-start(bf16[2,2,104,768]{3,2,0,1:T(8,128)(2,1)} %get-tuple-element.241), channel_id=1, source_target_pairs={{0,16},{4,20},{8,24},{12,28},{16,0},{20,4},{24,8},{28,12},{1,17},{... | collective-permute-start | bytes 1916936 | tf_op jit(solution)/shard_map/ppermute | solution.py:84
  317.9 27.5 %collective-permute-start.24 = (bf16[104,768]{1,0:T(8,128)(2,1)S(1)}, bf16[104,768]{1,0:T(8,128)(2,1)S(1)}, u32[]{:S(2)}, u32[]{:S(2)}) collective-permute-start(bf16[104,768]{1,0:T(8,128)(2,1)S(1)} %fusion.19), channel_id=1, source_target_pairs={{0,1},{1,2},{2,3},{3,0},{4,5},{5,6},{6,7},{7,4},{8,9},{9,10},{10,1... | collective-permute-start | bytes 479240 | tf_op jit(solution)/shard_map/ppermute | solution.py:91
  318.5 26.9 %collective-permute-start.25 = (bf16[104,768]{1,0:T(8,128)(2,1)S(1)}, bf16[104,768]{1,0:T(8,128)(2,1)S(1)}, u32[]{:S(2)}, u32[]{:S(2)}) collective-permute-start(bf16[104,768]{1,0:T(8,128)(2,1)S(1)} %fusion.19), channel_id=1, source_target_pairs={{0,2},{1,3},{2,0},{3,1},{4,6},{5,7},{6,4},{7,5},{8,10},{9,11},{10,... | collective-permute-start | bytes 479240 | tf_op jit(solution)/shard_map/ppermute | solution.py:91
  320.5 24.9 %collective-permute-start.26 = (bf16[104,768]{1,0:T(8,128)(2,1)S(1)}, bf16[104,768]{1,0:T(8,128)(2,1)S(1)}, u32[]{:S(2)}, u32[]{:S(2)}) collective-permute-start(bf16[104,768]{1,0:T(8,128)(2,1)S(1)} %fusion.19), channel_id=1, source_target_pairs={{0,3},{1,0},{2,1},{3,2},{4,7},{5,4},{6,5},{7,6},{8,11},{9,8},{10,9... | collective-permute-start | bytes 479240 | tf_op jit(solution)/shard_map/ppermute | solution.py:91
  345.5 32.1 %collective-permute-start.31 = (bf16[4,96,2304]{2,1,0:T(8,128)(2,1)}, bf16[4,96,2304]{2,1,0:T(8,128)(2,1)S(1)}, u32[]{:S(2)}, u32[]{:S(2)}) collective-permute-start(bf16[4,96,2304]{2,1,0:T(8,128)(2,1)} %get-tuple-element.205), channel_id=1, source_target_pairs={{0,4},{4,0},{8,12},{12,8},{16,20},{20,16},{24,28},{28,24},{1,5},{5... | collective-permute-start | bytes 5308424 | tf_op jit(solution)/shard_map/ppermute | solution.py:84
  345.6 17.3 %collective-permute-start.30 = (bf16[1,2,104,768]{3,2,1,0:T(8,128)(2,1)S(1)}, bf16[1,2,104,768]{3,2,1,0:T(8,128)(2,1)S(1)}, u32[]{:S(2)}, u32[]{:S(2)}) collective-permute-start(bf16[1,2,104,768]{3,2,1,0:T(8,128)(2,1)S(1)} %maximum_bitcast_fusion.1), channel_id=1, source_target_pairs={{0,16},{4,20},{8,24},{12,28},{16,0},{20,4},{24,8},{28,12},{1,17},{... | collective-permute-start | bytes 958472 | tf_op jit(solution)/shard_map/ppermute | solution.py:84
  346.8 17.3 %collective-permute-start.29 = (bf16[1,2,104,768]{3,2,1,0:T(8,128)(2,1)S(1)}, bf16[1,2,104,768]{3,2,1,0:T(8,128)(2,1)S(1)}, u32[]{:S(2)}, u32[]{:S(2)}) collective-permute-start(bf16[1,2,104,768]{3,2,1,0:T(8,128)(2,1)S(1)} %maximum_bitcast_fusion), channel_id=1, source_target_pairs={{0,8},{4,12},{8,0},{12,4},{16,24},{20,28},{24,16},{28,20},{1,9},{5... | collective-permute-start | bytes 958472 | tf_op jit(solution)/shard_map/ppermute | solution.py:84
  347.9 29.7 %collective-permute-start.28 = (bf16[2,104,768]{2,1,0:T(8,128)(2,1)S(1)}, bf16[2,104,768]{2,1,0:T(8,128)(2,1)S(1)}, u32[]{:S(2)}, u32[]{:S(2)}) collective-permute-start(bf16[2,104,768]{2,1,0:T(8,128)(2,1)S(1)} %fusion.12), channel_id=1, source_target_pairs={{0,8},{4,12},{8,0},{12,4},{16,24},{20,28},{24,16},{28,20},{1,9},{5... | collective-permute-start | bytes 958472 | tf_op jit(solution)/shard_map/ppermute | solution.py:84
  349.2 28.4 %collective-permute-start.27 = (bf16[2,104,768]{2,1,0:T(8,128)(2,1)S(1)}, bf16[2,104,768]{2,1,0:T(8,128)(2,1)S(1)}, u32[]{:S(2)}, u32[]{:S(2)}) collective-permute-start(bf16[2,104,768]{2,1,0:T(8,128)(2,1)S(1)} %fusion.11), channel_id=1, source_target_pairs={{0,16},{4,20},{8,24},{12,28},{16,0},{20,4},{24,8},{28,12},{1,17},{... | collective-permute-start | bytes 958472 | tf_op jit(solution)/shard_map/ppermute | solution.py:84
  377.6 17.0 %collective-permute-start.36 = (bf16[2,2,104,768]{3,2,1,0:T(8,128)(2,1)S(1)}, bf16[2,2,104,768]{3,2,1,0:T(8,128)(2,1)S(1)}, u32[]{:S(2)}, u32[]{:S(2)}) collective-permute-start(bf16[2,2,104,768]{3,2,1,0:T(8,128)(2,1)S(1)} %pad_maximum_fusion.6), channel_id=1, source_target_pairs={{0,8},{4,12},{8,0},{12,4},{16,24},{20,28},{24,16},{28,20},{1,9},{5... | collective-permute-start | bytes 1916936 | tf_op jit(solution)/shard_map/ppermute | solution.py:84
  378.7 17.7 %collective-permute-start.35 = (bf16[2,2,104,768]{3,2,1,0:T(8,128)(2,1)S(1)}, bf16[2,2,104,768]{3,2,1,0:T(8,128)(2,1)S(1)}, u32[]{:S(2)}, u32[]{:S(2)}) collective-permute-start(bf16[2,2,104,768]{3,2,1,0:T(8,128)(2,1)S(1)} %pad_maximum_fusion.5), channel_id=1, source_target_pairs={{0,16},{4,20},{8,24},{12,28},{16,0},{20,4},{24,8},{28,12},{1,17},{... | collective-permute-start | bytes 1916936 | tf_op jit(solution)/shard_map/ppermute | solution.py:84
  380.3 6.2 %collective-permute-start.32 = (bf16[104,768]{1,0:T(8,128)(2,1)S(1)}, bf16[104,768]{1,0:T(8,128)(2,1)S(1)}, u32[]{:S(2)}, u32[]{:S(2)}) collective-permute-start(bf16[104,768]{1,0:T(8,128)(2,1)S(1)} %get-tuple-element.265), channel_id=1, source_target_pairs={{0,3},{1,0},{2,1},{3,2},{4,7},{5,4},{6,5},{7,6},{8,11},{9,8},{10,9... | collective-permute-start | bytes 479240 | tf_op jit(solution)/shard_map/ppermute | solution.py:91
  380.4 14.2 %collective-permute-start.33 = (bf16[104,768]{1,0:T(8,128)(2,1)S(1)}, bf16[104,768]{1,0:T(8,128)(2,1)S(1)}, u32[]{:S(2)}, u32[]{:S(2)}) collective-permute-start(bf16[104,768]{1,0:T(8,128)(2,1)S(1)} %get-tuple-element.264), channel_id=1, source_target_pairs={{0,2},{1,3},{2,0},{3,1},{4,6},{5,7},{6,4},{7,5},{8,10},{9,11},{10,... | collective-permute-start | bytes 479240 | tf_op jit(solution)/shard_map/ppermute | solution.py:91
  380.9 13.7 %collective-permute-start.34 = (bf16[104,768]{1,0:T(8,128)(2,1)S(1)}, bf16[104,768]{1,0:T(8,128)(2,1)S(1)}, u32[]{:S(2)}, u32[]{:S(2)}) collective-permute-start(bf16[104,768]{1,0:T(8,128)(2,1)S(1)} %get-tuple-element.266), channel_id=1, source_target_pairs={{0,1},{1,2},{2,3},{3,0},{4,5},{5,6},{6,7},{7,4},{8,9},{9,10},{10,1... | collective-permute-start | bytes 479240 | tf_op jit(solution)/shard_map/ppermute | solution.py:91
  396.5 16.9 %collective-permute-start.40 = (bf16[8,2,104,768]{3,2,1,0:T(8,128)(2,1)S(1)}, bf16[8,2,104,768]{3,2,1,0:T(8,128)(2,1)S(1)}, u32[]{:S(2)}, u32[]{:S(2)}) collective-permute-start(bf16[8,2,104,768]{3,2,1,0:T(8,128)(2,1)S(1)} %constant_dynamic-update-slice_fusion.12.refs_1_), channel_id=1, source_target_pairs={{0,4},{4,0},{8,12},{12,8},{16,20},{20,16},{24,28},{28,24},{1,5},{5... | collective-permute-start | bytes 7667720 | tf_op jit(solution)/shard_map/ppermute | solution.py:84
  398.2 35.9 %collective-permute-start.43 = (bf16[2,96,2304]{2,1,0:T(8,128)(2,1)}, bf16[2,96,2304]{2,1,0:T(8,128)(2,1)S(1)}, u32[]{:S(2)}, u32[]{:S(2)}) collective-permute-start(bf16[2,96,2304]{2,1,0:T(8,128)(2,1)} %get-tuple-element.253), channel_id=1, source_target_pairs={{0,8},{4,12},{8,0},{12,4},{16,24},{20,28},{24,16},{28,20},{1,9},{5... | collective-permute-start | bytes 2654216 | tf_op jit(solution)/shard_map/ppermute | solution.py:84
  398.4 8.3 %collective-permute-start.37 = (bf16[104,768]{1,0:T(8,128)(2,1)S(1)}, bf16[104,768]{1,0:T(8,128)(2,1)S(1)}, u32[]{:S(2)}, u32[]{:S(2)}) collective-permute-start(bf16[104,768]{1,0:T(8,128)(2,1)S(1)} %fusion.16), channel_id=1, source_target_pairs={{0,1},{1,2},{2,3},{3,0},{4,5},{5,6},{6,7},{7,4},{8,9},{9,10},{10,1... | collective-permute-start | bytes 479240 | tf_op jit(solution)/shard_map/ppermute | solution.py:91
  400.0 13.3 %collective-permute-start.38 = (bf16[104,768]{1,0:T(8,128)(2,1)S(1)}, bf16[104,768]{1,0:T(8,128)(2,1)S(1)}, u32[]{:S(2)}, u32[]{:S(2)}) collective-permute-start(bf16[104,768]{1,0:T(8,128)(2,1)S(1)} %fusion.16), channel_id=1, source_target_pairs={{0,2},{1,3},{2,0},{3,1},{4,6},{5,7},{6,4},{7,5},{8,10},{9,11},{10,... | collective-permute-start | bytes 479240 | tf_op jit(solution)/shard_map/ppermute | solution.py:91
  403.0 10.3 %collective-permute-start.39 = (bf16[104,768]{1,0:T(8,128)(2,1)S(1)}, bf16[104,768]{1,0:T(8,128)(2,1)S(1)}, u32[]{:S(2)}, u32[]{:S(2)}) collective-permute-start(bf16[104,768]{1,0:T(8,128)(2,1)S(1)} %fusion.16), channel_id=1, source_target_pairs={{0,3},{1,0},{2,1},{3,2},{4,7},{5,4},{6,5},{7,6},{8,11},{9,8},{10,9... | collective-permute-start | bytes 479240 | tf_op jit(solution)/shard_map/ppermute | solution.py:91
  415.0 19.1 %collective-permute-start.42 = (bf16[1,2,104,768]{3,2,1,0:T(8,128)(2,1)S(1)}, bf16[1,2,104,768]{3,2,1,0:T(8,128)(2,1)S(1)}, u32[]{:S(2)}, u32[]{:S(2)}) collective-permute-start(bf16[1,2,104,768]{3,2,1,0:T(8,128)(2,1)S(1)} %maximum_bitcast_fusion.3), channel_id=1, source_target_pairs={{0,16},{4,20},{8,24},{12,28},{16,0},{20,4},{24,8},{28,12},{1,17},{... | collective-permute-start | bytes 958472 | tf_op jit(solution)/shard_map/ppermute | solution.py:84
  417.6 23.1 %collective-permute-start.41 = (bf16[1,2,104,768]{3,2,1,0:T(8,128)(2,1)S(1)}, bf16[1,2,104,768]{3,2,1,0:T(8,128)(2,1)S(1)}, u32[]{:S(2)}, u32[]{:S(2)}) collective-permute-start(bf16[1,2,104,768]{3,2,1,0:T(8,128)(2,1)S(1)} %maximum_bitcast_fusion.2), channel_id=1, source_target_pairs={{0,8},{4,12},{8,0},{12,4},{16,24},{20,28},{24,16},{28,20},{1,9},{5... | collective-permute-start | bytes 958472 | tf_op jit(solution)/shard_map/ppermute | solution.py:84
  440.8 25.9 %collective-permute-start.45 = (bf16[2,2,104,768]{3,2,1,0:T(8,128)(2,1)S(1)}, bf16[2,2,104,768]{3,2,1,0:T(8,128)(2,1)S(1)}, u32[]{:S(2)}, u32[]{:S(2)}) collective-permute-start(bf16[2,2,104,768]{3,2,1,0:T(8,128)(2,1)S(1)} %pad_maximum_fusion.8), channel_id=1, source_target_pairs={{0,8},{4,12},{8,0},{12,4},{16,24},{20,28},{24,16},{28,20},{1,9},{5... | collective-permute-start | bytes 1916936 | tf_op jit(solution)/shard_map/ppermute | solution.py:84
  441.2 25.5 %copy-start.26 = (bf16[104,768]{1,0:T(8,128)(2,1)S(1)}, bf16[104,768]{1,0:T(8,128)(2,1)}, u32[]{:S(2)}) copy-start(bf16[104,768]{1,0:T(8,128)(2,1)} %copy-done.25) | copy-start | bytes 479236
  441.2 25.5 %copy-start.28 = (bf16[104,768]{1,0:T(8,128)(2,1)S(1)}, bf16[104,768]{1,0:T(8,128)(2,1)}, u32[]{:S(2)}) copy-start(bf16[104,768]{1,0:T(8,128)(2,1)} %copy-done.27) | copy-start | bytes 479236
  441.2 25.4 %collective-permute-start.44 = (bf16[2,2,104,768]{3,2,1,0:T(8,128)(2,1)S(1)}, bf16[2,2,104,768]{3,2,1,0:T(8,128)(2,1)S(1)}, u32[]{:S(2)}, u32[]{:S(2)}) collective-permute-start(bf16[2,2,104,768]{3,2,1,0:T(8,128)(2,1)S(1)} %pad_maximum_fusion.7), channel_id=1, source_target_pairs={{0,16},{4,20},{8,24},{12,28},{16,0},{20,4},{24,8},{28,12},{1,17},{... | collective-permute-start | bytes 1916936 | tf_op jit(solution)/shard_map/ppermute | solution.py:84
  443.9 22.9 %copy-start.19 = (bf16[1,2,104,768]{3,2,1,0:T(8,128)(2,1)S(1)}, bf16[1,2,104,768]{3,2,1,0:T(8,128)(2,1)}, u32[]{:S(2)}) copy-start(bf16[1,2,104,768]{3,2,1,0:T(8,128)(2,1)} %copy-done.18) | copy-start | bytes 958468
  443.9 15.0 %collective-permute-start.47 = (bf16[96,2304]{1,0:T(8,128)(2,1)S(1)}, bf16[96,2304]{1,0:T(8,128)(2,1)S(1)}, u32[]{:S(2)}, u32[]{:S(2)}) collective-permute-start(bf16[96,2304]{1,0:T(8,128)(2,1)S(1)} %get-tuple-element.228), channel_id=1, source_target_pairs={{0,1},{1,2},{2,3},{3,0},{4,5},{5,6},{6,7},{7,4},{8,9},{9,10},{10,1... | collective-permute-start | bytes 1327112 | tf_op jit(solution)/shard_map/ppermute | solution.py:91
  445.4 21.2 %collective-permute-start.46 = (bf16[96,2304]{1,0:T(8,128)(2,1)S(1)}, bf16[96,2304]{1,0:T(8,128)(2,1)S(1)}, u32[]{:S(2)}, u32[]{:S(2)}) collective-permute-start(bf16[96,2304]{1,0:T(8,128)(2,1)S(1)} %get-tuple-element.227), channel_id=1, source_target_pairs={{0,3},{1,0},{2,1},{3,2},{4,7},{5,4},{6,5},{7,6},{8,11},{9,8},{10,9... | collective-permute-start | bytes 1327112 | tf_op jit(solution)/shard_map/ppermute | solution.py:91
  466.9 4.9 collective-permute-start.48
  473.2 22.9 %collective-permute-start.49 = (bf16[96,2304]{1,0:T(8,128)(2,1)}, bf16[96,2304]{1,0:T(8,128)(2,1)}, u32[]{:S(2)}, u32[]{:S(2)}) collective-permute-start(bf16[96,2304]{1,0:T(8,128)(2,1)} %get-tuple-element.237), channel_id=1, source_target_pairs={{0,2},{1,3},{2,0},{3,1},{4,6},{5,7},{6,4},{7,5},{8,10},{9,11},{10,... | collective-permute-start | bytes 1327112 | tf_op jit(solution)/shard_map/ppermute | solution.py:91
  475.3 22.5 %collective-permute-start.50 = (bf16[1,96,2304]{2,1,0:T(8,128)(2,1)S(1)}, bf16[1,96,2304]{2,1,0:T(8,128)(2,1)}, u32[]{:S(2)}, u32[]{:S(2)}) collective-permute-start(bf16[1,96,2304]{2,1,0:T(8,128)(2,1)S(1)} %add_convert_fusion.10), channel_id=1, source_target_pairs={{0,16},{4,20},{8,24},{12,28},{16,0},{20,4},{24,8},{28,12},{1,17},{... | collective-permute-start | bytes 1327112 | tf_op jit(solution)/shard_map/ppermute | solution.py:84
  (39 other events, 245.8 us)
Sparse Core Ops, SparseCore 0:
  38.7 46.4 all-gather.8
  87.9 66.0 all-gather.10
  155.6 63.4 all-gather.12
  220.5 62.1 all-gather.14
  293.6 136.7 reduce-scatter.1
